TPU v7x, 32 devices: a whole 2x2x4 slice. The times are simulated.
32 devices in a mesh: dp: 8 (over z, x), section: 4 (over y, core).
Axes of the slice: x: 2, y: 2, z: 4, core: 2. Of those that a mesh axis runs over, the one named last changes fastest.
Arguments:
- patches: bfloat16 [256, 1600], P(('dp', 'section')), may hold values from -6 to 6
- gain: float32 [1600], replicated, may hold values from 0.5 to 2
- expand_weight: bfloat16 [1600, 8192], P('dp', 'section'), may hold values from -0.15625 to 0.15625
- project_weight: bfloat16 [8192, 1600], P('section', 'dp'), may hold values from -0.0625 to 0.0625
- counts: int32 [8, 4], P('dp'), may hold values from 1 to 8
- positions: int32 [32, 8], P(('dp', 'section')), may hold values from 0 to 15, as said below
- text: bfloat16 [512, 1600], P(('dp', 'section')), may hold values from -6 to 6
- cotangent: bfloat16 [512, 1600], P(('dp', 'section')), may hold values from -6 to 6
Outputs:
- embedded: bfloat16 [512, 1600], P(('dp', 'section'))
- grad_rows: bfloat16 [256, 1600], P(('dp', 'section'))
- expand_grad: bfloat16 [1600, 8192], P(None, 'section')
- project_grad: bfloat16 [8192, 1600], P('section')
Inputs may be any that keep to these rules, and one draw needn't show every extreme that they name: `positions`: within each row the values are distinct.
All inputs are finite; a program needn't handle non-finite values.
Results may differ from a plain program's by a relative error of at most 0.015.
Values may be sent and summed in bfloat16 or wider, within the bound.
No kernel may reach another device: no remote copies, remote signals or barrier semaphores. Data moves between devices by JAX's collectives and lax.ppermute only.
A program may use at most 64 MiB of HBM per device.

v0:
```python
import functools

import jax
import jax.numpy as jnp
from jax import lax
from jax.experimental import pallas as pl
from jax.experimental.pallas import tpu as pltpu
from jax.sharding import PartitionSpec as P


def gelu_pair(values):
    coeff = 0.7978845608
    inner = coeff * (values + 0.044715 * values * values * values)
    tangent = jnp.tanh(inner)
    activated = 0.5 * values * (1.0 + tangent)
    derivative = 0.5 * (1.0 + tangent) + 0.5 * values * (1.0 - tangent * tangent) * coeff * (
        1.0 + 3.0 * 0.044715 * values * values
    )
    return (activated, derivative)


def gather_weights_plan(
    patches, gain, expand_weight, project_weight, counts, positions, text, cotangent
):
    sections = lax.axis_size("section")
    slot_count = patches.shape[0]
    features = patches.shape[1]
    capacity = slot_count // sections
    inputs = patches.astype(jnp.float32)
    inv_rms = lax.rsqrt(jnp.mean(inputs * inputs, axis=-1, keepdims=True) + 1e-06)
    normed = (inputs * inv_rms * gain).astype(jnp.bfloat16)
    gathered = lax.all_gather(normed, "section", axis=0, tiled=True)
    expand_full, project_full = (
        lax.all_gather(expand_weight, "dp", axis=0, tiled=True),
        lax.all_gather(project_weight, "dp", axis=1, tiled=True),
    )
    preact = jnp.dot(gathered, expand_full, preferred_element_type=jnp.float32)
    activated, derivative = gelu_pair(preact)
    hidden = activated.astype(jnp.bfloat16)
    row_block = hidden
    mixed = lax.psum_scatter(
        jnp.dot(row_block, project_full, preferred_element_type=jnp.float32).astype(jnp.bfloat16),
        "section",
        scatter_dimension=0,
        tiled=True,
    ).astype(jnp.float32)
    out_rows = (inputs + mixed).astype(jnp.bfloat16)
    arrived = lax.all_to_all(out_rows, "section", split_axis=0, concat_axis=0, tiled=True)
    section_id = lax.axis_index("section")
    arrival = jnp.arange(slot_count, dtype=jnp.int32)
    source = arrival // capacity
    slot_index = section_id * capacity + arrival % capacity
    is_live = (slot_index < counts[0][source])[:, None]
    targets = positions[0]
    current = text[targets]
    embedded = text.at[targets].set(jnp.where(is_live, arrived, current))
    picked = jnp.where(is_live, cotangent[targets], jnp.zeros_like(current))
    collected = lax.all_gather(picked, "section", axis=0, tiled=True)
    grad_all = (
        collected.reshape(sections, sections, capacity, features)
        .transpose(1, 0, 2, 3)
        .reshape(sections * slot_count, features)
    )
    returned = lax.dynamic_slice_in_dim(grad_all, section_id * slot_count, slot_count, 0)
    grad_own = returned.astype(jnp.float32)
    project_local = lax.dot_general(
        hidden, grad_all, (((0,), (0,)), ((), ())), preferred_element_type=jnp.float32
    )
    grad_hidden = lax.dot_general(
        grad_all, project_full, (((1,), (1,)), ((), ())), preferred_element_type=jnp.float32
    )
    grad_pre = (grad_hidden * derivative).astype(jnp.bfloat16)
    row_block = grad_pre
    grad_normed = lax.psum_scatter(
        lax.dot_general(
            row_block, expand_full, (((1,), (1,)), ((), ())), preferred_element_type=jnp.float32
        ).astype(jnp.bfloat16),
        "section",
        scatter_dimension=0,
        tiled=True,
    ).astype(jnp.float32)
    expand_local = lax.dot_general(
        gathered, grad_pre, (((0,), (0,)), ((), ())), preferred_element_type=jnp.float32
    )
    project_total, expand_total = (
        lax.psum(project_local.astype(jnp.bfloat16), "dp").astype(jnp.float32),
        lax.psum(expand_local.astype(jnp.bfloat16), "dp").astype(jnp.float32),
    )
    scaled_grad = grad_normed * gain
    centred = jnp.mean(scaled_grad * inputs, axis=-1, keepdims=True)
    grad_rows = (grad_own + inv_rms * scaled_grad - inputs * inv_rms**3 * centred).astype(
        jnp.bfloat16
    )
    return (
        embedded,
        grad_rows,
        expand_total.astype(jnp.bfloat16),
        project_total.astype(jnp.bfloat16),
    )


def bit_steps(size):
    steps = []
    step = size // 2
    while step >= 1:
        steps.append(step)
        step //= 2
    return steps


def swap(array, axis, step):
    size = lax.axis_size(axis)
    return lax.ppermute(array, axis, [(i, i ^ step) for i in range(size)])


def masked_steps(index, steps):
    mask = 0
    for place, step in enumerate(steps):
        mask = mask + ((index >> place) & 1) * step
    return mask


VMEM_SPEC = pl.BlockSpec(memory_space=pltpu.VMEM)
SMEM_SPEC = pl.BlockSpec(memory_space=pltpu.SMEM)


def log2(value):
    return value.bit_length() - 1


def landing(place_ref, count_ref, section, slots, capacity, length):
    row = lax.broadcasted_iota(jnp.int32, (slots, length), 0)
    column = lax.broadcasted_iota(jnp.int32, (slots, length), 1)
    spot = jnp.full((slots, length), -1, jnp.int32)
    for q in range(slots):
        live = section * capacity + q % capacity < count_ref[0, q // capacity]
        spot = jnp.where(row == q, jnp.where(live, place_ref[0, q], -1), spot)
    return (spot == column).astype(jnp.float32)


def fetch(copies):
    for copy in copies:
        copy.start()
    for copy in copies:
        copy.wait()


def pick_kernel(
    capacity, counts_at, places_at, patches_at, cotangent_at, pair_ref,
    count_ref, place_ref, patch_ref, cotangent_ref, sems,
):
    ends = (
        (counts_at, count_ref), (places_at, place_ref),
        (patches_at, patch_ref), (cotangent_at, cotangent_ref),
    )
    fetch([pltpu.make_async_copy(a, b, sems.at[i]) for i, (a, b) in enumerate(ends)])
    slots = patch_ref.shape[0]
    section = lax.axis_index("section")
    chooser = landing(
        place_ref, count_ref, section, slots, capacity, cotangent_ref.shape[0]
    ).astype(jnp.bfloat16)
    picked = jnp.dot(chooser, cotangent_ref[...], preferred_element_type=jnp.float32)
    pair_ref[0] = jnp.concatenate(
        [patch_ref[...].astype(jnp.float32), picked], axis=0
    ).astype(jnp.bfloat16)


def repack_kernel(expand_at, project_at, *refs):
    blocks, sems = refs[:-1], refs[-1]
    units = blocks[0].shape[2]
    copies = []
    for i, block in enumerate(blocks):
        start = pl.multiple_of((lax.axis_index("dp") ^ (i + 1)) * units, 128)
        for k, source in enumerate((expand_at, project_at)):
            copies.append(
                pltpu.make_async_copy(
                    source.at[:, pl.ds(start, units)], block.at[k], sems.at[2 * i + k]
                )
            )
    fetch(copies)


def order_kernel(
    sections, capacity, dp_steps, section_steps,
    me_ref, near_ref, far_ref, gain_ref, normed_ref, grad_ref, extra_ref,
):
    rows = normed_ref.shape[0]
    slots = sections * capacity
    half = near_ref.shape[0] * near_ref.shape[1]
    me_dp, me_section = me_ref[0], me_ref[1]
    column = lax.broadcasted_iota(jnp.int32, (8, half), 1)
    row = lax.broadcasted_iota(jnp.int32, (rows, half), 0)
    kind = column & (2 * slots - 1)
    slot = kind & (slots - 1)
    inputs = grad = None
    for side, ref in enumerate((near_ref, far_ref)):
        block = (column >> log2(2 * slots)) + side * (half // (2 * slots))
        source_dp = me_dp ^ masked_steps(block, dp_steps)
        source_section = me_section ^ masked_steps(block >> len(dp_steps), section_steps)
        patch_at = (source_dp * sections + source_section) * slots + slot
        grad_at = (
            (source_dp * sections + (slot >> log2(capacity))) * slots
            + source_section * capacity
            + (slot & (capacity - 1))
        )
        patch_at = jnp.where(kind < slots, patch_at, -1)[:1]
        grad_at = jnp.where(kind >= slots, grad_at, -1)[:1]
        values = ref[...].reshape(half, ref.shape[2])
        chosen = (row == patch_at).astype(jnp.float32).astype(jnp.bfloat16)
        found = jnp.dot(chosen, values, preferred_element_type=jnp.float32)
        inputs = found if inputs is None else inputs + found
        chosen = (row == grad_at).astype(jnp.float32).astype(jnp.bfloat16)
        found = jnp.dot(chosen, values, preferred_element_type=jnp.float32)
        grad = found if grad is None else grad + found
    inv_rms = lax.rsqrt(jnp.mean(inputs * inputs, axis=-1, keepdims=True) + 1e-06)
    normed_ref[...] = (inputs * inv_rms * gain_ref[...]).astype(jnp.bfloat16)
    grad = grad.astype(jnp.bfloat16)
    grad_ref[...] = grad
    mine = lax.broadcasted_iota(jnp.int32, (slots, rows), 0)
    every = lax.broadcasted_iota(jnp.int32, (slots, rows), 1)
    coming_at = (
        (me_dp * sections + (mine >> log2(capacity))) * slots
        + me_section * capacity
        + (mine & (capacity - 1))
    )
    own_at = (me_dp * sections + me_section) * slots + mine
    coming = jnp.dot(
        (every == coming_at).astype(jnp.float32).astype(jnp.bfloat16),
        inputs.astype(jnp.bfloat16),
        preferred_element_type=jnp.float32,
    )
    own = jnp.dot(
        (every == own_at).astype(jnp.float32).astype(jnp.bfloat16),
        grad,
        preferred_element_type=jnp.float32,
    )
    extra_ref[...] = jnp.concatenate([coming, own], axis=0)


def hidden_kernel(normed_ref, grad_ref, expand_at, project_at, *refs):
    blocks = refs[:-5]
    hidden_ref, pre_ref, expand_ref, project_ref, sems = refs[-5:]
    part = expand_at.shape[0]
    units = hidden_ref.shape[2]
    me = lax.axis_index("dp")
    copies = []
    for k, (source, whole) in enumerate(((expand_at, expand_ref), (project_at, project_ref))):
        own = source.at[:, pl.ds(pl.multiple_of(me * units, 128), units)]
        for i, block in enumerate((own, *(block.at[k] for block in blocks))):
            at = pl.ds(pl.multiple_of((me ^ i) * part, 8), part)
            copies.append(
                pltpu.make_async_copy(
                    block, whole.at[at, :], sems.at[k * (len(blocks) + 1) + i]
                )
            )
    fetch(copies)
    preact = jnp.dot(normed_ref[...], expand_ref[...], preferred_element_type=jnp.float32)
    activated, derivative = gelu_pair(preact)
    hidden_ref[0] = activated.astype(jnp.bfloat16)
    grad_hidden = jnp.dot(grad_ref[...], project_ref[...], preferred_element_type=jnp.float32)
    pre_ref[0] = (grad_hidden * derivative).astype(jnp.bfloat16)


def share_kernel(
    sections, capacity, steps,
    me_ref, hidden_ref, pre_ref, expand_ref, project_ref, keep_ref, send_ref,
):
    rows = hidden_ref.shape[1]
    slots = sections * capacity
    row = lax.broadcasted_iota(jnp.int32, (rows, rows), 0)
    column = lax.broadcasted_iota(jnp.int32, (rows, rows), 1)
    inside = row & (slots - 1)
    replica = (row >> log2(slots)) & (rows // (sections * slots) - 1)
    away = row >> log2(rows // sections)
    goal = me_ref[1] ^ masked_steps(away, steps[::-1])
    base = replica * (slots * sections)
    mixed_from = (
        base + (inside >> log2(capacity)) * slots + goal * capacity + (inside & (capacity - 1))
    )
    normed_from = base + goal * slots + inside
    for k, (ref, source, weight_ref) in enumerate(
        ((hidden_ref, mixed_from, project_ref), (pre_ref, normed_from, expand_ref))
    ):
        turn = (column == source).astype(jnp.float32).astype(jnp.bfloat16)
        turned = jnp.dot(turn, ref[0], preferred_element_type=jnp.float32).astype(jnp.bfloat16)
        share = lax.dot_general(
            turned, weight_ref[...], (((1,), (1,)), ((), ())), preferred_element_type=jnp.float32
        )
        share = share.reshape(2, *keep_ref.shape[1:])
        keep_ref[k] = share[0]
        send_ref[k] = share[1].astype(jnp.bfloat16)


def halve_kernel(keep_ref, got_ref, next_keep_ref, next_send_ref):
    half = next_keep_ref.shape[1]
    total = keep_ref[...] + got_ref[...].astype(jnp.float32)
    next_keep_ref[...] = total[:, :half]
    next_send_ref[...] = total[:, half:].astype(jnp.bfloat16)


def address_kernel(keep_ref, got_ref, out_ref):
    total = keep_ref[...] + got_ref[...].astype(jnp.float32)
    for d in range(out_ref.shape[0]):
        out_ref[d] = jnp.concatenate([total[0, d], total[1, d]], axis=0).astype(jnp.bfloat16)


def weight_grad_kernel(me_ref, hidden_ref, pre_ref, normed_ref, grad_ref, *refs):
    expand_ref, project_ref = refs[-2:]
    contract = (((0,), (0,)), ((), ()))
    expand_ref[...] = lax.dot_general(
        normed_ref[...], pre_ref[0], contract, preferred_element_type=jnp.float32
    ).astype(jnp.bfloat16)
    project_ref[...] = lax.dot_general(
        grad_ref[...], hidden_ref[0], contract, preferred_element_type=jnp.float32
    ).astype(jnp.bfloat16)


def finish_kernel(
    capacity,
    me_ref, count_ref, place_ref, tail_ref, extra_ref, patch_ref, text_ref, gain_ref,
    embedded_ref, grad_rows_ref,
):
    slots = patch_ref.shape[0]
    total = tail_ref[0].astype(jnp.float32)
    for d in range(1, tail_ref.shape[0]):
        total += tail_ref[d].astype(jnp.float32)
    mixed, grad_normed = total[:slots], total[slots:]
    out_rows = (extra_ref[:slots, :] + mixed).astype(jnp.bfloat16)
    length = text_ref.shape[0]
    chooser = landing(place_ref, count_ref, me_ref[1], slots, capacity, length)
    contract = (((0,), (0,)), ((), ()))
    placed = lax.dot_general(
        chooser.astype(jnp.bfloat16), out_rows, contract, preferred_element_type=jnp.float32
    )
    taken = lax.dot_general(
        chooser.astype(jnp.bfloat16), jnp.ones((slots, 128), jnp.bfloat16),
        contract, preferred_element_type=jnp.float32,
    )[:, :1]
    embedded_ref[...] = jnp.where(
        taken > 0.5, placed, text_ref[...].astype(jnp.float32)
    ).astype(jnp.bfloat16)
    inputs = patch_ref[...].astype(jnp.float32)
    inv_rms = lax.rsqrt(jnp.mean(inputs * inputs, axis=-1, keepdims=True) + 1e-06)
    scaled_grad = grad_normed * gain_ref[...]
    centred = jnp.mean(scaled_grad * inputs, axis=-1, keepdims=True)
    grad_rows_ref[...] = (
        extra_ref[slots:, :] + inv_rms * scaled_grad - inputs * (inv_rms**3 * centred)
    ).astype(jnp.bfloat16)


def weight_grads(
    me, hidden, pre, first_index, hidden_steps, pre_steps, normed, grad_all, width, before
):
    count, rows, units = hidden.shape
    features = normed.shape[1]

    def column(steps):
        return lambda i, me_ref: (0, me_ref[0] ^ masked_steps(first_index + i, steps))

    whole = pl.BlockSpec((rows, features), lambda i, me_ref: (0, 0))
    block = pl.BlockSpec((1, rows, units), lambda i, me_ref: (i, 0, 0))
    return pl.pallas_call(
        weight_grad_kernel,
        grid_spec=pltpu.PrefetchScalarGridSpec(
            num_scalar_prefetch=1,
            grid=(count,),
            in_specs=[block, block, whole, whole]
            + [pl.BlockSpec(memory_space=pl.ANY)] * len(before),
            out_specs=[
                pl.BlockSpec((features, units), column(pre_steps)),
                pl.BlockSpec((features, units), column(hidden_steps)),
            ],
        ),
        out_shape=[jax.ShapeDtypeStruct((features, width), jnp.bfloat16)] * 2,
        input_output_aliases={5: 0, 6: 1} if before else {},
        compiler_params=pltpu.CompilerParams(
            dimension_semantics=("arbitrary",), vmem_limit_bytes=12 << 20
        ),
        cost_estimate=pl.CostEstimate(
            flops=4 * count * rows * features * units,
            bytes_accessed=4 * count * units * features + 4 * rows * features,
            transcendentals=0,
        ),
    )(me, hidden, pre, normed, grad_all, *before)


def call(kernel, out_shape, smem, vmem, scratch=()):
    single = not isinstance(out_shape, (list, tuple))
    return pl.pallas_call(
        kernel,
        out_shape=out_shape,
        in_specs=[SMEM_SPEC] * len(smem) + [VMEM_SPEC] * len(vmem),
        out_specs=VMEM_SPEC if single else [VMEM_SPEC] * len(out_shape),
        scratch_shapes=scratch,
        compiler_params=pltpu.CompilerParams(vmem_limit_bytes=12 << 20),
    )(*smem, *vmem)


def move_rows_plan(
    patches, gain, expand_weight, project_weight, counts, positions, text, cotangent
):
    sections = lax.axis_size("section")
    replicas = lax.axis_size("dp")
    devices = sections * replicas
    slots, features = patches.shape
    part, width = expand_weight.shape
    units = width // replicas
    capacity = slots // sections
    rows = devices * slots
    dp_steps, section_steps = bit_steps(replicas), bit_steps(sections)
    me = jnp.stack([lax.axis_index("dp"), lax.axis_index("section")]).astype(jnp.int32)
    gain = gain.reshape(1, features)
    project_turned = project_weight.T
    kept, wide = jnp.bfloat16, jnp.float32
    shape = jax.ShapeDtypeStruct

    hbm = pl.BlockSpec(memory_space=pltpu.HBM)

    def in_hbm(*arrays):
        return [pltpu.with_memory_space_constraint(array, pltpu.HBM) for array in arrays]

    held = pl.pallas_call(
        functools.partial(pick_kernel, capacity),
        out_shape=shape((1, 2 * slots, features), kept),
        in_specs=[hbm] * 4,
        out_specs=VMEM_SPEC,
        scratch_shapes=[
            pltpu.SMEM(counts.shape, counts.dtype),
            pltpu.SMEM(positions.shape, positions.dtype),
            pltpu.VMEM(patches.shape, kept),
            pltpu.VMEM(cotangent.shape, kept),
            pltpu.SemaphoreType.DMA((4,)),
        ],
        compiler_params=pltpu.CompilerParams(vmem_limit_bytes=12 << 20),
    )(*in_hbm(counts, positions, patches, cotangent))
    blocks = pl.pallas_call(
        repack_kernel,
        out_shape=[shape((2, part, units), kept)] * (replicas - 1),
        in_specs=[hbm] * 2,
        out_specs=[VMEM_SPEC] * (replicas - 1),
        scratch_shapes=[pltpu.SemaphoreType.DMA((2 * replicas - 2,))],
        compiler_params=pltpu.CompilerParams(vmem_limit_bytes=12 << 20),
    )(*in_hbm(expand_weight, project_turned))
    arrived = []
    for distance in range(1, replicas):
        arrived.append(swap(blocks[distance - 1], "dp", distance))

    exchanges = [("dp", step) for step in dp_steps] + [("section", step) for step in section_steps]
    for axis, step in exchanges:
        got = swap(held, axis, step)
        if held.shape[0] < devices // 2:
            held = jnp.concatenate([held, got], axis=0)
    normed, grad_all, extra = call(
        functools.partial(order_kernel, sections, capacity, dp_steps, section_steps),
        [shape((rows, features), kept), shape((rows, features), kept), shape((2 * slots, features), wide)],
        (me,), (held, got, gain),
    )

    hidden_near, pre_near, expand_slice, project_slice = pl.pallas_call(
        hidden_kernel,
        out_shape=[shape((1, rows, units), kept)] * 2 + [shape((features, units), kept)] * 2,
        in_specs=[VMEM_SPEC] * 2 + [hbm] * 2 + [pl.BlockSpec(memory_space=pl.ANY)] * len(arrived),
        out_specs=[VMEM_SPEC] * 4,
        scratch_shapes=[pltpu.SemaphoreType.DMA((2 * replicas,))],
        compiler_params=pltpu.CompilerParams(vmem_limit_bytes=12 << 20),
    )(normed, grad_all, *in_hbm(expand_weight, project_turned), *arrived)

    tail_steps = section_steps[::-1]
    keep, send = call(
        functools.partial(share_kernel, sections, capacity, tail_steps),
        [shape((2, devices // 2, slots, features), kind) for kind in (wide, kept)],
        (me,), (hidden_near, pre_near, expand_slice, project_slice),
    )
    for place, step in enumerate(tail_steps):
        got = swap(send, "section", step)
        if place < len(tail_steps) - 1:
            half = (2, send.shape[1] // 2, slots, features)
            keep, send = call(
                halve_kernel, [shape(half, wide), shape(half, kept)], (), (keep, got)
            )
    tail = call(address_kernel, shape((replicas, 2 * slots, features), kept), (), (keep, got))
    tail = lax.all_to_all(tail, "dp", split_axis=0, concat_axis=0, tiled=True)

    hidden_steps, pre_steps = dp_steps, dp_steps[-1:] + dp_steps[:-1]
    for hidden_step, pre_step in zip(hidden_steps, pre_steps):
        hidden_far = swap(hidden_near, "dp", hidden_step)
        pre_far = swap(pre_near, "dp", pre_step)
        if hidden_near.shape[0] < replicas // 2:
            hidden_near = jnp.concatenate([hidden_near, hidden_far], axis=0)
            pre_near = jnp.concatenate([pre_near, pre_far], axis=0)

    grads = weight_grads(
        me, hidden_near, pre_near, 0,
        hidden_steps, pre_steps, normed, grad_all, width, (),
    )
    expand_grad, project_grad = weight_grads(
        me, hidden_far, pre_far, replicas // 2,
        hidden_steps, pre_steps, normed, grad_all, width, grads,
    )
    embedded, grad_rows = call(
        functools.partial(finish_kernel, capacity),
        [shape(text.shape, kept), shape(patches.shape, kept)],
        (me, counts, positions), (tail, extra, patches, text, gain),
    )
    return (embedded, grad_rows, expand_grad, project_grad.T)


def power_of_two(value):
    return value > 0 and value & (value - 1) == 0


def shards(patches, gain, expand_weight, project_weight, counts, positions, text, cotangent):
    replicas, sections = lax.axis_size("dp"), lax.axis_size("section")
    slots, features = patches.shape
    width = expand_weight.shape[1]
    rows = replicas * sections * slots
    fits = rows * (features + width) <= features * width
    even = (
        all(power_of_two(n) for n in (replicas, sections, slots))
        and replicas > 1
        and sections > 1
        and slots % 8 == 0
        and width % (128 * replicas) == 0
    )
    if fits and even:
        plan = move_rows_plan
    else:
        plan = gather_weights_plan
    return plan(
        patches, gain, expand_weight, project_weight, counts, positions, text, cotangent
    )


def solution(mesh):
    return jax.shard_map(
        shards,
        mesh=mesh,
        in_specs=(
            P(("dp", "section"), None),
            P(),
            P("dp", "section"),
            P("section", "dp"),
            P("dp", None),
            P(("dp", "section"), None),
            P(("dp", "section"), None),
            P(("dp", "section"), None),
        ),
        out_specs=(
            P(("dp", "section"), None),
            P(("dp", "section"), None),
            P(None, "section"),
            P("section", None),
        ),
        check_vma=False,
    )
```

profile of v0, /device:TPU:0, one launch (start us, length us, event | category | flops | bytes accessed | tf_op | source)
XLA Modules:
  0.0 131.8 jit_solution(2168828828323462901)
XLA Ops:
  0.6 1.0 shard_map.111
  1.6 4.1 %collective-permute-start = (bf16[1,16,1600]{2,1,0:T(8,128)(2,1)S(1)}, bf16[1,16,1600]{2,1,0:T(8,128)(2,1)S(1)}, u32[]{:S(2)}, u32[]{:S(2)}) collective-permute-start(bf16[1,16,1600]{2,1,0:T(8,128)(2,1)S(1)} %shard_map.111), channel_id=1, source_target_pairs={{0,16},{4,20},{8,24},{12,28},{16,0},{20,4},{24,8},{28,12},{1,17},{... | collective-permute-start | bytes 153608 | tf_op jit(solution)/shard_map/ppermute | solution.py:113
  5.8 2.7 %collective-permute-done = bf16[1,16,1600]{2,1,0:T(8,128)(2,1)S(1)} collective-permute-done((bf16[1,16,1600]{2,1,0:T(8,128)(2,1)S(1)}, bf16[1,16,1600]{2,1,0:T(8,128)(2,1)S(1)}, u32[]{:S(2)}, u32[]{:S(2)}) %collective-permute-start) | collective-permute-done | bytes 51232 | tf_op jit(solution)/shard_map/ppermute | solution.py:113
  8.5 1.4 %collective-permute-start.1 = (bf16[2,16,1600]{2,1,0:T(8,128)(2,1)S(1)}, bf16[2,16,1600]{2,1,0:T(8,128)(2,1)S(1)}, u32[]{:S(2)}, u32[]{:S(2)}) collective-permute-start(bf16[2,16,1600]{2,1,0:T(8,128)(2,1)S(1)} %pad_maximum_fusion.4), channel_id=1, source_target_pairs={{0,8},{4,12},{8,0},{12,4},{16,24},{20,28},{24,16},{28,20},{1,9},{5... | collective-permute-start | bytes 307208 | tf_op jit(solution)/shard_map/ppermute | solution.py:113
  9.9 3.4 %collective-permute-done.1 = bf16[2,16,1600]{2,1,0:T(8,128)(2,1)S(1)} collective-permute-done((bf16[2,16,1600]{2,1,0:T(8,128)(2,1)S(1)}, bf16[2,16,1600]{2,1,0:T(8,128)(2,1)S(1)}, u32[]{:S(2)}, u32[]{:S(2)}) %collective-permute-start.1) | collective-permute-done | bytes 102432 | tf_op jit(solution)/shard_map/ppermute | solution.py:113
  13.3 1.8 %collective-permute-start.2 = (bf16[4,16,1600]{2,1,0:T(8,128)(2,1)S(1)}, bf16[4,16,1600]{2,1,0:T(8,128)(2,1)S(1)}, u32[]{:S(2)}, u32[]{:S(2)}) collective-permute-start(bf16[4,16,1600]{2,1,0:T(8,128)(2,1)S(1)} %pad_maximum_fusion.3), channel_id=1, source_target_pairs={{0,4},{4,0},{8,12},{12,8},{16,20},{20,16},{24,28},{28,24},{1,5},{5... | collective-permute-start | bytes 614408 | tf_op jit(solution)/shard_map/ppermute | solution.py:113
  15.1 4.1 %collective-permute-done.2 = bf16[4,16,1600]{2,1,0:T(8,128)(2,1)S(1)} collective-permute-done((bf16[4,16,1600]{2,1,0:T(8,128)(2,1)S(1)}, bf16[4,16,1600]{2,1,0:T(8,128)(2,1)S(1)}, u32[]{:S(2)}, u32[]{:S(2)}) %collective-permute-start.2) | collective-permute-done | bytes 204832 | tf_op jit(solution)/shard_map/ppermute | solution.py:113
  19.3 1.8 %collective-permute-start.3 = (bf16[8,16,1600]{2,1,0:T(8,128)(2,1)S(1)}, bf16[8,16,1600]{2,1,0:T(8,128)(2,1)S(1)}, u32[]{:S(2)}, u32[]{:S(2)}) collective-permute-start(bf16[8,16,1600]{2,1,0:T(8,128)(2,1)S(1)} %pad_maximum_fusion), channel_id=1, source_target_pairs={{0,2},{1,3},{2,0},{3,1},{4,6},{5,7},{6,4},{7,5},{8,10},{9,11},{10,... | collective-permute-start | bytes 1228808 | tf_op jit(solution)/shard_map/ppermute | solution.py:113
  21.1 6.3 %collective-permute-done.3 = bf16[8,16,1600]{2,1,0:T(8,128)(2,1)S(1)} collective-permute-done((bf16[8,16,1600]{2,1,0:T(8,128)(2,1)S(1)}, bf16[8,16,1600]{2,1,0:T(8,128)(2,1)S(1)}, u32[]{:S(2)}, u32[]{:S(2)}) %collective-permute-start.3) | collective-permute-done | bytes 409632 | tf_op jit(solution)/shard_map/ppermute | solution.py:113
  27.6 2.5 %shard_map.113 = (bf16[2,200,256]{2,1,0:T(8,128)(2,1)S(1)}, bf16[2,200,256]{2,1,0:T(8,128)(2,1)S(1)}, bf16[2,200,256]{2,1,0:T(8,128)(2,1)}, bf16[2,200,256]{2,1,...) custom-call(bf16[200,2048]{1,0:T(8,128)(2,1)} %expand_at.3, ...), custom_call_target="tpu_custom_call" | custom-call | tf_op jit(solution)/shard_map/pallas_call | solution.py:436
  30.1 1.8 %collective-permute-start.5 = (bf16[2,200,256]{2,1,0:T(8,128)(2,1)S(1)}, bf16[2,200,256]{2,1,0:T(8,128)(2,1)S(1)}, u32[]{:S(2)}, u32[]{:S(2)}) collective-permute-start(bf16[2,200,256]{2,1,0:T(8,128)(2,1)S(1)} %get-tuple-element.30), channel_id=1, source_target_pairs={{0,4},{4,0},{8,12},{12,8},{16,20},{20,16},{24,28},{28,24},{1,5},{5... | collective-permute-start | bytes 614408 | tf_op jit(solution)/shard_map/ppermute | solution.py:113
  31.9 1.1 collective-permute-start.6
  33.0 0.6 collective-permute-start.7
  33.7 2.6 %collective-permute-start.8 = (bf16[2,200,256]{2,1,0:T(8,128)(2,1)}, bf16[2,200,256]{2,1,0:T(8,128)(2,1)}, u32[]{:S(2)}, u32[]{:S(2)}) collective-permute-start(bf16[2,200,256]{2,1,0:T(8,128)(2,1)} %get-tuple-element.33), channel_id=1, source_target_pairs={{0,16},{4,20},{8,24},{12,28},{16,0},{20,4},{24,8},{28,12},{1,17},{... | collective-permute-start | bytes 614408 | tf_op jit(solution)/shard_map/ppermute | solution.py:113
  36.3 1.3 %collective-permute-done.5.refs_0_ = bf16[2,200,256]{2,1,0:T(8,128)(2,1)S(1)} collective-permute-done((bf16[2,200,256]{2,1,0:T(8,128)(2,1)S(1)}, bf16[2,200,256]{2,1,0:T(8,128)(2,1)S(1)}, u32[]{:S(2)}, u32[]{:S(2)}) %collective-permute-start.5) | collective-permute-done | bytes 204832 | tf_op jit(solution)/shard_map/ppermute | solution.py:113
  37.6 0.7 copy-done
  38.3 3.6 %collective-permute-start.9 = (bf16[2,200,256]{2,1,0:T(8,128)(2,1)}, bf16[2,200,256]{2,1,0:T(8,128)(2,1)}, u32[]{:S(2)}, u32[]{:S(2)}) collective-permute-start(bf16[2,200,256]{2,1,0:T(8,128)(2,1)} %get-tuple-element.34), channel_id=1, source_target_pairs={{0,20},{4,16},{8,28},{12,24},{16,4},{20,0},{24,12},{28,8},{1,21},{... | collective-permute-start | bytes 614408 | tf_op jit(solution)/shard_map/ppermute | solution.py:113
  41.9 4.9 %collective-permute-done.6.refs_1_ = bf16[2,200,256]{2,1,0:T(8,128)(2,1)S(1)} collective-permute-done((bf16[2,200,256]{2,1,0:T(8,128)(2,1)S(1)}, bf16[2,200,256]{2,1,0:T(8,128)(2,1)S(1)}, u32[]{:S(2)}, u32[]{:S(2)}) %collective-permute-start.6) | collective-permute-done | bytes 204832 | tf_op jit(solution)/shard_map/ppermute | solution.py:113
  46.8 0.7 copy-done.2
  47.5 1.5 %collective-permute-start.10 = (bf16[2,200,256]{2,1,0:T(8,128)(2,1)}, bf16[2,200,256]{2,1,0:T(8,128)(2,1)}, u32[]{:S(2)}, u32[]{:S(2)}) collective-permute-start(bf16[2,200,256]{2,1,0:T(8,128)(2,1)} %get-tuple-element.35), channel_id=1, source_target_pairs={{0,24},{4,28},{8,16},{12,20},{16,8},{20,12},{24,0},{28,4},{1,25},{... | collective-permute-start | bytes 614408 | tf_op jit(solution)/shard_map/ppermute | solution.py:113
  49.0 2.3 %collective-permute-start.11 = (bf16[2,200,256]{2,1,0:T(8,128)(2,1)}, bf16[2,200,256]{2,1,0:T(8,128)(2,1)}, u32[]{:S(2)}, u32[]{:S(2)}) collective-permute-start(bf16[2,200,256]{2,1,0:T(8,128)(2,1)} %get-tuple-element.36), channel_id=1, source_target_pairs={{0,28},{4,24},{8,20},{12,16},{16,12},{20,8},{24,4},{28,0},{1,29},{... | collective-permute-start | bytes 614408 | tf_op jit(solution)/shard_map/ppermute | solution.py:113
  51.3 0.7 reshape.11.gain_ref
  52.0 0.1 pad_add_fusion.me_ref
  52.0 2.0 %shard_map.112 = (bf16[256,1600]{1,0:T(8,128)(2,1)S(1)}, bf16[256,1600]{1,0:T(8,128)(2,1)S(1)}, f32[16,1600]{1,0:T(8,128)S(1)}) custom-call(s32[2]{0:T(128)S(1)} %pad_add_fusion.me_ref, bf16[16,16,1600]{2,1,0:T(8,128)(2,1)S(1)} %constant_dynamic-update-slice_fusion.near_ref, bf16[16,16,1600]{2,1,0:T(8,128)(2,1)S(1)} %collective-permute-done.4.far_ref, ...), custom_call_target="tpu_custom_call" | custom-call | tf_op jit(solution)/shard_map/pallas_call | solution.py:389
  54.0 11.9 %collective-permute-done.9.refs_4_ = bf16[2,200,256]{2,1,0:T(8,128)(2,1)} collective-permute-done((bf16[2,200,256]{2,1,0:T(8,128)(2,1)}, bf16[2,200,256]{2,1,0:T(8,128)(2,1)}, u32[]{:S(2)}, u32[]{:S(2)}) %collective-permute-start.9) | collective-permute-done | bytes 204832 | tf_op jit(solution)/shard_map/ppermute | solution.py:113
  65.9 0.9 copy-done.1
  66.9 0.9 copy-done.3
  67.8 2.5 %shard_map.114 = (bf16[1,256,256]{2,1,0:T(8,128)(2,1)S(1)}, bf16[1,256,256]{2,1,0:T(8,128)(2,1)S(1)}, bf16[1600,256]{1,0:T(8,128)(2,1)S(1)}, bf16[1600,256]{1,0:T(8,128)(2,1)S(1)}) custom-call(bf16[256,1600]{1,0:T(8,128)(2,1)S(1)} %get-tuple-element.28.normed_ref, bf16[256,1600]{1,0:T(8,128)(2,1)S(1)} %get-tuple-element.29.grad_ref, ...), custom_call_target="tpu_custom_call" | custom-call | tf_op jit(solution)/shard_map/pallas_call | solution.py:459
  70.3 1.4 %shard_map.115 = (f32[2,16,8,1600]{3,2,1,0:T(8,128)S(1)}, bf16[2,16,8,1600]{3,2,1,0:T(8,128)(2,1)S(1)}) custom-call(s32[2]{0:T(128)S(1)} %pad_add_fusion.me_ref, bf16[1,256,256]{2,1,0:T(8,128)(2,1)S(1)} %get-tuple-element.37.hidden_ref, bf16[1,256,256]{2,1,0:T(8,128)(2,1)S(1)} %get-tuple-element.38.pre_ref, ...), custom_call_target="tpu_custom_call" | custom-call | tf_op jit(solution)/shard_map/pallas_call | solution.py:389
  71.8 1.8 %collective-permute-start.17 = (bf16[1,256,256]{2,1,0:T(8,128)(2,1)S(1)}, bf16[1,256,256]{2,1,0:T(8,128)(2,1)S(1)}, u32[]{:S(2)}, u32[]{:S(2)}) collective-permute-start(bf16[1,256,256]{2,1,0:T(8,128)(2,1)S(1)} %get-tuple-element.38.pre_ref), channel_id=1, source_target_pairs={{0,4},{4,0},{8,12},{12,8},{16,20},{20,16},{24,28},{28,24},{1,5},{5... | collective-permute-start | bytes 393224 | tf_op jit(solution)/shard_map/ppermute | solution.py:113
  73.6 9.7 %collective-permute-start.14 = (bf16[1,256,256]{2,1,0:T(8,128)(2,1)S(1)}, bf16[1,256,256]{2,1,0:T(8,128)(2,1)S(1)}, u32[]{:S(2)}, u32[]{:S(2)}) collective-permute-start(bf16[1,256,256]{2,1,0:T(8,128)(2,1)S(1)} %get-tuple-element.37.hidden_ref), channel_id=1, source_target_pairs={{0,16},{4,20},{8,24},{12,28},{16,0},{20,4},{24,8},{28,12},{1,17},{... | collective-permute-start | bytes 393224 | tf_op jit(solution)/shard_map/ppermute | solution.py:113
  83.4 4.6 %collective-permute-start.18 = (bf16[2,256,256]{2,1,0:T(8,128)(2,1)S(1)}, bf16[2,256,256]{2,1,0:T(8,128)(2,1)S(1)}, u32[]{:S(2)}, u32[]{:S(2)}) collective-permute-start(bf16[2,256,256]{2,1,0:T(8,128)(2,1)S(1)} %pad_maximum_fusion.2), channel_id=1, source_target_pairs={{0,16},{4,20},{8,24},{12,28},{16,0},{20,4},{24,8},{28,12},{1,17},{... | collective-permute-start | bytes 786440 | tf_op jit(solution)/shard_map/ppermute | solution.py:113
  88.0 0.1 shard_map.116
  88.2 1.6 %collective-permute-start.13 = (bf16[2,8,8,1600]{3,2,1,0:T(8,128)(2,1)S(1)}, bf16[2,8,8,1600]{3,2,1,0:T(8,128)(2,1)S(1)}, u32[]{:S(2)}, u32[]{:S(2)}) collective-permute-start(bf16[2,8,8,1600]{3,2,1,0:T(8,128)(2,1)S(1)} %get-tuple-element.44), channel_id=1, source_target_pairs={{0,2},{1,3},{2,0},{3,1},{4,6},{5,7},{6,4},{7,5},{8,10},{9,11},{10,... | collective-permute-start | bytes 1228808 | tf_op jit(solution)/shard_map/ppermute | solution.py:113
  89.8 6.3 %collective-permute-done.14 = bf16[1,256,256]{2,1,0:T(8,128)(2,1)S(1)} collective-permute-done((bf16[1,256,256]{2,1,0:T(8,128)(2,1)S(1)}, bf16[1,256,256]{2,1,0:T(8,128)(2,1)S(1)}, u32[]{:S(2)}, u32[]{:S(2)}) %collective-permute-start.14) | collective-permute-done | bytes 131104 | tf_op jit(solution)/shard_map/ppermute | solution.py:113
  96.1 0.7 pad_maximum_fusion.1
  96.8 4.5 %collective-permute-done.18 = bf16[2,256,256]{2,1,0:T(8,128)(2,1)S(1)} collective-permute-done((bf16[2,256,256]{2,1,0:T(8,128)(2,1)S(1)}, bf16[2,256,256]{2,1,0:T(8,128)(2,1)S(1)}, u32[]{:S(2)}, u32[]{:S(2)}) %collective-permute-start.18) | collective-permute-done | bytes 262176 | tf_op jit(solution)/shard_map/ppermute | solution.py:113
  101.4 0.8 shard_map.117
  102.3 3.5 %all-to-all-start = ((bf16[8,16,1600]{2,1,0:T(8,128)(2,1)}), bf16[8,16,1600]{2,1,0:T(8,128)(2,1)S(1)}, u32[]{:S(2)}, u32[]{:S(2)}) async-start(bf16[8,16,1600]{2,1,0:T(8,128)(2,1)} %shard_map.117), calls=%async_computation | async-start | bytes 851968 | tf_op jit(solution)/shard_map/all_to_all | solution.py:482
  105.8 1.3 collective-permute-done.15
  107.0 1.7 %constant_dynamic-update-slice_fusion.5.hidden_ref = bf16[4,256,256]{2,1,0:T(8,128)(2,1)} fusion(bf16[4,256,256]{2,1,0:T(8,128)(2,1)} %copy-done.6, bf16[2,256,256]{2,1,0:T(8,128)(2,1)} %collective-permute-done.15), kind=kLoop, calls=%fused_computation.10 | loop fusion | bytes 524288 | tf_op jit(solution)/shard_map/concatenate | solution.py:489
  108.7 0.7 collective-permute-start.16
  109.4 1.1 copy-done.7
  110.5 4.8 %shard_map.119 = (bf16[1600,2048]{1,0:T(8,128)(2,1)}, bf16[1600,2048]{1,0:T(8,128)(2,1)}) custom-call(s32[2]{0:T(128)S(1)} %pad_add_fusion.me_ref, bf16[4,256,256]{2,1,0:T(8,128)(2,1)S(1)} %copy-done.7, bf16[4,256,256]{2,1,0:T(8,128)(2,1)S(1)} %constant_dynamic-update-slice_fusion.8.pre_ref, bf16[256,1600]{1,0:T(8,128)(2,1)S(1)} %get-tuple-element.28.normed_ref, ...), custom_call_target="tpu_custom_call" | custom-call | flops 1677721600 | bytes 8192000 | tf_op jit(solution)/shard_map/pallas_call | solution.py:362
  115.4 7.4 %collective-permute-done.19.pre_ref = bf16[4,256,256]{2,1,0:T(8,128)(2,1)S(1)} collective-permute-done((bf16[4,256,256]{2,1,0:T(8,128)(2,1)S(1)}, bf16[4,256,256]{2,1,0:T(8,128)(2,1)S(1)}, u32[]{:S(2)}, u32[]{:S(2)}) %collective-permute-start.19) | collective-permute-done | bytes 524320 | tf_op jit(solution)/shard_map/ppermute | solution.py:113
  122.7 2.7 %collective-permute-done.16.hidden_ref = bf16[4,256,256]{2,1,0:T(8,128)(2,1)S(1)} collective-permute-done((bf16[4,256,256]{2,1,0:T(8,128)(2,1)}, bf16[4,256,256]{2,1,0:T(8,128)(2,1)S(1)}, u32[]{:S(2)}, u32[]{:S(2)}) %collective-permute-start.16) | collective-permute-done | bytes 524320 | tf_op jit(solution)/shard_map/ppermute | solution.py:113
  125.5 4.8 %shard_map.120 = (bf16[1600,2048]{1,0:T(8,128)(2,1)}, bf16[1600,2048]{1,0:T(8,128)(2,1)}) custom-call(s32[2]{0:T(128)S(1)} %pad_add_fusion.me_ref, bf16[4,256,256]{2,1,0:T(8,128)(2,1)S(1)} %collective-permute-done.16.hidden_ref, bf16[4,256,256]{2,1,0:T(8,128)(2,1)S(1)} %collective-permute-done.19.pre_ref, ...), custom_call_target="tpu_custom_call", output_to_operand_aliasing={{0}: (5, {}), {1}: (6, {})} | custom-call | flops 1677721600 | bytes 8192000 | tf_op jit(solution)/shard_map/pallas_call | solution.py:362
  130.4 1.5 %shard_map.118 = (bf16[16,1600]{1,0:T(8,128)(2,1)}, bf16[8,1600]{1,0:T(8,128)(2,1)}) custom-call(s32[2]{0:T(128)S(1)} %pad_add_fusion.me_ref, s32[1,4]{1,0:T(1,128)S(1)} %copy-done.8, s32[1,8]{1,0:T(1,128)S(1)} %copy-done.9, bf16[8,16,1600]{2,1,0:T(8,128)(2,1)S(1)} %all-to-all-done.tail_ref, f32[16,1600]{1,0:T(8,128)S(1)} %get-tuple-element.45.extra_ref, ...), custom_call_target="tpu_custom_call" | custom-call | tf_op jit(solution)/shard_map/pallas_call | solution.py:389
  (41 shorter events, 0.6 us)
Async XLA Ops:
  1.6 6.8 %collective-permute-start = (bf16[1,16,1600]{2,1,0:T(8,128)(2,1)S(1)}, bf16[1,16,1600]{2,1,0:T(8,128)(2,1)S(1)}, u32[]{:S(2)}, u32[]{:S(2)}) collective-permute-start(bf16[1,16,1600]{2,1,0:T(8,128)(2,1)S(1)} %shard_map.111), channel_id=1, source_target_pairs={{0,16},{4,20},{8,24},{12,28},{16,0},{20,4},{24,8},{28,12},{1,17},{... | collective-permute-start | bytes 153608 | tf_op jit(solution)/shard_map/ppermute | solution.py:113
  8.5 4.8 %collective-permute-start.1 = (bf16[2,16,1600]{2,1,0:T(8,128)(2,1)S(1)}, bf16[2,16,1600]{2,1,0:T(8,128)(2,1)S(1)}, u32[]{:S(2)}, u32[]{:S(2)}) collective-permute-start(bf16[2,16,1600]{2,1,0:T(8,128)(2,1)S(1)} %pad_maximum_fusion.4), channel_id=1, source_target_pairs={{0,8},{4,12},{8,0},{12,4},{16,24},{20,28},{24,16},{28,20},{1,9},{5... | collective-permute-start | bytes 307208 | tf_op jit(solution)/shard_map/ppermute | solution.py:113
  13.3 5.9 %collective-permute-start.2 = (bf16[4,16,1600]{2,1,0:T(8,128)(2,1)S(1)}, bf16[4,16,1600]{2,1,0:T(8,128)(2,1)S(1)}, u32[]{:S(2)}, u32[]{:S(2)}) collective-permute-start(bf16[4,16,1600]{2,1,0:T(8,128)(2,1)S(1)} %pad_maximum_fusion.3), channel_id=1, source_target_pairs={{0,4},{4,0},{8,12},{12,8},{16,20},{20,16},{24,28},{28,24},{1,5},{5... | collective-permute-start | bytes 614408 | tf_op jit(solution)/shard_map/ppermute | solution.py:113
  19.3 8.2 %collective-permute-start.3 = (bf16[8,16,1600]{2,1,0:T(8,128)(2,1)S(1)}, bf16[8,16,1600]{2,1,0:T(8,128)(2,1)S(1)}, u32[]{:S(2)}, u32[]{:S(2)}) collective-permute-start(bf16[8,16,1600]{2,1,0:T(8,128)(2,1)S(1)} %pad_maximum_fusion), channel_id=1, source_target_pairs={{0,2},{1,3},{2,0},{3,1},{4,6},{5,7},{6,4},{7,5},{8,10},{9,11},{10,... | collective-permute-start | bytes 1228808 | tf_op jit(solution)/shard_map/ppermute | solution.py:113
  27.5 21.5 %collective-permute-start.4 = (bf16[16,16,1600]{2,1,0:T(8,128)(2,1)S(1)}, bf16[16,16,1600]{2,1,0:T(8,128)(2,1)S(1)}, u32[]{:S(2)}, u32[]{:S(2)}) collective-permute-start(bf16[16,16,1600]{2,1,0:T(8,128)(2,1)S(1)} %constant_dynamic-update-slice_fusion.near_ref), channel_id=1, source_target_pairs={{0,1},{1,0},{2,3},{3,2},{4,5},{5,4},{6,7},{7,6},{8,9},{9,8},{10,11... | collective-permute-start | bytes 2457608 | tf_op jit(solution)/shard_map/ppermute | solution.py:113
  30.1 7.5 %collective-permute-start.5 = (bf16[2,200,256]{2,1,0:T(8,128)(2,1)S(1)}, bf16[2,200,256]{2,1,0:T(8,128)(2,1)S(1)}, u32[]{:S(2)}, u32[]{:S(2)}) collective-permute-start(bf16[2,200,256]{2,1,0:T(8,128)(2,1)S(1)} %get-tuple-element.30), channel_id=1, source_target_pairs={{0,4},{4,0},{8,12},{12,8},{16,20},{20,16},{24,28},{28,24},{1,5},{5... | collective-permute-start | bytes 614408 | tf_op jit(solution)/shard_map/ppermute | solution.py:113
  31.9 14.9 %collective-permute-start.6 = (bf16[2,200,256]{2,1,0:T(8,128)(2,1)S(1)}, bf16[2,200,256]{2,1,0:T(8,128)(2,1)S(1)}, u32[]{:S(2)}, u32[]{:S(2)}) collective-permute-start(bf16[2,200,256]{2,1,0:T(8,128)(2,1)S(1)} %get-tuple-element.31), channel_id=1, source_target_pairs={{0,8},{4,12},{8,0},{12,4},{16,24},{20,28},{24,16},{28,20},{1,9},{5... | collective-permute-start | bytes 614408 | tf_op jit(solution)/shard_map/ppermute | solution.py:113
  33.0 21.0 %collective-permute-start.7 = (bf16[2,200,256]{2,1,0:T(8,128)(2,1)}, bf16[2,200,256]{2,1,0:T(8,128)(2,1)}, u32[]{:S(2)}, u32[]{:S(2)}) collective-permute-start(bf16[2,200,256]{2,1,0:T(8,128)(2,1)} %get-tuple-element.32), channel_id=1, source_target_pairs={{0,12},{4,8},{8,4},{12,0},{16,28},{20,24},{24,20},{28,16},{1,13},{... | collective-permute-start | bytes 614408 | tf_op jit(solution)/shard_map/ppermute | solution.py:113
  33.7 20.4 %collective-permute-start.8 = (bf16[2,200,256]{2,1,0:T(8,128)(2,1)}, bf16[2,200,256]{2,1,0:T(8,128)(2,1)}, u32[]{:S(2)}, u32[]{:S(2)}) collective-permute-start(bf16[2,200,256]{2,1,0:T(8,128)(2,1)} %get-tuple-element.33), channel_id=1, source_target_pairs={{0,16},{4,20},{8,24},{12,28},{16,0},{20,4},{24,8},{28,12},{1,17},{... | collective-permute-start | bytes 614408 | tf_op jit(solution)/shard_map/ppermute | solution.py:113
  37.6 0.7 copy-start
  38.3 27.6 %collective-permute-start.9 = (bf16[2,200,256]{2,1,0:T(8,128)(2,1)}, bf16[2,200,256]{2,1,0:T(8,128)(2,1)}, u32[]{:S(2)}, u32[]{:S(2)}) collective-permute-start(bf16[2,200,256]{2,1,0:T(8,128)(2,1)} %get-tuple-element.34), channel_id=1, source_target_pairs={{0,20},{4,16},{8,28},{12,24},{16,4},{20,0},{24,12},{28,8},{1,21},{... | collective-permute-start | bytes 614408 | tf_op jit(solution)/shard_map/ppermute | solution.py:113
  46.8 0.7 copy-start.2
  47.5 18.4 %collective-permute-start.10 = (bf16[2,200,256]{2,1,0:T(8,128)(2,1)}, bf16[2,200,256]{2,1,0:T(8,128)(2,1)}, u32[]{:S(2)}, u32[]{:S(2)}) collective-permute-start(bf16[2,200,256]{2,1,0:T(8,128)(2,1)} %get-tuple-element.35), channel_id=1, source_target_pairs={{0,24},{4,28},{8,16},{12,20},{16,8},{20,12},{24,0},{28,4},{1,25},{... | collective-permute-start | bytes 614408 | tf_op jit(solution)/shard_map/ppermute | solution.py:113
  49.0 16.9 %collective-permute-start.11 = (bf16[2,200,256]{2,1,0:T(8,128)(2,1)}, bf16[2,200,256]{2,1,0:T(8,128)(2,1)}, u32[]{:S(2)}, u32[]{:S(2)}) collective-permute-start(bf16[2,200,256]{2,1,0:T(8,128)(2,1)} %get-tuple-element.36), channel_id=1, source_target_pairs={{0,28},{4,24},{8,20},{12,16},{16,12},{20,8},{24,4},{28,0},{1,29},{... | collective-permute-start | bytes 614408 | tf_op jit(solution)/shard_map/ppermute | solution.py:113
  65.9 0.9 copy-start.1
  66.9 0.9 copy-start.3
  71.8 16.3 %collective-permute-start.12 = (bf16[2,16,8,1600]{3,2,1,0:T(8,128)(2,1)S(1)}, bf16[2,16,8,1600]{3,2,1,0:T(8,128)(2,1)S(1)}, u32[]{:S(2)}, u32[]{:S(2)}) collective-permute-start(bf16[2,16,8,1600]{3,2,1,0:T(8,128)(2,1)S(1)} %get-tuple-element.42), channel_id=1, source_target_pairs={{0,1},{1,0},{2,3},{3,2},{4,5},{5,4},{6,7},{7,6},{8,9},{9,8},{10,11... | collective-permute-start | bytes 2457608 | tf_op jit(solution)/shard_map/ppermute | solution.py:113
  71.8 11.5 %collective-permute-start.17 = (bf16[1,256,256]{2,1,0:T(8,128)(2,1)S(1)}, bf16[1,256,256]{2,1,0:T(8,128)(2,1)S(1)}, u32[]{:S(2)}, u32[]{:S(2)}) collective-permute-start(bf16[1,256,256]{2,1,0:T(8,128)(2,1)S(1)} %get-tuple-element.38.pre_ref), channel_id=1, source_target_pairs={{0,4},{4,0},{8,12},{12,8},{16,20},{20,16},{24,28},{28,24},{1,5},{5... | collective-permute-start | bytes 393224 | tf_op jit(solution)/shard_map/ppermute | solution.py:113
  73.6 22.4 %collective-permute-start.14 = (bf16[1,256,256]{2,1,0:T(8,128)(2,1)S(1)}, bf16[1,256,256]{2,1,0:T(8,128)(2,1)S(1)}, u32[]{:S(2)}, u32[]{:S(2)}) collective-permute-start(bf16[1,256,256]{2,1,0:T(8,128)(2,1)S(1)} %get-tuple-element.37.hidden_ref), channel_id=1, source_target_pairs={{0,16},{4,20},{8,24},{12,28},{16,0},{20,4},{24,8},{28,12},{1,17},{... | collective-permute-start | bytes 393224 | tf_op jit(solution)/shard_map/ppermute | solution.py:113
  83.4 17.9 %collective-permute-start.18 = (bf16[2,256,256]{2,1,0:T(8,128)(2,1)S(1)}, bf16[2,256,256]{2,1,0:T(8,128)(2,1)S(1)}, u32[]{:S(2)}, u32[]{:S(2)}) collective-permute-start(bf16[2,256,256]{2,1,0:T(8,128)(2,1)S(1)} %pad_maximum_fusion.2), channel_id=1, source_target_pairs={{0,16},{4,20},{8,24},{12,28},{16,0},{20,4},{24,8},{28,12},{1,17},{... | collective-permute-start | bytes 786440 | tf_op jit(solution)/shard_map/ppermute | solution.py:113
  88.2 13.3 %collective-permute-start.13 = (bf16[2,8,8,1600]{3,2,1,0:T(8,128)(2,1)S(1)}, bf16[2,8,8,1600]{3,2,1,0:T(8,128)(2,1)S(1)}, u32[]{:S(2)}, u32[]{:S(2)}) collective-permute-start(bf16[2,8,8,1600]{3,2,1,0:T(8,128)(2,1)S(1)} %get-tuple-element.44), channel_id=1, source_target_pairs={{0,2},{1,3},{2,0},{3,1},{4,6},{5,7},{6,4},{7,5},{8,10},{9,11},{10,... | collective-permute-start | bytes 1228808 | tf_op jit(solution)/shard_map/ppermute | solution.py:113
  96.8 10.2 %collective-permute-start.15 = (bf16[2,256,256]{2,1,0:T(8,128)(2,1)}, bf16[2,256,256]{2,1,0:T(8,128)(2,1)}, u32[]{:S(2)}, u32[]{:S(2)}) collective-permute-start(bf16[2,256,256]{2,1,0:T(8,128)(2,1)} %pad_maximum_fusion.1), channel_id=1, source_target_pairs={{0,8},{4,12},{8,0},{12,4},{16,24},{20,28},{24,16},{28,20},{1,9},{5... | collective-permute-start | bytes 786440 | tf_op jit(solution)/shard_map/ppermute | solution.py:113
  96.8 4.6 %copy-start.6 = (bf16[4,256,256]{2,1,0:T(8,128)(2,1)}, bf16[4,256,256]{2,1,0:T(8,128)(2,1)S(1)}, u32[]{:S(2)}) copy-start(bf16[4,256,256]{2,1,0:T(8,128)(2,1)S(1)} %constant_dynamic-update-slice_fusion.6) | copy-start | bytes 1572868
  101.3 21.4 %collective-permute-start.19 = (bf16[4,256,256]{2,1,0:T(8,128)(2,1)S(1)}, bf16[4,256,256]{2,1,0:T(8,128)(2,1)S(1)}, u32[]{:S(2)}, u32[]{:S(2)}) collective-permute-start(bf16[4,256,256]{2,1,0:T(8,128)(2,1)S(1)} %constant_dynamic-update-slice_fusion.8.pre_ref), channel_id=1, source_target_pairs={{0,8},{4,12},{8,0},{12,4},{16,24},{20,28},{24,16},{28,20},{1,9},{5... | collective-permute-start | bytes 1572872 | tf_op jit(solution)/shard_map/ppermute | solution.py:113
  102.3 28.0 %all-to-all-start = ((bf16[8,16,1600]{2,1,0:T(8,128)(2,1)}), bf16[8,16,1600]{2,1,0:T(8,128)(2,1)S(1)}, u32[]{:S(2)}, u32[]{:S(2)}) async-start(bf16[8,16,1600]{2,1,0:T(8,128)(2,1)} %shard_map.117), calls=%async_computation | async-start | bytes 851968 | tf_op jit(solution)/shard_map/all_to_all | solution.py:482
  108.7 16.7 %collective-permute-start.16 = (bf16[4,256,256]{2,1,0:T(8,128)(2,1)}, bf16[4,256,256]{2,1,0:T(8,128)(2,1)S(1)}, u32[]{:S(2)}, u32[]{:S(2)}) collective-permute-start(bf16[4,256,256]{2,1,0:T(8,128)(2,1)} %constant_dynamic-update-slice_fusion.5.hidden_ref), channel_id=1, source_target_pairs={{0,4},{4,0},{8,12},{12,8},{16,20},{20,16},{24,28},{28,24},{1,5},{5... | collective-permute-start | bytes 1572872 | tf_op jit(solution)/shard_map/ppermute | solution.py:113
  109.4 1.1 copy-start.7
  125.5 4.9 %copy-start.4 = (bf16[8,1600]{1,0:T(8,128)(2,1)S(1)}, bf16[8,1600]{1,0:T(8,128)(2,1)}, u32[]{:S(2)}) copy-start(bf16[8,1600]{1,0:T(8,128)(2,1)} %patch_ref.1) | copy-start | bytes 76804
  125.5 4.9 %copy-start.5 = (bf16[16,1600]{1,0:T(8,128)(2,1)S(1)}, bf16[16,1600]{1,0:T(8,128)(2,1)}, u32[]{:S(2)}) copy-start(bf16[16,1600]{1,0:T(8,128)(2,1)} %text_ref.1) | copy-start | bytes 153604
  125.5 4.9 %copy-start.8 = (s32[1,4]{1,0:T(1,128)S(1)}, s32[1,4]{1,0:T(1,128)}, u32[]{:S(2)}) copy-start(s32[1,4]{1,0:T(1,128)} %count_ref.1) | copy-start | bytes 52
  125.5 4.9 %copy-start.9 = (s32[1,8]{1,0:T(1,128)S(1)}, s32[1,8]{1,0:T(1,128)}, u32[]{:S(2)}) copy-start(s32[1,8]{1,0:T(1,128)} %place_ref.1) | copy-start | bytes 100
where the time goes:
time: 132 us
  waiting for transfers between devices  56.9 us (43%)
  starting transfers between devices  44.8 us (34%)
  Pallas kernels  21.6 us (16%)
  local copies, waits for them, and re-layouts  6.82 us (5%)
    ppermute x20, waiting for transfers between devices, swap(): return lax.ppermute(array, axis, [(i, i ^ step) for i in range(size)])  56.9 us
    ppermute x20, starting transfers between devices, swap(): return lax.ppermute(array, axis, [(i, i ^ step) for i in range(size)])  41.3 us
    pallas_call x2, Pallas kernels, weight_grads(): pl.pallas_call(weight_grad_kernel, grid_spec=pltpu.PrefetchScalarGridSpec...  9.69 us
    pallas_call x5, Pallas kernels, call(): pl.pallas_call(kernel, out_shape=out_shape, in_specs=[SMEM_SPEC] * len(sm...  5.86 us
    unnamed x27, local copies, waits for them, and re-layouts  4.39 us
    all_to_all x1, starting transfers between devices, move_rows_plan(): tail = lax.all_to_all(tail, 'dp', split_axis=0, concat_axis=0, tiled=True)  3.46 us
  transfers between devices with their start and end apart: 21, of which 12 were waited for; matrix products, arithmetic and copies ran while one was open for 3% of the time, Pallas kernels for 12%

commit v1 on v0

--- a/solution.py
+++ b/solution.py
@@ -178,6 +178,12 @@
                 )
             )
     fetch(copies)
+
+
+def join_kernel(first_ref, second_ref, out_ref):
+    count = first_ref.shape[0]
+    out_ref[:count] = first_ref[...]
+    out_ref[count:] = second_ref[...]
 
 
 def order_kernel(
@@ -396,6 +402,11 @@
     )(*smem, *vmem)
 
 
+def join(first, second):
+    both = (first.shape[0] + second.shape[0], *first.shape[1:])
+    return call(join_kernel, jax.ShapeDtypeStruct(both, first.dtype), (), (first, second))
+
+
 def move_rows_plan(
     patches, gain, expand_weight, project_weight, counts, positions, text, cotangent
 ):
@@ -449,7 +460,7 @@
     for axis, step in exchanges:
         got = swap(held, axis, step)
         if held.shape[0] < devices // 2:
-            held = jnp.concatenate([held, got], axis=0)
+            held = join(held, got)
     normed, grad_all, extra = call(
         functools.partial(order_kernel, sections, capacity, dp_steps, section_steps),
         [shape((rows, features), kept), shape((rows, features), kept), shape((2 * slots, features), wide)],
@@ -486,8 +497,8 @@
         hidden_far = swap(hidden_near, "dp", hidden_step)
         pre_far = swap(pre_near, "dp", pre_step)
         if hidden_near.shape[0] < replicas // 2:
-            hidden_near = jnp.concatenate([hidden_near, hidden_far], axis=0)
-            pre_near = jnp.concatenate([pre_near, pre_far], axis=0)
+            hidden_near = join(hidden_near, hidden_far)
+            pre_near = join(pre_near, pre_far)
 
     grads = weight_grads(
         me, hidden_near, pre_near, 0,

time: 132 us -> 131 us (level)
  waiting for transfers between devices: 56.9 us -> 61.3 us
  local copies, waits for them, and re-layouts: 6.82 us -> 3.94 us
  starting transfers between devices: 44.8 us -> 42.7 us
    ppermute x20, starting transfers between devices: 41.3 us -> 36.4 us  [swap(): return lax.ppermute(array, axis, [(i, i ^ step) for i in range(size)])]
    ppermute x20, waiting for transfers between devices: 56.9 us -> 61.3 us  [swap(): return lax.ppermute(array, axis, [(i, i ^ step) for i in range(size)])]
    all_to_all x1, starting transfers between devices: 3.46 us -> 6.33 us  [move_rows_plan(): tail = lax.all_to_all(tail, 'dp', split_axis=0, concat_axis=0, tiled=True)]
    concatenate x3 -> x0, local copies, waits for them, and re-layouts: 1.72 us -> none  [the longest x1 1.67 us: move_rows_plan(): hidden_near = jnp.concatenate([hidden_near, hidden_far], axis=0)]
    unnamed x27 -> x16, local copies, waits for them, and re-layouts: 4.39 us -> 3.24 us
    pallas_call x5 -> x13, Pallas kernels: 5.86 us -> 6.12 us  [call(): pl.pallas_call(kernel, out_shape=out_shape, in_specs=[SMEM_SPEC] * len(sm...]
  transfers between devices with their start and end apart: 21 -> 21, of which waited for: 12 -> 13; matrix products, arithmetic and copies ran while one was open for 3% -> 1% of each run, Pallas kernels for 12% -> 12%
where the time goes in v1:
time: 131 us
  waiting for transfers between devices  61.3 us (47%)
  starting transfers between devices  42.7 us (33%)
  Pallas kernels  21.9 us (17%)
  local copies, waits for them, and re-layouts  3.94 us (3%)
    ppermute x20, waiting for transfers between devices, swap(): return lax.ppermute(array, axis, [(i, i ^ step) for i in range(size)])  61.3 us
    ppermute x20, starting transfers between devices, swap(): return lax.ppermute(array, axis, [(i, i ^ step) for i in range(size)])  36.4 us
    pallas_call x2, Pallas kernels, weight_grads(): pl.pallas_call(weight_grad_kernel, grid_spec=pltpu.PrefetchScalarGridSpec...  9.72 us
    all_to_all x1, starting transfers between devices, move_rows_plan(): tail = lax.all_to_all(tail, 'dp', split_axis=0, concat_axis=0, tiled=True)  6.33 us
    pallas_call x13, Pallas kernels, call(): pl.pallas_call(kernel, out_shape=out_shape, in_specs=[SMEM_SPEC] * len(sm...  6.12 us
    unnamed x16, local copies, waits for them, and re-layouts  3.24 us
  transfers between devices with their start and end apart: 21, of which 13 were waited for; matrix products, arithmetic and copies ran while one was open for 1% of the time, Pallas kernels for 12%

profile of v1, /device:TPU:0, one launch (start us, length us, event | category | flops | bytes accessed | tf_op | source)
XLA Modules:
  0.0 130.8 jit_solution(7419147751969233583)
XLA Ops:
  0.6 1.0 shard_map.111.first_ref
  1.6 4.1 %collective-permute-start = (bf16[1,16,1600]{2,1,0:T(8,128)(2,1)S(1)}, bf16[1,16,1600]{2,1,0:T(8,128)(2,1)S(1)}, u32[]{:S(2)}, u32[]{:S(2)}) collective-permute-start(bf16[1,16,1600]{2,1,0:T(8,128)(2,1)S(1)} %shard_map.111.first_ref), channel_id=1, source_target_pairs={{0,16},{4,20},{8,24},{12,28},{16,0},{20,4},{24,8},{28,12},{1,17},{... | collective-permute-start | bytes 153608 | tf_op jit(solution)/shard_map/ppermute | solution.py:113
  5.8 2.7 %collective-permute-done.second_ref = bf16[1,16,1600]{2,1,0:T(8,128)(2,1)S(1)} collective-permute-done((bf16[1,16,1600]{2,1,0:T(8,128)(2,1)S(1)}, bf16[1,16,1600]{2,1,0:T(8,128)(2,1)S(1)}, u32[]{:S(2)}, u32[]{:S(2)}) %collective-permute-start) | collective-permute-done | bytes 51232 | tf_op jit(solution)/shard_map/ppermute | solution.py:113
  8.5 1.4 %collective-permute-start.1 = (bf16[2,16,1600]{2,1,0:T(8,128)(2,1)S(1)}, bf16[2,16,1600]{2,1,0:T(8,128)(2,1)S(1)}, u32[]{:S(2)}, u32[]{:S(2)}) collective-permute-start(bf16[2,16,1600]{2,1,0:T(8,128)(2,1)S(1)} %shard_map.112.first_ref), channel_id=1, source_target_pairs={{0,8},{4,12},{8,0},{12,4},{16,24},{20,28},{24,16},{28,20},{1,9},{5... | collective-permute-start | bytes 307208 | tf_op jit(solution)/shard_map/ppermute | solution.py:113
  9.9 3.4 %collective-permute-done.1.second_ref = bf16[2,16,1600]{2,1,0:T(8,128)(2,1)S(1)} collective-permute-done((bf16[2,16,1600]{2,1,0:T(8,128)(2,1)S(1)}, bf16[2,16,1600]{2,1,0:T(8,128)(2,1)S(1)}, u32[]{:S(2)}, u32[]{:S(2)}) %collective-permute-start.1) | collective-permute-done | bytes 102432 | tf_op jit(solution)/shard_map/ppermute | solution.py:113
  13.3 1.8 %collective-permute-start.2 = (bf16[4,16,1600]{2,1,0:T(8,128)(2,1)S(1)}, bf16[4,16,1600]{2,1,0:T(8,128)(2,1)S(1)}, u32[]{:S(2)}, u32[]{:S(2)}) collective-permute-start(bf16[4,16,1600]{2,1,0:T(8,128)(2,1)S(1)} %shard_map.113.first_ref), channel_id=1, source_target_pairs={{0,4},{4,0},{8,12},{12,8},{16,20},{20,16},{24,28},{28,24},{1,5},{5... | collective-permute-start | bytes 614408 | tf_op jit(solution)/shard_map/ppermute | solution.py:113
  15.0 4.1 %collective-permute-done.2.second_ref = bf16[4,16,1600]{2,1,0:T(8,128)(2,1)S(1)} collective-permute-done((bf16[4,16,1600]{2,1,0:T(8,128)(2,1)S(1)}, bf16[4,16,1600]{2,1,0:T(8,128)(2,1)S(1)}, u32[]{:S(2)}, u32[]{:S(2)}) %collective-permute-start.2) | collective-permute-done | bytes 204832 | tf_op jit(solution)/shard_map/ppermute | solution.py:113
  19.2 1.8 %collective-permute-start.3 = (bf16[8,16,1600]{2,1,0:T(8,128)(2,1)S(1)}, bf16[8,16,1600]{2,1,0:T(8,128)(2,1)S(1)}, u32[]{:S(2)}, u32[]{:S(2)}) collective-permute-start(bf16[8,16,1600]{2,1,0:T(8,128)(2,1)S(1)} %shard_map.114.first_ref), channel_id=1, source_target_pairs={{0,2},{1,3},{2,0},{3,1},{4,6},{5,7},{6,4},{7,5},{8,10},{9,11},{10,... | collective-permute-start | bytes 1228808 | tf_op jit(solution)/shard_map/ppermute | solution.py:113
  21.0 6.4 %collective-permute-done.3.second_ref = bf16[8,16,1600]{2,1,0:T(8,128)(2,1)S(1)} collective-permute-done((bf16[8,16,1600]{2,1,0:T(8,128)(2,1)S(1)}, bf16[8,16,1600]{2,1,0:T(8,128)(2,1)S(1)}, u32[]{:S(2)}, u32[]{:S(2)}) %collective-permute-start.3) | collective-permute-done | bytes 409632 | tf_op jit(solution)/shard_map/ppermute | solution.py:113
  27.5 0.1 collective-permute-start.4
  27.5 2.5 %shard_map.117 = (bf16[2,200,256]{2,1,0:T(8,128)(2,1)S(1)}, bf16[2,200,256]{2,1,0:T(8,128)(2,1)S(1)}, bf16[2,200,256]{2,1,0:T(8,128)(2,1)}, bf16[2,200,256]{2,1,...) custom-call(bf16[200,2048]{1,0:T(8,128)(2,1)} %expand_at.3, ...), custom_call_target="tpu_custom_call" | custom-call | tf_op jit(solution)/shard_map/pallas_call | solution.py:447
  30.1 1.8 %collective-permute-start.5 = (bf16[2,200,256]{2,1,0:T(8,128)(2,1)S(1)}, bf16[2,200,256]{2,1,0:T(8,128)(2,1)S(1)}, u32[]{:S(2)}, u32[]{:S(2)}) collective-permute-start(bf16[2,200,256]{2,1,0:T(8,128)(2,1)S(1)} %get-tuple-element.30), channel_id=1, source_target_pairs={{0,4},{4,0},{8,12},{12,8},{16,20},{20,16},{24,28},{28,24},{1,5},{5... | collective-permute-start | bytes 614408 | tf_op jit(solution)/shard_map/ppermute | solution.py:113
  31.9 1.1 collective-permute-start.6
  33.0 0.6 collective-permute-start.7
  33.6 2.6 %collective-permute-start.8 = (bf16[2,200,256]{2,1,0:T(8,128)(2,1)}, bf16[2,200,256]{2,1,0:T(8,128)(2,1)}, u32[]{:S(2)}, u32[]{:S(2)}) collective-permute-start(bf16[2,200,256]{2,1,0:T(8,128)(2,1)} %get-tuple-element.33), channel_id=1, source_target_pairs={{0,16},{4,20},{8,24},{12,28},{16,0},{20,4},{24,8},{28,12},{1,17},{... | collective-permute-start | bytes 614408 | tf_op jit(solution)/shard_map/ppermute | solution.py:113
  36.3 1.3 %collective-permute-done.5.refs_0_ = bf16[2,200,256]{2,1,0:T(8,128)(2,1)S(1)} collective-permute-done((bf16[2,200,256]{2,1,0:T(8,128)(2,1)S(1)}, bf16[2,200,256]{2,1,0:T(8,128)(2,1)S(1)}, u32[]{:S(2)}, u32[]{:S(2)}) %collective-permute-start.5) | collective-permute-done | bytes 204832 | tf_op jit(solution)/shard_map/ppermute | solution.py:113
  37.6 0.7 copy-done
  38.3 3.6 %collective-permute-start.9 = (bf16[2,200,256]{2,1,0:T(8,128)(2,1)}, bf16[2,200,256]{2,1,0:T(8,128)(2,1)}, u32[]{:S(2)}, u32[]{:S(2)}) collective-permute-start(bf16[2,200,256]{2,1,0:T(8,128)(2,1)} %get-tuple-element.34), channel_id=1, source_target_pairs={{0,20},{4,16},{8,28},{12,24},{16,4},{20,0},{24,12},{28,8},{1,21},{... | collective-permute-start | bytes 614408 | tf_op jit(solution)/shard_map/ppermute | solution.py:113
  41.9 4.9 %collective-permute-done.6.refs_1_ = bf16[2,200,256]{2,1,0:T(8,128)(2,1)S(1)} collective-permute-done((bf16[2,200,256]{2,1,0:T(8,128)(2,1)S(1)}, bf16[2,200,256]{2,1,0:T(8,128)(2,1)S(1)}, u32[]{:S(2)}, u32[]{:S(2)}) %collective-permute-start.6) | collective-permute-done | bytes 204832 | tf_op jit(solution)/shard_map/ppermute | solution.py:113
  46.8 0.7 copy-done.2
  47.5 1.5 %collective-permute-start.10 = (bf16[2,200,256]{2,1,0:T(8,128)(2,1)}, bf16[2,200,256]{2,1,0:T(8,128)(2,1)}, u32[]{:S(2)}, u32[]{:S(2)}) collective-permute-start(bf16[2,200,256]{2,1,0:T(8,128)(2,1)} %get-tuple-element.35), channel_id=1, source_target_pairs={{0,24},{4,28},{8,16},{12,20},{16,8},{20,12},{24,0},{28,4},{1,25},{... | collective-permute-start | bytes 614408 | tf_op jit(solution)/shard_map/ppermute | solution.py:113
  49.0 2.3 %collective-permute-start.11 = (bf16[2,200,256]{2,1,0:T(8,128)(2,1)}, bf16[2,200,256]{2,1,0:T(8,128)(2,1)}, u32[]{:S(2)}, u32[]{:S(2)}) collective-permute-start(bf16[2,200,256]{2,1,0:T(8,128)(2,1)} %get-tuple-element.36), channel_id=1, source_target_pairs={{0,28},{4,24},{8,20},{12,16},{16,12},{20,8},{24,4},{28,0},{1,29},{... | collective-permute-start | bytes 614408 | tf_op jit(solution)/shard_map/ppermute | solution.py:113
  51.3 0.7 reshape.11.gain_ref
  52.0 0.1 pad_add_fusion.me_ref
  52.0 2.0 %shard_map.116 = (bf16[256,1600]{1,0:T(8,128)(2,1)S(1)}, bf16[256,1600]{1,0:T(8,128)(2,1)S(1)}, f32[16,1600]{1,0:T(8,128)S(1)}) custom-call(s32[2]{0:T(128)S(1)} %pad_add_fusion.me_ref, bf16[16,16,1600]{2,1,0:T(8,128)(2,1)S(1)} %shard_map.115.near_ref, bf16[16,16,1600]{2,1,0:T(8,128)(2,1)S(1)} %collective-permute-done.4.far_ref, f32[1,1600]{1,0:T(1,128)S(1)} %reshape.11.gain_ref), custom_call_target="tpu_custom_call" | custom-call | tf_op jit(solution)/shard_map/pallas_call | solution.py:395
  54.0 11.9 %collective-permute-done.9.refs_4_ = bf16[2,200,256]{2,1,0:T(8,128)(2,1)} collective-permute-done((bf16[2,200,256]{2,1,0:T(8,128)(2,1)}, bf16[2,200,256]{2,1,0:T(8,128)(2,1)}, u32[]{:S(2)}, u32[]{:S(2)}) %collective-permute-start.9) | collective-permute-done | bytes 204832 | tf_op jit(solution)/shard_map/ppermute | solution.py:113
  65.9 0.9 copy-done.1
  66.8 0.9 copy-done.3
  67.8 2.5 %shard_map.118 = (bf16[1,256,256]{2,1,0:T(8,128)(2,1)S(1)}, bf16[1,256,256]{2,1,0:T(8,128)(2,1)S(1)}, bf16[1600,256]{1,0:T(8,128)(2,1)S(1)}, bf16[1600,256]{1,0:T(8,128)(2,1)S(1)}) custom-call(bf16[256,1600]{1,0:T(8,128)(2,1)S(1)} %get-tuple-element.28.normed_ref, bf16[256,1600]{1,0:T(8,128)(2,1)S(1)} %get-tuple-element.29.grad_ref, ...), custom_call_target="tpu_custom_call" | custom-call | tf_op jit(solution)/shard_map/pallas_call | solution.py:470
  70.3 1.4 %shard_map.119 = (f32[2,16,8,1600]{3,2,1,0:T(8,128)S(1)}, bf16[2,16,8,1600]{3,2,1,0:T(8,128)(2,1)S(1)}) custom-call(s32[2]{0:T(128)S(1)} %pad_add_fusion.me_ref, bf16[1,256,256]{2,1,0:T(8,128)(2,1)S(1)} %get-tuple-element.37.hidden_ref.first_ref, bf16[1,256,256]{2,1,0:T(8,128)(2,1)S(1)} %get-tuple-element.38.pre_ref.first_ref, ...), custom_call_target="tpu_custom_call" | custom-call | tf_op jit(solution)/shard_map/pallas_call | solution.py:395
  71.8 2.4 %collective-permute-done.12.got_ref = bf16[2,16,8,1600]{3,2,1,0:T(8,128)(2,1)S(1)} collective-permute-done((bf16[2,16,8,1600]{3,2,1,0:T(8,128)(2,1)S(1)}, bf16[2,16,8,1600]{3,2,1,0:T(8,128)(2,1)S(1)}, u32[]{:S(2)}, u32[]{:S(2)}) %collective-permute-start.12) | collective-permute-done | bytes 819232 | tf_op jit(solution)/shard_map/ppermute | solution.py:113
  74.2 0.2 shard_map.120
  74.4 1.8 %collective-permute-start.13 = (bf16[2,8,8,1600]{3,2,1,0:T(8,128)(2,1)S(1)}, bf16[2,8,8,1600]{3,2,1,0:T(8,128)(2,1)S(1)}, u32[]{:S(2)}, u32[]{:S(2)}) collective-permute-start(bf16[2,8,8,1600]{3,2,1,0:T(8,128)(2,1)S(1)} %get-tuple-element.44), channel_id=1, source_target_pairs={{0,2},{1,3},{2,0},{3,1},{4,6},{5,7},{6,4},{7,5},{8,10},{9,11},{10,... | collective-permute-start | bytes 1228808 | tf_op jit(solution)/shard_map/ppermute | solution.py:113
  76.2 10.0 %collective-permute-start.14 = (bf16[1,256,256]{2,1,0:T(8,128)(2,1)S(1)}, bf16[1,256,256]{2,1,0:T(8,128)(2,1)S(1)}, u32[]{:S(2)}, u32[]{:S(2)}) collective-permute-start(bf16[1,256,256]{2,1,0:T(8,128)(2,1)S(1)} %get-tuple-element.37.hidden_ref.first_ref), channel_id=1, source_target_pairs={{0,16},{4,20},{8,24},{12,28},{16,0},{20,4},{24,8},{28,12},{1,17},{... | collective-permute-start | bytes 393224 | tf_op jit(solution)/shard_map/ppermute | solution.py:113
  86.2 1.3 collective-permute-start.17
  87.4 5.0 %collective-permute-done.14.second_ref = bf16[1,256,256]{2,1,0:T(8,128)(2,1)S(1)} collective-permute-done((bf16[1,256,256]{2,1,0:T(8,128)(2,1)S(1)}, bf16[1,256,256]{2,1,0:T(8,128)(2,1)S(1)}, u32[]{:S(2)}, u32[]{:S(2)}) %collective-permute-start.14) | collective-permute-done | bytes 131104 | tf_op jit(solution)/shard_map/ppermute | solution.py:113
  92.5 0.1 collective-permute-start.15
  92.6 0.1 collective-permute-start.18
  92.7 0.8 shard_map.121
  93.6 6.3 %all-to-all-start = ((bf16[8,16,1600]{2,1,0:T(8,128)(2,1)}), bf16[8,16,1600]{2,1,0:T(8,128)(2,1)S(1)}, u32[]{:S(2)}, u32[]{:S(2)}) async-start(bf16[8,16,1600]{2,1,0:T(8,128)(2,1)} %shard_map.121), calls=%async_computation | async-start | bytes 851968 | tf_op jit(solution)/shard_map/all_to_all | solution.py:493
  99.9 6.8 %collective-permute-done.15.second_ref = bf16[2,256,256]{2,1,0:T(8,128)(2,1)S(1)} collective-permute-done((bf16[2,256,256]{2,1,0:T(8,128)(2,1)S(1)}, bf16[2,256,256]{2,1,0:T(8,128)(2,1)S(1)}, u32[]{:S(2)}, u32[]{:S(2)}) %collective-permute-start.15) | collective-permute-done | bytes 262176 | tf_op jit(solution)/shard_map/ppermute | solution.py:113
  106.7 0.3 collective-permute-start.16
  107.0 5.3 %collective-permute-done.18.second_ref = bf16[2,256,256]{2,1,0:T(8,128)(2,1)S(1)} collective-permute-done((bf16[2,256,256]{2,1,0:T(8,128)(2,1)S(1)}, bf16[2,256,256]{2,1,0:T(8,128)(2,1)S(1)}, u32[]{:S(2)}, u32[]{:S(2)}) %collective-permute-start.18) | collective-permute-done | bytes 262176 | tf_op jit(solution)/shard_map/ppermute | solution.py:113
  112.4 4.9 %shard_map.127 = (bf16[1600,2048]{1,0:T(8,128)(2,1)}, bf16[1600,2048]{1,0:T(8,128)(2,1)}) custom-call(s32[2]{0:T(128)S(1)} %pad_add_fusion.me_ref, bf16[4,256,256]{2,1,0:T(8,128)(2,1)S(1)} %shard_map.124.hidden_ref, bf16[4,256,256]{2,1,0:T(8,128)(2,1)S(1)} %shard_map.126.pre_ref, bf16[256,1600]{1,0:T(8,128)(2,1)S(1)} %get-tuple-element.28.normed_ref, ...), custom_call_target="tpu_custom_call" | custom-call | flops 1677721600 | bytes 8192000 | tf_op jit(solution)/shard_map/pallas_call | solution.py:368
  117.3 3.0 %collective-permute-done.16.hidden_ref = bf16[4,256,256]{2,1,0:T(8,128)(2,1)S(1)} collective-permute-done((bf16[4,256,256]{2,1,0:T(8,128)(2,1)S(1)}, bf16[4,256,256]{2,1,0:T(8,128)(2,1)S(1)}, u32[]{:S(2)}, u32[]{:S(2)}) %collective-permute-start.16) | collective-permute-done | bytes 524320 | tf_op jit(solution)/shard_map/ppermute | solution.py:113
  120.3 4.1 %collective-permute-done.19.pre_ref = bf16[4,256,256]{2,1,0:T(8,128)(2,1)S(1)} collective-permute-done((bf16[4,256,256]{2,1,0:T(8,128)(2,1)S(1)}, bf16[4,256,256]{2,1,0:T(8,128)(2,1)S(1)}, u32[]{:S(2)}, u32[]{:S(2)}) %collective-permute-start.19) | collective-permute-done | bytes 524320 | tf_op jit(solution)/shard_map/ppermute | solution.py:113
  124.4 4.9 %shard_map.128 = (bf16[1600,2048]{1,0:T(8,128)(2,1)}, bf16[1600,2048]{1,0:T(8,128)(2,1)}) custom-call(s32[2]{0:T(128)S(1)} %pad_add_fusion.me_ref, bf16[4,256,256]{2,1,0:T(8,128)(2,1)S(1)} %collective-permute-done.16.hidden_ref, bf16[4,256,256]{2,1,0:T(8,128)(2,1)S(1)} %collective-permute-done.19.pre_ref, ...), custom_call_target="tpu_custom_call", output_to_operand_aliasing={{0}: (5, {}), {1}: (6, {})} | custom-call | flops 1677721600 | bytes 8192000 | tf_op jit(solution)/shard_map/pallas_call | solution.py:368
  129.3 1.5 %shard_map.122 = (bf16[16,1600]{1,0:T(8,128)(2,1)}, bf16[8,1600]{1,0:T(8,128)(2,1)}) custom-call(s32[2]{0:T(128)S(1)} %pad_add_fusion.me_ref, s32[1,4]{1,0:T(1,128)S(1)} %copy-done.6, s32[1,8]{1,0:T(1,128)S(1)} %copy-done.7, bf16[8,16,1600]{2,1,0:T(8,128)(2,1)S(1)} %all-to-all-done.tail_ref, f32[16,1600]{1,0:T(8,128)S(1)} %get-tuple-element.45.extra_ref, ...), custom_call_target="tpu_custom_call" | custom-call | tf_op jit(solution)/shard_map/pallas_call | solution.py:395
  (30 shorter events, 0.4 us)
Async XLA Ops:
  1.6 6.8 %collective-permute-start = (bf16[1,16,1600]{2,1,0:T(8,128)(2,1)S(1)}, bf16[1,16,1600]{2,1,0:T(8,128)(2,1)S(1)}, u32[]{:S(2)}, u32[]{:S(2)}) collective-permute-start(bf16[1,16,1600]{2,1,0:T(8,128)(2,1)S(1)} %shard_map.111.first_ref), channel_id=1, source_target_pairs={{0,16},{4,20},{8,24},{12,28},{16,0},{20,4},{24,8},{28,12},{1,17},{... | collective-permute-start | bytes 153608 | tf_op jit(solution)/shard_map/ppermute | solution.py:113
  8.5 4.8 %collective-permute-start.1 = (bf16[2,16,1600]{2,1,0:T(8,128)(2,1)S(1)}, bf16[2,16,1600]{2,1,0:T(8,128)(2,1)S(1)}, u32[]{:S(2)}, u32[]{:S(2)}) collective-permute-start(bf16[2,16,1600]{2,1,0:T(8,128)(2,1)S(1)} %shard_map.112.first_ref), channel_id=1, source_target_pairs={{0,8},{4,12},{8,0},{12,4},{16,24},{20,28},{24,16},{28,20},{1,9},{5... | collective-permute-start | bytes 307208 | tf_op jit(solution)/shard_map/ppermute | solution.py:113
  13.3 5.9 %collective-permute-start.2 = (bf16[4,16,1600]{2,1,0:T(8,128)(2,1)S(1)}, bf16[4,16,1600]{2,1,0:T(8,128)(2,1)S(1)}, u32[]{:S(2)}, u32[]{:S(2)}) collective-permute-start(bf16[4,16,1600]{2,1,0:T(8,128)(2,1)S(1)} %shard_map.113.first_ref), channel_id=1, source_target_pairs={{0,4},{4,0},{8,12},{12,8},{16,20},{20,16},{24,28},{28,24},{1,5},{5... | collective-permute-start | bytes 614408 | tf_op jit(solution)/shard_map/ppermute | solution.py:113
  19.2 8.2 %collective-permute-start.3 = (bf16[8,16,1600]{2,1,0:T(8,128)(2,1)S(1)}, bf16[8,16,1600]{2,1,0:T(8,128)(2,1)S(1)}, u32[]{:S(2)}, u32[]{:S(2)}) collective-permute-start(bf16[8,16,1600]{2,1,0:T(8,128)(2,1)S(1)} %shard_map.114.first_ref), channel_id=1, source_target_pairs={{0,2},{1,3},{2,0},{3,1},{4,6},{5,7},{6,4},{7,5},{8,10},{9,11},{10,... | collective-permute-start | bytes 1228808 | tf_op jit(solution)/shard_map/ppermute | solution.py:113
  27.5 21.5 %collective-permute-start.4 = (bf16[16,16,1600]{2,1,0:T(8,128)(2,1)S(1)}, bf16[16,16,1600]{2,1,0:T(8,128)(2,1)S(1)}, u32[]{:S(2)}, u32[]{:S(2)}) collective-permute-start(bf16[16,16,1600]{2,1,0:T(8,128)(2,1)S(1)} %shard_map.115.near_ref), channel_id=1, source_target_pairs={{0,1},{1,0},{2,3},{3,2},{4,5},{5,4},{6,7},{7,6},{8,9},{9,8},{10,11... | collective-permute-start | bytes 2457608 | tf_op jit(solution)/shard_map/ppermute | solution.py:113
  30.1 7.5 %collective-permute-start.5 = (bf16[2,200,256]{2,1,0:T(8,128)(2,1)S(1)}, bf16[2,200,256]{2,1,0:T(8,128)(2,1)S(1)}, u32[]{:S(2)}, u32[]{:S(2)}) collective-permute-start(bf16[2,200,256]{2,1,0:T(8,128)(2,1)S(1)} %get-tuple-element.30), channel_id=1, source_target_pairs={{0,4},{4,0},{8,12},{12,8},{16,20},{20,16},{24,28},{28,24},{1,5},{5... | collective-permute-start | bytes 614408 | tf_op jit(solution)/shard_map/ppermute | solution.py:113
  31.9 14.9 %collective-permute-start.6 = (bf16[2,200,256]{2,1,0:T(8,128)(2,1)S(1)}, bf16[2,200,256]{2,1,0:T(8,128)(2,1)S(1)}, u32[]{:S(2)}, u32[]{:S(2)}) collective-permute-start(bf16[2,200,256]{2,1,0:T(8,128)(2,1)S(1)} %get-tuple-element.31), channel_id=1, source_target_pairs={{0,8},{4,12},{8,0},{12,4},{16,24},{20,28},{24,16},{28,20},{1,9},{5... | collective-permute-start | bytes 614408 | tf_op jit(solution)/shard_map/ppermute | solution.py:113
  33.0 21.0 %collective-permute-start.7 = (bf16[2,200,256]{2,1,0:T(8,128)(2,1)}, bf16[2,200,256]{2,1,0:T(8,128)(2,1)}, u32[]{:S(2)}, u32[]{:S(2)}) collective-permute-start(bf16[2,200,256]{2,1,0:T(8,128)(2,1)} %get-tuple-element.32), channel_id=1, source_target_pairs={{0,12},{4,8},{8,4},{12,0},{16,28},{20,24},{24,20},{28,16},{1,13},{... | collective-permute-start | bytes 614408 | tf_op jit(solution)/shard_map/ppermute | solution.py:113
  33.6 20.4 %collective-permute-start.8 = (bf16[2,200,256]{2,1,0:T(8,128)(2,1)}, bf16[2,200,256]{2,1,0:T(8,128)(2,1)}, u32[]{:S(2)}, u32[]{:S(2)}) collective-permute-start(bf16[2,200,256]{2,1,0:T(8,128)(2,1)} %get-tuple-element.33), channel_id=1, source_target_pairs={{0,16},{4,20},{8,24},{12,28},{16,0},{20,4},{24,8},{28,12},{1,17},{... | collective-permute-start | bytes 614408 | tf_op jit(solution)/shard_map/ppermute | solution.py:113
  37.6 0.7 copy-start
  38.3 27.6 %collective-permute-start.9 = (bf16[2,200,256]{2,1,0:T(8,128)(2,1)}, bf16[2,200,256]{2,1,0:T(8,128)(2,1)}, u32[]{:S(2)}, u32[]{:S(2)}) collective-permute-start(bf16[2,200,256]{2,1,0:T(8,128)(2,1)} %get-tuple-element.34), channel_id=1, source_target_pairs={{0,20},{4,16},{8,28},{12,24},{16,4},{20,0},{24,12},{28,8},{1,21},{... | collective-permute-start | bytes 614408 | tf_op jit(solution)/shard_map/ppermute | solution.py:113
  46.8 0.7 copy-start.2
  47.5 18.4 %collective-permute-start.10 = (bf16[2,200,256]{2,1,0:T(8,128)(2,1)}, bf16[2,200,256]{2,1,0:T(8,128)(2,1)}, u32[]{:S(2)}, u32[]{:S(2)}) collective-permute-start(bf16[2,200,256]{2,1,0:T(8,128)(2,1)} %get-tuple-element.35), channel_id=1, source_target_pairs={{0,24},{4,28},{8,16},{12,20},{16,8},{20,12},{24,0},{28,4},{1,25},{... | collective-permute-start | bytes 614408 | tf_op jit(solution)/shard_map/ppermute | solution.py:113
  49.0 16.9 %collective-permute-start.11 = (bf16[2,200,256]{2,1,0:T(8,128)(2,1)}, bf16[2,200,256]{2,1,0:T(8,128)(2,1)}, u32[]{:S(2)}, u32[]{:S(2)}) collective-permute-start(bf16[2,200,256]{2,1,0:T(8,128)(2,1)} %get-tuple-element.36), channel_id=1, source_target_pairs={{0,28},{4,24},{8,20},{12,16},{16,12},{20,8},{24,4},{28,0},{1,29},{... | collective-permute-start | bytes 614408 | tf_op jit(solution)/shard_map/ppermute | solution.py:113
  65.9 0.9 copy-start.1
  66.8 0.9 copy-start.3
  71.8 2.4 %collective-permute-start.12 = (bf16[2,16,8,1600]{3,2,1,0:T(8,128)(2,1)S(1)}, bf16[2,16,8,1600]{3,2,1,0:T(8,128)(2,1)S(1)}, u32[]{:S(2)}, u32[]{:S(2)}) collective-permute-start(bf16[2,16,8,1600]{3,2,1,0:T(8,128)(2,1)S(1)} %get-tuple-element.42), channel_id=1, source_target_pairs={{0,1},{1,0},{2,3},{3,2},{4,5},{5,4},{6,7},{7,6},{8,9},{9,8},{10,11... | collective-permute-start | bytes 2457608 | tf_op jit(solution)/shard_map/ppermute | solution.py:113
  74.4 18.3 %collective-permute-start.13 = (bf16[2,8,8,1600]{3,2,1,0:T(8,128)(2,1)S(1)}, bf16[2,8,8,1600]{3,2,1,0:T(8,128)(2,1)S(1)}, u32[]{:S(2)}, u32[]{:S(2)}) collective-permute-start(bf16[2,8,8,1600]{3,2,1,0:T(8,128)(2,1)S(1)} %get-tuple-element.44), channel_id=1, source_target_pairs={{0,2},{1,3},{2,0},{3,1},{4,6},{5,7},{6,4},{7,5},{8,10},{9,11},{10,... | collective-permute-start | bytes 1228808 | tf_op jit(solution)/shard_map/ppermute | solution.py:113
  76.2 16.3 %collective-permute-start.14 = (bf16[1,256,256]{2,1,0:T(8,128)(2,1)S(1)}, bf16[1,256,256]{2,1,0:T(8,128)(2,1)S(1)}, u32[]{:S(2)}, u32[]{:S(2)}) collective-permute-start(bf16[1,256,256]{2,1,0:T(8,128)(2,1)S(1)} %get-tuple-element.37.hidden_ref.first_ref), channel_id=1, source_target_pairs={{0,16},{4,20},{8,24},{12,28},{16,0},{20,4},{24,8},{28,12},{1,17},{... | collective-permute-start | bytes 393224 | tf_op jit(solution)/shard_map/ppermute | solution.py:113
  86.2 6.4 %collective-permute-start.17 = (bf16[1,256,256]{2,1,0:T(8,128)(2,1)S(1)}, bf16[1,256,256]{2,1,0:T(8,128)(2,1)S(1)}, u32[]{:S(2)}, u32[]{:S(2)}) collective-permute-start(bf16[1,256,256]{2,1,0:T(8,128)(2,1)S(1)} %get-tuple-element.38.pre_ref.first_ref), channel_id=1, source_target_pairs={{0,4},{4,0},{8,12},{12,8},{16,20},{20,16},{24,28},{28,24},{1,5},{5... | collective-permute-start | bytes 393224 | tf_op jit(solution)/shard_map/ppermute | solution.py:113
  92.5 14.1 %collective-permute-start.15 = (bf16[2,256,256]{2,1,0:T(8,128)(2,1)S(1)}, bf16[2,256,256]{2,1,0:T(8,128)(2,1)S(1)}, u32[]{:S(2)}, u32[]{:S(2)}) collective-permute-start(bf16[2,256,256]{2,1,0:T(8,128)(2,1)S(1)} %shard_map.123.first_ref), channel_id=1, source_target_pairs={{0,8},{4,12},{8,0},{12,4},{16,24},{20,28},{24,16},{28,20},{1,9},{5... | collective-permute-start | bytes 786440 | tf_op jit(solution)/shard_map/ppermute | solution.py:113
  92.6 19.7 %collective-permute-start.18 = (bf16[2,256,256]{2,1,0:T(8,128)(2,1)S(1)}, bf16[2,256,256]{2,1,0:T(8,128)(2,1)S(1)}, u32[]{:S(2)}, u32[]{:S(2)}) collective-permute-start(bf16[2,256,256]{2,1,0:T(8,128)(2,1)S(1)} %shard_map.125.first_ref), channel_id=1, source_target_pairs={{0,16},{4,20},{8,24},{12,28},{16,0},{20,4},{24,8},{28,12},{1,17},{... | collective-permute-start | bytes 786440 | tf_op jit(solution)/shard_map/ppermute | solution.py:113
  93.6 35.7 %all-to-all-start = ((bf16[8,16,1600]{2,1,0:T(8,128)(2,1)}), bf16[8,16,1600]{2,1,0:T(8,128)(2,1)S(1)}, u32[]{:S(2)}, u32[]{:S(2)}) async-start(bf16[8,16,1600]{2,1,0:T(8,128)(2,1)} %shard_map.121), calls=%async_computation | async-start | bytes 851968 | tf_op jit(solution)/shard_map/all_to_all | solution.py:493
  106.7 13.6 %collective-permute-start.16 = (bf16[4,256,256]{2,1,0:T(8,128)(2,1)S(1)}, bf16[4,256,256]{2,1,0:T(8,128)(2,1)S(1)}, u32[]{:S(2)}, u32[]{:S(2)}) collective-permute-start(bf16[4,256,256]{2,1,0:T(8,128)(2,1)S(1)} %shard_map.124.hidden_ref), channel_id=1, source_target_pairs={{0,4},{4,0},{8,12},{12,8},{16,20},{20,16},{24,28},{28,24},{1,5},{5... | collective-permute-start | bytes 1572872 | tf_op jit(solution)/shard_map/ppermute | solution.py:113
  112.4 12.0 %collective-permute-start.19 = (bf16[4,256,256]{2,1,0:T(8,128)(2,1)S(1)}, bf16[4,256,256]{2,1,0:T(8,128)(2,1)S(1)}, u32[]{:S(2)}, u32[]{:S(2)}) collective-permute-start(bf16[4,256,256]{2,1,0:T(8,128)(2,1)S(1)} %shard_map.126.pre_ref), channel_id=1, source_target_pairs={{0,8},{4,12},{8,0},{12,4},{16,24},{20,28},{24,16},{28,20},{1,9},{5... | collective-permute-start | bytes 1572872 | tf_op jit(solution)/shard_map/ppermute | solution.py:113
  124.4 4.9 %copy-start.4 = (bf16[8,1600]{1,0:T(8,128)(2,1)S(1)}, bf16[8,1600]{1,0:T(8,128)(2,1)}, u32[]{:S(2)}) copy-start(bf16[8,1600]{1,0:T(8,128)(2,1)} %patch_ref.1) | copy-start | bytes 76804
  124.4 4.9 %copy-start.5 = (bf16[16,1600]{1,0:T(8,128)(2,1)S(1)}, bf16[16,1600]{1,0:T(8,128)(2,1)}, u32[]{:S(2)}) copy-start(bf16[16,1600]{1,0:T(8,128)(2,1)} %text_ref.1) | copy-start | bytes 153604
  124.4 4.9 %copy-start.6 = (s32[1,4]{1,0:T(1,128)S(1)}, s32[1,4]{1,0:T(1,128)}, u32[]{:S(2)}) copy-start(s32[1,4]{1,0:T(1,128)} %count_ref.1) | copy-start | bytes 52
  124.4 4.9 %copy-start.7 = (s32[1,8]{1,0:T(1,128)S(1)}, s32[1,8]{1,0:T(1,128)}, u32[]{:S(2)}) copy-start(s32[1,8]{1,0:T(1,128)} %place_ref.1) | copy-start | bytes 100

commit v2 on v1

--- a/solution.py
+++ b/solution.py
@@ -244,10 +244,10 @@
 
 
 def hidden_kernel(normed_ref, grad_ref, expand_at, project_at, *refs):
-    blocks = refs[:-5]
-    hidden_ref, pre_ref, expand_ref, project_ref, sems = refs[-5:]
+    blocks = refs[:-4]
+    both_ref, expand_ref, project_ref, sems = refs[-4:]
     part = expand_at.shape[0]
-    units = hidden_ref.shape[2]
+    units = both_ref.shape[2]
     me = lax.axis_index("dp")
     copies = []
     for k, (source, whole) in enumerate(((expand_at, expand_ref), (project_at, project_ref))):
@@ -262,16 +262,16 @@
     fetch(copies)
     preact = jnp.dot(normed_ref[...], expand_ref[...], preferred_element_type=jnp.float32)
     activated, derivative = gelu_pair(preact)
-    hidden_ref[0] = activated.astype(jnp.bfloat16)
+    both_ref[0] = activated.astype(jnp.bfloat16)
     grad_hidden = jnp.dot(grad_ref[...], project_ref[...], preferred_element_type=jnp.float32)
-    pre_ref[0] = (grad_hidden * derivative).astype(jnp.bfloat16)
+    both_ref[1] = (grad_hidden * derivative).astype(jnp.bfloat16)
 
 
 def share_kernel(
     sections, capacity, steps,
-    me_ref, hidden_ref, pre_ref, expand_ref, project_ref, keep_ref, send_ref,
+    me_ref, both_ref, expand_ref, project_ref, keep_ref, send_ref,
 ):
-    rows = hidden_ref.shape[1]
+    rows = both_ref.shape[1]
     slots = sections * capacity
     row = lax.broadcasted_iota(jnp.int32, (rows, rows), 0)
     column = lax.broadcasted_iota(jnp.int32, (rows, rows), 1)
@@ -284,11 +284,11 @@
         base + (inside >> log2(capacity)) * slots + goal * capacity + (inside & (capacity - 1))
     )
     normed_from = base + goal * slots + inside
-    for k, (ref, source, weight_ref) in enumerate(
-        ((hidden_ref, mixed_from, project_ref), (pre_ref, normed_from, expand_ref))
+    for k, (source, weight_ref) in enumerate(
+        ((mixed_from, project_ref), (normed_from, expand_ref))
     ):
         turn = (column == source).astype(jnp.float32).astype(jnp.bfloat16)
-        turned = jnp.dot(turn, ref[0], preferred_element_type=jnp.float32).astype(jnp.bfloat16)
+        turned = jnp.dot(turn, both_ref[k], preferred_element_type=jnp.float32).astype(jnp.bfloat16)
         share = lax.dot_general(
             turned, weight_ref[...], (((1,), (1,)), ((), ())), preferred_element_type=jnp.float32
         )
@@ -310,14 +310,9 @@
         out_ref[d] = jnp.concatenate([total[0, d], total[1, d]], axis=0).astype(jnp.bfloat16)
 
 
-def weight_grad_kernel(me_ref, hidden_ref, pre_ref, normed_ref, grad_ref, *refs):
-    expand_ref, project_ref = refs[-2:]
-    contract = (((0,), (0,)), ((), ()))
-    expand_ref[...] = lax.dot_general(
-        normed_ref[...], pre_ref[0], contract, preferred_element_type=jnp.float32
-    ).astype(jnp.bfloat16)
-    project_ref[...] = lax.dot_general(
-        grad_ref[...], hidden_ref[0], contract, preferred_element_type=jnp.float32
+def weight_grad_kernel(me_ref, block_ref, rows_ref, *refs):
+    refs[-1][...] = lax.dot_general(
+        rows_ref[...], block_ref[0], (((0,), (0,)), ((), ())), preferred_element_type=jnp.float32
     ).astype(jnp.bfloat16)
 
 
@@ -354,40 +349,35 @@
     ).astype(jnp.bfloat16)
 
 
-def weight_grads(
-    me, hidden, pre, first_index, hidden_steps, pre_steps, normed, grad_all, width, before
-):
-    count, rows, units = hidden.shape
-    features = normed.shape[1]
-
-    def column(steps):
-        return lambda i, me_ref: (0, me_ref[0] ^ masked_steps(first_index + i, steps))
-
-    whole = pl.BlockSpec((rows, features), lambda i, me_ref: (0, 0))
-    block = pl.BlockSpec((1, rows, units), lambda i, me_ref: (i, 0, 0))
+def weight_grads(me, blocks, first_index, steps, values, width, before=()):
+    count, rows, units = blocks.shape
+    features = values.shape[1]
     return pl.pallas_call(
         weight_grad_kernel,
         grid_spec=pltpu.PrefetchScalarGridSpec(
             num_scalar_prefetch=1,
             grid=(count,),
-            in_specs=[block, block, whole, whole]
+            in_specs=[
+                pl.BlockSpec((1, rows, units), lambda i, me_ref: (i, 0, 0)),
+                pl.BlockSpec((rows, features), lambda i, me_ref: (0, 0)),
+            ]
             + [pl.BlockSpec(memory_space=pl.ANY)] * len(before),
-            out_specs=[
-                pl.BlockSpec((features, units), column(pre_steps)),
-                pl.BlockSpec((features, units), column(hidden_steps)),
-            ],
+            out_specs=pl.BlockSpec(
+                (features, units),
+                lambda i, me_ref: (0, me_ref[0] ^ masked_steps(first_index + i, steps)),
+            ),
         ),
-        out_shape=[jax.ShapeDtypeStruct((features, width), jnp.bfloat16)] * 2,
-        input_output_aliases={5: 0, 6: 1} if before else {},
+        out_shape=jax.ShapeDtypeStruct((features, width), jnp.bfloat16),
+        input_output_aliases={3: 0} if before else {},
         compiler_params=pltpu.CompilerParams(
             dimension_semantics=("arbitrary",), vmem_limit_bytes=12 << 20
         ),
         cost_estimate=pl.CostEstimate(
-            flops=4 * count * rows * features * units,
-            bytes_accessed=4 * count * units * features + 4 * rows * features,
+            flops=2 * count * rows * features * units,
+            bytes_accessed=2 * count * units * features + 2 * rows * features,
             transcendentals=0,
         ),
-    )(me, hidden, pre, normed, grad_all, *before)
+    )(me, blocks, values, *before)
 
 
 def call(kernel, out_shape, smem, vmem, scratch=()):
@@ -405,6 +395,17 @@
 def join(first, second):
     both = (first.shape[0] + second.shape[0], *first.shape[1:])
     return call(join_kernel, jax.ShapeDtypeStruct(both, first.dtype), (), (first, second))
+
+
+def join_pairs_kernel(first_ref, second_ref, hidden_ref, pre_ref):
+    for k, out_ref in enumerate((hidden_ref, pre_ref)):
+        out_ref[0] = first_ref[k]
+        out_ref[1] = second_ref[k]
+
+
+def join_pairs(first, second):
+    out = jax.ShapeDtypeStruct(first.shape, first.dtype)
+    return call(join_pairs_kernel, [out, out], (), (first, second))
 
 
 def move_rows_plan(
@@ -467,11 +468,11 @@
         (me,), (held, got, gain),
     )
 
-    hidden_near, pre_near, expand_slice, project_slice = pl.pallas_call(
+    both, expand_slice, project_slice = pl.pallas_call(
         hidden_kernel,
-        out_shape=[shape((1, rows, units), kept)] * 2 + [shape((features, units), kept)] * 2,
+        out_shape=[shape((2, rows, units), kept)] + [shape((features, units), kept)] * 2,
         in_specs=[VMEM_SPEC] * 2 + [hbm] * 2 + [pl.BlockSpec(memory_space=pl.ANY)] * len(arrived),
-        out_specs=[VMEM_SPEC] * 4,
+        out_specs=[VMEM_SPEC] * 3,
         scratch_shapes=[pltpu.SemaphoreType.DMA((2 * replicas,))],
         compiler_params=pltpu.CompilerParams(vmem_limit_bytes=12 << 20),
     )(normed, grad_all, *in_hbm(expand_weight, project_turned), *arrived)
@@ -480,7 +481,7 @@
     keep, send = call(
         functools.partial(share_kernel, sections, capacity, tail_steps),
         [shape((2, devices // 2, slots, features), kind) for kind in (wide, kept)],
-        (me,), (hidden_near, pre_near, expand_slice, project_slice),
+        (me,), (both, expand_slice, project_slice),
     )
     for place, step in enumerate(tail_steps):
         got = swap(send, "section", step)
@@ -492,22 +493,22 @@
     tail = call(address_kernel, shape((replicas, 2 * slots, features), kept), (), (keep, got))
     tail = lax.all_to_all(tail, "dp", split_axis=0, concat_axis=0, tiled=True)
 
-    hidden_steps, pre_steps = dp_steps, dp_steps[-1:] + dp_steps[:-1]
-    for hidden_step, pre_step in zip(hidden_steps, pre_steps):
-        hidden_far = swap(hidden_near, "dp", hidden_step)
-        pre_far = swap(pre_near, "dp", pre_step)
-        if hidden_near.shape[0] < replicas // 2:
-            hidden_near = join(hidden_near, hidden_far)
-            pre_near = join(pre_near, pre_far)
-
-    grads = weight_grads(
-        me, hidden_near, pre_near, 0,
-        hidden_steps, pre_steps, normed, grad_all, width, (),
-    )
-    expand_grad, project_grad = weight_grads(
-        me, hidden_far, pre_far, replicas // 2,
-        hidden_steps, pre_steps, normed, grad_all, width, grads,
-    )
+    far_both = swap(both, "dp", dp_steps[0])
+    hidden_steps, pre_steps = dp_steps, dp_steps[:1] + dp_steps[:0:-1]
+    hidden, pre = join_pairs(both, far_both)
+    for place, (hidden_step, pre_step) in enumerate(zip(hidden_steps[1:], pre_steps[1:]), 1):
+        hidden_far = swap(hidden, "dp", hidden_step)
+        pre_far = swap(pre, "dp", pre_step)
+        if hidden.shape[0] < replicas // 2:
+            hidden, pre = join(hidden, hidden_far), join(pre, pre_far)
+
+    half = replicas // 2
+    project_grad = weight_grads(me, hidden, 0, hidden_steps, grad_all, width)
+    expand_grad = weight_grads(me, pre, 0, pre_steps, normed, width)
+    project_grad = weight_grads(
+        me, hidden_far, half, hidden_steps, grad_all, width, (project_grad,)
+    )
+    expand_grad = weight_grads(me, pre_far, half, pre_steps, normed, width, (expand_grad,))
     embedded, grad_rows = call(
         functools.partial(finish_kernel, capacity),
         [shape(text.shape, kept), shape(patches.shape, kept)],
@@ -528,7 +529,7 @@
     fits = rows * (features + width) <= features * width
     even = (
         all(power_of_two(n) for n in (replicas, sections, slots))
-        and replicas > 1
+        and replicas > 2
         and sections > 1
         and slots % 8 == 0
         and width % (128 * replicas) == 0

time: 131 us -> 128 us (0.977)
  waiting for transfers between devices: 61.3 us -> 53.8 us
  Pallas kernels: 21.9 us -> 26.6 us
    ppermute x20 -> x19, waiting for transfers between devices: 61.3 us -> 53.8 us  [swap(): return lax.ppermute(array, axis, [(i, i ^ step) for i in range(size)])]
    pallas_call x2 -> x4, Pallas kernels: 9.72 us -> 14.4 us  [weight_grads(): pl.pallas_call(weight_grad_kernel, grid_spec=pltpu.PrefetchScalarGridSpec...]
    ppermute x20 -> x19, starting transfers between devices: 36.4 us -> 39.3 us  [swap(): return lax.ppermute(array, axis, [(i, i ^ step) for i in range(size)])]
    all_to_all x1, starting transfers between devices: 6.33 us -> 3.46 us  [move_rows_plan(): tail = lax.all_to_all(tail, 'dp', split_axis=0, concat_axis=0, tiled=True)]
    pallas_call x13 -> x12, Pallas kernels: 6.12 us -> 6.13 us  [call(): pl.pallas_call(kernel, out_shape=out_shape, in_specs=[SMEM_SPEC] * len(sm...]
  transfers between devices with their start and end apart: 21 -> 20, of which waited for: 13 -> 10; matrix products, arithmetic and copies ran while one was open for 1% -> 1% of each run, Pallas kernels for 12% -> 16%
where the time goes in v2:
time: 128 us
  waiting for transfers between devices  53.8 us (42%)
  starting transfers between devices  42.8 us (33%)
  Pallas kernels  26.6 us (21%)
  local copies, waits for them, and re-layouts  3.94 us (3%)
    ppermute x19, waiting for transfers between devices, swap(): return lax.ppermute(array, axis, [(i, i ^ step) for i in range(size)])  53.8 us
    ppermute x19, starting transfers between devices, swap(): return lax.ppermute(array, axis, [(i, i ^ step) for i in range(size)])  39.3 us
    pallas_call x4, Pallas kernels, weight_grads(): pl.pallas_call(weight_grad_kernel, grid_spec=pltpu.PrefetchScalarGridSpec...  14.4 us
    pallas_call x12, Pallas kernels, call(): pl.pallas_call(kernel, out_shape=out_shape, in_specs=[SMEM_SPEC] * len(sm...  6.13 us
    all_to_all x1, starting transfers between devices, move_rows_plan(): tail = lax.all_to_all(tail, 'dp', split_axis=0, concat_axis=0, tiled=True)  3.46 us
    unnamed x16, local copies, waits for them, and re-layouts  3.24 us
  transfers between devices with their start and end apart: 20, of which 10 were waited for; matrix products, arithmetic and copies ran while one was open for 1% of the time, Pallas kernels for 16%

profile of v2, /device:TPU:0, one launch (start us, length us, event | category | flops | bytes accessed | tf_op | source)
XLA Modules:
  0.0 128.0 jit_solution(3696611767547469738)
XLA Ops:
  0.6 1.0 shard_map.111.first_ref
  1.6 4.1 %collective-permute-start = (bf16[1,16,1600]{2,1,0:T(8,128)(2,1)S(1)}, bf16[1,16,1600]{2,1,0:T(8,128)(2,1)S(1)}, u32[]{:S(2)}, u32[]{:S(2)}) collective-permute-start(bf16[1,16,1600]{2,1,0:T(8,128)(2,1)S(1)} %shard_map.111.first_ref), channel_id=1, source_target_pairs={{0,16},{4,20},{8,24},{12,28},{16,0},{20,4},{24,8},{28,12},{1,17},{... | collective-permute-start | bytes 153608 | tf_op jit(solution)/shard_map/ppermute | solution.py:113
  5.8 2.7 %collective-permute-done.second_ref = bf16[1,16,1600]{2,1,0:T(8,128)(2,1)S(1)} collective-permute-done((bf16[1,16,1600]{2,1,0:T(8,128)(2,1)S(1)}, bf16[1,16,1600]{2,1,0:T(8,128)(2,1)S(1)}, u32[]{:S(2)}, u32[]{:S(2)}) %collective-permute-start) | collective-permute-done | bytes 51232 | tf_op jit(solution)/shard_map/ppermute | solution.py:113
  8.5 1.4 %collective-permute-start.1 = (bf16[2,16,1600]{2,1,0:T(8,128)(2,1)S(1)}, bf16[2,16,1600]{2,1,0:T(8,128)(2,1)S(1)}, u32[]{:S(2)}, u32[]{:S(2)}) collective-permute-start(bf16[2,16,1600]{2,1,0:T(8,128)(2,1)S(1)} %shard_map.112.first_ref), channel_id=1, source_target_pairs={{0,8},{4,12},{8,0},{12,4},{16,24},{20,28},{24,16},{28,20},{1,9},{5... | collective-permute-start | bytes 307208 | tf_op jit(solution)/shard_map/ppermute | solution.py:113
  9.9 3.4 %collective-permute-done.1.second_ref = bf16[2,16,1600]{2,1,0:T(8,128)(2,1)S(1)} collective-permute-done((bf16[2,16,1600]{2,1,0:T(8,128)(2,1)S(1)}, bf16[2,16,1600]{2,1,0:T(8,128)(2,1)S(1)}, u32[]{:S(2)}, u32[]{:S(2)}) %collective-permute-start.1) | collective-permute-done | bytes 102432 | tf_op jit(solution)/shard_map/ppermute | solution.py:113
  13.3 1.8 %collective-permute-start.2 = (bf16[4,16,1600]{2,1,0:T(8,128)(2,1)S(1)}, bf16[4,16,1600]{2,1,0:T(8,128)(2,1)S(1)}, u32[]{:S(2)}, u32[]{:S(2)}) collective-permute-start(bf16[4,16,1600]{2,1,0:T(8,128)(2,1)S(1)} %shard_map.113.first_ref), channel_id=1, source_target_pairs={{0,4},{4,0},{8,12},{12,8},{16,20},{20,16},{24,28},{28,24},{1,5},{5... | collective-permute-start | bytes 614408 | tf_op jit(solution)/shard_map/ppermute | solution.py:113
  15.0 4.1 %collective-permute-done.2.second_ref = bf16[4,16,1600]{2,1,0:T(8,128)(2,1)S(1)} collective-permute-done((bf16[4,16,1600]{2,1,0:T(8,128)(2,1)S(1)}, bf16[4,16,1600]{2,1,0:T(8,128)(2,1)S(1)}, u32[]{:S(2)}, u32[]{:S(2)}) %collective-permute-start.2) | collective-permute-done | bytes 204832 | tf_op jit(solution)/shard_map/ppermute | solution.py:113
  19.2 1.8 %collective-permute-start.3 = (bf16[8,16,1600]{2,1,0:T(8,128)(2,1)S(1)}, bf16[8,16,1600]{2,1,0:T(8,128)(2,1)S(1)}, u32[]{:S(2)}, u32[]{:S(2)}) collective-permute-start(bf16[8,16,1600]{2,1,0:T(8,128)(2,1)S(1)} %shard_map.114.first_ref), channel_id=1, source_target_pairs={{0,2},{1,3},{2,0},{3,1},{4,6},{5,7},{6,4},{7,5},{8,10},{9,11},{10,... | collective-permute-start | bytes 1228808 | tf_op jit(solution)/shard_map/ppermute | solution.py:113
  21.0 6.4 %collective-permute-done.3.second_ref = bf16[8,16,1600]{2,1,0:T(8,128)(2,1)S(1)} collective-permute-done((bf16[8,16,1600]{2,1,0:T(8,128)(2,1)S(1)}, bf16[8,16,1600]{2,1,0:T(8,128)(2,1)S(1)}, u32[]{:S(2)}, u32[]{:S(2)}) %collective-permute-start.3) | collective-permute-done | bytes 409632 | tf_op jit(solution)/shard_map/ppermute | solution.py:113
  27.5 0.1 collective-permute-start.4
  27.5 2.5 %shard_map.117 = (bf16[2,200,256]{2,1,0:T(8,128)(2,1)S(1)}, bf16[2,200,256]{2,1,0:T(8,128)(2,1)S(1)}, bf16[2,200,256]{2,1,0:T(8,128)(2,1)}, bf16[2,200,256]{2,1,...) custom-call(bf16[200,2048]{1,0:T(8,128)(2,1)} %expand_at.3, ...), custom_call_target="tpu_custom_call" | custom-call | tf_op jit(solution)/shard_map/pallas_call | solution.py:448
  30.1 1.8 %collective-permute-start.5 = (bf16[2,200,256]{2,1,0:T(8,128)(2,1)S(1)}, bf16[2,200,256]{2,1,0:T(8,128)(2,1)S(1)}, u32[]{:S(2)}, u32[]{:S(2)}) collective-permute-start(bf16[2,200,256]{2,1,0:T(8,128)(2,1)S(1)} %get-tuple-element.27), channel_id=1, source_target_pairs={{0,4},{4,0},{8,12},{12,8},{16,20},{20,16},{24,28},{28,24},{1,5},{5... | collective-permute-start | bytes 614408 | tf_op jit(solution)/shard_map/ppermute | solution.py:113
  31.9 1.1 collective-permute-start.6
  33.0 0.6 collective-permute-start.7
  33.6 2.6 %collective-permute-start.8 = (bf16[2,200,256]{2,1,0:T(8,128)(2,1)}, bf16[2,200,256]{2,1,0:T(8,128)(2,1)}, u32[]{:S(2)}, u32[]{:S(2)}) collective-permute-start(bf16[2,200,256]{2,1,0:T(8,128)(2,1)} %get-tuple-element.30), channel_id=1, source_target_pairs={{0,16},{4,20},{8,24},{12,28},{16,0},{20,4},{24,8},{28,12},{1,17},{... | collective-permute-start | bytes 614408 | tf_op jit(solution)/shard_map/ppermute | solution.py:113
  36.3 1.3 %collective-permute-done.5.refs_0_ = bf16[2,200,256]{2,1,0:T(8,128)(2,1)S(1)} collective-permute-done((bf16[2,200,256]{2,1,0:T(8,128)(2,1)S(1)}, bf16[2,200,256]{2,1,0:T(8,128)(2,1)S(1)}, u32[]{:S(2)}, u32[]{:S(2)}) %collective-permute-start.5) | collective-permute-done | bytes 204832 | tf_op jit(solution)/shard_map/ppermute | solution.py:113
  37.6 0.7 copy-done
  38.3 3.6 %collective-permute-start.9 = (bf16[2,200,256]{2,1,0:T(8,128)(2,1)}, bf16[2,200,256]{2,1,0:T(8,128)(2,1)}, u32[]{:S(2)}, u32[]{:S(2)}) collective-permute-start(bf16[2,200,256]{2,1,0:T(8,128)(2,1)} %get-tuple-element.31), channel_id=1, source_target_pairs={{0,20},{4,16},{8,28},{12,24},{16,4},{20,0},{24,12},{28,8},{1,21},{... | collective-permute-start | bytes 614408 | tf_op jit(solution)/shard_map/ppermute | solution.py:113
  41.9 4.9 %collective-permute-done.6.refs_1_ = bf16[2,200,256]{2,1,0:T(8,128)(2,1)S(1)} collective-permute-done((bf16[2,200,256]{2,1,0:T(8,128)(2,1)S(1)}, bf16[2,200,256]{2,1,0:T(8,128)(2,1)S(1)}, u32[]{:S(2)}, u32[]{:S(2)}) %collective-permute-start.6) | collective-permute-done | bytes 204832 | tf_op jit(solution)/shard_map/ppermute | solution.py:113
  46.8 0.7 copy-done.2
  47.5 1.5 %collective-permute-start.10 = (bf16[2,200,256]{2,1,0:T(8,128)(2,1)}, bf16[2,200,256]{2,1,0:T(8,128)(2,1)}, u32[]{:S(2)}, u32[]{:S(2)}) collective-permute-start(bf16[2,200,256]{2,1,0:T(8,128)(2,1)} %get-tuple-element.32), channel_id=1, source_target_pairs={{0,24},{4,28},{8,16},{12,20},{16,8},{20,12},{24,0},{28,4},{1,25},{... | collective-permute-start | bytes 614408 | tf_op jit(solution)/shard_map/ppermute | solution.py:113
  49.0 2.3 %collective-permute-start.11 = (bf16[2,200,256]{2,1,0:T(8,128)(2,1)}, bf16[2,200,256]{2,1,0:T(8,128)(2,1)}, u32[]{:S(2)}, u32[]{:S(2)}) collective-permute-start(bf16[2,200,256]{2,1,0:T(8,128)(2,1)} %get-tuple-element.33), channel_id=1, source_target_pairs={{0,28},{4,24},{8,20},{12,16},{16,12},{20,8},{24,4},{28,0},{1,29},{... | collective-permute-start | bytes 614408 | tf_op jit(solution)/shard_map/ppermute | solution.py:113
  51.3 0.7 reshape.11.gain_ref
  52.0 0.1 pad_add_fusion.me_ref
  52.0 2.0 %shard_map.116 = (bf16[256,1600]{1,0:T(8,128)(2,1)S(1)}, bf16[256,1600]{1,0:T(8,128)(2,1)S(1)}, f32[16,1600]{1,0:T(8,128)S(1)}) custom-call(s32[2]{0:T(128)S(1)} %pad_add_fusion.me_ref, bf16[16,16,1600]{2,1,0:T(8,128)(2,1)S(1)} %shard_map.115.near_ref, bf16[16,16,1600]{2,1,0:T(8,128)(2,1)S(1)} %collective-permute-done.4.far_ref, f32[1,1600]{1,0:T(1,128)S(1)} %reshape.11.gain_ref), custom_call_target="tpu_custom_call" | custom-call | tf_op jit(solution)/shard_map/pallas_call | solution.py:385
  54.0 11.9 %collective-permute-done.9.refs_4_ = bf16[2,200,256]{2,1,0:T(8,128)(2,1)} collective-permute-done((bf16[2,200,256]{2,1,0:T(8,128)(2,1)}, bf16[2,200,256]{2,1,0:T(8,128)(2,1)}, u32[]{:S(2)}, u32[]{:S(2)}) %collective-permute-start.9) | collective-permute-done | bytes 204832 | tf_op jit(solution)/shard_map/ppermute | solution.py:113
  65.9 0.9 copy-done.1
  66.9 0.9 copy-done.3
  67.8 2.5 %shard_map.118 = (bf16[2,256,256]{2,1,0:T(8,128)(2,1)S(1)}, bf16[1600,256]{1,0:T(8,128)(2,1)S(1)}, bf16[1600,256]{1,0:T(8,128)(2,1)S(1)}) custom-call(bf16[256,1600]{1,0:T(8,128)(2,1)S(1)} %get-tuple-element.25.normed_ref.rows_ref, bf16[256,1600]{1,0:T(8,128)(2,1)S(1)} %get-tuple-element.26.grad_ref.rows_ref, bf16[200,2048]{1,0:T(8,128)(2,1)} %expand_at.3, ...), custom_call_target="tpu_custom_call" | custom-call | tf_op jit(solution)/shard_map/pallas_call | solution.py:471
  70.3 1.4 %shard_map.119 = (f32[2,16,8,1600]{3,2,1,0:T(8,128)S(1)}, bf16[2,16,8,1600]{3,2,1,0:T(8,128)(2,1)S(1)}) custom-call(s32[2]{0:T(128)S(1)} %pad_add_fusion.me_ref, bf16[2,256,256]{2,1,0:T(8,128)(2,1)S(1)} %get-tuple-element.34.both_ref.first_ref, bf16[1600,256]{1,0:T(8,128)(2,1)S(1)} %get-tuple-element.35.expand_ref, ...), custom_call_target="tpu_custom_call" | custom-call | tf_op jit(solution)/shard_map/pallas_call | solution.py:385
  71.8 0.1 collective-permute-start.12
  71.9 10.2 %collective-permute-start.14 = (bf16[2,256,256]{2,1,0:T(8,128)(2,1)S(1)}, bf16[2,256,256]{2,1,0:T(8,128)(2,1)S(1)}, u32[]{:S(2)}, u32[]{:S(2)}) collective-permute-start(bf16[2,256,256]{2,1,0:T(8,128)(2,1)S(1)} %get-tuple-element.34.both_ref.first_ref), channel_id=1, source_target_pairs={{0,16},{4,20},{8,24},{12,28},{16,0},{20,4},{24,8},{28,12},{1,17},{... | collective-permute-start | bytes 786440 | tf_op jit(solution)/shard_map/ppermute | solution.py:113
  82.1 0.2 shard_map.120
  82.3 1.6 %collective-permute-start.13 = (bf16[2,8,8,1600]{3,2,1,0:T(8,128)(2,1)S(1)}, bf16[2,8,8,1600]{3,2,1,0:T(8,128)(2,1)S(1)}, u32[]{:S(2)}, u32[]{:S(2)}) collective-permute-start(bf16[2,8,8,1600]{3,2,1,0:T(8,128)(2,1)S(1)} %get-tuple-element.40), channel_id=1, source_target_pairs={{0,2},{1,3},{2,0},{3,1},{4,6},{5,7},{6,4},{7,5},{8,10},{9,11},{10,... | collective-permute-start | bytes 1228808 | tf_op jit(solution)/shard_map/ppermute | solution.py:113
  83.9 10.7 %collective-permute-done.14.second_ref = bf16[2,256,256]{2,1,0:T(8,128)(2,1)S(1)} collective-permute-done((bf16[2,256,256]{2,1,0:T(8,128)(2,1)S(1)}, bf16[2,256,256]{2,1,0:T(8,128)(2,1)S(1)}, u32[]{:S(2)}, u32[]{:S(2)}) %collective-permute-start.14) | collective-permute-done | bytes 262176 | tf_op jit(solution)/shard_map/ppermute | solution.py:113
  94.6 0.1 collective-permute-start.17
  94.7 1.4 %collective-permute-start.15 = (bf16[2,256,256]{2,1,0:T(8,128)(2,1)S(1)}, bf16[2,256,256]{2,1,0:T(8,128)(2,1)S(1)}, u32[]{:S(2)}, u32[]{:S(2)}) collective-permute-start(bf16[2,256,256]{2,1,0:T(8,128)(2,1)S(1)} %get-tuple-element.44.first_ref), channel_id=1, source_target_pairs={{0,4},{4,0},{8,12},{12,8},{16,20},{20,16},{24,28},{28,24},{1,5},{5... | collective-permute-start | bytes 786440 | tf_op jit(solution)/shard_map/ppermute | solution.py:113
  96.1 0.8 shard_map.121
  96.9 3.5 %all-to-all-start = ((bf16[8,16,1600]{2,1,0:T(8,128)(2,1)}), bf16[8,16,1600]{2,1,0:T(8,128)(2,1)S(1)}, u32[]{:S(2)}, u32[]{:S(2)}) async-start(bf16[8,16,1600]{2,1,0:T(8,128)(2,1)} %shard_map.121), calls=%async_computation | async-start | bytes 851968 | tf_op jit(solution)/shard_map/all_to_all | solution.py:494
  100.4 3.0 %collective-permute-done.17.second_ref = bf16[2,256,256]{2,1,0:T(8,128)(2,1)S(1)} collective-permute-done((bf16[2,256,256]{2,1,0:T(8,128)(2,1)S(1)}, bf16[2,256,256]{2,1,0:T(8,128)(2,1)S(1)}, u32[]{:S(2)}, u32[]{:S(2)}) %collective-permute-start.17) | collective-permute-done | bytes 262176 | tf_op jit(solution)/shard_map/ppermute | solution.py:113
  103.4 0.8 collective-permute-start.18
  104.2 2.5 %collective-permute-start.16 = (bf16[4,256,256]{2,1,0:T(8,128)(2,1)S(1)}, bf16[4,256,256]{2,1,0:T(8,128)(2,1)S(1)}, u32[]{:S(2)}, u32[]{:S(2)}) collective-permute-start(bf16[4,256,256]{2,1,0:T(8,128)(2,1)S(1)} %shard_map.124.block_ref), channel_id=1, source_target_pairs={{0,8},{4,12},{8,0},{12,4},{16,24},{20,28},{24,16},{28,20},{1,9},{5... | collective-permute-start | bytes 1572872 | tf_op jit(solution)/shard_map/ppermute | solution.py:113
  106.7 3.6 %shard_map.128.refs_0_ = bf16[1600,2048]{1,0:T(8,128)(2,1)} custom-call(s32[2]{0:T(128)S(1)} %pad_add_fusion.me_ref, bf16[4,256,256]{2,1,0:T(8,128)(2,1)S(1)} %shard_map.127.block_ref, bf16[256,1600]{1,0:T(8,128)(2,1)S(1)} %get-tuple-element.26.grad_ref.rows_ref), custom_call_target="tpu_custom_call" | custom-call | flops 838860800 | bytes 4096000 | tf_op jit(solution)/shard_map/pallas_call | solution.py:355
  110.3 3.6 %shard_map.125.refs_0_ = bf16[1600,2048]{1,0:T(8,128)(2,1)} custom-call(s32[2]{0:T(128)S(1)} %pad_add_fusion.me_ref, bf16[4,256,256]{2,1,0:T(8,128)(2,1)S(1)} %shard_map.124.block_ref, bf16[256,1600]{1,0:T(8,128)(2,1)S(1)} %get-tuple-element.25.normed_ref.rows_ref), custom_call_target="tpu_custom_call" | custom-call | flops 838860800 | bytes 4096000 | tf_op jit(solution)/shard_map/pallas_call | solution.py:355
  113.9 5.4 %collective-permute-done.18.block_ref = bf16[4,256,256]{2,1,0:T(8,128)(2,1)S(1)} collective-permute-done((bf16[4,256,256]{2,1,0:T(8,128)(2,1)S(1)}, bf16[4,256,256]{2,1,0:T(8,128)(2,1)S(1)}, u32[]{:S(2)}, u32[]{:S(2)}) %collective-permute-start.18) | collective-permute-done | bytes 524320 | tf_op jit(solution)/shard_map/ppermute | solution.py:113
  119.3 3.6 %shard_map.129 = bf16[1600,2048]{1,0:T(8,128)(2,1)} custom-call(s32[2]{0:T(128)S(1)} %pad_add_fusion.me_ref, bf16[4,256,256]{2,1,0:T(8,128)(2,1)S(1)} %collective-permute-done.18.block_ref, bf16[256,1600]{1,0:T(8,128)(2,1)S(1)} %get-tuple-element.26.grad_ref.rows_ref, bf16[1600,2048]{1,0:T(8,128)(2,1)} %shard_map.128.refs_0_), custom_call_target="tpu_custom_call", output_to_operand_aliasing={{}: (3, {})} | custom-call | flops 838860800 | bytes 4096000 | tf_op jit(solution)/shard_map/pallas_call | solution.py:355
  122.9 3.6 %shard_map.126 = bf16[1600,2048]{1,0:T(8,128)(2,1)} custom-call(s32[2]{0:T(128)S(1)} %pad_add_fusion.me_ref, bf16[4,256,256]{2,1,0:T(8,128)(2,1)S(1)} %collective-permute-done.16.block_ref, bf16[256,1600]{1,0:T(8,128)(2,1)S(1)} %get-tuple-element.25.normed_ref.rows_ref, bf16[1600,2048]{1,0:T(8,128)(2,1)} %shard_map.125.refs_0_), custom_call_target="tpu_custom_call", output_to_operand_aliasing={{}: (3, {})} | custom-call | flops 838860800 | bytes 4096000 | tf_op jit(solution)/shard_map/pallas_call | solution.py:355
  126.5 1.5 %shard_map.122 = (bf16[16,1600]{1,0:T(8,128)(2,1)}, bf16[8,1600]{1,0:T(8,128)(2,1)}) custom-call(s32[2]{0:T(128)S(1)} %pad_add_fusion.me_ref, s32[1,4]{1,0:T(1,128)S(1)} %copy-done.6, s32[1,8]{1,0:T(1,128)S(1)} %copy-done.7, bf16[8,16,1600]{2,1,0:T(8,128)(2,1)S(1)} %all-to-all-done.tail_ref, f32[16,1600]{1,0:T(8,128)S(1)} %get-tuple-element.41.extra_ref, ...), custom_call_target="tpu_custom_call" | custom-call | tf_op jit(solution)/shard_map/pallas_call | solution.py:385
  (29 shorter events, 0.3 us)
Async XLA Ops:
  1.6 6.8 %collective-permute-start = (bf16[1,16,1600]{2,1,0:T(8,128)(2,1)S(1)}, bf16[1,16,1600]{2,1,0:T(8,128)(2,1)S(1)}, u32[]{:S(2)}, u32[]{:S(2)}) collective-permute-start(bf16[1,16,1600]{2,1,0:T(8,128)(2,1)S(1)} %shard_map.111.first_ref), channel_id=1, source_target_pairs={{0,16},{4,20},{8,24},{12,28},{16,0},{20,4},{24,8},{28,12},{1,17},{... | collective-permute-start | bytes 153608 | tf_op jit(solution)/shard_map/ppermute | solution.py:113
  8.5 4.8 %collective-permute-start.1 = (bf16[2,16,1600]{2,1,0:T(8,128)(2,1)S(1)}, bf16[2,16,1600]{2,1,0:T(8,128)(2,1)S(1)}, u32[]{:S(2)}, u32[]{:S(2)}) collective-permute-start(bf16[2,16,1600]{2,1,0:T(8,128)(2,1)S(1)} %shard_map.112.first_ref), channel_id=1, source_target_pairs={{0,8},{4,12},{8,0},{12,4},{16,24},{20,28},{24,16},{28,20},{1,9},{5... | collective-permute-start | bytes 307208 | tf_op jit(solution)/shard_map/ppermute | solution.py:113
  13.3 5.9 %collective-permute-start.2 = (bf16[4,16,1600]{2,1,0:T(8,128)(2,1)S(1)}, bf16[4,16,1600]{2,1,0:T(8,128)(2,1)S(1)}, u32[]{:S(2)}, u32[]{:S(2)}) collective-permute-start(bf16[4,16,1600]{2,1,0:T(8,128)(2,1)S(1)} %shard_map.113.first_ref), channel_id=1, source_target_pairs={{0,4},{4,0},{8,12},{12,8},{16,20},{20,16},{24,28},{28,24},{1,5},{5... | collective-permute-start | bytes 614408 | tf_op jit(solution)/shard_map/ppermute | solution.py:113
  19.2 8.2 %collective-permute-start.3 = (bf16[8,16,1600]{2,1,0:T(8,128)(2,1)S(1)}, bf16[8,16,1600]{2,1,0:T(8,128)(2,1)S(1)}, u32[]{:S(2)}, u32[]{:S(2)}) collective-permute-start(bf16[8,16,1600]{2,1,0:T(8,128)(2,1)S(1)} %shard_map.114.first_ref), channel_id=1, source_target_pairs={{0,2},{1,3},{2,0},{3,1},{4,6},{5,7},{6,4},{7,5},{8,10},{9,11},{10,... | collective-permute-start | bytes 1228808 | tf_op jit(solution)/shard_map/ppermute | solution.py:113
  27.5 21.5 %collective-permute-start.4 = (bf16[16,16,1600]{2,1,0:T(8,128)(2,1)S(1)}, bf16[16,16,1600]{2,1,0:T(8,128)(2,1)S(1)}, u32[]{:S(2)}, u32[]{:S(2)}) collective-permute-start(bf16[16,16,1600]{2,1,0:T(8,128)(2,1)S(1)} %shard_map.115.near_ref), channel_id=1, source_target_pairs={{0,1},{1,0},{2,3},{3,2},{4,5},{5,4},{6,7},{7,6},{8,9},{9,8},{10,11... | collective-permute-start | bytes 2457608 | tf_op jit(solution)/shard_map/ppermute | solution.py:113
  30.1 7.5 %collective-permute-start.5 = (bf16[2,200,256]{2,1,0:T(8,128)(2,1)S(1)}, bf16[2,200,256]{2,1,0:T(8,128)(2,1)S(1)}, u32[]{:S(2)}, u32[]{:S(2)}) collective-permute-start(bf16[2,200,256]{2,1,0:T(8,128)(2,1)S(1)} %get-tuple-element.27), channel_id=1, source_target_pairs={{0,4},{4,0},{8,12},{12,8},{16,20},{20,16},{24,28},{28,24},{1,5},{5... | collective-permute-start | bytes 614408 | tf_op jit(solution)/shard_map/ppermute | solution.py:113
  31.9 14.9 %collective-permute-start.6 = (bf16[2,200,256]{2,1,0:T(8,128)(2,1)S(1)}, bf16[2,200,256]{2,1,0:T(8,128)(2,1)S(1)}, u32[]{:S(2)}, u32[]{:S(2)}) collective-permute-start(bf16[2,200,256]{2,1,0:T(8,128)(2,1)S(1)} %get-tuple-element.28), channel_id=1, source_target_pairs={{0,8},{4,12},{8,0},{12,4},{16,24},{20,28},{24,16},{28,20},{1,9},{5... | collective-permute-start | bytes 614408 | tf_op jit(solution)/shard_map/ppermute | solution.py:113
  33.0 21.0 %collective-permute-start.7 = (bf16[2,200,256]{2,1,0:T(8,128)(2,1)}, bf16[2,200,256]{2,1,0:T(8,128)(2,1)}, u32[]{:S(2)}, u32[]{:S(2)}) collective-permute-start(bf16[2,200,256]{2,1,0:T(8,128)(2,1)} %get-tuple-element.29), channel_id=1, source_target_pairs={{0,12},{4,8},{8,4},{12,0},{16,28},{20,24},{24,20},{28,16},{1,13},{... | collective-permute-start | bytes 614408 | tf_op jit(solution)/shard_map/ppermute | solution.py:113
  33.6 20.4 %collective-permute-start.8 = (bf16[2,200,256]{2,1,0:T(8,128)(2,1)}, bf16[2,200,256]{2,1,0:T(8,128)(2,1)}, u32[]{:S(2)}, u32[]{:S(2)}) collective-permute-start(bf16[2,200,256]{2,1,0:T(8,128)(2,1)} %get-tuple-element.30), channel_id=1, source_target_pairs={{0,16},{4,20},{8,24},{12,28},{16,0},{20,4},{24,8},{28,12},{1,17},{... | collective-permute-start | bytes 614408 | tf_op jit(solution)/shard_map/ppermute | solution.py:113
  37.6 0.7 copy-start
  38.3 27.6 %collective-permute-start.9 = (bf16[2,200,256]{2,1,0:T(8,128)(2,1)}, bf16[2,200,256]{2,1,0:T(8,128)(2,1)}, u32[]{:S(2)}, u32[]{:S(2)}) collective-permute-start(bf16[2,200,256]{2,1,0:T(8,128)(2,1)} %get-tuple-element.31), channel_id=1, source_target_pairs={{0,20},{4,16},{8,28},{12,24},{16,4},{20,0},{24,12},{28,8},{1,21},{... | collective-permute-start | bytes 614408 | tf_op jit(solution)/shard_map/ppermute | solution.py:113
  46.8 0.7 copy-start.2
  47.5 18.5 %collective-permute-start.10 = (bf16[2,200,256]{2,1,0:T(8,128)(2,1)}, bf16[2,200,256]{2,1,0:T(8,128)(2,1)}, u32[]{:S(2)}, u32[]{:S(2)}) collective-permute-start(bf16[2,200,256]{2,1,0:T(8,128)(2,1)} %get-tuple-element.32), channel_id=1, source_target_pairs={{0,24},{4,28},{8,16},{12,20},{16,8},{20,12},{24,0},{28,4},{1,25},{... | collective-permute-start | bytes 614408 | tf_op jit(solution)/shard_map/ppermute | solution.py:113
  49.0 16.9 %collective-permute-start.11 = (bf16[2,200,256]{2,1,0:T(8,128)(2,1)}, bf16[2,200,256]{2,1,0:T(8,128)(2,1)}, u32[]{:S(2)}, u32[]{:S(2)}) collective-permute-start(bf16[2,200,256]{2,1,0:T(8,128)(2,1)} %get-tuple-element.33), channel_id=1, source_target_pairs={{0,28},{4,24},{8,20},{12,16},{16,12},{20,8},{24,4},{28,0},{1,29},{... | collective-permute-start | bytes 614408 | tf_op jit(solution)/shard_map/ppermute | solution.py:113
  65.9 0.9 copy-start.1
  66.9 0.9 copy-start.3
  71.8 10.3 %collective-permute-start.12 = (bf16[2,16,8,1600]{3,2,1,0:T(8,128)(2,1)S(1)}, bf16[2,16,8,1600]{3,2,1,0:T(8,128)(2,1)S(1)}, u32[]{:S(2)}, u32[]{:S(2)}) collective-permute-start(bf16[2,16,8,1600]{3,2,1,0:T(8,128)(2,1)S(1)} %get-tuple-element.38), channel_id=1, source_target_pairs={{0,1},{1,0},{2,3},{3,2},{4,5},{5,4},{6,7},{7,6},{8,9},{9,8},{10,11... | collective-permute-start | bytes 2457608 | tf_op jit(solution)/shard_map/ppermute | solution.py:113
  71.9 22.7 %collective-permute-start.14 = (bf16[2,256,256]{2,1,0:T(8,128)(2,1)S(1)}, bf16[2,256,256]{2,1,0:T(8,128)(2,1)S(1)}, u32[]{:S(2)}, u32[]{:S(2)}) collective-permute-start(bf16[2,256,256]{2,1,0:T(8,128)(2,1)S(1)} %get-tuple-element.34.both_ref.first_ref), channel_id=1, source_target_pairs={{0,16},{4,20},{8,24},{12,28},{16,0},{20,4},{24,8},{28,12},{1,17},{... | collective-permute-start | bytes 786440 | tf_op jit(solution)/shard_map/ppermute | solution.py:113
  82.3 13.8 %collective-permute-start.13 = (bf16[2,8,8,1600]{3,2,1,0:T(8,128)(2,1)S(1)}, bf16[2,8,8,1600]{3,2,1,0:T(8,128)(2,1)S(1)}, u32[]{:S(2)}, u32[]{:S(2)}) collective-permute-start(bf16[2,8,8,1600]{3,2,1,0:T(8,128)(2,1)S(1)} %get-tuple-element.40), channel_id=1, source_target_pairs={{0,2},{1,3},{2,0},{3,1},{4,6},{5,7},{6,4},{7,5},{8,10},{9,11},{10,... | collective-permute-start | bytes 1228808 | tf_op jit(solution)/shard_map/ppermute | solution.py:113
  94.6 8.7 %collective-permute-start.17 = (bf16[2,256,256]{2,1,0:T(8,128)(2,1)S(1)}, bf16[2,256,256]{2,1,0:T(8,128)(2,1)S(1)}, u32[]{:S(2)}, u32[]{:S(2)}) collective-permute-start(bf16[2,256,256]{2,1,0:T(8,128)(2,1)S(1)} %get-tuple-element.45.first_ref), channel_id=1, source_target_pairs={{0,8},{4,12},{8,0},{12,4},{16,24},{20,28},{24,16},{28,20},{1,9},{5... | collective-permute-start | bytes 786440 | tf_op jit(solution)/shard_map/ppermute | solution.py:113
  94.7 9.5 %collective-permute-start.15 = (bf16[2,256,256]{2,1,0:T(8,128)(2,1)S(1)}, bf16[2,256,256]{2,1,0:T(8,128)(2,1)S(1)}, u32[]{:S(2)}, u32[]{:S(2)}) collective-permute-start(bf16[2,256,256]{2,1,0:T(8,128)(2,1)S(1)} %get-tuple-element.44.first_ref), channel_id=1, source_target_pairs={{0,4},{4,0},{8,12},{12,8},{16,20},{20,16},{24,28},{28,24},{1,5},{5... | collective-permute-start | bytes 786440 | tf_op jit(solution)/shard_map/ppermute | solution.py:113
  96.9 29.6 %all-to-all-start = ((bf16[8,16,1600]{2,1,0:T(8,128)(2,1)}), bf16[8,16,1600]{2,1,0:T(8,128)(2,1)S(1)}, u32[]{:S(2)}, u32[]{:S(2)}) async-start(bf16[8,16,1600]{2,1,0:T(8,128)(2,1)} %shard_map.121), calls=%async_computation | async-start | bytes 851968 | tf_op jit(solution)/shard_map/all_to_all | solution.py:494
  103.4 15.9 %collective-permute-start.18 = (bf16[4,256,256]{2,1,0:T(8,128)(2,1)S(1)}, bf16[4,256,256]{2,1,0:T(8,128)(2,1)S(1)}, u32[]{:S(2)}, u32[]{:S(2)}) collective-permute-start(bf16[4,256,256]{2,1,0:T(8,128)(2,1)S(1)} %shard_map.127.block_ref), channel_id=1, source_target_pairs={{0,4},{4,0},{8,12},{12,8},{16,20},{20,16},{24,28},{28,24},{1,5},{5... | collective-permute-start | bytes 1572872 | tf_op jit(solution)/shard_map/ppermute | solution.py:113
  104.2 18.7 %collective-permute-start.16 = (bf16[4,256,256]{2,1,0:T(8,128)(2,1)S(1)}, bf16[4,256,256]{2,1,0:T(8,128)(2,1)S(1)}, u32[]{:S(2)}, u32[]{:S(2)}) collective-permute-start(bf16[4,256,256]{2,1,0:T(8,128)(2,1)S(1)} %shard_map.124.block_ref), channel_id=1, source_target_pairs={{0,8},{4,12},{8,0},{12,4},{16,24},{20,28},{24,16},{28,20},{1,9},{5... | collective-permute-start | bytes 1572872 | tf_op jit(solution)/shard_map/ppermute | solution.py:113
  122.9 3.6 %copy-start.4 = (bf16[8,1600]{1,0:T(8,128)(2,1)S(1)}, bf16[8,1600]{1,0:T(8,128)(2,1)}, u32[]{:S(2)}) copy-start(bf16[8,1600]{1,0:T(8,128)(2,1)} %patch_ref.1) | copy-start | bytes 76804
  122.9 3.6 %copy-start.5 = (bf16[16,1600]{1,0:T(8,128)(2,1)S(1)}, bf16[16,1600]{1,0:T(8,128)(2,1)}, u32[]{:S(2)}) copy-start(bf16[16,1600]{1,0:T(8,128)(2,1)} %text_ref.1) | copy-start | bytes 153604
  122.9 3.6 %copy-start.6 = (s32[1,4]{1,0:T(1,128)S(1)}, s32[1,4]{1,0:T(1,128)}, u32[]{:S(2)}) copy-start(s32[1,4]{1,0:T(1,128)} %count_ref.1) | copy-start | bytes 52
  122.9 3.6 %copy-start.7 = (s32[1,8]{1,0:T(1,128)S(1)}, s32[1,8]{1,0:T(1,128)}, u32[]{:S(2)}) copy-start(s32[1,8]{1,0:T(1,128)} %place_ref.1) | copy-start | bytes 100

commit v3 on v2

--- a/solution.py
+++ b/solution.py
@@ -145,15 +145,27 @@
         copy.wait()
 
 
+def weight_copies(expand_at, project_at, distance, block, sems, first):
+    units = block.shape[2]
+    start = pl.multiple_of((lax.axis_index("dp") ^ distance) * units, 128)
+    return [
+        pltpu.make_async_copy(source.at[:, pl.ds(start, units)], block.at[k], sems.at[first + k])
+        for k, source in enumerate((expand_at, project_at))
+    ]
+
+
 def pick_kernel(
-    capacity, counts_at, places_at, patches_at, cotangent_at, pair_ref,
-    count_ref, place_ref, patch_ref, cotangent_ref, sems,
+    capacity, distance, counts_at, places_at, patches_at, cotangent_at, expand_at, project_at,
+    pair_ref, block_ref, count_ref, place_ref, patch_ref, cotangent_ref, sems,
 ):
     ends = (
         (counts_at, count_ref), (places_at, place_ref),
         (patches_at, patch_ref), (cotangent_at, cotangent_ref),
     )
-    fetch([pltpu.make_async_copy(a, b, sems.at[i]) for i, (a, b) in enumerate(ends)])
+    fetch(
+        [pltpu.make_async_copy(a, b, sems.at[i]) for i, (a, b) in enumerate(ends)]
+        + weight_copies(expand_at, project_at, distance, block_ref, sems, 4)
+    )
     slots = patch_ref.shape[0]
     section = lax.axis_index("section")
     chooser = landing(
@@ -165,19 +177,17 @@
     ).astype(jnp.bfloat16)
 
 
-def repack_kernel(expand_at, project_at, *refs):
+def repack_kernel(distances, expand_at, project_at, *refs):
     blocks, sems = refs[:-1], refs[-1]
-    units = blocks[0].shape[2]
     copies = []
-    for i, block in enumerate(blocks):
-        start = pl.multiple_of((lax.axis_index("dp") ^ (i + 1)) * units, 128)
-        for k, source in enumerate((expand_at, project_at)):
-            copies.append(
-                pltpu.make_async_copy(
-                    source.at[:, pl.ds(start, units)], block.at[k], sems.at[2 * i + k]
-                )
-            )
+    for i, (distance, block) in enumerate(zip(distances, blocks)):
+        copies += weight_copies(expand_at, project_at, distance, block, sems, 2 * i)
     fetch(copies)
+
+
+def turn_kernel(normed_ref, grad_ref, normed_turned_ref, grad_turned_ref):
+    normed_turned_ref[...] = normed_ref[...].T
+    grad_turned_ref[...] = grad_ref[...].T
 
 
 def join_kernel(first_ref, second_ref, out_ref):
@@ -311,8 +321,8 @@
 
 
 def weight_grad_kernel(me_ref, block_ref, rows_ref, *refs):
-    refs[-1][...] = lax.dot_general(
-        rows_ref[...], block_ref[0], (((0,), (0,)), ((), ())), preferred_element_type=jnp.float32
+    refs[-1][...] = jnp.dot(
+        rows_ref[...], block_ref[0], preferred_element_type=jnp.float32
     ).astype(jnp.bfloat16)
 
 
@@ -351,7 +361,7 @@
 
 def weight_grads(me, blocks, first_index, steps, values, width, before=()):
     count, rows, units = blocks.shape
-    features = values.shape[1]
+    features = values.shape[0]
     return pl.pallas_call(
         weight_grad_kernel,
         grid_spec=pltpu.PrefetchScalarGridSpec(
@@ -359,7 +369,7 @@
             grid=(count,),
             in_specs=[
                 pl.BlockSpec((1, rows, units), lambda i, me_ref: (i, 0, 0)),
-                pl.BlockSpec((rows, features), lambda i, me_ref: (0, 0)),
+                pl.BlockSpec((features, rows), lambda i, me_ref: (0, 0)),
             ]
             + [pl.BlockSpec(memory_space=pl.ANY)] * len(before),
             out_specs=pl.BlockSpec(
@@ -431,31 +441,35 @@
     def in_hbm(*arrays):
         return [pltpu.with_memory_space_constraint(array, pltpu.HBM) for array in arrays]
 
-    held = pl.pallas_call(
-        functools.partial(pick_kernel, capacity),
-        out_shape=shape((1, 2 * slots, features), kept),
-        in_specs=[hbm] * 4,
-        out_specs=VMEM_SPEC,
+    first = dp_steps[0]
+    others = [distance for distance in range(1, replicas) if distance != first]
+    sources = in_hbm(expand_weight, project_turned)
+    held, block = pl.pallas_call(
+        functools.partial(pick_kernel, capacity, first),
+        out_shape=[shape((1, 2 * slots, features), kept), shape((2, part, units), kept)],
+        in_specs=[hbm] * 6,
+        out_specs=[VMEM_SPEC] * 2,
         scratch_shapes=[
             pltpu.SMEM(counts.shape, counts.dtype),
             pltpu.SMEM(positions.shape, positions.dtype),
             pltpu.VMEM(patches.shape, kept),
             pltpu.VMEM(cotangent.shape, kept),
-            pltpu.SemaphoreType.DMA((4,)),
+            pltpu.SemaphoreType.DMA((6,)),
         ],
         compiler_params=pltpu.CompilerParams(vmem_limit_bytes=12 << 20),
-    )(*in_hbm(counts, positions, patches, cotangent))
-    blocks = pl.pallas_call(
-        repack_kernel,
-        out_shape=[shape((2, part, units), kept)] * (replicas - 1),
+    )(*in_hbm(counts, positions, patches, cotangent), *sources)
+    rest = pl.pallas_call(
+        functools.partial(repack_kernel, others),
+        out_shape=[shape((2, part, units), kept)] * len(others),
         in_specs=[hbm] * 2,
-        out_specs=[VMEM_SPEC] * (replicas - 1),
-        scratch_shapes=[pltpu.SemaphoreType.DMA((2 * replicas - 2,))],
+        out_specs=[VMEM_SPEC] * len(others),
+        scratch_shapes=[pltpu.SemaphoreType.DMA((2 * len(others),))],
         compiler_params=pltpu.CompilerParams(vmem_limit_bytes=12 << 20),
-    )(*in_hbm(expand_weight, project_turned))
+    )(*sources)
+    blocks = dict(zip([first, *others], [block, *rest]))
     arrived = []
     for distance in range(1, replicas):
-        arrived.append(swap(blocks[distance - 1], "dp", distance))
+        arrived.append(swap(blocks[distance], "dp", distance))
 
     exchanges = [("dp", step) for step in dp_steps] + [("section", step) for step in section_steps]
     for axis, step in exchanges:
@@ -468,6 +482,9 @@
         (me,), (held, got, gain),
     )
 
+    normed_turned, grad_turned = call(
+        turn_kernel, [shape((features, rows), kept)] * 2, (), (normed, grad_all)
+    )
     both, expand_slice, project_slice = pl.pallas_call(
         hidden_kernel,
         out_shape=[shape((2, rows, units), kept)] + [shape((features, units), kept)] * 2,
@@ -475,7 +492,7 @@
         out_specs=[VMEM_SPEC] * 3,
         scratch_shapes=[pltpu.SemaphoreType.DMA((2 * replicas,))],
         compiler_params=pltpu.CompilerParams(vmem_limit_bytes=12 << 20),
-    )(normed, grad_all, *in_hbm(expand_weight, project_turned), *arrived)
+    )(normed, grad_all, *sources, *arrived)
 
     tail_steps = section_steps[::-1]
     keep, send = call(
@@ -496,25 +513,28 @@
     far_both = swap(both, "dp", dp_steps[0])
     hidden_steps, pre_steps = dp_steps, dp_steps[:1] + dp_steps[:0:-1]
     hidden, pre = join_pairs(both, far_both)
-    for place, (hidden_step, pre_step) in enumerate(zip(hidden_steps[1:], pre_steps[1:]), 1):
-        hidden_far = swap(hidden, "dp", hidden_step)
-        pre_far = swap(pre, "dp", pre_step)
-        if hidden.shape[0] < replicas // 2:
-            hidden, pre = join(hidden, hidden_far), join(pre, pre_far)
-
-    half = replicas // 2
-    project_grad = weight_grads(me, hidden, 0, hidden_steps, grad_all, width)
-    expand_grad = weight_grads(me, pre, 0, pre_steps, normed, width)
-    project_grad = weight_grads(
-        me, hidden_far, half, hidden_steps, grad_all, width, (project_grad,)
-    )
-    expand_grad = weight_grads(me, pre_far, half, pre_steps, normed, width, (expand_grad,))
+    hidden_new, pre_new, new_at = hidden, pre, 0
+    project_grad = expand_grad = ()
+    for place in range(1, len(dp_steps) + 1):
+        project_grad = (
+            weight_grads(me, hidden_new, new_at, hidden_steps, grad_turned, width, project_grad),
+        )
+        expand_grad = (
+            weight_grads(me, pre_new, new_at, pre_steps, normed_turned, width, expand_grad),
+        )
+        if place == len(dp_steps):
+            break
+        new_at = hidden.shape[0]
+        hidden_new = swap(hidden, "dp", hidden_steps[place])
+        pre_new = swap(pre, "dp", pre_steps[place])
+        if place < len(dp_steps) - 1:
+            hidden, pre = join(hidden, hidden_new), join(pre, pre_new)
     embedded, grad_rows = call(
         functools.partial(finish_kernel, capacity),
         [shape(text.shape, kept), shape(patches.shape, kept)],
         (me, counts, positions), (tail, extra, patches, text, gain),
     )
-    return (embedded, grad_rows, expand_grad, project_grad.T)
+    return (embedded, grad_rows, expand_grad[0], project_grad[0].T)
 
 
 def power_of_two(value):

time: 128 us -> 129 us (level)
  starting transfers between devices: 42.8 us -> 37.2 us
  waiting for transfers between devices: 53.8 us -> 58.9 us
  Pallas kernels: 26.6 us -> 28.7 us
    ppermute x19, starting transfers between devices: 39.3 us -> 33.7 us  [swap(): return lax.ppermute(array, axis, [(i, i ^ step) for i in range(size)])]
    ppermute x19, waiting for transfers between devices: 53.8 us -> 58.9 us  [swap(): return lax.ppermute(array, axis, [(i, i ^ step) for i in range(size)])]
    pallas_call x4 -> x6, Pallas kernels: 14.4 us -> 16 us  [weight_grads(): pl.pallas_call(weight_grad_kernel, grid_spec=pltpu.PrefetchScalarGridSpec...]
    pallas_call x12 -> x13, Pallas kernels: 6.13 us -> 6.61 us  [call(): pl.pallas_call(kernel, out_shape=out_shape, in_specs=[SMEM_SPEC] * len(sm...]
    unnamed x16 -> x18, local copies, waits for them, and re-layouts: 3.24 us -> 3.23 us
  transfers between devices with their start and end apart: 20 -> 20, of which waited for: 10 -> 11; matrix products, arithmetic and copies ran while one was open for 1% -> 0% of each run, Pallas kernels for 16% -> 17%
where the time goes in v3:
time: 129 us
  waiting for transfers between devices  58.9 us (46%)
  starting transfers between devices  37.2 us (29%)
  Pallas kernels  28.7 us (22%)
  local copies, waits for them, and re-layouts  3.23 us (3%)
    ppermute x19, waiting for transfers between devices, swap(): return lax.ppermute(array, axis, [(i, i ^ step) for i in range(size)])  58.9 us
    ppermute x19, starting transfers between devices, swap(): return lax.ppermute(array, axis, [(i, i ^ step) for i in range(size)])  33.7 us
    pallas_call x6, Pallas kernels, weight_grads(): pl.pallas_call(weight_grad_kernel, grid_spec=pltpu.PrefetchScalarGridSpec...  16 us
    pallas_call x13, Pallas kernels, call(): pl.pallas_call(kernel, out_shape=out_shape, in_specs=[SMEM_SPEC] * len(sm...  6.61 us
    all_to_all x1, starting transfers between devices, move_rows_plan(): tail = lax.all_to_all(tail, 'dp', split_axis=0, concat_axis=0, tiled=True)  3.46 us
    unnamed x18, local copies, waits for them, and re-layouts  3.23 us
  transfers between devices with their start and end apart: 20, of which 11 were waited for; matrix products, arithmetic and copies ran while one was open for 0% of the time, Pallas kernels for 17%

profile of v3, /device:TPU:0, one launch (start us, length us, event | category | flops | bytes accessed | tf_op | source)
XLA Modules:
  0.0 128.9 jit_solution(11520037391151271534)
XLA Ops:
  0.6 1.2 shard_map.111
  1.9 4.1 %collective-permute-start = (bf16[1,16,1600]{2,1,0:T(8,128)(2,1)S(1)}, bf16[1,16,1600]{2,1,0:T(8,128)(2,1)S(1)}, u32[]{:S(2)}, u32[]{:S(2)}) collective-permute-start(bf16[1,16,1600]{2,1,0:T(8,128)(2,1)S(1)} %get-tuple-element.28.first_ref), channel_id=1, source_target_pairs={{0,16},{4,20},{8,24},{12,28},{16,0},{20,4},{24,8},{28,12},{1,17},{... | collective-permute-start | bytes 153608 | tf_op jit(solution)/shard_map/ppermute | solution.py:113
  6.0 2.7 %collective-permute-done.second_ref = bf16[1,16,1600]{2,1,0:T(8,128)(2,1)S(1)} collective-permute-done((bf16[1,16,1600]{2,1,0:T(8,128)(2,1)S(1)}, bf16[1,16,1600]{2,1,0:T(8,128)(2,1)S(1)}, u32[]{:S(2)}, u32[]{:S(2)}) %collective-permute-start) | collective-permute-done | bytes 51232 | tf_op jit(solution)/shard_map/ppermute | solution.py:113
  8.7 1.4 %collective-permute-start.1 = (bf16[2,16,1600]{2,1,0:T(8,128)(2,1)S(1)}, bf16[2,16,1600]{2,1,0:T(8,128)(2,1)S(1)}, u32[]{:S(2)}, u32[]{:S(2)}) collective-permute-start(bf16[2,16,1600]{2,1,0:T(8,128)(2,1)S(1)} %shard_map.112.first_ref), channel_id=1, source_target_pairs={{0,8},{4,12},{8,0},{12,4},{16,24},{20,28},{24,16},{28,20},{1,9},{5... | collective-permute-start | bytes 307208 | tf_op jit(solution)/shard_map/ppermute | solution.py:113
  10.1 3.4 %collective-permute-done.1.second_ref = bf16[2,16,1600]{2,1,0:T(8,128)(2,1)S(1)} collective-permute-done((bf16[2,16,1600]{2,1,0:T(8,128)(2,1)S(1)}, bf16[2,16,1600]{2,1,0:T(8,128)(2,1)S(1)}, u32[]{:S(2)}, u32[]{:S(2)}) %collective-permute-start.1) | collective-permute-done | bytes 102432 | tf_op jit(solution)/shard_map/ppermute | solution.py:113
  13.5 1.8 %collective-permute-start.2 = (bf16[4,16,1600]{2,1,0:T(8,128)(2,1)S(1)}, bf16[4,16,1600]{2,1,0:T(8,128)(2,1)S(1)}, u32[]{:S(2)}, u32[]{:S(2)}) collective-permute-start(bf16[4,16,1600]{2,1,0:T(8,128)(2,1)S(1)} %shard_map.113.first_ref), channel_id=1, source_target_pairs={{0,4},{4,0},{8,12},{12,8},{16,20},{20,16},{24,28},{28,24},{1,5},{5... | collective-permute-start | bytes 614408 | tf_op jit(solution)/shard_map/ppermute | solution.py:113
  15.2 4.1 %collective-permute-done.2.second_ref = bf16[4,16,1600]{2,1,0:T(8,128)(2,1)S(1)} collective-permute-done((bf16[4,16,1600]{2,1,0:T(8,128)(2,1)S(1)}, bf16[4,16,1600]{2,1,0:T(8,128)(2,1)S(1)}, u32[]{:S(2)}, u32[]{:S(2)}) %collective-permute-start.2) | collective-permute-done | bytes 204832 | tf_op jit(solution)/shard_map/ppermute | solution.py:113
  19.4 1.8 %collective-permute-start.3 = (bf16[8,16,1600]{2,1,0:T(8,128)(2,1)S(1)}, bf16[8,16,1600]{2,1,0:T(8,128)(2,1)S(1)}, u32[]{:S(2)}, u32[]{:S(2)}) collective-permute-start(bf16[8,16,1600]{2,1,0:T(8,128)(2,1)S(1)} %shard_map.114.first_ref), channel_id=1, source_target_pairs={{0,2},{1,3},{2,0},{3,1},{4,6},{5,7},{6,4},{7,5},{8,10},{9,11},{10,... | collective-permute-start | bytes 1228808 | tf_op jit(solution)/shard_map/ppermute | solution.py:113
  21.2 6.4 %collective-permute-done.3.second_ref = bf16[8,16,1600]{2,1,0:T(8,128)(2,1)S(1)} collective-permute-done((bf16[8,16,1600]{2,1,0:T(8,128)(2,1)S(1)}, bf16[8,16,1600]{2,1,0:T(8,128)(2,1)S(1)}, u32[]{:S(2)}, u32[]{:S(2)}) %collective-permute-start.3) | collective-permute-done | bytes 409632 | tf_op jit(solution)/shard_map/ppermute | solution.py:113
  27.7 0.1 collective-permute-start.4
  27.8 2.7 %collective-permute-start.8 = (bf16[2,200,256]{2,1,0:T(8,128)(2,1)S(1)}, bf16[2,200,256]{2,1,0:T(8,128)(2,1)S(1)}, u32[]{:S(2)}, u32[]{:S(2)}) collective-permute-start(bf16[2,200,256]{2,1,0:T(8,128)(2,1)S(1)} %get-tuple-element.34), channel_id=1, source_target_pairs={{0,16},{4,20},{8,24},{12,28},{16,0},{20,4},{24,8},{28,12},{1,17},{... | collective-permute-start | bytes 614408 | tf_op jit(solution)/shard_map/ppermute | solution.py:113
  30.4 2.4 %shard_map.117 = (bf16[2,200,256]{2,1,0:T(8,128)(2,1)S(1)}, bf16[2,200,256]{2,1,0:T(8,128)(2,1)}, bf16[2,200,256]{2,1,0:T(8,128)(2,1)}, bf16[2,200,256]{2,1,0:T(...) custom-call(bf16[200,2048]{1,0:T(8,128)(2,1)} %expand_at.5, bf16[200,2048]{1,0:T(8,128)(2,1)} %bitcast.6), custom_call_target="tpu_custom_call" | custom-call | tf_op jit(solution)/shard_map/pallas_call | solution.py:461
  32.9 1.6 %collective-permute-start.5 = (bf16[2,200,256]{2,1,0:T(8,128)(2,1)S(1)}, bf16[2,200,256]{2,1,0:T(8,128)(2,1)S(1)}, u32[]{:S(2)}, u32[]{:S(2)}) collective-permute-start(bf16[2,200,256]{2,1,0:T(8,128)(2,1)S(1)} %get-tuple-element.31), channel_id=1, source_target_pairs={{0,4},{4,0},{8,12},{12,8},{16,20},{20,16},{24,28},{28,24},{1,5},{5... | collective-permute-start | bytes 614408 | tf_op jit(solution)/shard_map/ppermute | solution.py:113
  34.4 1.8 %collective-permute-start.6 = (bf16[2,200,256]{2,1,0:T(8,128)(2,1)}, bf16[2,200,256]{2,1,0:T(8,128)(2,1)}, u32[]{:S(2)}, u32[]{:S(2)}) collective-permute-start(bf16[2,200,256]{2,1,0:T(8,128)(2,1)} %get-tuple-element.32), channel_id=1, source_target_pairs={{0,8},{4,12},{8,0},{12,4},{16,24},{20,28},{24,16},{28,20},{1,9},{5... | collective-permute-start | bytes 614408 | tf_op jit(solution)/shard_map/ppermute | solution.py:113
  36.2 0.2 collective-permute-start.7
  36.4 4.2 %collective-permute-done.8.refs_3_ = bf16[2,200,256]{2,1,0:T(8,128)(2,1)S(1)} collective-permute-done((bf16[2,200,256]{2,1,0:T(8,128)(2,1)S(1)}, bf16[2,200,256]{2,1,0:T(8,128)(2,1)S(1)}, u32[]{:S(2)}, u32[]{:S(2)}) %collective-permute-start.8) | collective-permute-done | bytes 204832 | tf_op jit(solution)/shard_map/ppermute | solution.py:113
  40.6 0.7 copy-done
  41.3 0.6 collective-permute-start.9
  41.9 0.7 copy-done.2
  42.6 3.3 %collective-permute-start.10 = (bf16[2,200,256]{2,1,0:T(8,128)(2,1)}, bf16[2,200,256]{2,1,0:T(8,128)(2,1)}, u32[]{:S(2)}, u32[]{:S(2)}) collective-permute-start(bf16[2,200,256]{2,1,0:T(8,128)(2,1)} %get-tuple-element.36), channel_id=1, source_target_pairs={{0,24},{4,28},{8,16},{12,20},{16,8},{20,12},{24,0},{28,4},{1,25},{... | collective-permute-start | bytes 614408 | tf_op jit(solution)/shard_map/ppermute | solution.py:113
  45.9 1.0 collective-permute-start.11
  47.0 0.1 pad_add_fusion.me_ref
  47.0 2.0 %shard_map.116 = (bf16[256,1600]{1,0:T(8,128)(2,1)S(1)}, bf16[256,1600]{1,0:T(8,128)(2,1)S(1)}, f32[16,1600]{1,0:T(8,128)S(1)}) custom-call(s32[2]{0:T(128)S(1)} %pad_add_fusion.me_ref, bf16[16,16,1600]{2,1,0:T(8,128)(2,1)S(1)} %shard_map.115.near_ref, bf16[16,16,1600]{2,1,0:T(8,128)(2,1)S(1)} %collective-permute-done.4.far_ref, f32[1,1600]{1,0:T(1,128)S(1)} %reshape.11.gain_ref), custom_call_target="tpu_custom_call" | custom-call | tf_op jit(solution)/shard_map/pallas_call | solution.py:395
  49.0 2.3 %collective-permute-done.7.refs_2_ = bf16[2,200,256]{2,1,0:T(8,128)(2,1)} collective-permute-done((bf16[2,200,256]{2,1,0:T(8,128)(2,1)}, bf16[2,200,256]{2,1,0:T(8,128)(2,1)}, u32[]{:S(2)}, u32[]{:S(2)}) %collective-permute-start.7) | collective-permute-done | bytes 204832 | tf_op jit(solution)/shard_map/ppermute | solution.py:113
  51.3 13.2 %collective-permute-done.9.refs_4_ = bf16[2,200,256]{2,1,0:T(8,128)(2,1)} collective-permute-done((bf16[2,200,256]{2,1,0:T(8,128)(2,1)}, bf16[2,200,256]{2,1,0:T(8,128)(2,1)}, u32[]{:S(2)}, u32[]{:S(2)}) %collective-permute-start.9) | collective-permute-done | bytes 204832 | tf_op jit(solution)/shard_map/ppermute | solution.py:113
  64.5 0.9 copy-done.1
  65.5 0.9 copy-done.3
  66.4 2.5 %shard_map.118 = (bf16[2,256,256]{2,1,0:T(8,128)(2,1)S(1)}, bf16[1600,256]{1,0:T(8,128)(2,1)S(1)}, bf16[1600,256]{1,0:T(8,128)(2,1)S(1)}) custom-call(bf16[256,1600]{1,0:T(8,128)(2,1)S(1)} %get-tuple-element.29.normed_ref, bf16[256,1600]{1,0:T(8,128)(2,1)S(1)} %get-tuple-element.30.grad_ref, bf16[200,2048]{1,0:T(8,128)(2,1)} %expand_at.5, ...), custom_call_target="tpu_custom_call" | custom-call | tf_op jit(solution)/shard_map/pallas_call | solution.py:488
  68.9 1.4 %shard_map.119 = (f32[2,16,8,1600]{3,2,1,0:T(8,128)S(1)}, bf16[2,16,8,1600]{3,2,1,0:T(8,128)(2,1)S(1)}) custom-call(s32[2]{0:T(128)S(1)} %pad_add_fusion.me_ref, bf16[2,256,256]{2,1,0:T(8,128)(2,1)S(1)} %get-tuple-element.38.both_ref.first_ref, bf16[1600,256]{1,0:T(8,128)(2,1)S(1)} %get-tuple-element.39.expand_ref, ...), custom_call_target="tpu_custom_call" | custom-call | tf_op jit(solution)/shard_map/pallas_call | solution.py:395
  70.4 10.0 %collective-permute-start.14 = (bf16[2,256,256]{2,1,0:T(8,128)(2,1)S(1)}, bf16[2,256,256]{2,1,0:T(8,128)(2,1)S(1)}, u32[]{:S(2)}, u32[]{:S(2)}) collective-permute-start(bf16[2,256,256]{2,1,0:T(8,128)(2,1)S(1)} %get-tuple-element.38.both_ref.first_ref), channel_id=1, source_target_pairs={{0,16},{4,20},{8,24},{12,28},{16,0},{20,4},{24,8},{28,12},{1,17},{... | collective-permute-start | bytes 786440 | tf_op jit(solution)/shard_map/ppermute | solution.py:113
  80.4 0.2 shard_map.120
  80.6 1.6 %collective-permute-start.13 = (bf16[2,8,8,1600]{3,2,1,0:T(8,128)(2,1)S(1)}, bf16[2,8,8,1600]{3,2,1,0:T(8,128)(2,1)S(1)}, u32[]{:S(2)}, u32[]{:S(2)}) collective-permute-start(bf16[2,8,8,1600]{3,2,1,0:T(8,128)(2,1)S(1)} %get-tuple-element.44), channel_id=1, source_target_pairs={{0,2},{1,3},{2,0},{3,1},{4,6},{5,7},{6,4},{7,5},{8,10},{9,11},{10,... | collective-permute-start | bytes 1228808 | tf_op jit(solution)/shard_map/ppermute | solution.py:113
  82.2 10.7 %collective-permute-done.14.second_ref = bf16[2,256,256]{2,1,0:T(8,128)(2,1)S(1)} collective-permute-done((bf16[2,256,256]{2,1,0:T(8,128)(2,1)S(1)}, bf16[2,256,256]{2,1,0:T(8,128)(2,1)S(1)}, u32[]{:S(2)}, u32[]{:S(2)}) %collective-permute-start.14) | collective-permute-done | bytes 262176 | tf_op jit(solution)/shard_map/ppermute | solution.py:113
  92.9 1.6 %collective-permute-start.15 = (bf16[2,256,256]{2,1,0:T(8,128)(2,1)S(1)}, bf16[2,256,256]{2,1,0:T(8,128)(2,1)S(1)}, u32[]{:S(2)}, u32[]{:S(2)}) collective-permute-start(bf16[2,256,256]{2,1,0:T(8,128)(2,1)S(1)} %get-tuple-element.48.first_ref.block_ref), channel_id=1, source_target_pairs={{0,4},{4,0},{8,12},{12,8},{16,20},{20,16},{24,28},{28,24},{1,5},{5... | collective-permute-start | bytes 786440 | tf_op jit(solution)/shard_map/ppermute | solution.py:113
  94.5 0.8 shard_map.121
  95.4 3.5 %all-to-all-start = ((bf16[8,16,1600]{2,1,0:T(8,128)(2,1)}), bf16[8,16,1600]{2,1,0:T(8,128)(2,1)S(1)}, u32[]{:S(2)}, u32[]{:S(2)}) async-start(bf16[8,16,1600]{2,1,0:T(8,128)(2,1)} %shard_map.121), calls=%async_computation | async-start | bytes 851968 | tf_op jit(solution)/shard_map/all_to_all | solution.py:511
  98.8 2.3 %collective-permute-done.15.second_ref.block_ref = bf16[2,256,256]{2,1,0:T(8,128)(2,1)S(1)} collective-permute-done((bf16[2,256,256]{2,1,0:T(8,128)(2,1)S(1)}, bf16[2,256,256]{2,1,0:T(8,128)(2,1)S(1)}, u32[]{:S(2)}, u32[]{:S(2)}) %collective-permute-start.15) | collective-permute-done | bytes 262176 | tf_op jit(solution)/shard_map/ppermute | solution.py:113
  101.1 0.1 collective-permute-start.16
  101.2 3.4 %collective-permute-done.17.second_ref.block_ref = bf16[2,256,256]{2,1,0:T(8,128)(2,1)S(1)} collective-permute-done((bf16[2,256,256]{2,1,0:T(8,128)(2,1)S(1)}, bf16[2,256,256]{2,1,0:T(8,128)(2,1)S(1)}, u32[]{:S(2)}, u32[]{:S(2)}) %collective-permute-start.17) | collective-permute-done | bytes 262176 | tf_op jit(solution)/shard_map/ppermute | solution.py:113
  104.8 0.5 shard_map.125
  105.3 2.2 %shard_map.126.refs_0_ = bf16[1600,2048]{1,0:T(8,128)(2,1)} custom-call(s32[2]{0:T(128)S(1)} %pad_add_fusion.me_ref, bf16[2,256,256]{2,1,0:T(8,128)(2,1)S(1)} %get-tuple-element.48.first_ref.block_ref, bf16[1600,256]{1,0:T(8,128)(2,1)S(1)} %get-tuple-element.49.rows_ref), custom_call_target="tpu_custom_call" | custom-call | flops 419430400 | bytes 2457600 | tf_op jit(solution)/shard_map/pallas_call | solution.py:365
  107.5 2.2 %shard_map.130.refs_0_ = bf16[1600,2048]{1,0:T(8,128)(2,1)} custom-call(s32[2]{0:T(128)S(1)} %pad_add_fusion.me_ref, bf16[2,256,256]{2,1,0:T(8,128)(2,1)S(1)} %get-tuple-element.50.first_ref.block_ref, bf16[1600,256]{1,0:T(8,128)(2,1)S(1)} %get-tuple-element.51.rows_ref), custom_call_target="tpu_custom_call" | custom-call | flops 419430400 | bytes 2457600 | tf_op jit(solution)/shard_map/pallas_call | solution.py:365
  109.7 2.2 %shard_map.127.refs_0_ = bf16[1600,2048]{1,0:T(8,128)(2,1)} custom-call(s32[2]{0:T(128)S(1)} %pad_add_fusion.me_ref, bf16[2,256,256]{2,1,0:T(8,128)(2,1)S(1)} %collective-permute-done.15.second_ref.block_ref, bf16[1600,256]{1,0:T(8,128)(2,1)S(1)} %get-tuple-element.49.rows_ref, bf16[1600,2048]{1,0:T(8,128)(2,1)} %shard_map.126.refs_0_), custom_call_target="tpu_custom_call", output_to_operand_aliasing={{}: (3, {})} | custom-call | flops 419430400 | bytes 2457600 | tf_op jit(solution)/shard_map/pallas_call | solution.py:365
  112.0 2.2 %shard_map.131.refs_0_ = bf16[1600,2048]{1,0:T(8,128)(2,1)} custom-call(s32[2]{0:T(128)S(1)} %pad_add_fusion.me_ref, bf16[2,256,256]{2,1,0:T(8,128)(2,1)S(1)} %collective-permute-done.17.second_ref.block_ref, bf16[1600,256]{1,0:T(8,128)(2,1)S(1)} %get-tuple-element.51.rows_ref, bf16[1600,2048]{1,0:T(8,128)(2,1)} %shard_map.130.refs_0_), custom_call_target="tpu_custom_call", output_to_operand_aliasing={{}: (3, {})} | custom-call | flops 419430400 | bytes 2457600 | tf_op jit(solution)/shard_map/pallas_call | solution.py:365
  114.2 6.2 %collective-permute-done.16.block_ref = bf16[4,256,256]{2,1,0:T(8,128)(2,1)S(1)} collective-permute-done((bf16[4,256,256]{2,1,0:T(8,128)(2,1)S(1)}, bf16[4,256,256]{2,1,0:T(8,128)(2,1)S(1)}, u32[]{:S(2)}, u32[]{:S(2)}) %collective-permute-start.16) | collective-permute-done | bytes 524320 | tf_op jit(solution)/shard_map/ppermute | solution.py:113
  120.4 3.5 %shard_map.128 = bf16[1600,2048]{1,0:T(8,128)(2,1)} custom-call(s32[2]{0:T(128)S(1)} %pad_add_fusion.me_ref, bf16[4,256,256]{2,1,0:T(8,128)(2,1)S(1)} %collective-permute-done.16.block_ref, bf16[1600,256]{1,0:T(8,128)(2,1)S(1)} %get-tuple-element.49.rows_ref, bf16[1600,2048]{1,0:T(8,128)(2,1)} %shard_map.127.refs_0_), custom_call_target="tpu_custom_call", output_to_operand_aliasing={{}: (3, {})} | custom-call | flops 838860800 | bytes 4096000 | tf_op jit(solution)/shard_map/pallas_call | solution.py:365
  123.9 3.5 %shard_map.132 = bf16[1600,2048]{1,0:T(8,128)(2,1)} custom-call(s32[2]{0:T(128)S(1)} %pad_add_fusion.me_ref, bf16[4,256,256]{2,1,0:T(8,128)(2,1)S(1)} %collective-permute-done.18.block_ref, bf16[1600,256]{1,0:T(8,128)(2,1)S(1)} %get-tuple-element.51.rows_ref, bf16[1600,2048]{1,0:T(8,128)(2,1)} %shard_map.131.refs_0_), custom_call_target="tpu_custom_call", output_to_operand_aliasing={{}: (3, {})} | custom-call | flops 838860800 | bytes 4096000 | tf_op jit(solution)/shard_map/pallas_call | solution.py:365
  127.5 1.5 %shard_map.122 = (bf16[16,1600]{1,0:T(8,128)(2,1)}, bf16[8,1600]{1,0:T(8,128)(2,1)}) custom-call(s32[2]{0:T(128)S(1)} %pad_add_fusion.me_ref, s32[1,4]{1,0:T(1,128)S(1)} %copy-done.6, s32[1,8]{1,0:T(1,128)S(1)} %copy-done.7, bf16[8,16,1600]{2,1,0:T(8,128)(2,1)S(1)} %all-to-all-done.tail_ref, f32[16,1600]{1,0:T(8,128)S(1)} %get-tuple-element.45.extra_ref, ...), custom_call_target="tpu_custom_call" | custom-call | tf_op jit(solution)/shard_map/pallas_call | solution.py:395
  (34 shorter events, 0.4 us)
Async XLA Ops:
  0.6 46.3 %copy-start.8 = (f32[1600]{0:T(1024)S(1)}, f32[1600]{0:T(1024)}, u32[]{:S(2)}) copy-start(f32[1600]{0:T(1024)} %param.9) | copy-start | bytes 19204
  1.9 6.8 %collective-permute-start = (bf16[1,16,1600]{2,1,0:T(8,128)(2,1)S(1)}, bf16[1,16,1600]{2,1,0:T(8,128)(2,1)S(1)}, u32[]{:S(2)}, u32[]{:S(2)}) collective-permute-start(bf16[1,16,1600]{2,1,0:T(8,128)(2,1)S(1)} %get-tuple-element.28.first_ref), channel_id=1, source_target_pairs={{0,16},{4,20},{8,24},{12,28},{16,0},{20,4},{24,8},{28,12},{1,17},{... | collective-permute-start | bytes 153608 | tf_op jit(solution)/shard_map/ppermute | solution.py:113
  8.7 4.8 %collective-permute-start.1 = (bf16[2,16,1600]{2,1,0:T(8,128)(2,1)S(1)}, bf16[2,16,1600]{2,1,0:T(8,128)(2,1)S(1)}, u32[]{:S(2)}, u32[]{:S(2)}) collective-permute-start(bf16[2,16,1600]{2,1,0:T(8,128)(2,1)S(1)} %shard_map.112.first_ref), channel_id=1, source_target_pairs={{0,8},{4,12},{8,0},{12,4},{16,24},{20,28},{24,16},{28,20},{1,9},{5... | collective-permute-start | bytes 307208 | tf_op jit(solution)/shard_map/ppermute | solution.py:113
  13.5 5.9 %collective-permute-start.2 = (bf16[4,16,1600]{2,1,0:T(8,128)(2,1)S(1)}, bf16[4,16,1600]{2,1,0:T(8,128)(2,1)S(1)}, u32[]{:S(2)}, u32[]{:S(2)}) collective-permute-start(bf16[4,16,1600]{2,1,0:T(8,128)(2,1)S(1)} %shard_map.113.first_ref), channel_id=1, source_target_pairs={{0,4},{4,0},{8,12},{12,8},{16,20},{20,16},{24,28},{28,24},{1,5},{5... | collective-permute-start | bytes 614408 | tf_op jit(solution)/shard_map/ppermute | solution.py:113
  19.4 8.2 %collective-permute-start.3 = (bf16[8,16,1600]{2,1,0:T(8,128)(2,1)S(1)}, bf16[8,16,1600]{2,1,0:T(8,128)(2,1)S(1)}, u32[]{:S(2)}, u32[]{:S(2)}) collective-permute-start(bf16[8,16,1600]{2,1,0:T(8,128)(2,1)S(1)} %shard_map.114.first_ref), channel_id=1, source_target_pairs={{0,2},{1,3},{2,0},{3,1},{4,6},{5,7},{6,4},{7,5},{8,10},{9,11},{10,... | collective-permute-start | bytes 1228808 | tf_op jit(solution)/shard_map/ppermute | solution.py:113
  27.7 18.3 %collective-permute-start.4 = (bf16[16,16,1600]{2,1,0:T(8,128)(2,1)S(1)}, bf16[16,16,1600]{2,1,0:T(8,128)(2,1)S(1)}, u32[]{:S(2)}, u32[]{:S(2)}) collective-permute-start(bf16[16,16,1600]{2,1,0:T(8,128)(2,1)S(1)} %shard_map.115.near_ref), channel_id=1, source_target_pairs={{0,1},{1,0},{2,3},{3,2},{4,5},{5,4},{6,7},{7,6},{8,9},{9,8},{10,11... | collective-permute-start | bytes 2457608 | tf_op jit(solution)/shard_map/ppermute | solution.py:113
  27.8 12.9 %collective-permute-start.8 = (bf16[2,200,256]{2,1,0:T(8,128)(2,1)S(1)}, bf16[2,200,256]{2,1,0:T(8,128)(2,1)S(1)}, u32[]{:S(2)}, u32[]{:S(2)}) collective-permute-start(bf16[2,200,256]{2,1,0:T(8,128)(2,1)S(1)} %get-tuple-element.34), channel_id=1, source_target_pairs={{0,16},{4,20},{8,24},{12,28},{16,0},{20,4},{24,8},{28,12},{1,17},{... | collective-permute-start | bytes 614408 | tf_op jit(solution)/shard_map/ppermute | solution.py:113
  32.9 9.1 %collective-permute-start.5 = (bf16[2,200,256]{2,1,0:T(8,128)(2,1)S(1)}, bf16[2,200,256]{2,1,0:T(8,128)(2,1)S(1)}, u32[]{:S(2)}, u32[]{:S(2)}) collective-permute-start(bf16[2,200,256]{2,1,0:T(8,128)(2,1)S(1)} %get-tuple-element.31), channel_id=1, source_target_pairs={{0,4},{4,0},{8,12},{12,8},{16,20},{20,16},{24,28},{28,24},{1,5},{5... | collective-permute-start | bytes 614408 | tf_op jit(solution)/shard_map/ppermute | solution.py:113
  34.4 14.6 %collective-permute-start.6 = (bf16[2,200,256]{2,1,0:T(8,128)(2,1)}, bf16[2,200,256]{2,1,0:T(8,128)(2,1)}, u32[]{:S(2)}, u32[]{:S(2)}) collective-permute-start(bf16[2,200,256]{2,1,0:T(8,128)(2,1)} %get-tuple-element.32), channel_id=1, source_target_pairs={{0,8},{4,12},{8,0},{12,4},{16,24},{20,28},{24,16},{28,20},{1,9},{5... | collective-permute-start | bytes 614408 | tf_op jit(solution)/shard_map/ppermute | solution.py:113
  36.2 15.1 %collective-permute-start.7 = (bf16[2,200,256]{2,1,0:T(8,128)(2,1)}, bf16[2,200,256]{2,1,0:T(8,128)(2,1)}, u32[]{:S(2)}, u32[]{:S(2)}) collective-permute-start(bf16[2,200,256]{2,1,0:T(8,128)(2,1)} %get-tuple-element.33), channel_id=1, source_target_pairs={{0,12},{4,8},{8,4},{12,0},{16,28},{20,24},{24,20},{28,16},{1,13},{... | collective-permute-start | bytes 614408 | tf_op jit(solution)/shard_map/ppermute | solution.py:113
  40.6 0.7 copy-start
  41.3 23.2 %collective-permute-start.9 = (bf16[2,200,256]{2,1,0:T(8,128)(2,1)}, bf16[2,200,256]{2,1,0:T(8,128)(2,1)}, u32[]{:S(2)}, u32[]{:S(2)}) collective-permute-start(bf16[2,200,256]{2,1,0:T(8,128)(2,1)} %get-tuple-element.35), channel_id=1, source_target_pairs={{0,20},{4,16},{8,28},{12,24},{16,4},{20,0},{24,12},{28,8},{1,21},{... | collective-permute-start | bytes 614408 | tf_op jit(solution)/shard_map/ppermute | solution.py:113
  41.9 0.7 copy-start.2
  42.6 21.9 %collective-permute-start.10 = (bf16[2,200,256]{2,1,0:T(8,128)(2,1)}, bf16[2,200,256]{2,1,0:T(8,128)(2,1)}, u32[]{:S(2)}, u32[]{:S(2)}) collective-permute-start(bf16[2,200,256]{2,1,0:T(8,128)(2,1)} %get-tuple-element.36), channel_id=1, source_target_pairs={{0,24},{4,28},{8,16},{12,20},{16,8},{20,12},{24,0},{28,4},{1,25},{... | collective-permute-start | bytes 614408 | tf_op jit(solution)/shard_map/ppermute | solution.py:113
  45.9 18.6 %collective-permute-start.11 = (bf16[2,200,256]{2,1,0:T(8,128)(2,1)}, bf16[2,200,256]{2,1,0:T(8,128)(2,1)}, u32[]{:S(2)}, u32[]{:S(2)}) collective-permute-start(bf16[2,200,256]{2,1,0:T(8,128)(2,1)} %get-tuple-element.37), channel_id=1, source_target_pairs={{0,28},{4,24},{8,20},{12,16},{16,12},{20,8},{24,4},{28,0},{1,29},{... | collective-permute-start | bytes 614408 | tf_op jit(solution)/shard_map/ppermute | solution.py:113
  64.5 0.9 copy-start.1
  65.4 0.9 copy-start.3
  70.3 10.0 %collective-permute-start.12 = (bf16[2,16,8,1600]{3,2,1,0:T(8,128)(2,1)S(1)}, bf16[2,16,8,1600]{3,2,1,0:T(8,128)(2,1)S(1)}, u32[]{:S(2)}, u32[]{:S(2)}) collective-permute-start(bf16[2,16,8,1600]{3,2,1,0:T(8,128)(2,1)S(1)} %get-tuple-element.42), channel_id=1, source_target_pairs={{0,1},{1,0},{2,3},{3,2},{4,5},{5,4},{6,7},{7,6},{8,9},{9,8},{10,11... | collective-permute-start | bytes 2457608 | tf_op jit(solution)/shard_map/ppermute | solution.py:113
  70.4 22.5 %collective-permute-start.14 = (bf16[2,256,256]{2,1,0:T(8,128)(2,1)S(1)}, bf16[2,256,256]{2,1,0:T(8,128)(2,1)S(1)}, u32[]{:S(2)}, u32[]{:S(2)}) collective-permute-start(bf16[2,256,256]{2,1,0:T(8,128)(2,1)S(1)} %get-tuple-element.38.both_ref.first_ref), channel_id=1, source_target_pairs={{0,16},{4,20},{8,24},{12,28},{16,0},{20,4},{24,8},{28,12},{1,17},{... | collective-permute-start | bytes 786440 | tf_op jit(solution)/shard_map/ppermute | solution.py:113
  80.6 13.9 %collective-permute-start.13 = (bf16[2,8,8,1600]{3,2,1,0:T(8,128)(2,1)S(1)}, bf16[2,8,8,1600]{3,2,1,0:T(8,128)(2,1)S(1)}, u32[]{:S(2)}, u32[]{:S(2)}) collective-permute-start(bf16[2,8,8,1600]{3,2,1,0:T(8,128)(2,1)S(1)} %get-tuple-element.44), channel_id=1, source_target_pairs={{0,2},{1,3},{2,0},{3,1},{4,6},{5,7},{6,4},{7,5},{8,10},{9,11},{10,... | collective-permute-start | bytes 1228808 | tf_op jit(solution)/shard_map/ppermute | solution.py:113
  92.9 8.2 %collective-permute-start.15 = (bf16[2,256,256]{2,1,0:T(8,128)(2,1)S(1)}, bf16[2,256,256]{2,1,0:T(8,128)(2,1)S(1)}, u32[]{:S(2)}, u32[]{:S(2)}) collective-permute-start(bf16[2,256,256]{2,1,0:T(8,128)(2,1)S(1)} %get-tuple-element.48.first_ref.block_ref), channel_id=1, source_target_pairs={{0,4},{4,0},{8,12},{12,8},{16,20},{20,16},{24,28},{28,24},{1,5},{5... | collective-permute-start | bytes 786440 | tf_op jit(solution)/shard_map/ppermute | solution.py:113
  94.5 10.1 %collective-permute-start.17 = (bf16[2,256,256]{2,1,0:T(8,128)(2,1)S(1)}, bf16[2,256,256]{2,1,0:T(8,128)(2,1)S(1)}, u32[]{:S(2)}, u32[]{:S(2)}) collective-permute-start(bf16[2,256,256]{2,1,0:T(8,128)(2,1)S(1)} %get-tuple-element.50.first_ref.block_ref), channel_id=1, source_target_pairs={{0,8},{4,12},{8,0},{12,4},{16,24},{20,28},{24,16},{28,20},{1,9},{5... | collective-permute-start | bytes 786440 | tf_op jit(solution)/shard_map/ppermute | solution.py:113
  95.4 32.1 %all-to-all-start = ((bf16[8,16,1600]{2,1,0:T(8,128)(2,1)}), bf16[8,16,1600]{2,1,0:T(8,128)(2,1)S(1)}, u32[]{:S(2)}, u32[]{:S(2)}) async-start(bf16[8,16,1600]{2,1,0:T(8,128)(2,1)} %shard_map.121), calls=%async_computation | async-start | bytes 851968 | tf_op jit(solution)/shard_map/all_to_all | solution.py:511
  101.1 19.2 %collective-permute-start.16 = (bf16[4,256,256]{2,1,0:T(8,128)(2,1)S(1)}, bf16[4,256,256]{2,1,0:T(8,128)(2,1)S(1)}, u32[]{:S(2)}, u32[]{:S(2)}) collective-permute-start(bf16[4,256,256]{2,1,0:T(8,128)(2,1)S(1)} %shard_map.124), channel_id=1, source_target_pairs={{0,8},{4,12},{8,0},{12,4},{16,24},{20,28},{24,16},{28,20},{1,9},{5... | collective-permute-start | bytes 1572872 | tf_op jit(solution)/shard_map/ppermute | solution.py:113
  104.7 19.2 %collective-permute-start.18 = (bf16[4,256,256]{2,1,0:T(8,128)(2,1)S(1)}, bf16[4,256,256]{2,1,0:T(8,128)(2,1)S(1)}, u32[]{:S(2)}, u32[]{:S(2)}) collective-permute-start(bf16[4,256,256]{2,1,0:T(8,128)(2,1)S(1)} %shard_map.129), channel_id=1, source_target_pairs={{0,4},{4,0},{8,12},{12,8},{16,20},{20,16},{24,28},{28,24},{1,5},{5... | collective-permute-start | bytes 1572872 | tf_op jit(solution)/shard_map/ppermute | solution.py:113
  123.9 3.5 %copy-start.4 = (bf16[8,1600]{1,0:T(8,128)(2,1)S(1)}, bf16[8,1600]{1,0:T(8,128)(2,1)}, u32[]{:S(2)}) copy-start(bf16[8,1600]{1,0:T(8,128)(2,1)} %patch_ref.1) | copy-start | bytes 76804
  123.9 3.5 %copy-start.5 = (bf16[16,1600]{1,0:T(8,128)(2,1)S(1)}, bf16[16,1600]{1,0:T(8,128)(2,1)}, u32[]{:S(2)}) copy-start(bf16[16,1600]{1,0:T(8,128)(2,1)} %text_ref.1) | copy-start | bytes 153604
  123.9 3.5 %copy-start.6 = (s32[1,4]{1,0:T(1,128)S(1)}, s32[1,4]{1,0:T(1,128)}, u32[]{:S(2)}) copy-start(s32[1,4]{1,0:T(1,128)} %count_ref.1) | copy-start | bytes 52
  123.9 3.6 %copy-start.7 = (s32[1,8]{1,0:T(1,128)S(1)}, s32[1,8]{1,0:T(1,128)}, u32[]{:S(2)}) copy-start(s32[1,8]{1,0:T(1,128)} %place_ref.1) | copy-start | bytes 100

commit v4 on v2

--- a/solution.py
+++ b/solution.py
@@ -178,6 +178,11 @@
                 )
             )
     fetch(copies)
+
+
+def turn_kernel(normed_ref, grad_ref, normed_turned_ref, grad_turned_ref):
+    normed_turned_ref[...] = normed_ref[...].T
+    grad_turned_ref[...] = grad_ref[...].T
 
 
 def join_kernel(first_ref, second_ref, out_ref):
@@ -310,10 +315,27 @@
         out_ref[d] = jnp.concatenate([total[0, d], total[1, d]], axis=0).astype(jnp.bfloat16)
 
 
-def weight_grad_kernel(me_ref, block_ref, rows_ref, *refs):
-    refs[-1][...] = lax.dot_general(
-        rows_ref[...], block_ref[0], (((0,), (0,)), ((), ())), preferred_element_type=jnp.float32
-    ).astype(jnp.bfloat16)
+def weight_grad_kernel(distances, block_ref, rows_ref, *refs):
+    out_at, result_ref, sems = refs[-3:]
+    count, features, units = result_ref.shape
+    piece = features // sems.shape[1]
+    copies = []
+    for i in range(count):
+        result_ref[i] = jnp.dot(
+            rows_ref[...], block_ref[i], preferred_element_type=jnp.float32
+        ).astype(jnp.bfloat16)
+        source = lax.axis_index("dp") ^ distances[i]
+        columns = pl.ds(pl.multiple_of(source * units, 128), units)
+        for k in range(sems.shape[1]):
+            at = pl.ds(k * piece, piece)
+            copies.append(
+                pltpu.make_async_copy(
+                    result_ref.at[i, at, :], out_at.at[at, columns], sems.at[i, k]
+                )
+            )
+            copies[-1].start()
+    for copy in copies:
+        copy.wait()
 
 
 def finish_kernel(
@@ -349,35 +371,28 @@
     ).astype(jnp.bfloat16)
 
 
-def weight_grads(me, blocks, first_index, steps, values, width, before=()):
+def weight_grads(blocks, distances, values, width, before=()):
     count, rows, units = blocks.shape
-    features = values.shape[1]
+    features = values.shape[0]
+    pieces = 4 if features % 64 == 0 else 1
+    anywhere = pl.BlockSpec(memory_space=pl.ANY)
     return pl.pallas_call(
-        weight_grad_kernel,
-        grid_spec=pltpu.PrefetchScalarGridSpec(
-            num_scalar_prefetch=1,
-            grid=(count,),
-            in_specs=[
-                pl.BlockSpec((1, rows, units), lambda i, me_ref: (i, 0, 0)),
-                pl.BlockSpec((rows, features), lambda i, me_ref: (0, 0)),
-            ]
-            + [pl.BlockSpec(memory_space=pl.ANY)] * len(before),
-            out_specs=pl.BlockSpec(
-                (features, units),
-                lambda i, me_ref: (0, me_ref[0] ^ masked_steps(first_index + i, steps)),
-            ),
-        ),
+        functools.partial(weight_grad_kernel, distances),
+        in_specs=[VMEM_SPEC] * 2 + [anywhere] * len(before),
+        out_specs=anywhere,
         out_shape=jax.ShapeDtypeStruct((features, width), jnp.bfloat16),
-        input_output_aliases={3: 0} if before else {},
-        compiler_params=pltpu.CompilerParams(
-            dimension_semantics=("arbitrary",), vmem_limit_bytes=12 << 20
-        ),
+        scratch_shapes=[
+            pltpu.VMEM((count, features, units), jnp.bfloat16),
+            pltpu.SemaphoreType.DMA((count, pieces)),
+        ],
+        input_output_aliases={2: 0} if before else {},
+        compiler_params=pltpu.CompilerParams(vmem_limit_bytes=12 << 20),
         cost_estimate=pl.CostEstimate(
             flops=2 * count * rows * features * units,
             bytes_accessed=2 * count * units * features + 2 * rows * features,
             transcendentals=0,
         ),
-    )(me, blocks, values, *before)
+    )(blocks, values, *before)
 
 
 def call(kernel, out_shape, smem, vmem, scratch=()):
@@ -468,6 +483,9 @@
         (me,), (held, got, gain),
     )
 
+    normed_turned, grad_turned = call(
+        turn_kernel, [shape((features, rows), kept)] * 2, (), (normed, grad_all)
+    )
     both, expand_slice, project_slice = pl.pallas_call(
         hidden_kernel,
         out_shape=[shape((2, rows, units), kept)] + [shape((features, units), kept)] * 2,
@@ -494,21 +512,20 @@
     tail = lax.all_to_all(tail, "dp", split_axis=0, concat_axis=0, tiled=True)
 
     far_both = swap(both, "dp", dp_steps[0])
-    hidden_steps, pre_steps = dp_steps, dp_steps[:1] + dp_steps[:0:-1]
-    hidden, pre = join_pairs(both, far_both)
-    for place, (hidden_step, pre_step) in enumerate(zip(hidden_steps[1:], pre_steps[1:]), 1):
-        hidden_far = swap(hidden, "dp", hidden_step)
-        pre_far = swap(pre, "dp", pre_step)
-        if hidden.shape[0] < replicas // 2:
-            hidden, pre = join(hidden, hidden_far), join(pre, pre_far)
-
-    half = replicas // 2
-    project_grad = weight_grads(me, hidden, 0, hidden_steps, grad_all, width)
-    expand_grad = weight_grads(me, pre, 0, pre_steps, normed, width)
-    project_grad = weight_grads(
-        me, hidden_far, half, hidden_steps, grad_all, width, (project_grad,)
-    )
-    expand_grad = weight_grads(me, pre_far, half, pre_steps, normed, width, (expand_grad,))
+    pairs = join_pairs(both, far_both)
+    grads = []
+    for pair, values, steps in (
+        (pairs[0], grad_turned, dp_steps[1:]), (pairs[1], normed_turned, dp_steps[:0:-1])
+    ):
+        held_pairs = {0: pair}
+        for step in steps:
+            for mask, array in list(held_pairs.items()):
+                held_pairs[mask ^ step] = swap(array, "dp", step)
+        grad = ()
+        for mask, array in held_pairs.items():
+            grad = (weight_grads(array, (mask, mask ^ dp_steps[0]), values, width, grad),)
+        grads += grad
+    project_grad, expand_grad = grads
     embedded, grad_rows = call(
         functools.partial(finish_kernel, capacity),
         [shape(text.shape, kept), shape(patches.shape, kept)],

time: 128 us -> 133 us (1.039)
  starting transfers between devices: 42.8 us -> 53.6 us
  waiting for transfers between devices: 53.8 us -> 47 us
    all_to_all x1, starting transfers between devices: 3.46 us -> 12.2 us  [move_rows_plan(): tail = lax.all_to_all(tail, 'dp', split_axis=0, concat_axis=0, tiled=True)]
    ppermute x19 -> x21, waiting for transfers between devices: 53.8 us -> 47 us  [swap(): return lax.ppermute(array, axis, [(i, i ^ step) for i in range(size)])]
    ppermute x19 -> x21, starting transfers between devices: 39.3 us -> 41.5 us  [swap(): return lax.ppermute(array, axis, [(i, i ^ step) for i in range(size)])]
    pallas_call x12 -> x11, Pallas kernels: 6.13 us -> 6.54 us  [call(): pl.pallas_call(kernel, out_shape=out_shape, in_specs=[SMEM_SPEC] * len(sm...]
    pallas_call x4 -> x8, Pallas kernels: 14.4 us -> 14.5 us  [weight_grads(): pl.pallas_call(functools.partial(weight_grad_kernel, distances), in_specs...]
  transfers between devices with their start and end apart: 20 -> 22, of which waited for: 10 -> 11; matrix products, arithmetic and copies ran while one was open for 1% -> 1% of each run, Pallas kernels for 16% -> 15%
where the time goes in v4:
time: 133 us
  starting transfers between devices  53.6 us (40%)
  waiting for transfers between devices  47 us (35%)
  Pallas kernels  27.1 us (20%)
  local copies, waits for them, and re-layouts  3.93 us (3%)
    ppermute x21, waiting for transfers between devices, swap(): return lax.ppermute(array, axis, [(i, i ^ step) for i in range(size)])  47 us
    ppermute x21, starting transfers between devices, swap(): return lax.ppermute(array, axis, [(i, i ^ step) for i in range(size)])  41.5 us
    pallas_call x8, Pallas kernels, weight_grads(): pl.pallas_call(functools.partial(weight_grad_kernel, distances), in_specs...  14.5 us
    all_to_all x1, starting transfers between devices, move_rows_plan(): tail = lax.all_to_all(tail, 'dp', split_axis=0, concat_axis=0, tiled=True)  12.2 us
    pallas_call x11, Pallas kernels, call(): pl.pallas_call(kernel, out_shape=out_shape, in_specs=[SMEM_SPEC] * len(sm...  6.54 us
    unnamed x16, local copies, waits for them, and re-layouts  3.23 us
  transfers between devices with their start and end apart: 22, of which 11 were waited for; matrix products, arithmetic and copies ran while one was open for 1% of the time, Pallas kernels for 15%

profile of v4, /device:TPU:0, one launch (start us, length us, event | category | flops | bytes accessed | tf_op | source)
XLA Modules:
  0.0 132.6 jit_solution(7467321279102966946)
XLA Ops:
  0.6 1.0 shard_map.111.first_ref
  1.6 4.1 %collective-permute-start = (bf16[1,16,1600]{2,1,0:T(8,128)(2,1)S(1)}, bf16[1,16,1600]{2,1,0:T(8,128)(2,1)S(1)}, u32[]{:S(2)}, u32[]{:S(2)}) collective-permute-start(bf16[1,16,1600]{2,1,0:T(8,128)(2,1)S(1)} %shard_map.111.first_ref), channel_id=1, source_target_pairs={{0,16},{4,20},{8,24},{12,28},{16,0},{20,4},{24,8},{28,12},{1,17},{... | collective-permute-start | bytes 153608 | tf_op jit(solution)/shard_map/ppermute | solution.py:113
  5.8 2.7 %collective-permute-done.second_ref = bf16[1,16,1600]{2,1,0:T(8,128)(2,1)S(1)} collective-permute-done((bf16[1,16,1600]{2,1,0:T(8,128)(2,1)S(1)}, bf16[1,16,1600]{2,1,0:T(8,128)(2,1)S(1)}, u32[]{:S(2)}, u32[]{:S(2)}) %collective-permute-start) | collective-permute-done | bytes 51232 | tf_op jit(solution)/shard_map/ppermute | solution.py:113
  8.5 1.4 %collective-permute-start.1 = (bf16[2,16,1600]{2,1,0:T(8,128)(2,1)S(1)}, bf16[2,16,1600]{2,1,0:T(8,128)(2,1)S(1)}, u32[]{:S(2)}, u32[]{:S(2)}) collective-permute-start(bf16[2,16,1600]{2,1,0:T(8,128)(2,1)S(1)} %shard_map.112.first_ref), channel_id=1, source_target_pairs={{0,8},{4,12},{8,0},{12,4},{16,24},{20,28},{24,16},{28,20},{1,9},{5... | collective-permute-start | bytes 307208 | tf_op jit(solution)/shard_map/ppermute | solution.py:113
  9.9 3.4 %collective-permute-done.1.second_ref = bf16[2,16,1600]{2,1,0:T(8,128)(2,1)S(1)} collective-permute-done((bf16[2,16,1600]{2,1,0:T(8,128)(2,1)S(1)}, bf16[2,16,1600]{2,1,0:T(8,128)(2,1)S(1)}, u32[]{:S(2)}, u32[]{:S(2)}) %collective-permute-start.1) | collective-permute-done | bytes 102432 | tf_op jit(solution)/shard_map/ppermute | solution.py:113
  13.3 1.8 %collective-permute-start.2 = (bf16[4,16,1600]{2,1,0:T(8,128)(2,1)S(1)}, bf16[4,16,1600]{2,1,0:T(8,128)(2,1)S(1)}, u32[]{:S(2)}, u32[]{:S(2)}) collective-permute-start(bf16[4,16,1600]{2,1,0:T(8,128)(2,1)S(1)} %shard_map.113.first_ref), channel_id=1, source_target_pairs={{0,4},{4,0},{8,12},{12,8},{16,20},{20,16},{24,28},{28,24},{1,5},{5... | collective-permute-start | bytes 614408 | tf_op jit(solution)/shard_map/ppermute | solution.py:113
  15.0 4.1 %collective-permute-done.2.second_ref = bf16[4,16,1600]{2,1,0:T(8,128)(2,1)S(1)} collective-permute-done((bf16[4,16,1600]{2,1,0:T(8,128)(2,1)S(1)}, bf16[4,16,1600]{2,1,0:T(8,128)(2,1)S(1)}, u32[]{:S(2)}, u32[]{:S(2)}) %collective-permute-start.2) | collective-permute-done | bytes 204832 | tf_op jit(solution)/shard_map/ppermute | solution.py:113
  19.2 1.8 %collective-permute-start.3 = (bf16[8,16,1600]{2,1,0:T(8,128)(2,1)S(1)}, bf16[8,16,1600]{2,1,0:T(8,128)(2,1)S(1)}, u32[]{:S(2)}, u32[]{:S(2)}) collective-permute-start(bf16[8,16,1600]{2,1,0:T(8,128)(2,1)S(1)} %shard_map.114.first_ref), channel_id=1, source_target_pairs={{0,2},{1,3},{2,0},{3,1},{4,6},{5,7},{6,4},{7,5},{8,10},{9,11},{10,... | collective-permute-start | bytes 1228808 | tf_op jit(solution)/shard_map/ppermute | solution.py:113
  21.0 6.4 %collective-permute-done.3.second_ref = bf16[8,16,1600]{2,1,0:T(8,128)(2,1)S(1)} collective-permute-done((bf16[8,16,1600]{2,1,0:T(8,128)(2,1)S(1)}, bf16[8,16,1600]{2,1,0:T(8,128)(2,1)S(1)}, u32[]{:S(2)}, u32[]{:S(2)}) %collective-permute-start.3) | collective-permute-done | bytes 409632 | tf_op jit(solution)/shard_map/ppermute | solution.py:113
  27.5 2.5 %shard_map.117 = (bf16[2,200,256]{2,1,0:T(8,128)(2,1)S(1)}, bf16[2,200,256]{2,1,0:T(8,128)(2,1)S(1)}, bf16[2,200,256]{2,1,0:T(8,128)(2,1)}, bf16[2,200,256]{2,1,...) custom-call(bf16[200,2048]{1,0:T(8,128)(2,1)} %expand_at.3, ...), custom_call_target="tpu_custom_call" | custom-call | tf_op jit(solution)/shard_map/pallas_call | solution.py:463
  30.1 1.8 %collective-permute-start.5 = (bf16[2,200,256]{2,1,0:T(8,128)(2,1)S(1)}, bf16[2,200,256]{2,1,0:T(8,128)(2,1)S(1)}, u32[]{:S(2)}, u32[]{:S(2)}) collective-permute-start(bf16[2,200,256]{2,1,0:T(8,128)(2,1)S(1)} %get-tuple-element.29), channel_id=1, source_target_pairs={{0,4},{4,0},{8,12},{12,8},{16,20},{20,16},{24,28},{28,24},{1,5},{5... | collective-permute-start | bytes 614408 | tf_op jit(solution)/shard_map/ppermute | solution.py:113
  31.9 1.1 collective-permute-start.6
  33.0 0.6 collective-permute-start.7
  33.6 2.6 %collective-permute-start.8 = (bf16[2,200,256]{2,1,0:T(8,128)(2,1)}, bf16[2,200,256]{2,1,0:T(8,128)(2,1)}, u32[]{:S(2)}, u32[]{:S(2)}) collective-permute-start(bf16[2,200,256]{2,1,0:T(8,128)(2,1)} %get-tuple-element.32), channel_id=1, source_target_pairs={{0,16},{4,20},{8,24},{12,28},{16,0},{20,4},{24,8},{28,12},{1,17},{... | collective-permute-start | bytes 614408 | tf_op jit(solution)/shard_map/ppermute | solution.py:113
  36.3 1.3 %collective-permute-done.5.refs_0_ = bf16[2,200,256]{2,1,0:T(8,128)(2,1)S(1)} collective-permute-done((bf16[2,200,256]{2,1,0:T(8,128)(2,1)S(1)}, bf16[2,200,256]{2,1,0:T(8,128)(2,1)S(1)}, u32[]{:S(2)}, u32[]{:S(2)}) %collective-permute-start.5) | collective-permute-done | bytes 204832 | tf_op jit(solution)/shard_map/ppermute | solution.py:113
  37.6 0.7 copy-done
  38.3 3.6 %collective-permute-start.9 = (bf16[2,200,256]{2,1,0:T(8,128)(2,1)}, bf16[2,200,256]{2,1,0:T(8,128)(2,1)}, u32[]{:S(2)}, u32[]{:S(2)}) collective-permute-start(bf16[2,200,256]{2,1,0:T(8,128)(2,1)} %get-tuple-element.33), channel_id=1, source_target_pairs={{0,20},{4,16},{8,28},{12,24},{16,4},{20,0},{24,12},{28,8},{1,21},{... | collective-permute-start | bytes 614408 | tf_op jit(solution)/shard_map/ppermute | solution.py:113
  41.9 4.9 %collective-permute-done.6.refs_1_ = bf16[2,200,256]{2,1,0:T(8,128)(2,1)S(1)} collective-permute-done((bf16[2,200,256]{2,1,0:T(8,128)(2,1)S(1)}, bf16[2,200,256]{2,1,0:T(8,128)(2,1)S(1)}, u32[]{:S(2)}, u32[]{:S(2)}) %collective-permute-start.6) | collective-permute-done | bytes 204832 | tf_op jit(solution)/shard_map/ppermute | solution.py:113
  46.8 0.7 copy-done.2
  47.5 1.5 %collective-permute-start.10 = (bf16[2,200,256]{2,1,0:T(8,128)(2,1)}, bf16[2,200,256]{2,1,0:T(8,128)(2,1)}, u32[]{:S(2)}, u32[]{:S(2)}) collective-permute-start(bf16[2,200,256]{2,1,0:T(8,128)(2,1)} %get-tuple-element.34), channel_id=1, source_target_pairs={{0,24},{4,28},{8,16},{12,20},{16,8},{20,12},{24,0},{28,4},{1,25},{... | collective-permute-start | bytes 614408 | tf_op jit(solution)/shard_map/ppermute | solution.py:113
  49.0 2.3 %collective-permute-start.11 = (bf16[2,200,256]{2,1,0:T(8,128)(2,1)}, bf16[2,200,256]{2,1,0:T(8,128)(2,1)}, u32[]{:S(2)}, u32[]{:S(2)}) collective-permute-start(bf16[2,200,256]{2,1,0:T(8,128)(2,1)} %get-tuple-element.35), channel_id=1, source_target_pairs={{0,28},{4,24},{8,20},{12,16},{16,12},{20,8},{24,4},{28,0},{1,29},{... | collective-permute-start | bytes 614408 | tf_op jit(solution)/shard_map/ppermute | solution.py:113
  51.2 0.7 reshape.11.gain_ref
  52.0 2.0 %shard_map.116 = (bf16[256,1600]{1,0:T(8,128)(2,1)S(1)}, bf16[256,1600]{1,0:T(8,128)(2,1)S(1)}, f32[16,1600]{1,0:T(8,128)S(1)}) custom-call(s32[2]{0:T(128)S(1)} %pad_add_fusion.me_ref, bf16[16,16,1600]{2,1,0:T(8,128)(2,1)S(1)} %shard_map.115.near_ref, bf16[16,16,1600]{2,1,0:T(8,128)(2,1)S(1)} %collective-permute-done.4.far_ref, f32[1,1600]{1,0:T(1,128)S(1)} %reshape.11.gain_ref), custom_call_target="tpu_custom_call" | custom-call | tf_op jit(solution)/shard_map/pallas_call | solution.py:400
  54.0 11.9 %collective-permute-done.9.refs_4_ = bf16[2,200,256]{2,1,0:T(8,128)(2,1)} collective-permute-done((bf16[2,200,256]{2,1,0:T(8,128)(2,1)}, bf16[2,200,256]{2,1,0:T(8,128)(2,1)}, u32[]{:S(2)}, u32[]{:S(2)}) %collective-permute-start.9) | collective-permute-done | bytes 204832 | tf_op jit(solution)/shard_map/ppermute | solution.py:113
  65.9 0.9 copy-done.1
  66.8 0.9 copy-done.3
  67.8 2.5 %shard_map.118 = (bf16[2,256,256]{2,1,0:T(8,128)(2,1)S(1)}, bf16[1600,256]{1,0:T(8,128)(2,1)S(1)}, bf16[1600,256]{1,0:T(8,128)(2,1)S(1)}) custom-call(bf16[256,1600]{1,0:T(8,128)(2,1)S(1)} %get-tuple-element.27.normed_ref, bf16[256,1600]{1,0:T(8,128)(2,1)S(1)} %get-tuple-element.28.grad_ref, bf16[200,2048]{1,0:T(8,128)(2,1)} %expand_at.3, ...), custom_call_target="tpu_custom_call" | custom-call | tf_op jit(solution)/shard_map/pallas_call | solution.py:489
  70.3 1.4 %shard_map.119 = (f32[2,16,8,1600]{3,2,1,0:T(8,128)S(1)}, bf16[2,16,8,1600]{3,2,1,0:T(8,128)(2,1)S(1)}) custom-call(s32[2]{0:T(128)S(1)} %pad_add_fusion.me_ref, bf16[2,256,256]{2,1,0:T(8,128)(2,1)S(1)} %get-tuple-element.36.both_ref.first_ref, bf16[1600,256]{1,0:T(8,128)(2,1)S(1)} %get-tuple-element.37.expand_ref, ...), custom_call_target="tpu_custom_call" | custom-call | tf_op jit(solution)/shard_map/pallas_call | solution.py:400
  71.8 2.4 %collective-permute-done.12.got_ref = bf16[2,16,8,1600]{3,2,1,0:T(8,128)(2,1)S(1)} collective-permute-done((bf16[2,16,8,1600]{3,2,1,0:T(8,128)(2,1)S(1)}, bf16[2,16,8,1600]{3,2,1,0:T(8,128)(2,1)S(1)}, u32[]{:S(2)}, u32[]{:S(2)}) %collective-permute-start.12) | collective-permute-done | bytes 819232 | tf_op jit(solution)/shard_map/ppermute | solution.py:113
  74.4 1.8 %collective-permute-start.13 = (bf16[2,8,8,1600]{3,2,1,0:T(8,128)(2,1)S(1)}, bf16[2,8,8,1600]{3,2,1,0:T(8,128)(2,1)S(1)}, u32[]{:S(2)}, u32[]{:S(2)}) collective-permute-start(bf16[2,8,8,1600]{3,2,1,0:T(8,128)(2,1)S(1)} %get-tuple-element.42), channel_id=1, source_target_pairs={{0,2},{1,3},{2,0},{3,1},{4,6},{5,7},{6,4},{7,5},{8,10},{9,11},{10,... | collective-permute-start | bytes 1228808 | tf_op jit(solution)/shard_map/ppermute | solution.py:113
  76.2 10.0 %collective-permute-start.14 = (bf16[2,256,256]{2,1,0:T(8,128)(2,1)S(1)}, bf16[2,256,256]{2,1,0:T(8,128)(2,1)S(1)}, u32[]{:S(2)}, u32[]{:S(2)}) collective-permute-start(bf16[2,256,256]{2,1,0:T(8,128)(2,1)S(1)} %get-tuple-element.36.both_ref.first_ref), channel_id=1, source_target_pairs={{0,16},{4,20},{8,24},{12,28},{16,0},{20,4},{24,8},{28,12},{1,17},{... | collective-permute-start | bytes 786440 | tf_op jit(solution)/shard_map/ppermute | solution.py:113
  86.3 0.8 shard_map.121
  87.2 12.2 %all-to-all-start = ((bf16[8,16,1600]{2,1,0:T(8,128)(2,1)}), bf16[8,16,1600]{2,1,0:T(8,128)(2,1)S(1)}, u32[]{:S(2)}, u32[]{:S(2)}) async-start(bf16[8,16,1600]{2,1,0:T(8,128)(2,1)} %shard_map.121), calls=%async_computation | async-start | bytes 851968 | tf_op jit(solution)/shard_map/all_to_all | solution.py:512
  99.4 2.1 %collective-permute-start.15 = (bf16[2,256,256]{2,1,0:T(8,128)(2,1)S(1)}, bf16[2,256,256]{2,1,0:T(8,128)(2,1)S(1)}, u32[]{:S(2)}, u32[]{:S(2)}) collective-permute-start(bf16[2,256,256]{2,1,0:T(8,128)(2,1)S(1)} %get-tuple-element.46.block_ref), channel_id=1, source_target_pairs={{0,4},{4,0},{8,12},{12,8},{16,20},{20,16},{24,28},{28,24},{1,5},{5... | collective-permute-start | bytes 786440 | tf_op jit(solution)/shard_map/ppermute | solution.py:113
  101.5 1.5 %collective-permute-start.18 = (bf16[2,256,256]{2,1,0:T(8,128)(2,1)S(1)}, bf16[2,256,256]{2,1,0:T(8,128)(2,1)S(1)}, u32[]{:S(2)}, u32[]{:S(2)}) collective-permute-start(bf16[2,256,256]{2,1,0:T(8,128)(2,1)S(1)} %get-tuple-element.48.block_ref), channel_id=1, source_target_pairs={{0,8},{4,12},{8,0},{12,4},{16,24},{20,28},{24,16},{28,20},{1,9},{5... | collective-permute-start | bytes 786440 | tf_op jit(solution)/shard_map/ppermute | solution.py:113
  102.9 0.6 collective-permute-start.17
  103.6 9.3 %collective-permute-done.15.block_ref = bf16[2,256,256]{2,1,0:T(8,128)(2,1)S(1)} collective-permute-done((bf16[2,256,256]{2,1,0:T(8,128)(2,1)S(1)}, bf16[2,256,256]{2,1,0:T(8,128)(2,1)S(1)}, u32[]{:S(2)}, u32[]{:S(2)}) %collective-permute-start.15) | collective-permute-done | bytes 262176 | tf_op jit(solution)/shard_map/ppermute | solution.py:113
  112.9 1.8 %collective-permute-start.16 = (bf16[2,256,256]{2,1,0:T(8,128)(2,1)S(1)}, bf16[2,256,256]{2,1,0:T(8,128)(2,1)S(1)}, u32[]{:S(2)}, u32[]{:S(2)}) collective-permute-start(bf16[2,256,256]{2,1,0:T(8,128)(2,1)S(1)} %collective-permute-done.15.block_ref), channel_id=1, source_target_pairs={{0,8},{4,12},{8,0},{12,4},{16,24},{20,28},{24,16},{28,20},{1,9},{5... | collective-permute-start | bytes 786440 | tf_op jit(solution)/shard_map/ppermute | solution.py:113
  115.6 0.9 collective-permute-start.19
  116.5 1.8 %shard_map.125.refs_0_ = bf16[1600,2048]{1,0:T(8,128)(2,1)} custom-call(bf16[2,256,256]{2,1,0:T(8,128)(2,1)S(1)} %get-tuple-element.46.block_ref, bf16[1600,256]{1,0:T(8,128)(2,1)S(1)} %get-tuple-element.47.rows_ref), custom_call_target="tpu_custom_call" | custom-call | flops 419430400 | bytes 2457600 | tf_op jit(solution)/shard_map/pallas_call | solution.py:379
  118.3 1.8 %shard_map.129.refs_0_ = bf16[1600,2048]{1,0:T(8,128)(2,1)} custom-call(bf16[2,256,256]{2,1,0:T(8,128)(2,1)S(1)} %get-tuple-element.48.block_ref, bf16[1600,256]{1,0:T(8,128)(2,1)S(1)} %get-tuple-element.49.rows_ref), custom_call_target="tpu_custom_call" | custom-call | flops 419430400 | bytes 2457600 | tf_op jit(solution)/shard_map/pallas_call | solution.py:379
  120.1 1.8 %shard_map.126.refs_0_ = bf16[1600,2048]{1,0:T(8,128)(2,1)} custom-call(bf16[2,256,256]{2,1,0:T(8,128)(2,1)S(1)} %collective-permute-done.15.block_ref, bf16[1600,256]{1,0:T(8,128)(2,1)S(1)} %get-tuple-element.47.rows_ref, bf16[1600,2048]{1,0:T(8,128)(2,1)} %shard_map.125.refs_0_), custom_call_target="tpu_custom_call", output_to_operand_aliasing={{}: (2, {})} | custom-call | flops 419430400 | bytes 2457600 | tf_op jit(solution)/shard_map/pallas_call | solution.py:379
  121.9 1.8 %shard_map.130.refs_0_ = bf16[1600,2048]{1,0:T(8,128)(2,1)} custom-call(bf16[2,256,256]{2,1,0:T(8,128)(2,1)S(1)} %collective-permute-done.18.block_ref, bf16[1600,256]{1,0:T(8,128)(2,1)S(1)} %get-tuple-element.49.rows_ref, bf16[1600,2048]{1,0:T(8,128)(2,1)} %shard_map.129.refs_0_), custom_call_target="tpu_custom_call", output_to_operand_aliasing={{}: (2, {})} | custom-call | flops 419430400 | bytes 2457600 | tf_op jit(solution)/shard_map/pallas_call | solution.py:379
  123.7 1.8 %shard_map.127.refs_0_ = bf16[1600,2048]{1,0:T(8,128)(2,1)} custom-call(bf16[2,256,256]{2,1,0:T(8,128)(2,1)S(1)} %collective-permute-done.17.block_ref, bf16[1600,256]{1,0:T(8,128)(2,1)S(1)} %get-tuple-element.47.rows_ref, bf16[1600,2048]{1,0:T(8,128)(2,1)} %shard_map.126.refs_0_), custom_call_target="tpu_custom_call", output_to_operand_aliasing={{}: (2, {})} | custom-call | flops 419430400 | bytes 2457600 | tf_op jit(solution)/shard_map/pallas_call | solution.py:379
  125.6 1.8 %shard_map.131.refs_0_ = bf16[1600,2048]{1,0:T(8,128)(2,1)} custom-call(bf16[2,256,256]{2,1,0:T(8,128)(2,1)S(1)} %collective-permute-done.20.block_ref, bf16[1600,256]{1,0:T(8,128)(2,1)S(1)} %get-tuple-element.49.rows_ref, bf16[1600,2048]{1,0:T(8,128)(2,1)} %shard_map.130.refs_0_), custom_call_target="tpu_custom_call", output_to_operand_aliasing={{}: (2, {})} | custom-call | flops 419430400 | bytes 2457600 | tf_op jit(solution)/shard_map/pallas_call | solution.py:379
  127.4 1.8 %shard_map.128 = bf16[1600,2048]{1,0:T(8,128)(2,1)} custom-call(bf16[2,256,256]{2,1,0:T(8,128)(2,1)S(1)} %collective-permute-done.16.block_ref, bf16[1600,256]{1,0:T(8,128)(2,1)S(1)} %get-tuple-element.47.rows_ref, bf16[1600,2048]{1,0:T(8,128)(2,1)} %shard_map.127.refs_0_), custom_call_target="tpu_custom_call", output_to_operand_aliasing={{}: (2, {})} | custom-call | flops 419430400 | bytes 2457600 | tf_op jit(solution)/shard_map/pallas_call | solution.py:379
  129.3 1.8 %shard_map.132 = bf16[1600,2048]{1,0:T(8,128)(2,1)} custom-call(bf16[2,256,256]{2,1,0:T(8,128)(2,1)S(1)} %collective-permute-done.19.block_ref, bf16[1600,256]{1,0:T(8,128)(2,1)S(1)} %get-tuple-element.49.rows_ref, bf16[1600,2048]{1,0:T(8,128)(2,1)} %shard_map.131.refs_0_), custom_call_target="tpu_custom_call", output_to_operand_aliasing={{}: (2, {})} | custom-call | flops 419430400 | bytes 2457600 | tf_op jit(solution)/shard_map/pallas_call | solution.py:379
  131.1 1.5 %shard_map.122 = (bf16[16,1600]{1,0:T(8,128)(2,1)}, bf16[8,1600]{1,0:T(8,128)(2,1)}) custom-call(s32[2]{0:T(128)S(1)} %pad_add_fusion.me_ref, s32[1,4]{1,0:T(1,128)S(1)} %copy-done.6, s32[1,8]{1,0:T(1,128)S(1)} %copy-done.7, bf16[8,16,1600]{2,1,0:T(8,128)(2,1)S(1)} %all-to-all-done.tail_ref, f32[16,1600]{1,0:T(8,128)S(1)} %get-tuple-element.43.extra_ref, ...), custom_call_target="tpu_custom_call" | custom-call | tf_op jit(solution)/shard_map/pallas_call | solution.py:400
  (36 shorter events, 1.7 us)
Async XLA Ops:
  1.6 6.8 %collective-permute-start = (bf16[1,16,1600]{2,1,0:T(8,128)(2,1)S(1)}, bf16[1,16,1600]{2,1,0:T(8,128)(2,1)S(1)}, u32[]{:S(2)}, u32[]{:S(2)}) collective-permute-start(bf16[1,16,1600]{2,1,0:T(8,128)(2,1)S(1)} %shard_map.111.first_ref), channel_id=1, source_target_pairs={{0,16},{4,20},{8,24},{12,28},{16,0},{20,4},{24,8},{28,12},{1,17},{... | collective-permute-start | bytes 153608 | tf_op jit(solution)/shard_map/ppermute | solution.py:113
  8.5 4.8 %collective-permute-start.1 = (bf16[2,16,1600]{2,1,0:T(8,128)(2,1)S(1)}, bf16[2,16,1600]{2,1,0:T(8,128)(2,1)S(1)}, u32[]{:S(2)}, u32[]{:S(2)}) collective-permute-start(bf16[2,16,1600]{2,1,0:T(8,128)(2,1)S(1)} %shard_map.112.first_ref), channel_id=1, source_target_pairs={{0,8},{4,12},{8,0},{12,4},{16,24},{20,28},{24,16},{28,20},{1,9},{5... | collective-permute-start | bytes 307208 | tf_op jit(solution)/shard_map/ppermute | solution.py:113
  13.3 5.9 %collective-permute-start.2 = (bf16[4,16,1600]{2,1,0:T(8,128)(2,1)S(1)}, bf16[4,16,1600]{2,1,0:T(8,128)(2,1)S(1)}, u32[]{:S(2)}, u32[]{:S(2)}) collective-permute-start(bf16[4,16,1600]{2,1,0:T(8,128)(2,1)S(1)} %shard_map.113.first_ref), channel_id=1, source_target_pairs={{0,4},{4,0},{8,12},{12,8},{16,20},{20,16},{24,28},{28,24},{1,5},{5... | collective-permute-start | bytes 614408 | tf_op jit(solution)/shard_map/ppermute | solution.py:113
  19.2 8.2 %collective-permute-start.3 = (bf16[8,16,1600]{2,1,0:T(8,128)(2,1)S(1)}, bf16[8,16,1600]{2,1,0:T(8,128)(2,1)S(1)}, u32[]{:S(2)}, u32[]{:S(2)}) collective-permute-start(bf16[8,16,1600]{2,1,0:T(8,128)(2,1)S(1)} %shard_map.114.first_ref), channel_id=1, source_target_pairs={{0,2},{1,3},{2,0},{3,1},{4,6},{5,7},{6,4},{7,5},{8,10},{9,11},{10,... | collective-permute-start | bytes 1228808 | tf_op jit(solution)/shard_map/ppermute | solution.py:113
  27.5 21.5 %collective-permute-start.4 = (bf16[16,16,1600]{2,1,0:T(8,128)(2,1)S(1)}, bf16[16,16,1600]{2,1,0:T(8,128)(2,1)S(1)}, u32[]{:S(2)}, u32[]{:S(2)}) collective-permute-start(bf16[16,16,1600]{2,1,0:T(8,128)(2,1)S(1)} %shard_map.115.near_ref), channel_id=1, source_target_pairs={{0,1},{1,0},{2,3},{3,2},{4,5},{5,4},{6,7},{7,6},{8,9},{9,8},{10,11... | collective-permute-start | bytes 2457608 | tf_op jit(solution)/shard_map/ppermute | solution.py:113
  30.1 7.5 %collective-permute-start.5 = (bf16[2,200,256]{2,1,0:T(8,128)(2,1)S(1)}, bf16[2,200,256]{2,1,0:T(8,128)(2,1)S(1)}, u32[]{:S(2)}, u32[]{:S(2)}) collective-permute-start(bf16[2,200,256]{2,1,0:T(8,128)(2,1)S(1)} %get-tuple-element.29), channel_id=1, source_target_pairs={{0,4},{4,0},{8,12},{12,8},{16,20},{20,16},{24,28},{28,24},{1,5},{5... | collective-permute-start | bytes 614408 | tf_op jit(solution)/shard_map/ppermute | solution.py:113
  31.9 14.9 %collective-permute-start.6 = (bf16[2,200,256]{2,1,0:T(8,128)(2,1)S(1)}, bf16[2,200,256]{2,1,0:T(8,128)(2,1)S(1)}, u32[]{:S(2)}, u32[]{:S(2)}) collective-permute-start(bf16[2,200,256]{2,1,0:T(8,128)(2,1)S(1)} %get-tuple-element.30), channel_id=1, source_target_pairs={{0,8},{4,12},{8,0},{12,4},{16,24},{20,28},{24,16},{28,20},{1,9},{5... | collective-permute-start | bytes 614408 | tf_op jit(solution)/shard_map/ppermute | solution.py:113
  33.0 21.0 %collective-permute-start.7 = (bf16[2,200,256]{2,1,0:T(8,128)(2,1)}, bf16[2,200,256]{2,1,0:T(8,128)(2,1)}, u32[]{:S(2)}, u32[]{:S(2)}) collective-permute-start(bf16[2,200,256]{2,1,0:T(8,128)(2,1)} %get-tuple-element.31), channel_id=1, source_target_pairs={{0,12},{4,8},{8,4},{12,0},{16,28},{20,24},{24,20},{28,16},{1,13},{... | collective-permute-start | bytes 614408 | tf_op jit(solution)/shard_map/ppermute | solution.py:113
  33.6 20.4 %collective-permute-start.8 = (bf16[2,200,256]{2,1,0:T(8,128)(2,1)}, bf16[2,200,256]{2,1,0:T(8,128)(2,1)}, u32[]{:S(2)}, u32[]{:S(2)}) collective-permute-start(bf16[2,200,256]{2,1,0:T(8,128)(2,1)} %get-tuple-element.32), channel_id=1, source_target_pairs={{0,16},{4,20},{8,24},{12,28},{16,0},{20,4},{24,8},{28,12},{1,17},{... | collective-permute-start | bytes 614408 | tf_op jit(solution)/shard_map/ppermute | solution.py:113
  37.6 0.7 copy-start
  38.3 27.6 %collective-permute-start.9 = (bf16[2,200,256]{2,1,0:T(8,128)(2,1)}, bf16[2,200,256]{2,1,0:T(8,128)(2,1)}, u32[]{:S(2)}, u32[]{:S(2)}) collective-permute-start(bf16[2,200,256]{2,1,0:T(8,128)(2,1)} %get-tuple-element.33), channel_id=1, source_target_pairs={{0,20},{4,16},{8,28},{12,24},{16,4},{20,0},{24,12},{28,8},{1,21},{... | collective-permute-start | bytes 614408 | tf_op jit(solution)/shard_map/ppermute | solution.py:113
  46.8 0.7 copy-start.2
  47.5 18.4 %collective-permute-start.10 = (bf16[2,200,256]{2,1,0:T(8,128)(2,1)}, bf16[2,200,256]{2,1,0:T(8,128)(2,1)}, u32[]{:S(2)}, u32[]{:S(2)}) collective-permute-start(bf16[2,200,256]{2,1,0:T(8,128)(2,1)} %get-tuple-element.34), channel_id=1, source_target_pairs={{0,24},{4,28},{8,16},{12,20},{16,8},{20,12},{24,0},{28,4},{1,25},{... | collective-permute-start | bytes 614408 | tf_op jit(solution)/shard_map/ppermute | solution.py:113
  49.0 16.9 %collective-permute-start.11 = (bf16[2,200,256]{2,1,0:T(8,128)(2,1)}, bf16[2,200,256]{2,1,0:T(8,128)(2,1)}, u32[]{:S(2)}, u32[]{:S(2)}) collective-permute-start(bf16[2,200,256]{2,1,0:T(8,128)(2,1)} %get-tuple-element.35), channel_id=1, source_target_pairs={{0,28},{4,24},{8,20},{12,16},{16,12},{20,8},{24,4},{28,0},{1,29},{... | collective-permute-start | bytes 614408 | tf_op jit(solution)/shard_map/ppermute | solution.py:113
  65.9 0.9 copy-start.1
  66.8 0.9 copy-start.3
  71.8 2.4 %collective-permute-start.12 = (bf16[2,16,8,1600]{3,2,1,0:T(8,128)(2,1)S(1)}, bf16[2,16,8,1600]{3,2,1,0:T(8,128)(2,1)S(1)}, u32[]{:S(2)}, u32[]{:S(2)}) collective-permute-start(bf16[2,16,8,1600]{3,2,1,0:T(8,128)(2,1)S(1)} %get-tuple-element.40), channel_id=1, source_target_pairs={{0,1},{1,0},{2,3},{3,2},{4,5},{5,4},{6,7},{7,6},{8,9},{9,8},{10,11... | collective-permute-start | bytes 2457608 | tf_op jit(solution)/shard_map/ppermute | solution.py:113
  74.4 11.9 %collective-permute-start.13 = (bf16[2,8,8,1600]{3,2,1,0:T(8,128)(2,1)S(1)}, bf16[2,8,8,1600]{3,2,1,0:T(8,128)(2,1)S(1)}, u32[]{:S(2)}, u32[]{:S(2)}) collective-permute-start(bf16[2,8,8,1600]{3,2,1,0:T(8,128)(2,1)S(1)} %get-tuple-element.42), channel_id=1, source_target_pairs={{0,2},{1,3},{2,0},{3,1},{4,6},{5,7},{6,4},{7,5},{8,10},{9,11},{10,... | collective-permute-start | bytes 1228808 | tf_op jit(solution)/shard_map/ppermute | solution.py:113
  76.2 23.1 %collective-permute-start.14 = (bf16[2,256,256]{2,1,0:T(8,128)(2,1)S(1)}, bf16[2,256,256]{2,1,0:T(8,128)(2,1)S(1)}, u32[]{:S(2)}, u32[]{:S(2)}) collective-permute-start(bf16[2,256,256]{2,1,0:T(8,128)(2,1)S(1)} %get-tuple-element.36.both_ref.first_ref), channel_id=1, source_target_pairs={{0,16},{4,20},{8,24},{12,28},{16,0},{20,4},{24,8},{28,12},{1,17},{... | collective-permute-start | bytes 786440 | tf_op jit(solution)/shard_map/ppermute | solution.py:113
  87.2 43.9 %all-to-all-start = ((bf16[8,16,1600]{2,1,0:T(8,128)(2,1)}), bf16[8,16,1600]{2,1,0:T(8,128)(2,1)S(1)}, u32[]{:S(2)}, u32[]{:S(2)}) async-start(bf16[8,16,1600]{2,1,0:T(8,128)(2,1)} %shard_map.121), calls=%async_computation | async-start | bytes 851968 | tf_op jit(solution)/shard_map/all_to_all | solution.py:512
  99.4 13.5 %collective-permute-start.15 = (bf16[2,256,256]{2,1,0:T(8,128)(2,1)S(1)}, bf16[2,256,256]{2,1,0:T(8,128)(2,1)S(1)}, u32[]{:S(2)}, u32[]{:S(2)}) collective-permute-start(bf16[2,256,256]{2,1,0:T(8,128)(2,1)S(1)} %get-tuple-element.46.block_ref), channel_id=1, source_target_pairs={{0,4},{4,0},{8,12},{12,8},{16,20},{20,16},{24,28},{28,24},{1,5},{5... | collective-permute-start | bytes 786440 | tf_op jit(solution)/shard_map/ppermute | solution.py:113
  101.5 14.1 %collective-permute-start.18 = (bf16[2,256,256]{2,1,0:T(8,128)(2,1)S(1)}, bf16[2,256,256]{2,1,0:T(8,128)(2,1)S(1)}, u32[]{:S(2)}, u32[]{:S(2)}) collective-permute-start(bf16[2,256,256]{2,1,0:T(8,128)(2,1)S(1)} %get-tuple-element.48.block_ref), channel_id=1, source_target_pairs={{0,8},{4,12},{8,0},{12,4},{16,24},{20,28},{24,16},{28,20},{1,9},{5... | collective-permute-start | bytes 786440 | tf_op jit(solution)/shard_map/ppermute | solution.py:113
  102.9 20.8 %collective-permute-start.17 = (bf16[2,256,256]{2,1,0:T(8,128)(2,1)S(1)}, bf16[2,256,256]{2,1,0:T(8,128)(2,1)S(1)}, u32[]{:S(2)}, u32[]{:S(2)}) collective-permute-start(bf16[2,256,256]{2,1,0:T(8,128)(2,1)S(1)} %get-tuple-element.46.block_ref), channel_id=1, source_target_pairs={{0,8},{4,12},{8,0},{12,4},{16,24},{20,28},{24,16},{28,20},{1,9},{5... | collective-permute-start | bytes 786440 | tf_op jit(solution)/shard_map/ppermute | solution.py:113
  103.5 22.1 %collective-permute-start.20 = (bf16[2,256,256]{2,1,0:T(8,128)(2,1)S(1)}, bf16[2,256,256]{2,1,0:T(8,128)(2,1)S(1)}, u32[]{:S(2)}, u32[]{:S(2)}) collective-permute-start(bf16[2,256,256]{2,1,0:T(8,128)(2,1)S(1)} %get-tuple-element.48.block_ref), channel_id=1, source_target_pairs={{0,4},{4,0},{8,12},{12,8},{16,20},{20,16},{24,28},{28,24},{1,5},{5... | collective-permute-start | bytes 786440 | tf_op jit(solution)/shard_map/ppermute | solution.py:113
  112.9 14.5 %collective-permute-start.16 = (bf16[2,256,256]{2,1,0:T(8,128)(2,1)S(1)}, bf16[2,256,256]{2,1,0:T(8,128)(2,1)S(1)}, u32[]{:S(2)}, u32[]{:S(2)}) collective-permute-start(bf16[2,256,256]{2,1,0:T(8,128)(2,1)S(1)} %collective-permute-done.15.block_ref), channel_id=1, source_target_pairs={{0,8},{4,12},{8,0},{12,4},{16,24},{20,28},{24,16},{28,20},{1,9},{5... | collective-permute-start | bytes 786440 | tf_op jit(solution)/shard_map/ppermute | solution.py:113
  115.6 13.7 %collective-permute-start.19 = (bf16[2,256,256]{2,1,0:T(8,128)(2,1)S(1)}, bf16[2,256,256]{2,1,0:T(8,128)(2,1)S(1)}, u32[]{:S(2)}, u32[]{:S(2)}) collective-permute-start(bf16[2,256,256]{2,1,0:T(8,128)(2,1)S(1)} %collective-permute-done.18.block_ref), channel_id=1, source_target_pairs={{0,4},{4,0},{8,12},{12,8},{16,20},{20,16},{24,28},{28,24},{1,5},{5... | collective-permute-start | bytes 786440 | tf_op jit(solution)/shard_map/ppermute | solution.py:113
  129.2 1.9 %copy-start.4 = (bf16[8,1600]{1,0:T(8,128)(2,1)S(1)}, bf16[8,1600]{1,0:T(8,128)(2,1)}, u32[]{:S(2)}) copy-start(bf16[8,1600]{1,0:T(8,128)(2,1)} %patch_ref.1) | copy-start | bytes 76804
  129.2 1.9 %copy-start.5 = (bf16[16,1600]{1,0:T(8,128)(2,1)S(1)}, bf16[16,1600]{1,0:T(8,128)(2,1)}, u32[]{:S(2)}) copy-start(bf16[16,1600]{1,0:T(8,128)(2,1)} %text_ref.1) | copy-start | bytes 153604
  129.2 1.9 %copy-start.6 = (s32[1,4]{1,0:T(1,128)S(1)}, s32[1,4]{1,0:T(1,128)}, u32[]{:S(2)}) copy-start(s32[1,4]{1,0:T(1,128)} %count_ref.1) | copy-start | bytes 52
  129.3 1.9 %copy-start.7 = (s32[1,8]{1,0:T(1,128)S(1)}, s32[1,8]{1,0:T(1,128)}, u32[]{:S(2)}) copy-start(s32[1,8]{1,0:T(1,128)} %place_ref.1) | copy-start | bytes 100

commit v5 on v4

--- a/solution.py
+++ b/solution.py
@@ -315,25 +315,34 @@
         out_ref[d] = jnp.concatenate([total[0, d], total[1, d]], axis=0).astype(jnp.bfloat16)
 
 
-def weight_grad_kernel(distances, block_ref, rows_ref, *refs):
-    out_at, result_ref, sems = refs[-3:]
-    count, features, units = result_ref.shape
-    piece = features // sems.shape[1]
+def weight_grad_kernel(
+    hidden_distances, pre_distances, hidden_ref, pre_ref, grad_ref, normed_ref, *refs
+):
+    project_at, expand_at, result_ref, sems = refs[-4:]
+    _, count, features, units = result_ref.shape
+    pieces = sems.shape[2]
+    piece = features // pieces
     copies = []
     for i in range(count):
-        result_ref[i] = jnp.dot(
-            rows_ref[...], block_ref[i], preferred_element_type=jnp.float32
-        ).astype(jnp.bfloat16)
-        source = lax.axis_index("dp") ^ distances[i]
-        columns = pl.ds(pl.multiple_of(source * units, 128), units)
-        for k in range(sems.shape[1]):
-            at = pl.ds(k * piece, piece)
-            copies.append(
-                pltpu.make_async_copy(
-                    result_ref.at[i, at, :], out_at.at[at, columns], sems.at[i, k]
+        for k, (block_ref, rows_ref, out_at, distances) in enumerate(
+            (
+                (pre_ref, normed_ref, expand_at, pre_distances),
+                (hidden_ref, grad_ref, project_at, hidden_distances),
+            )
+        ):
+            result_ref[k, i] = jnp.dot(
+                rows_ref[...], block_ref[i], preferred_element_type=jnp.float32
+            ).astype(jnp.bfloat16)
+            source = lax.axis_index("dp") ^ distances[i]
+            columns = pl.ds(pl.multiple_of(source * units, 128), units)
+            for j in range(pieces):
+                at = pl.ds(j * piece, piece)
+                copies.append(
+                    pltpu.make_async_copy(
+                        result_ref.at[k, i, at, :], out_at.at[at, columns], sems.at[k, i, j]
+                    )
                 )
-            )
-            copies[-1].start()
+                copies[-1].start()
     for copy in copies:
         copy.wait()
 
@@ -371,28 +380,30 @@
     ).astype(jnp.bfloat16)
 
 
-def weight_grads(blocks, distances, values, width, before=()):
-    count, rows, units = blocks.shape
-    features = values.shape[0]
-    pieces = 4 if features % 64 == 0 else 1
+def weight_grads(
+    hidden, hidden_distances, pre, pre_distances, grad_turned, normed_turned, width, before
+):
+    count, rows, units = hidden.shape
+    features = grad_turned.shape[0]
+    pieces = 2 if features % 32 == 0 else 1
     anywhere = pl.BlockSpec(memory_space=pl.ANY)
     return pl.pallas_call(
-        functools.partial(weight_grad_kernel, distances),
-        in_specs=[VMEM_SPEC] * 2 + [anywhere] * len(before),
-        out_specs=anywhere,
-        out_shape=jax.ShapeDtypeStruct((features, width), jnp.bfloat16),
+        functools.partial(weight_grad_kernel, hidden_distances, pre_distances),
+        in_specs=[VMEM_SPEC] * 4 + [anywhere] * len(before),
+        out_specs=[anywhere] * 2,
+        out_shape=[jax.ShapeDtypeStruct((features, width), jnp.bfloat16)] * 2,
         scratch_shapes=[
-            pltpu.VMEM((count, features, units), jnp.bfloat16),
-            pltpu.SemaphoreType.DMA((count, pieces)),
+            pltpu.VMEM((2, count, features, units), jnp.bfloat16),
+            pltpu.SemaphoreType.DMA((2, count, pieces)),
         ],
-        input_output_aliases={2: 0} if before else {},
+        input_output_aliases={4: 0, 5: 1} if before else {},
         compiler_params=pltpu.CompilerParams(vmem_limit_bytes=12 << 20),
         cost_estimate=pl.CostEstimate(
-            flops=2 * count * rows * features * units,
-            bytes_accessed=2 * count * units * features + 2 * rows * features,
+            flops=4 * count * rows * features * units,
+            bytes_accessed=4 * count * units * features + 4 * rows * features,
             transcendentals=0,
         ),
-    )(blocks, values, *before)
+    )(hidden, pre, grad_turned, normed_turned, *before)
 
 
 def call(kernel, out_shape, smem, vmem, scratch=()):
@@ -513,18 +524,20 @@
 
     far_both = swap(both, "dp", dp_steps[0])
     pairs = join_pairs(both, far_both)
-    grads = []
-    for pair, values, steps in (
-        (pairs[0], grad_turned, dp_steps[1:]), (pairs[1], normed_turned, dp_steps[:0:-1])
-    ):
+    gathered = []
+    for pair, steps in ((pairs[0], dp_steps[1:]), (pairs[1], dp_steps[:0:-1])):
         held_pairs = {0: pair}
         for step in steps:
             for mask, array in list(held_pairs.items()):
                 held_pairs[mask ^ step] = swap(array, "dp", step)
-        grad = ()
-        for mask, array in held_pairs.items():
-            grad = (weight_grads(array, (mask, mask ^ dp_steps[0]), values, width, grad),)
-        grads += grad
+        gathered.append(held_pairs.items())
+    grads = ()
+    for (hidden_mask, hidden), (pre_mask, pre) in zip(*gathered):
+        far = dp_steps[0]
+        grads = weight_grads(
+            hidden, (hidden_mask, hidden_mask ^ far), pre, (pre_mask, pre_mask ^ far),
+            grad_turned, normed_turned, width, grads,
+        )
     project_grad, expand_grad = grads
     embedded, grad_rows = call(
         functools.partial(finish_kernel, capacity),

time: 133 us -> 130 us (0.977)
  Pallas kernels: 27.1 us -> 22 us
  waiting for transfers between devices: 47 us -> 49.2 us
    pallas_call x8 -> x4, Pallas kernels: 14.5 us -> 9.43 us  [weight_grads(): pl.pallas_call(functools.partial(weight_grad_kernel, hidden_distances, pr...]
    ppermute x21, waiting for transfers between devices: 47 us -> 49.2 us  [swap(): return lax.ppermute(array, axis, [(i, i ^ step) for i in range(size)])]
  transfers between devices with their start and end apart: 22 -> 22, of which waited for: 11 -> 10; matrix products, arithmetic and copies ran while one was open for 1% -> 1% of each run, Pallas kernels for 15% -> 12%
where the time goes in v5:
time: 130 us; the launch traced here: 129 us
  starting transfers between devices  53 us (41%)
  waiting for transfers between devices  49.2 us (38%)
  Pallas kernels  22 us (17%)
  local copies, waits for them, and re-layouts  3.96 us (3%)
    ppermute x21, waiting for transfers between devices, swap(): return lax.ppermute(array, axis, [(i, i ^ step) for i in range(size)])  49.2 us
    ppermute x21, starting transfers between devices, swap(): return lax.ppermute(array, axis, [(i, i ^ step) for i in range(size)])  40.8 us
    all_to_all x1, starting transfers between devices, move_rows_plan(): tail = lax.all_to_all(tail, 'dp', split_axis=0, concat_axis=0, tiled=True)  12.2 us
    pallas_call x4, Pallas kernels, weight_grads(): pl.pallas_call(functools.partial(weight_grad_kernel, hidden_distances, pr...  9.43 us
    pallas_call x11, Pallas kernels, call(): pl.pallas_call(kernel, out_shape=out_shape, in_specs=[SMEM_SPEC] * len(sm...  6.54 us
    unnamed x16, local copies, waits for them, and re-layouts  3.25 us
  transfers between devices with their start and end apart: 22, of which 10 were waited for; matrix products, arithmetic and copies ran while one was open for 1% of the time, Pallas kernels for 12%

profile of v5, /device:TPU:0, one launch (start us, length us, event | category | flops | bytes accessed | tf_op | source)
XLA Modules:
  0.0 129.2 jit_solution(5887560057174367426)
XLA Ops:
  0.6 1.0 shard_map.111.first_ref
  1.6 4.1 %collective-permute-start = (bf16[1,16,1600]{2,1,0:T(8,128)(2,1)S(1)}, bf16[1,16,1600]{2,1,0:T(8,128)(2,1)S(1)}, u32[]{:S(2)}, u32[]{:S(2)}) collective-permute-start(bf16[1,16,1600]{2,1,0:T(8,128)(2,1)S(1)} %shard_map.111.first_ref), channel_id=1, source_target_pairs={{0,16},{4,20},{8,24},{12,28},{16,0},{20,4},{24,8},{28,12},{1,17},{... | collective-permute-start | bytes 153608 | tf_op jit(solution)/shard_map/ppermute | solution.py:113
  5.8 2.7 %collective-permute-done.second_ref = bf16[1,16,1600]{2,1,0:T(8,128)(2,1)S(1)} collective-permute-done((bf16[1,16,1600]{2,1,0:T(8,128)(2,1)S(1)}, bf16[1,16,1600]{2,1,0:T(8,128)(2,1)S(1)}, u32[]{:S(2)}, u32[]{:S(2)}) %collective-permute-start) | collective-permute-done | bytes 51232 | tf_op jit(solution)/shard_map/ppermute | solution.py:113
  8.5 1.4 %collective-permute-start.1 = (bf16[2,16,1600]{2,1,0:T(8,128)(2,1)S(1)}, bf16[2,16,1600]{2,1,0:T(8,128)(2,1)S(1)}, u32[]{:S(2)}, u32[]{:S(2)}) collective-permute-start(bf16[2,16,1600]{2,1,0:T(8,128)(2,1)S(1)} %shard_map.112.first_ref), channel_id=1, source_target_pairs={{0,8},{4,12},{8,0},{12,4},{16,24},{20,28},{24,16},{28,20},{1,9},{5... | collective-permute-start | bytes 307208 | tf_op jit(solution)/shard_map/ppermute | solution.py:113
  9.9 3.4 %collective-permute-done.1.second_ref = bf16[2,16,1600]{2,1,0:T(8,128)(2,1)S(1)} collective-permute-done((bf16[2,16,1600]{2,1,0:T(8,128)(2,1)S(1)}, bf16[2,16,1600]{2,1,0:T(8,128)(2,1)S(1)}, u32[]{:S(2)}, u32[]{:S(2)}) %collective-permute-start.1) | collective-permute-done | bytes 102432 | tf_op jit(solution)/shard_map/ppermute | solution.py:113
  13.3 1.8 %collective-permute-start.2 = (bf16[4,16,1600]{2,1,0:T(8,128)(2,1)S(1)}, bf16[4,16,1600]{2,1,0:T(8,128)(2,1)S(1)}, u32[]{:S(2)}, u32[]{:S(2)}) collective-permute-start(bf16[4,16,1600]{2,1,0:T(8,128)(2,1)S(1)} %shard_map.113.first_ref), channel_id=1, source_target_pairs={{0,4},{4,0},{8,12},{12,8},{16,20},{20,16},{24,28},{28,24},{1,5},{5... | collective-permute-start | bytes 614408 | tf_op jit(solution)/shard_map/ppermute | solution.py:113
  15.0 4.1 %collective-permute-done.2.second_ref = bf16[4,16,1600]{2,1,0:T(8,128)(2,1)S(1)} collective-permute-done((bf16[4,16,1600]{2,1,0:T(8,128)(2,1)S(1)}, bf16[4,16,1600]{2,1,0:T(8,128)(2,1)S(1)}, u32[]{:S(2)}, u32[]{:S(2)}) %collective-permute-start.2) | collective-permute-done | bytes 204832 | tf_op jit(solution)/shard_map/ppermute | solution.py:113
  19.2 1.8 %collective-permute-start.3 = (bf16[8,16,1600]{2,1,0:T(8,128)(2,1)S(1)}, bf16[8,16,1600]{2,1,0:T(8,128)(2,1)S(1)}, u32[]{:S(2)}, u32[]{:S(2)}) collective-permute-start(bf16[8,16,1600]{2,1,0:T(8,128)(2,1)S(1)} %shard_map.114.first_ref), channel_id=1, source_target_pairs={{0,2},{1,3},{2,0},{3,1},{4,6},{5,7},{6,4},{7,5},{8,10},{9,11},{10,... | collective-permute-start | bytes 1228808 | tf_op jit(solution)/shard_map/ppermute | solution.py:113
  21.0 6.4 %collective-permute-done.3.second_ref = bf16[8,16,1600]{2,1,0:T(8,128)(2,1)S(1)} collective-permute-done((bf16[8,16,1600]{2,1,0:T(8,128)(2,1)S(1)}, bf16[8,16,1600]{2,1,0:T(8,128)(2,1)S(1)}, u32[]{:S(2)}, u32[]{:S(2)}) %collective-permute-start.3) | collective-permute-done | bytes 409632 | tf_op jit(solution)/shard_map/ppermute | solution.py:113
  27.5 2.5 %shard_map.117 = (bf16[2,200,256]{2,1,0:T(8,128)(2,1)S(1)}, bf16[2,200,256]{2,1,0:T(8,128)(2,1)S(1)}, bf16[2,200,256]{2,1,0:T(8,128)(2,1)}, bf16[2,200,256]{2,1,...) custom-call(bf16[200,2048]{1,0:T(8,128)(2,1)} %expand_at.3, ...), custom_call_target="tpu_custom_call" | custom-call | tf_op jit(solution)/shard_map/pallas_call | solution.py:474
  30.1 1.8 %collective-permute-start.5 = (bf16[2,200,256]{2,1,0:T(8,128)(2,1)S(1)}, bf16[2,200,256]{2,1,0:T(8,128)(2,1)S(1)}, u32[]{:S(2)}, u32[]{:S(2)}) collective-permute-start(bf16[2,200,256]{2,1,0:T(8,128)(2,1)S(1)} %get-tuple-element.37), channel_id=1, source_target_pairs={{0,4},{4,0},{8,12},{12,8},{16,20},{20,16},{24,28},{28,24},{1,5},{5... | collective-permute-start | bytes 614408 | tf_op jit(solution)/shard_map/ppermute | solution.py:113
  31.9 1.1 collective-permute-start.6
  33.0 0.6 collective-permute-start.7
  33.6 2.6 %collective-permute-start.8 = (bf16[2,200,256]{2,1,0:T(8,128)(2,1)}, bf16[2,200,256]{2,1,0:T(8,128)(2,1)}, u32[]{:S(2)}, u32[]{:S(2)}) collective-permute-start(bf16[2,200,256]{2,1,0:T(8,128)(2,1)} %get-tuple-element.40), channel_id=1, source_target_pairs={{0,16},{4,20},{8,24},{12,28},{16,0},{20,4},{24,8},{28,12},{1,17},{... | collective-permute-start | bytes 614408 | tf_op jit(solution)/shard_map/ppermute | solution.py:113
  36.3 1.3 %collective-permute-done.5.refs_0_ = bf16[2,200,256]{2,1,0:T(8,128)(2,1)S(1)} collective-permute-done((bf16[2,200,256]{2,1,0:T(8,128)(2,1)S(1)}, bf16[2,200,256]{2,1,0:T(8,128)(2,1)S(1)}, u32[]{:S(2)}, u32[]{:S(2)}) %collective-permute-start.5) | collective-permute-done | bytes 204832 | tf_op jit(solution)/shard_map/ppermute | solution.py:113
  37.6 0.7 copy-done
  38.3 3.6 %collective-permute-start.9 = (bf16[2,200,256]{2,1,0:T(8,128)(2,1)}, bf16[2,200,256]{2,1,0:T(8,128)(2,1)}, u32[]{:S(2)}, u32[]{:S(2)}) collective-permute-start(bf16[2,200,256]{2,1,0:T(8,128)(2,1)} %get-tuple-element.41), channel_id=1, source_target_pairs={{0,20},{4,16},{8,28},{12,24},{16,4},{20,0},{24,12},{28,8},{1,21},{... | collective-permute-start | bytes 614408 | tf_op jit(solution)/shard_map/ppermute | solution.py:113
  41.9 4.9 %collective-permute-done.6.refs_1_ = bf16[2,200,256]{2,1,0:T(8,128)(2,1)S(1)} collective-permute-done((bf16[2,200,256]{2,1,0:T(8,128)(2,1)S(1)}, bf16[2,200,256]{2,1,0:T(8,128)(2,1)S(1)}, u32[]{:S(2)}, u32[]{:S(2)}) %collective-permute-start.6) | collective-permute-done | bytes 204832 | tf_op jit(solution)/shard_map/ppermute | solution.py:113
  46.8 0.7 copy-done.2
  47.4 1.5 %collective-permute-start.10 = (bf16[2,200,256]{2,1,0:T(8,128)(2,1)}, bf16[2,200,256]{2,1,0:T(8,128)(2,1)}, u32[]{:S(2)}, u32[]{:S(2)}) collective-permute-start(bf16[2,200,256]{2,1,0:T(8,128)(2,1)} %get-tuple-element.42), channel_id=1, source_target_pairs={{0,24},{4,28},{8,16},{12,20},{16,8},{20,12},{24,0},{28,4},{1,25},{... | collective-permute-start | bytes 614408 | tf_op jit(solution)/shard_map/ppermute | solution.py:113
  49.0 2.3 %collective-permute-start.11 = (bf16[2,200,256]{2,1,0:T(8,128)(2,1)}, bf16[2,200,256]{2,1,0:T(8,128)(2,1)}, u32[]{:S(2)}, u32[]{:S(2)}) collective-permute-start(bf16[2,200,256]{2,1,0:T(8,128)(2,1)} %get-tuple-element.43), channel_id=1, source_target_pairs={{0,28},{4,24},{8,20},{12,16},{16,12},{20,8},{24,4},{28,0},{1,29},{... | collective-permute-start | bytes 614408 | tf_op jit(solution)/shard_map/ppermute | solution.py:113
  51.2 0.7 reshape.11.gain_ref
  52.0 2.0 %shard_map.116 = (bf16[256,1600]{1,0:T(8,128)(2,1)S(1)}, bf16[256,1600]{1,0:T(8,128)(2,1)S(1)}, f32[16,1600]{1,0:T(8,128)S(1)}) custom-call(s32[2]{0:T(128)S(1)} %pad_add_fusion.me_ref, bf16[16,16,1600]{2,1,0:T(8,128)(2,1)S(1)} %shard_map.115.near_ref, bf16[16,16,1600]{2,1,0:T(8,128)(2,1)S(1)} %collective-permute-done.4.far_ref, f32[1,1600]{1,0:T(1,128)S(1)} %reshape.11.gain_ref), custom_call_target="tpu_custom_call" | custom-call | tf_op jit(solution)/shard_map/pallas_call | solution.py:411
  54.0 11.9 %collective-permute-done.9.refs_4_ = bf16[2,200,256]{2,1,0:T(8,128)(2,1)} collective-permute-done((bf16[2,200,256]{2,1,0:T(8,128)(2,1)}, bf16[2,200,256]{2,1,0:T(8,128)(2,1)}, u32[]{:S(2)}, u32[]{:S(2)}) %collective-permute-start.9) | collective-permute-done | bytes 204832 | tf_op jit(solution)/shard_map/ppermute | solution.py:113
  65.9 0.9 copy-done.1
  66.9 0.9 copy-done.3
  67.8 2.5 %shard_map.118 = (bf16[2,256,256]{2,1,0:T(8,128)(2,1)S(1)}, bf16[1600,256]{1,0:T(8,128)(2,1)S(1)}, bf16[1600,256]{1,0:T(8,128)(2,1)S(1)}) custom-call(bf16[256,1600]{1,0:T(8,128)(2,1)S(1)} %get-tuple-element.35.normed_ref, bf16[256,1600]{1,0:T(8,128)(2,1)S(1)} %get-tuple-element.36.grad_ref, bf16[200,2048]{1,0:T(8,128)(2,1)} %expand_at.3, ...), custom_call_target="tpu_custom_call" | custom-call | tf_op jit(solution)/shard_map/pallas_call | solution.py:500
  70.3 1.4 %shard_map.119 = (f32[2,16,8,1600]{3,2,1,0:T(8,128)S(1)}, bf16[2,16,8,1600]{3,2,1,0:T(8,128)(2,1)S(1)}) custom-call(s32[2]{0:T(128)S(1)} %pad_add_fusion.me_ref, bf16[2,256,256]{2,1,0:T(8,128)(2,1)S(1)} %get-tuple-element.44.both_ref.first_ref, bf16[1600,256]{1,0:T(8,128)(2,1)S(1)} %get-tuple-element.45.expand_ref, ...), custom_call_target="tpu_custom_call" | custom-call | tf_op jit(solution)/shard_map/pallas_call | solution.py:411
  71.8 2.4 %collective-permute-done.12.got_ref = bf16[2,16,8,1600]{3,2,1,0:T(8,128)(2,1)S(1)} collective-permute-done((bf16[2,16,8,1600]{3,2,1,0:T(8,128)(2,1)S(1)}, bf16[2,16,8,1600]{3,2,1,0:T(8,128)(2,1)S(1)}, u32[]{:S(2)}, u32[]{:S(2)}) %collective-permute-start.12) | collective-permute-done | bytes 819232 | tf_op jit(solution)/shard_map/ppermute | solution.py:113
  74.2 0.2 shard_map.120
  74.4 1.8 %collective-permute-start.13 = (bf16[2,8,8,1600]{3,2,1,0:T(8,128)(2,1)S(1)}, bf16[2,8,8,1600]{3,2,1,0:T(8,128)(2,1)S(1)}, u32[]{:S(2)}, u32[]{:S(2)}) collective-permute-start(bf16[2,8,8,1600]{3,2,1,0:T(8,128)(2,1)S(1)} %get-tuple-element.50), channel_id=1, source_target_pairs={{0,2},{1,3},{2,0},{3,1},{4,6},{5,7},{6,4},{7,5},{8,10},{9,11},{10,... | collective-permute-start | bytes 1228808 | tf_op jit(solution)/shard_map/ppermute | solution.py:113
  76.2 10.0 %collective-permute-start.14 = (bf16[2,256,256]{2,1,0:T(8,128)(2,1)S(1)}, bf16[2,256,256]{2,1,0:T(8,128)(2,1)S(1)}, u32[]{:S(2)}, u32[]{:S(2)}) collective-permute-start(bf16[2,256,256]{2,1,0:T(8,128)(2,1)S(1)} %get-tuple-element.44.both_ref.first_ref), channel_id=1, source_target_pairs={{0,16},{4,20},{8,24},{12,28},{16,0},{20,4},{24,8},{28,12},{1,17},{... | collective-permute-start | bytes 786440 | tf_op jit(solution)/shard_map/ppermute | solution.py:113
  86.2 0.2 collective-permute-done.13.got_ref
  86.3 0.8 shard_map.121
  87.2 12.2 %all-to-all-start = ((bf16[8,16,1600]{2,1,0:T(8,128)(2,1)}), bf16[8,16,1600]{2,1,0:T(8,128)(2,1)S(1)}, u32[]{:S(2)}, u32[]{:S(2)}) async-start(bf16[8,16,1600]{2,1,0:T(8,128)(2,1)} %shard_map.121), calls=%async_computation | async-start | bytes 851968 | tf_op jit(solution)/shard_map/all_to_all | solution.py:523
  99.4 2.1 %collective-permute-start.15 = (bf16[2,256,256]{2,1,0:T(8,128)(2,1)S(1)}, bf16[2,256,256]{2,1,0:T(8,128)(2,1)S(1)}, u32[]{:S(2)}, u32[]{:S(2)}) collective-permute-start(bf16[2,256,256]{2,1,0:T(8,128)(2,1)S(1)} %get-tuple-element.54.hidden_ref), channel_id=1, source_target_pairs={{0,8},{4,12},{8,0},{12,4},{16,24},{20,28},{24,16},{28,20},{1,9},{5... | collective-permute-start | bytes 786440 | tf_op jit(solution)/shard_map/ppermute | solution.py:113
  101.5 1.5 %collective-permute-start.17 = (bf16[2,256,256]{2,1,0:T(8,128)(2,1)S(1)}, bf16[2,256,256]{2,1,0:T(8,128)(2,1)S(1)}, u32[]{:S(2)}, u32[]{:S(2)}) collective-permute-start(bf16[2,256,256]{2,1,0:T(8,128)(2,1)S(1)} %get-tuple-element.55.pre_ref), channel_id=1, source_target_pairs={{0,4},{4,0},{8,12},{12,8},{16,20},{20,16},{24,28},{28,24},{1,5},{5... | collective-permute-start | bytes 786440 | tf_op jit(solution)/shard_map/ppermute | solution.py:113
  102.9 0.6 collective-permute-start.19
  103.5 0.1 collective-permute-start.20
  103.6 12.0 %collective-permute-done.15.hidden_ref = bf16[2,256,256]{2,1,0:T(8,128)(2,1)S(1)} collective-permute-done((bf16[2,256,256]{2,1,0:T(8,128)(2,1)S(1)}, bf16[2,256,256]{2,1,0:T(8,128)(2,1)S(1)}, u32[]{:S(2)}, u32[]{:S(2)}) %collective-permute-start.15) | collective-permute-done | bytes 262176 | tf_op jit(solution)/shard_map/ppermute | solution.py:113
  115.6 0.9 collective-permute-start.16
  116.5 1.1 collective-permute-start.18
  117.6 0.5 shard_map.124
  118.1 2.4 %shard_map.125 = (bf16[1600,2048]{1,0:T(8,128)(2,1)}, bf16[1600,2048]{1,0:T(8,128)(2,1)}) custom-call(bf16[2,256,256]{2,1,0:T(8,128)(2,1)S(1)} %get-tuple-element.54.hidden_ref, bf16[2,256,256]{2,1,0:T(8,128)(2,1)S(1)} %get-tuple-element.55.pre_ref, bf16[1600,256]{1,0:T(8,128)(2,1)S(1)} %get-tuple-element.56.grad_ref, ...), custom_call_target="tpu_custom_call" | custom-call | flops 838860800 | bytes 4915200 | tf_op jit(solution)/shard_map/pallas_call | solution.py:390
  120.5 2.4 %shard_map.126 = (bf16[1600,2048]{1,0:T(8,128)(2,1)}, bf16[1600,2048]{1,0:T(8,128)(2,1)}) custom-call(bf16[2,256,256]{2,1,0:T(8,128)(2,1)S(1)} %collective-permute-done.15.hidden_ref, bf16[2,256,256]{2,1,0:T(8,128)(2,1)S(1)} %collective-permute-done.17.pre_ref, ...), custom_call_target="tpu_custom_call", output_to_operand_aliasing={{0}: (4, {}), {1}: (5, {})} | custom-call | flops 838860800 | bytes 4915200 | tf_op jit(solution)/shard_map/pallas_call | solution.py:390
  122.8 2.4 %shard_map.127 = (bf16[1600,2048]{1,0:T(8,128)(2,1)}, bf16[1600,2048]{1,0:T(8,128)(2,1)}) custom-call(bf16[2,256,256]{2,1,0:T(8,128)(2,1)S(1)} %collective-permute-done.19.hidden_ref, bf16[2,256,256]{2,1,0:T(8,128)(2,1)S(1)} %collective-permute-done.20.pre_ref, ...), custom_call_target="tpu_custom_call", output_to_operand_aliasing={{0}: (4, {}), {1}: (5, {})} | custom-call | flops 838860800 | bytes 4915200 | tf_op jit(solution)/shard_map/pallas_call | solution.py:390
  125.3 2.4 %shard_map.128 = (bf16[1600,2048]{1,0:T(8,128)(2,1)}, bf16[1600,2048]{1,0:T(8,128)(2,1)}) custom-call(bf16[2,256,256]{2,1,0:T(8,128)(2,1)S(1)} %collective-permute-done.16.hidden_ref, bf16[2,256,256]{2,1,0:T(8,128)(2,1)S(1)} %collective-permute-done.18.pre_ref, ...), custom_call_target="tpu_custom_call", output_to_operand_aliasing={{0}: (4, {}), {1}: (5, {})} | custom-call | flops 838860800 | bytes 4915200 | tf_op jit(solution)/shard_map/pallas_call | solution.py:390
  127.7 1.5 %shard_map.122 = (bf16[16,1600]{1,0:T(8,128)(2,1)}, bf16[8,1600]{1,0:T(8,128)(2,1)}) custom-call(s32[2]{0:T(128)S(1)} %pad_add_fusion.me_ref, s32[1,4]{1,0:T(1,128)S(1)} %copy-done.6, s32[1,8]{1,0:T(1,128)S(1)} %copy-done.7, bf16[8,16,1600]{2,1,0:T(8,128)(2,1)S(1)} %all-to-all-done.tail_ref, f32[16,1600]{1,0:T(8,128)S(1)} %get-tuple-element.51.extra_ref, ...), custom_call_target="tpu_custom_call" | custom-call | tf_op jit(solution)/shard_map/pallas_call | solution.py:411
  (32 shorter events, 0.4 us)
Async XLA Ops:
  1.6 6.8 %collective-permute-start = (bf16[1,16,1600]{2,1,0:T(8,128)(2,1)S(1)}, bf16[1,16,1600]{2,1,0:T(8,128)(2,1)S(1)}, u32[]{:S(2)}, u32[]{:S(2)}) collective-permute-start(bf16[1,16,1600]{2,1,0:T(8,128)(2,1)S(1)} %shard_map.111.first_ref), channel_id=1, source_target_pairs={{0,16},{4,20},{8,24},{12,28},{16,0},{20,4},{24,8},{28,12},{1,17},{... | collective-permute-start | bytes 153608 | tf_op jit(solution)/shard_map/ppermute | solution.py:113
  8.5 4.8 %collective-permute-start.1 = (bf16[2,16,1600]{2,1,0:T(8,128)(2,1)S(1)}, bf16[2,16,1600]{2,1,0:T(8,128)(2,1)S(1)}, u32[]{:S(2)}, u32[]{:S(2)}) collective-permute-start(bf16[2,16,1600]{2,1,0:T(8,128)(2,1)S(1)} %shard_map.112.first_ref), channel_id=1, source_target_pairs={{0,8},{4,12},{8,0},{12,4},{16,24},{20,28},{24,16},{28,20},{1,9},{5... | collective-permute-start | bytes 307208 | tf_op jit(solution)/shard_map/ppermute | solution.py:113
  13.3 5.9 %collective-permute-start.2 = (bf16[4,16,1600]{2,1,0:T(8,128)(2,1)S(1)}, bf16[4,16,1600]{2,1,0:T(8,128)(2,1)S(1)}, u32[]{:S(2)}, u32[]{:S(2)}) collective-permute-start(bf16[4,16,1600]{2,1,0:T(8,128)(2,1)S(1)} %shard_map.113.first_ref), channel_id=1, source_target_pairs={{0,4},{4,0},{8,12},{12,8},{16,20},{20,16},{24,28},{28,24},{1,5},{5... | collective-permute-start | bytes 614408 | tf_op jit(solution)/shard_map/ppermute | solution.py:113
  19.2 8.2 %collective-permute-start.3 = (bf16[8,16,1600]{2,1,0:T(8,128)(2,1)S(1)}, bf16[8,16,1600]{2,1,0:T(8,128)(2,1)S(1)}, u32[]{:S(2)}, u32[]{:S(2)}) collective-permute-start(bf16[8,16,1600]{2,1,0:T(8,128)(2,1)S(1)} %shard_map.114.first_ref), channel_id=1, source_target_pairs={{0,2},{1,3},{2,0},{3,1},{4,6},{5,7},{6,4},{7,5},{8,10},{9,11},{10,... | collective-permute-start | bytes 1228808 | tf_op jit(solution)/shard_map/ppermute | solution.py:113
  27.5 21.5 %collective-permute-start.4 = (bf16[16,16,1600]{2,1,0:T(8,128)(2,1)S(1)}, bf16[16,16,1600]{2,1,0:T(8,128)(2,1)S(1)}, u32[]{:S(2)}, u32[]{:S(2)}) collective-permute-start(bf16[16,16,1600]{2,1,0:T(8,128)(2,1)S(1)} %shard_map.115.near_ref), channel_id=1, source_target_pairs={{0,1},{1,0},{2,3},{3,2},{4,5},{5,4},{6,7},{7,6},{8,9},{9,8},{10,11... | collective-permute-start | bytes 2457608 | tf_op jit(solution)/shard_map/ppermute | solution.py:113
  30.1 7.5 %collective-permute-start.5 = (bf16[2,200,256]{2,1,0:T(8,128)(2,1)S(1)}, bf16[2,200,256]{2,1,0:T(8,128)(2,1)S(1)}, u32[]{:S(2)}, u32[]{:S(2)}) collective-permute-start(bf16[2,200,256]{2,1,0:T(8,128)(2,1)S(1)} %get-tuple-element.37), channel_id=1, source_target_pairs={{0,4},{4,0},{8,12},{12,8},{16,20},{20,16},{24,28},{28,24},{1,5},{5... | collective-permute-start | bytes 614408 | tf_op jit(solution)/shard_map/ppermute | solution.py:113
  31.9 14.9 %collective-permute-start.6 = (bf16[2,200,256]{2,1,0:T(8,128)(2,1)S(1)}, bf16[2,200,256]{2,1,0:T(8,128)(2,1)S(1)}, u32[]{:S(2)}, u32[]{:S(2)}) collective-permute-start(bf16[2,200,256]{2,1,0:T(8,128)(2,1)S(1)} %get-tuple-element.38), channel_id=1, source_target_pairs={{0,8},{4,12},{8,0},{12,4},{16,24},{20,28},{24,16},{28,20},{1,9},{5... | collective-permute-start | bytes 614408 | tf_op jit(solution)/shard_map/ppermute | solution.py:113
  33.0 21.0 %collective-permute-start.7 = (bf16[2,200,256]{2,1,0:T(8,128)(2,1)}, bf16[2,200,256]{2,1,0:T(8,128)(2,1)}, u32[]{:S(2)}, u32[]{:S(2)}) collective-permute-start(bf16[2,200,256]{2,1,0:T(8,128)(2,1)} %get-tuple-element.39), channel_id=1, source_target_pairs={{0,12},{4,8},{8,4},{12,0},{16,28},{20,24},{24,20},{28,16},{1,13},{... | collective-permute-start | bytes 614408 | tf_op jit(solution)/shard_map/ppermute | solution.py:113
  33.6 20.4 %collective-permute-start.8 = (bf16[2,200,256]{2,1,0:T(8,128)(2,1)}, bf16[2,200,256]{2,1,0:T(8,128)(2,1)}, u32[]{:S(2)}, u32[]{:S(2)}) collective-permute-start(bf16[2,200,256]{2,1,0:T(8,128)(2,1)} %get-tuple-element.40), channel_id=1, source_target_pairs={{0,16},{4,20},{8,24},{12,28},{16,0},{20,4},{24,8},{28,12},{1,17},{... | collective-permute-start | bytes 614408 | tf_op jit(solution)/shard_map/ppermute | solution.py:113
  37.6 0.7 copy-start
  38.3 27.6 %collective-permute-start.9 = (bf16[2,200,256]{2,1,0:T(8,128)(2,1)}, bf16[2,200,256]{2,1,0:T(8,128)(2,1)}, u32[]{:S(2)}, u32[]{:S(2)}) collective-permute-start(bf16[2,200,256]{2,1,0:T(8,128)(2,1)} %get-tuple-element.41), channel_id=1, source_target_pairs={{0,20},{4,16},{8,28},{12,24},{16,4},{20,0},{24,12},{28,8},{1,21},{... | collective-permute-start | bytes 614408 | tf_op jit(solution)/shard_map/ppermute | solution.py:113
  46.8 0.7 copy-start.2
  47.4 18.5 %collective-permute-start.10 = (bf16[2,200,256]{2,1,0:T(8,128)(2,1)}, bf16[2,200,256]{2,1,0:T(8,128)(2,1)}, u32[]{:S(2)}, u32[]{:S(2)}) collective-permute-start(bf16[2,200,256]{2,1,0:T(8,128)(2,1)} %get-tuple-element.42), channel_id=1, source_target_pairs={{0,24},{4,28},{8,16},{12,20},{16,8},{20,12},{24,0},{28,4},{1,25},{... | collective-permute-start | bytes 614408 | tf_op jit(solution)/shard_map/ppermute | solution.py:113
  49.0 16.9 %collective-permute-start.11 = (bf16[2,200,256]{2,1,0:T(8,128)(2,1)}, bf16[2,200,256]{2,1,0:T(8,128)(2,1)}, u32[]{:S(2)}, u32[]{:S(2)}) collective-permute-start(bf16[2,200,256]{2,1,0:T(8,128)(2,1)} %get-tuple-element.43), channel_id=1, source_target_pairs={{0,28},{4,24},{8,20},{12,16},{16,12},{20,8},{24,4},{28,0},{1,29},{... | collective-permute-start | bytes 614408 | tf_op jit(solution)/shard_map/ppermute | solution.py:113
  65.9 0.9 copy-start.1
  66.9 0.9 copy-start.3
  71.8 2.4 %collective-permute-start.12 = (bf16[2,16,8,1600]{3,2,1,0:T(8,128)(2,1)S(1)}, bf16[2,16,8,1600]{3,2,1,0:T(8,128)(2,1)S(1)}, u32[]{:S(2)}, u32[]{:S(2)}) collective-permute-start(bf16[2,16,8,1600]{3,2,1,0:T(8,128)(2,1)S(1)} %get-tuple-element.48), channel_id=1, source_target_pairs={{0,1},{1,0},{2,3},{3,2},{4,5},{5,4},{6,7},{7,6},{8,9},{9,8},{10,11... | collective-permute-start | bytes 2457608 | tf_op jit(solution)/shard_map/ppermute | solution.py:113
  74.4 11.9 %collective-permute-start.13 = (bf16[2,8,8,1600]{3,2,1,0:T(8,128)(2,1)S(1)}, bf16[2,8,8,1600]{3,2,1,0:T(8,128)(2,1)S(1)}, u32[]{:S(2)}, u32[]{:S(2)}) collective-permute-start(bf16[2,8,8,1600]{3,2,1,0:T(8,128)(2,1)S(1)} %get-tuple-element.50), channel_id=1, source_target_pairs={{0,2},{1,3},{2,0},{3,1},{4,6},{5,7},{6,4},{7,5},{8,10},{9,11},{10,... | collective-permute-start | bytes 1228808 | tf_op jit(solution)/shard_map/ppermute | solution.py:113
  76.2 23.1 %collective-permute-start.14 = (bf16[2,256,256]{2,1,0:T(8,128)(2,1)S(1)}, bf16[2,256,256]{2,1,0:T(8,128)(2,1)S(1)}, u32[]{:S(2)}, u32[]{:S(2)}) collective-permute-start(bf16[2,256,256]{2,1,0:T(8,128)(2,1)S(1)} %get-tuple-element.44.both_ref.first_ref), channel_id=1, source_target_pairs={{0,16},{4,20},{8,24},{12,28},{16,0},{20,4},{24,8},{28,12},{1,17},{... | collective-permute-start | bytes 786440 | tf_op jit(solution)/shard_map/ppermute | solution.py:113
  87.2 40.5 %all-to-all-start = ((bf16[8,16,1600]{2,1,0:T(8,128)(2,1)}), bf16[8,16,1600]{2,1,0:T(8,128)(2,1)S(1)}, u32[]{:S(2)}, u32[]{:S(2)}) async-start(bf16[8,16,1600]{2,1,0:T(8,128)(2,1)} %shard_map.121), calls=%async_computation | async-start | bytes 851968 | tf_op jit(solution)/shard_map/all_to_all | solution.py:523
  99.4 16.2 %collective-permute-start.15 = (bf16[2,256,256]{2,1,0:T(8,128)(2,1)S(1)}, bf16[2,256,256]{2,1,0:T(8,128)(2,1)S(1)}, u32[]{:S(2)}, u32[]{:S(2)}) collective-permute-start(bf16[2,256,256]{2,1,0:T(8,128)(2,1)S(1)} %get-tuple-element.54.hidden_ref), channel_id=1, source_target_pairs={{0,8},{4,12},{8,0},{12,4},{16,24},{20,28},{24,16},{28,20},{1,9},{5... | collective-permute-start | bytes 786440 | tf_op jit(solution)/shard_map/ppermute | solution.py:113
  101.5 15.0 %collective-permute-start.17 = (bf16[2,256,256]{2,1,0:T(8,128)(2,1)S(1)}, bf16[2,256,256]{2,1,0:T(8,128)(2,1)S(1)}, u32[]{:S(2)}, u32[]{:S(2)}) collective-permute-start(bf16[2,256,256]{2,1,0:T(8,128)(2,1)S(1)} %get-tuple-element.55.pre_ref), channel_id=1, source_target_pairs={{0,4},{4,0},{8,12},{12,8},{16,20},{20,16},{24,28},{28,24},{1,5},{5... | collective-permute-start | bytes 786440 | tf_op jit(solution)/shard_map/ppermute | solution.py:113
  102.9 19.9 %collective-permute-start.19 = (bf16[2,256,256]{2,1,0:T(8,128)(2,1)S(1)}, bf16[2,256,256]{2,1,0:T(8,128)(2,1)S(1)}, u32[]{:S(2)}, u32[]{:S(2)}) collective-permute-start(bf16[2,256,256]{2,1,0:T(8,128)(2,1)S(1)} %get-tuple-element.54.hidden_ref), channel_id=1, source_target_pairs={{0,4},{4,0},{8,12},{12,8},{16,20},{20,16},{24,28},{28,24},{1,5},{5... | collective-permute-start | bytes 786440 | tf_op jit(solution)/shard_map/ppermute | solution.py:113
  103.5 19.3 %collective-permute-start.20 = (bf16[2,256,256]{2,1,0:T(8,128)(2,1)S(1)}, bf16[2,256,256]{2,1,0:T(8,128)(2,1)S(1)}, u32[]{:S(2)}, u32[]{:S(2)}) collective-permute-start(bf16[2,256,256]{2,1,0:T(8,128)(2,1)S(1)} %get-tuple-element.55.pre_ref), channel_id=1, source_target_pairs={{0,8},{4,12},{8,0},{12,4},{16,24},{20,28},{24,16},{28,20},{1,9},{5... | collective-permute-start | bytes 786440 | tf_op jit(solution)/shard_map/ppermute | solution.py:113
  115.6 9.6 %collective-permute-start.16 = (bf16[2,256,256]{2,1,0:T(8,128)(2,1)S(1)}, bf16[2,256,256]{2,1,0:T(8,128)(2,1)S(1)}, u32[]{:S(2)}, u32[]{:S(2)}) collective-permute-start(bf16[2,256,256]{2,1,0:T(8,128)(2,1)S(1)} %collective-permute-done.15.hidden_ref), channel_id=1, source_target_pairs={{0,4},{4,0},{8,12},{12,8},{16,20},{20,16},{24,28},{28,24},{1,5},{5... | collective-permute-start | bytes 786440 | tf_op jit(solution)/shard_map/ppermute | solution.py:113
  116.5 8.8 %collective-permute-start.18 = (bf16[2,256,256]{2,1,0:T(8,128)(2,1)S(1)}, bf16[2,256,256]{2,1,0:T(8,128)(2,1)S(1)}, u32[]{:S(2)}, u32[]{:S(2)}) collective-permute-start(bf16[2,256,256]{2,1,0:T(8,128)(2,1)S(1)} %collective-permute-done.17.pre_ref), channel_id=1, source_target_pairs={{0,8},{4,12},{8,0},{12,4},{16,24},{20,28},{24,16},{28,20},{1,9},{5... | collective-permute-start | bytes 786440 | tf_op jit(solution)/shard_map/ppermute | solution.py:113
  125.2 2.4 %copy-start.4 = (bf16[8,1600]{1,0:T(8,128)(2,1)S(1)}, bf16[8,1600]{1,0:T(8,128)(2,1)}, u32[]{:S(2)}) copy-start(bf16[8,1600]{1,0:T(8,128)(2,1)} %patch_ref.1) | copy-start | bytes 76804
  125.2 2.4 %copy-start.5 = (bf16[16,1600]{1,0:T(8,128)(2,1)S(1)}, bf16[16,1600]{1,0:T(8,128)(2,1)}, u32[]{:S(2)}) copy-start(bf16[16,1600]{1,0:T(8,128)(2,1)} %text_ref.1) | copy-start | bytes 153604
  125.3 2.4 %copy-start.6 = (s32[1,4]{1,0:T(1,128)S(1)}, s32[1,4]{1,0:T(1,128)}, u32[]{:S(2)}) copy-start(s32[1,4]{1,0:T(1,128)} %count_ref.1) | copy-start | bytes 52
  125.3 2.4 %copy-start.7 = (s32[1,8]{1,0:T(1,128)S(1)}, s32[1,8]{1,0:T(1,128)}, u32[]{:S(2)}) copy-start(s32[1,8]{1,0:T(1,128)} %place_ref.1) | copy-start | bytes 100

commit v6 on v5

--- a/solution.py
+++ b/solution.py
@@ -248,23 +248,50 @@
     extra_ref[...] = jnp.concatenate([coming, own], axis=0)
 
 
-def hidden_kernel(normed_ref, grad_ref, expand_at, project_at, *refs):
-    blocks = refs[:-4]
-    both_ref, expand_ref, project_ref, sems = refs[-4:]
-    part = expand_at.shape[0]
-    units = both_ref.shape[2]
+def place_blocks(distances, sources, targets, sems):
     me = lax.axis_index("dp")
     copies = []
-    for k, (source, whole) in enumerate(((expand_at, expand_ref), (project_at, project_ref))):
-        own = source.at[:, pl.ds(pl.multiple_of(me * units, 128), units)]
-        for i, block in enumerate((own, *(block.at[k] for block in blocks))):
-            at = pl.ds(pl.multiple_of((me ^ i) * part, 8), part)
+    for i, (distance, source) in enumerate(zip(distances, sources)):
+        part = source.shape[1]
+        at = pl.ds(pl.multiple_of((me ^ distance) * part, 8), part)
+        for k, target in enumerate(targets):
             copies.append(
-                pltpu.make_async_copy(
-                    block, whole.at[at, :], sems.at[k * (len(blocks) + 1) + i]
-                )
+                pltpu.make_async_copy(source.at[k], target.at[at, :], sems.at[2 * i + k])
             )
     fetch(copies)
+
+
+def first_unpack_kernel(distances, own_expand_at, own_project_at, *refs):
+    sources, (expand_ref, project_ref, sems) = refs[: len(distances)], refs[-3:]
+    part, units = own_expand_at.shape[0], expand_ref.shape[1]
+    me = lax.axis_index("dp")
+    mine = pl.ds(pl.multiple_of(me * units, 128), units)
+    at = pl.ds(pl.multiple_of(me * part, 8), part)
+    own = [
+        pltpu.make_async_copy(
+            source.at[:, mine], target.at[at, :], sems.at[2 * len(distances) + k]
+        )
+        for k, (source, target) in enumerate(
+            ((own_expand_at, expand_ref), (own_project_at, project_ref))
+        )
+    ]
+    for copy in own:
+        copy.start()
+    place_blocks(distances, sources, (expand_ref, project_ref), sems)
+    for copy in own:
+        copy.wait()
+
+
+def next_unpack_kernel(distances, expand_part_ref, project_part_ref, *refs):
+    sources, (expand_ref, project_ref, sems) = refs[: len(distances)], refs[-3:]
+    place_blocks(distances, sources, (expand_ref, project_ref), sems)
+
+
+def hidden_kernel(
+    distances, expand_part_ref, project_part_ref, normed_ref, grad_ref, *refs
+):
+    sources, (expand_ref, project_ref, both_ref, sems) = refs[: len(distances)], refs[-4:]
+    place_blocks(distances, sources, (expand_ref, project_ref), sems)
     preact = jnp.dot(normed_ref[...], expand_ref[...], preferred_element_type=jnp.float32)
     activated, derivative = gelu_pair(preact)
     both_ref[0] = activated.astype(jnp.bfloat16)
@@ -418,6 +445,14 @@
     )(*smem, *vmem)
 
 
+def arrival_groups(dp):
+    half, quarter = 1 << (dp - 1), 1 << (dp - 2)
+    last = (2 * quarter - 1,) if quarter > 1 else (2 * half - 1,)
+    middle = tuple(i for i in (quarter, 2 * half - 1) if i not in last)
+    early = tuple(i for i in range(1, 2 * half) if i not in last + middle)
+    return early, middle, last
+
+
 def join(first, second):
     both = (first.shape[0] + second.shape[0], *first.shape[1:])
     return call(join_kernel, jax.ShapeDtypeStruct(both, first.dtype), (), (first, second))
@@ -490,21 +525,38 @@
             held = join(held, got)
     normed, grad_all, extra = call(
         functools.partial(order_kernel, sections, capacity, dp_steps, section_steps),
-        [shape((rows, features), kept), shape((rows, features), kept), shape((2 * slots, features), wide)],
+        [shape((rows, features), kept)] * 2 + [shape((2 * slots, features), wide)],
         (me,), (held, got, gain),
     )
-
     normed_turned, grad_turned = call(
         turn_kernel, [shape((features, rows), kept)] * 2, (), (normed, grad_all)
     )
-    both, expand_slice, project_slice = pl.pallas_call(
-        hidden_kernel,
-        out_shape=[shape((2, rows, units), kept)] + [shape((features, units), kept)] * 2,
-        in_specs=[VMEM_SPEC] * 2 + [hbm] * 2 + [pl.BlockSpec(memory_space=pl.ANY)] * len(arrived),
-        out_specs=[VMEM_SPEC] * 3,
-        scratch_shapes=[pltpu.SemaphoreType.DMA((2 * replicas,))],
-        compiler_params=pltpu.CompilerParams(vmem_limit_bytes=12 << 20),
-    )(normed, grad_all, *in_hbm(expand_weight, project_turned), *arrived)
+    anywhere = pl.BlockSpec(memory_space=pl.ANY)
+    slices = [shape((features, units), kept)] * 2
+    groups = arrival_groups(log2(replicas))
+
+    def unpacking(kernel, group, operands, specs, extra=(), aliases=()):
+        return pl.pallas_call(
+            functools.partial(kernel, group),
+            out_shape=[*slices, *extra],
+            in_specs=[*specs, *[anywhere] * len(group)],
+            out_specs=[VMEM_SPEC] * (2 + len(extra)),
+            scratch_shapes=[pltpu.SemaphoreType.DMA((2 * len(group) + 2,))],
+            input_output_aliases=dict(aliases),
+            compiler_params=pltpu.CompilerParams(vmem_limit_bytes=12 << 20),
+        )(*operands, *(arrived[distance - 1] for distance in group))
+
+    in_place = ((0, 0), (1, 1))
+    held_slices = unpacking(
+        first_unpack_kernel, groups[0], in_hbm(expand_weight, project_turned), [hbm] * 2
+    )
+    held_slices = unpacking(
+        next_unpack_kernel, groups[1], held_slices, [VMEM_SPEC] * 2, aliases=in_place
+    )
+    expand_slice, project_slice, both = unpacking(
+        hidden_kernel, groups[2], (*held_slices, normed, grad_all), [VMEM_SPEC] * 4,
+        [shape((2, rows, units), kept)], in_place,
+    )
 
     tail_steps = section_steps[::-1]
     keep, send = call(

time: 130 us -> 126 us (0.969)
  starting transfers between devices: 53 us -> 43.8 us
  waiting for transfers between devices: 49.2 us -> 57.8 us
  local copies, waits for them, and re-layouts: 3.96 us -> 0.73 us
    ppermute x21, waiting for transfers between devices: 49.2 us -> 57.8 us  [swap(): return lax.ppermute(array, axis, [(i, i ^ step) for i in range(size)])]
    ppermute x21, starting transfers between devices: 40.8 us -> 35.3 us  [swap(): return lax.ppermute(array, axis, [(i, i ^ step) for i in range(size)])]
    all_to_all x1, starting transfers between devices: 12.2 us -> 8.46 us  [move_rows_plan(): tail = lax.all_to_all(tail, 'dp', split_axis=0, concat_axis=0, tiled=True)]
    unnamed x16 -> x8, local copies, waits for them, and re-layouts: 3.25 us -> 0.03 us
    pallas_call x1 -> x3, Pallas kernels: 2.54 us -> 3.51 us  [unpacking(): pl.pallas_call(functools.partial(kernel, group), out_shape=[*slices, *ext...]
  transfers between devices with their start and end apart: 22 -> 22, of which waited for: 10 -> 10; matrix products, arithmetic and copies ran while one was open for 1% -> 1% of each run, Pallas kernels for 12% -> 13%
where the time goes in v6:
time: 126 us
  waiting for transfers between devices  57.8 us (46%)
  starting transfers between devices  43.8 us (35%)
  Pallas kernels  22.8 us (18%)
    ppermute x21, waiting for transfers between devices, swap(): return lax.ppermute(array, axis, [(i, i ^ step) for i in range(size)])  57.8 us
    ppermute x21, starting transfers between devices, swap(): return lax.ppermute(array, axis, [(i, i ^ step) for i in range(size)])  35.3 us
    pallas_call x4, Pallas kernels, weight_grads(): pl.pallas_call(functools.partial(weight_grad_kernel, hidden_distances, pr...  9.43 us
    all_to_all x1, starting transfers between devices, move_rows_plan(): tail = lax.all_to_all(tail, 'dp', split_axis=0, concat_axis=0, tiled=True)  8.46 us
    pallas_call x11, Pallas kernels, call(): pl.pallas_call(kernel, out_shape=out_shape, in_specs=[SMEM_SPEC] * len(sm...  6.54 us
    pallas_call x3, Pallas kernels, unpacking(): pl.pallas_call(functools.partial(kernel, group), out_shape=[*slices, *ext...  3.51 us
  transfers between devices with their start and end apart: 22, of which 10 were waited for; matrix products, arithmetic and copies ran while one was open for 1% of the time, Pallas kernels for 13%

profile of v6, /device:TPU:0, one launch (start us, length us, event | category | flops | bytes accessed | tf_op | source)
XLA Modules:
  0.0 126.1 jit_solution(8641670506604527206)
XLA Ops:
  0.6 1.0 shard_map.114.first_ref
  1.6 4.1 %collective-permute-start.6 = (bf16[1,16,1600]{2,1,0:T(8,128)(2,1)S(1)}, bf16[1,16,1600]{2,1,0:T(8,128)(2,1)S(1)}, u32[]{:S(2)}, u32[]{:S(2)}) collective-permute-start(bf16[1,16,1600]{2,1,0:T(8,128)(2,1)S(1)} %shard_map.114.first_ref), channel_id=1, source_target_pairs={{0,16},{4,20},{8,24},{12,28},{16,0},{20,4},{24,8},{28,12},{1,17},{... | collective-permute-start | bytes 153608 | tf_op jit(solution)/shard_map/ppermute | solution.py:113
  5.8 2.7 %collective-permute-done.6.second_ref = bf16[1,16,1600]{2,1,0:T(8,128)(2,1)S(1)} collective-permute-done((bf16[1,16,1600]{2,1,0:T(8,128)(2,1)S(1)}, bf16[1,16,1600]{2,1,0:T(8,128)(2,1)S(1)}, u32[]{:S(2)}, u32[]{:S(2)}) %collective-permute-start.6) | collective-permute-done | bytes 51232 | tf_op jit(solution)/shard_map/ppermute | solution.py:113
  8.5 1.4 %collective-permute-start.7 = (bf16[2,16,1600]{2,1,0:T(8,128)(2,1)S(1)}, bf16[2,16,1600]{2,1,0:T(8,128)(2,1)S(1)}, u32[]{:S(2)}, u32[]{:S(2)}) collective-permute-start(bf16[2,16,1600]{2,1,0:T(8,128)(2,1)S(1)} %shard_map.115.first_ref), channel_id=1, source_target_pairs={{0,8},{4,12},{8,0},{12,4},{16,24},{20,28},{24,16},{28,20},{1,9},{5... | collective-permute-start | bytes 307208 | tf_op jit(solution)/shard_map/ppermute | solution.py:113
  9.9 3.4 %collective-permute-done.7.second_ref = bf16[2,16,1600]{2,1,0:T(8,128)(2,1)S(1)} collective-permute-done((bf16[2,16,1600]{2,1,0:T(8,128)(2,1)S(1)}, bf16[2,16,1600]{2,1,0:T(8,128)(2,1)S(1)}, u32[]{:S(2)}, u32[]{:S(2)}) %collective-permute-start.7) | collective-permute-done | bytes 102432 | tf_op jit(solution)/shard_map/ppermute | solution.py:113
  13.3 1.8 %collective-permute-start.8 = (bf16[4,16,1600]{2,1,0:T(8,128)(2,1)S(1)}, bf16[4,16,1600]{2,1,0:T(8,128)(2,1)S(1)}, u32[]{:S(2)}, u32[]{:S(2)}) collective-permute-start(bf16[4,16,1600]{2,1,0:T(8,128)(2,1)S(1)} %shard_map.116.first_ref), channel_id=1, source_target_pairs={{0,4},{4,0},{8,12},{12,8},{16,20},{20,16},{24,28},{28,24},{1,5},{5... | collective-permute-start | bytes 614408 | tf_op jit(solution)/shard_map/ppermute | solution.py:113
  15.0 4.1 %collective-permute-done.8.second_ref = bf16[4,16,1600]{2,1,0:T(8,128)(2,1)S(1)} collective-permute-done((bf16[4,16,1600]{2,1,0:T(8,128)(2,1)S(1)}, bf16[4,16,1600]{2,1,0:T(8,128)(2,1)S(1)}, u32[]{:S(2)}, u32[]{:S(2)}) %collective-permute-start.8) | collective-permute-done | bytes 204832 | tf_op jit(solution)/shard_map/ppermute | solution.py:113
  19.2 1.8 %collective-permute-start.9 = (bf16[8,16,1600]{2,1,0:T(8,128)(2,1)S(1)}, bf16[8,16,1600]{2,1,0:T(8,128)(2,1)S(1)}, u32[]{:S(2)}, u32[]{:S(2)}) collective-permute-start(bf16[8,16,1600]{2,1,0:T(8,128)(2,1)S(1)} %shard_map.117.first_ref), channel_id=1, source_target_pairs={{0,2},{1,3},{2,0},{3,1},{4,6},{5,7},{6,4},{7,5},{8,10},{9,11},{10,... | collective-permute-start | bytes 1228808 | tf_op jit(solution)/shard_map/ppermute | solution.py:113
  21.0 6.4 %collective-permute-done.9.second_ref = bf16[8,16,1600]{2,1,0:T(8,128)(2,1)S(1)} collective-permute-done((bf16[8,16,1600]{2,1,0:T(8,128)(2,1)S(1)}, bf16[8,16,1600]{2,1,0:T(8,128)(2,1)S(1)}, u32[]{:S(2)}, u32[]{:S(2)}) %collective-permute-start.9) | collective-permute-done | bytes 409632 | tf_op jit(solution)/shard_map/ppermute | solution.py:113
  27.5 0.1 collective-permute-start.10
  27.5 2.3 %shard_map.111 = (bf16[2,200,256]{2,1,0:T(8,128)(2,1)S(1)}, bf16[2,200,256]{2,1,0:T(8,128)(2,1)S(1)}, bf16[2,200,256]{2,1,0:T(8,128)(2,1)}, bf16[2,200,256]{2,1,...) custom-call(bf16[200,2048]{1,0:T(8,128)(2,1)} %own_expand_at.1, ...), custom_call_target="tpu_custom_call" | custom-call | tf_op jit(solution)/shard_map/pallas_call | solution.py:509
  29.9 1.8 %collective-permute-start = (bf16[2,200,256]{2,1,0:T(8,128)(2,1)S(1)}, bf16[2,200,256]{2,1,0:T(8,128)(2,1)S(1)}, u32[]{:S(2)}, u32[]{:S(2)}) collective-permute-start(bf16[2,200,256]{2,1,0:T(8,128)(2,1)S(1)} %get-tuple-element.39), channel_id=1, source_target_pairs={{0,4},{4,0},{8,12},{12,8},{16,20},{20,16},{24,28},{28,24},{1,5},{5... | collective-permute-start | bytes 614408 | tf_op jit(solution)/shard_map/ppermute | solution.py:113
  31.7 2.4 %collective-permute-start.1 = (bf16[2,200,256]{2,1,0:T(8,128)(2,1)S(1)}, bf16[2,200,256]{2,1,0:T(8,128)(2,1)S(1)}, u32[]{:S(2)}, u32[]{:S(2)}) collective-permute-start(bf16[2,200,256]{2,1,0:T(8,128)(2,1)S(1)} %get-tuple-element.40), channel_id=1, source_target_pairs={{0,16},{4,20},{8,24},{12,28},{16,0},{20,4},{24,8},{28,12},{1,17},{... | collective-permute-start | bytes 614408 | tf_op jit(solution)/shard_map/ppermute | solution.py:113
  34.1 0.3 collective-permute-start.2
  34.3 3.8 %collective-permute-start.3 = (bf16[2,200,256]{2,1,0:T(8,128)(2,1)}, bf16[2,200,256]{2,1,0:T(8,128)(2,1)S(1)}, u32[]{:S(2)}, u32[]{:S(2)}) collective-permute-start(bf16[2,200,256]{2,1,0:T(8,128)(2,1)} %get-tuple-element.42), channel_id=1, source_target_pairs={{0,24},{4,28},{8,16},{12,20},{16,8},{20,12},{24,0},{28,4},{1,25},{... | collective-permute-start | bytes 614408 | tf_op jit(solution)/shard_map/ppermute | solution.py:113
  38.2 0.7 collective-permute-start.4
  38.8 14.9 %collective-permute-done.1.refs_1_ = bf16[2,200,256]{2,1,0:T(8,128)(2,1)S(1)} collective-permute-done((bf16[2,200,256]{2,1,0:T(8,128)(2,1)S(1)}, bf16[2,200,256]{2,1,0:T(8,128)(2,1)S(1)}, u32[]{:S(2)}, u32[]{:S(2)}) %collective-permute-start.1) | collective-permute-done | bytes 204832 | tf_op jit(solution)/shard_map/ppermute | solution.py:113
  53.7 2.7 %collective-permute-start.5 = (bf16[2,200,256]{2,1,0:T(8,128)(2,1)S(1)}, bf16[2,200,256]{2,1,0:T(8,128)(2,1)S(1)}, u32[]{:S(2)}, u32[]{:S(2)}) collective-permute-start(bf16[2,200,256]{2,1,0:T(8,128)(2,1)S(1)} %get-tuple-element.46), channel_id=1, source_target_pairs={{0,28},{4,24},{8,20},{12,16},{16,12},{20,8},{24,4},{28,0},{1,29},{... | collective-permute-start | bytes 614408 | tf_op jit(solution)/shard_map/ppermute | solution.py:113
  56.4 5.9 %collective-permute-done.2.refs_2_ = bf16[2,200,256]{2,1,0:T(8,128)(2,1)S(1)} collective-permute-done((bf16[2,200,256]{2,1,0:T(8,128)(2,1)S(1)}, bf16[2,200,256]{2,1,0:T(8,128)(2,1)S(1)}, u32[]{:S(2)}, u32[]{:S(2)}) %collective-permute-start.2) | collective-permute-done | bytes 204832 | tf_op jit(solution)/shard_map/ppermute | solution.py:113
  62.2 0.7 reshape.11.gain_ref
  62.9 0.1 pad_add_fusion.me_ref
  63.0 1.1 shard_map.112
  64.2 0.6 shard_map.113
  64.8 2.0 %shard_map.119 = (bf16[256,1600]{1,0:T(8,128)(2,1)S(1)}, bf16[256,1600]{1,0:T(8,128)(2,1)S(1)}, f32[16,1600]{1,0:T(8,128)S(1)}) custom-call(s32[2]{0:T(128)S(1)} %pad_add_fusion.me_ref, bf16[16,16,1600]{2,1,0:T(8,128)(2,1)S(1)} %shard_map.118.near_ref, bf16[16,16,1600]{2,1,0:T(8,128)(2,1)S(1)} %collective-permute-done.10.far_ref, f32[1,1600]{1,0:T(1,128)S(1)} %reshape.11.gain_ref), custom_call_target="tpu_custom_call" | custom-call | tf_op jit(solution)/shard_map/pallas_call | solution.py:438
  66.8 2.4 %collective-permute-done.11.refs_0_ = bf16[2,200,256]{2,1,0:T(8,128)(2,1)} collective-permute-done((bf16[2,200,256]{2,1,0:T(8,128)(2,1)}, bf16[2,200,256]{2,1,0:T(8,128)(2,1)}, u32[]{:S(2)}, u32[]{:S(2)}) %collective-permute-start.11) | collective-permute-done | bytes 204832 | tf_op jit(solution)/shard_map/ppermute | solution.py:113
  69.2 1.8 %shard_map.120 = (bf16[1600,256]{1,0:T(8,128)(2,1)S(1)}, bf16[1600,256]{1,0:T(8,128)(2,1)S(1)}, bf16[2,256,256]{2,1,0:T(8,128)(2,1)S(1)}) custom-call(bf16[1600,256]{1,0:T(8,128)(2,1)S(1)} %get-tuple-element.47.expand_part_ref, bf16[1600,256]{1,0:T(8,128)(2,1)S(1)} %get-tuple-element.48.project_part_ref, ...), custom_call_target="tpu_custom_call", output_to_operand_aliasing={{0}: (0, {}), {1}: (1, {})} | custom-call | tf_op jit(solution)/shard_map/pallas_call | solution.py:539
  71.0 1.4 %shard_map.121 = (f32[2,16,8,1600]{3,2,1,0:T(8,128)S(1)}, bf16[2,16,8,1600]{3,2,1,0:T(8,128)(2,1)S(1)}) custom-call(s32[2]{0:T(128)S(1)} %pad_add_fusion.me_ref, bf16[2,256,256]{2,1,0:T(8,128)(2,1)S(1)} %get-tuple-element.52.both_ref.first_ref, bf16[1600,256]{1,0:T(8,128)(2,1)S(1)} %get-tuple-element.53.expand_ref, ...), custom_call_target="tpu_custom_call" | custom-call | tf_op jit(solution)/shard_map/pallas_call | solution.py:438
  72.4 0.1 collective-permute-start.12
  72.5 2.4 %collective-permute-done.12.got_ref = bf16[2,16,8,1600]{3,2,1,0:T(8,128)(2,1)S(1)} collective-permute-done((bf16[2,16,8,1600]{3,2,1,0:T(8,128)(2,1)S(1)}, bf16[2,16,8,1600]{3,2,1,0:T(8,128)(2,1)S(1)}, u32[]{:S(2)}, u32[]{:S(2)}) %collective-permute-start.12) | collective-permute-done | bytes 819232 | tf_op jit(solution)/shard_map/ppermute | solution.py:113
  74.9 0.2 shard_map.122
  75.1 1.8 %collective-permute-start.13 = (bf16[2,8,8,1600]{3,2,1,0:T(8,128)(2,1)S(1)}, bf16[2,8,8,1600]{3,2,1,0:T(8,128)(2,1)S(1)}, u32[]{:S(2)}, u32[]{:S(2)}) collective-permute-start(bf16[2,8,8,1600]{3,2,1,0:T(8,128)(2,1)S(1)} %get-tuple-element.58), channel_id=1, source_target_pairs={{0,2},{1,3},{2,0},{3,1},{4,6},{5,7},{6,4},{7,5},{8,10},{9,11},{10,... | collective-permute-start | bytes 1228808 | tf_op jit(solution)/shard_map/ppermute | solution.py:113
  76.9 6.4 %collective-permute-start.14 = (bf16[2,256,256]{2,1,0:T(8,128)(2,1)S(1)}, bf16[2,256,256]{2,1,0:T(8,128)(2,1)S(1)}, u32[]{:S(2)}, u32[]{:S(2)}) collective-permute-start(bf16[2,256,256]{2,1,0:T(8,128)(2,1)S(1)} %get-tuple-element.52.both_ref.first_ref), channel_id=1, source_target_pairs={{0,16},{4,20},{8,24},{12,28},{16,0},{20,4},{24,8},{28,12},{1,17},{... | collective-permute-start | bytes 786440 | tf_op jit(solution)/shard_map/ppermute | solution.py:113
  83.3 3.7 %collective-permute-done.13.got_ref = bf16[2,8,8,1600]{3,2,1,0:T(8,128)(2,1)S(1)} collective-permute-done((bf16[2,8,8,1600]{3,2,1,0:T(8,128)(2,1)S(1)}, bf16[2,8,8,1600]{3,2,1,0:T(8,128)(2,1)S(1)}, u32[]{:S(2)}, u32[]{:S(2)}) %collective-permute-start.13) | collective-permute-done | bytes 409632 | tf_op jit(solution)/shard_map/ppermute | solution.py:113
  87.0 0.8 shard_map.123
  87.8 8.5 %all-to-all-start = ((bf16[8,16,1600]{2,1,0:T(8,128)(2,1)}), bf16[8,16,1600]{2,1,0:T(8,128)(2,1)S(1)}, u32[]{:S(2)}, u32[]{:S(2)}) async-start(bf16[8,16,1600]{2,1,0:T(8,128)(2,1)} %shard_map.123), calls=%async_computation | async-start | bytes 851968 | tf_op jit(solution)/shard_map/all_to_all | solution.py:575
  96.3 2.1 %collective-permute-start.15 = (bf16[2,256,256]{2,1,0:T(8,128)(2,1)S(1)}, bf16[2,256,256]{2,1,0:T(8,128)(2,1)S(1)}, u32[]{:S(2)}, u32[]{:S(2)}) collective-permute-start(bf16[2,256,256]{2,1,0:T(8,128)(2,1)S(1)} %get-tuple-element.62.hidden_ref), channel_id=1, source_target_pairs={{0,8},{4,12},{8,0},{12,4},{16,24},{20,28},{24,16},{28,20},{1,9},{5... | collective-permute-start | bytes 786440 | tf_op jit(solution)/shard_map/ppermute | solution.py:113
  98.4 1.5 %collective-permute-start.17 = (bf16[2,256,256]{2,1,0:T(8,128)(2,1)S(1)}, bf16[2,256,256]{2,1,0:T(8,128)(2,1)S(1)}, u32[]{:S(2)}, u32[]{:S(2)}) collective-permute-start(bf16[2,256,256]{2,1,0:T(8,128)(2,1)S(1)} %get-tuple-element.63.pre_ref), channel_id=1, source_target_pairs={{0,4},{4,0},{8,12},{12,8},{16,20},{20,16},{24,28},{28,24},{1,5},{5... | collective-permute-start | bytes 786440 | tf_op jit(solution)/shard_map/ppermute | solution.py:113
  99.9 0.6 collective-permute-start.19
  100.4 0.1 collective-permute-start.20
  100.5 12.0 %collective-permute-done.15.hidden_ref = bf16[2,256,256]{2,1,0:T(8,128)(2,1)S(1)} collective-permute-done((bf16[2,256,256]{2,1,0:T(8,128)(2,1)S(1)}, bf16[2,256,256]{2,1,0:T(8,128)(2,1)S(1)}, u32[]{:S(2)}, u32[]{:S(2)}) %collective-permute-start.15) | collective-permute-done | bytes 262176 | tf_op jit(solution)/shard_map/ppermute | solution.py:113
  112.5 0.9 collective-permute-start.16
  113.4 1.1 collective-permute-start.18
  114.5 0.5 shard_map.126
  115.0 2.4 %shard_map.127 = (bf16[1600,2048]{1,0:T(8,128)(2,1)}, bf16[1600,2048]{1,0:T(8,128)(2,1)}) custom-call(bf16[2,256,256]{2,1,0:T(8,128)(2,1)S(1)} %get-tuple-element.62.hidden_ref, bf16[2,256,256]{2,1,0:T(8,128)(2,1)S(1)} %get-tuple-element.63.pre_ref, bf16[1600,256]{1,0:T(8,128)(2,1)S(1)} %get-tuple-element.64.grad_ref, ...), custom_call_target="tpu_custom_call" | custom-call | flops 838860800 | bytes 4915200 | tf_op jit(solution)/shard_map/pallas_call | solution.py:417
  117.4 2.4 %shard_map.128 = (bf16[1600,2048]{1,0:T(8,128)(2,1)}, bf16[1600,2048]{1,0:T(8,128)(2,1)}) custom-call(bf16[2,256,256]{2,1,0:T(8,128)(2,1)S(1)} %collective-permute-done.15.hidden_ref, bf16[2,256,256]{2,1,0:T(8,128)(2,1)S(1)} %collective-permute-done.17.pre_ref, ...), custom_call_target="tpu_custom_call", output_to_operand_aliasing={{0}: (4, {}), {1}: (5, {})} | custom-call | flops 838860800 | bytes 4915200 | tf_op jit(solution)/shard_map/pallas_call | solution.py:417
  119.8 2.4 %shard_map.129 = (bf16[1600,2048]{1,0:T(8,128)(2,1)}, bf16[1600,2048]{1,0:T(8,128)(2,1)}) custom-call(bf16[2,256,256]{2,1,0:T(8,128)(2,1)S(1)} %collective-permute-done.19.hidden_ref, bf16[2,256,256]{2,1,0:T(8,128)(2,1)S(1)} %collective-permute-done.20.pre_ref, ...), custom_call_target="tpu_custom_call", output_to_operand_aliasing={{0}: (4, {}), {1}: (5, {})} | custom-call | flops 838860800 | bytes 4915200 | tf_op jit(solution)/shard_map/pallas_call | solution.py:417
  122.2 2.4 %shard_map.130 = (bf16[1600,2048]{1,0:T(8,128)(2,1)}, bf16[1600,2048]{1,0:T(8,128)(2,1)}) custom-call(bf16[2,256,256]{2,1,0:T(8,128)(2,1)S(1)} %collective-permute-done.16.hidden_ref, bf16[2,256,256]{2,1,0:T(8,128)(2,1)S(1)} %collective-permute-done.18.pre_ref, ...), custom_call_target="tpu_custom_call", output_to_operand_aliasing={{0}: (4, {}), {1}: (5, {})} | custom-call | flops 838860800 | bytes 4915200 | tf_op jit(solution)/shard_map/pallas_call | solution.py:417
  124.6 1.5 %shard_map.124 = (bf16[16,1600]{1,0:T(8,128)(2,1)}, bf16[8,1600]{1,0:T(8,128)(2,1)}) custom-call(s32[2]{0:T(128)S(1)} %pad_add_fusion.me_ref, s32[1,4]{1,0:T(1,128)S(1)} %copy-done.2, s32[1,8]{1,0:T(1,128)S(1)} %copy-done.3, bf16[8,16,1600]{2,1,0:T(8,128)(2,1)S(1)} %all-to-all-done.tail_ref, f32[16,1600]{1,0:T(8,128)S(1)} %get-tuple-element.59.extra_ref, ...), custom_call_target="tpu_custom_call" | custom-call | tf_op jit(solution)/shard_map/pallas_call | solution.py:438
  (26 shorter events, 0.2 us)
Async XLA Ops:
  1.6 6.8 %collective-permute-start.6 = (bf16[1,16,1600]{2,1,0:T(8,128)(2,1)S(1)}, bf16[1,16,1600]{2,1,0:T(8,128)(2,1)S(1)}, u32[]{:S(2)}, u32[]{:S(2)}) collective-permute-start(bf16[1,16,1600]{2,1,0:T(8,128)(2,1)S(1)} %shard_map.114.first_ref), channel_id=1, source_target_pairs={{0,16},{4,20},{8,24},{12,28},{16,0},{20,4},{24,8},{28,12},{1,17},{... | collective-permute-start | bytes 153608 | tf_op jit(solution)/shard_map/ppermute | solution.py:113
  8.5 4.8 %collective-permute-start.7 = (bf16[2,16,1600]{2,1,0:T(8,128)(2,1)S(1)}, bf16[2,16,1600]{2,1,0:T(8,128)(2,1)S(1)}, u32[]{:S(2)}, u32[]{:S(2)}) collective-permute-start(bf16[2,16,1600]{2,1,0:T(8,128)(2,1)S(1)} %shard_map.115.first_ref), channel_id=1, source_target_pairs={{0,8},{4,12},{8,0},{12,4},{16,24},{20,28},{24,16},{28,20},{1,9},{5... | collective-permute-start | bytes 307208 | tf_op jit(solution)/shard_map/ppermute | solution.py:113
  13.3 5.9 %collective-permute-start.8 = (bf16[4,16,1600]{2,1,0:T(8,128)(2,1)S(1)}, bf16[4,16,1600]{2,1,0:T(8,128)(2,1)S(1)}, u32[]{:S(2)}, u32[]{:S(2)}) collective-permute-start(bf16[4,16,1600]{2,1,0:T(8,128)(2,1)S(1)} %shard_map.116.first_ref), channel_id=1, source_target_pairs={{0,4},{4,0},{8,12},{12,8},{16,20},{20,16},{24,28},{28,24},{1,5},{5... | collective-permute-start | bytes 614408 | tf_op jit(solution)/shard_map/ppermute | solution.py:113
  19.2 8.2 %collective-permute-start.9 = (bf16[8,16,1600]{2,1,0:T(8,128)(2,1)S(1)}, bf16[8,16,1600]{2,1,0:T(8,128)(2,1)S(1)}, u32[]{:S(2)}, u32[]{:S(2)}) collective-permute-start(bf16[8,16,1600]{2,1,0:T(8,128)(2,1)S(1)} %shard_map.117.first_ref), channel_id=1, source_target_pairs={{0,2},{1,3},{2,0},{3,1},{4,6},{5,7},{6,4},{7,5},{8,10},{9,11},{10,... | collective-permute-start | bytes 1228808 | tf_op jit(solution)/shard_map/ppermute | solution.py:113
  27.5 37.3 %collective-permute-start.10 = (bf16[16,16,1600]{2,1,0:T(8,128)(2,1)S(1)}, bf16[16,16,1600]{2,1,0:T(8,128)(2,1)S(1)}, u32[]{:S(2)}, u32[]{:S(2)}) collective-permute-start(bf16[16,16,1600]{2,1,0:T(8,128)(2,1)S(1)} %shard_map.118.near_ref), channel_id=1, source_target_pairs={{0,1},{1,0},{2,3},{3,2},{4,5},{5,4},{6,7},{7,6},{8,9},{9,8},{10,11... | collective-permute-start | bytes 2457608 | tf_op jit(solution)/shard_map/ppermute | solution.py:113
  29.9 8.3 %collective-permute-start = (bf16[2,200,256]{2,1,0:T(8,128)(2,1)S(1)}, bf16[2,200,256]{2,1,0:T(8,128)(2,1)S(1)}, u32[]{:S(2)}, u32[]{:S(2)}) collective-permute-start(bf16[2,200,256]{2,1,0:T(8,128)(2,1)S(1)} %get-tuple-element.39), channel_id=1, source_target_pairs={{0,4},{4,0},{8,12},{12,8},{16,20},{20,16},{24,28},{28,24},{1,5},{5... | collective-permute-start | bytes 614408 | tf_op jit(solution)/shard_map/ppermute | solution.py:113
  31.7 22.0 %collective-permute-start.1 = (bf16[2,200,256]{2,1,0:T(8,128)(2,1)S(1)}, bf16[2,200,256]{2,1,0:T(8,128)(2,1)S(1)}, u32[]{:S(2)}, u32[]{:S(2)}) collective-permute-start(bf16[2,200,256]{2,1,0:T(8,128)(2,1)S(1)} %get-tuple-element.40), channel_id=1, source_target_pairs={{0,16},{4,20},{8,24},{12,28},{16,0},{20,4},{24,8},{28,12},{1,17},{... | collective-permute-start | bytes 614408 | tf_op jit(solution)/shard_map/ppermute | solution.py:113
  34.1 28.2 %collective-permute-start.2 = (bf16[2,200,256]{2,1,0:T(8,128)(2,1)S(1)}, bf16[2,200,256]{2,1,0:T(8,128)(2,1)S(1)}, u32[]{:S(2)}, u32[]{:S(2)}) collective-permute-start(bf16[2,200,256]{2,1,0:T(8,128)(2,1)S(1)} %get-tuple-element.41), channel_id=1, source_target_pairs={{0,20},{4,16},{8,28},{12,24},{16,4},{20,0},{24,12},{28,8},{1,21},{... | collective-permute-start | bytes 614408 | tf_op jit(solution)/shard_map/ppermute | solution.py:113
  34.3 28.7 %collective-permute-start.3 = (bf16[2,200,256]{2,1,0:T(8,128)(2,1)}, bf16[2,200,256]{2,1,0:T(8,128)(2,1)S(1)}, u32[]{:S(2)}, u32[]{:S(2)}) collective-permute-start(bf16[2,200,256]{2,1,0:T(8,128)(2,1)} %get-tuple-element.42), channel_id=1, source_target_pairs={{0,24},{4,28},{8,16},{12,20},{16,8},{20,12},{24,0},{28,4},{1,25},{... | collective-permute-start | bytes 614408 | tf_op jit(solution)/shard_map/ppermute | solution.py:113
  38.2 26.0 %collective-permute-start.4 = (bf16[2,200,256]{2,1,0:T(8,128)(2,1)S(1)}, bf16[2,200,256]{2,1,0:T(8,128)(2,1)S(1)}, u32[]{:S(2)}, u32[]{:S(2)}) collective-permute-start(bf16[2,200,256]{2,1,0:T(8,128)(2,1)S(1)} %get-tuple-element.45), channel_id=1, source_target_pairs={{0,8},{4,12},{8,0},{12,4},{16,24},{20,28},{24,16},{28,20},{1,9},{5... | collective-permute-start | bytes 614408 | tf_op jit(solution)/shard_map/ppermute | solution.py:113
  53.7 10.5 %collective-permute-start.5 = (bf16[2,200,256]{2,1,0:T(8,128)(2,1)S(1)}, bf16[2,200,256]{2,1,0:T(8,128)(2,1)S(1)}, u32[]{:S(2)}, u32[]{:S(2)}) collective-permute-start(bf16[2,200,256]{2,1,0:T(8,128)(2,1)S(1)} %get-tuple-element.46), channel_id=1, source_target_pairs={{0,28},{4,24},{8,20},{12,16},{16,12},{20,8},{24,4},{28,0},{1,29},{... | collective-permute-start | bytes 614408 | tf_op jit(solution)/shard_map/ppermute | solution.py:113
  62.2 7.0 %collective-permute-start.11 = (bf16[2,200,256]{2,1,0:T(8,128)(2,1)}, bf16[2,200,256]{2,1,0:T(8,128)(2,1)}, u32[]{:S(2)}, u32[]{:S(2)}) collective-permute-start(bf16[2,200,256]{2,1,0:T(8,128)(2,1)} %get-tuple-element.51), channel_id=1, source_target_pairs={{0,12},{4,8},{8,4},{12,0},{16,28},{20,24},{24,20},{28,16},{1,13},{... | collective-permute-start | bytes 614408 | tf_op jit(solution)/shard_map/ppermute | solution.py:113
  72.4 2.4 %collective-permute-start.12 = (bf16[2,16,8,1600]{3,2,1,0:T(8,128)(2,1)S(1)}, bf16[2,16,8,1600]{3,2,1,0:T(8,128)(2,1)S(1)}, u32[]{:S(2)}, u32[]{:S(2)}) collective-permute-start(bf16[2,16,8,1600]{3,2,1,0:T(8,128)(2,1)S(1)} %get-tuple-element.56), channel_id=1, source_target_pairs={{0,1},{1,0},{2,3},{3,2},{4,5},{5,4},{6,7},{7,6},{8,9},{9,8},{10,11... | collective-permute-start | bytes 2457608 | tf_op jit(solution)/shard_map/ppermute | solution.py:113
  75.1 11.9 %collective-permute-start.13 = (bf16[2,8,8,1600]{3,2,1,0:T(8,128)(2,1)S(1)}, bf16[2,8,8,1600]{3,2,1,0:T(8,128)(2,1)S(1)}, u32[]{:S(2)}, u32[]{:S(2)}) collective-permute-start(bf16[2,8,8,1600]{3,2,1,0:T(8,128)(2,1)S(1)} %get-tuple-element.58), channel_id=1, source_target_pairs={{0,2},{1,3},{2,0},{3,1},{4,6},{5,7},{6,4},{7,5},{8,10},{9,11},{10,... | collective-permute-start | bytes 1228808 | tf_op jit(solution)/shard_map/ppermute | solution.py:113
  76.9 19.4 %collective-permute-start.14 = (bf16[2,256,256]{2,1,0:T(8,128)(2,1)S(1)}, bf16[2,256,256]{2,1,0:T(8,128)(2,1)S(1)}, u32[]{:S(2)}, u32[]{:S(2)}) collective-permute-start(bf16[2,256,256]{2,1,0:T(8,128)(2,1)S(1)} %get-tuple-element.52.both_ref.first_ref), channel_id=1, source_target_pairs={{0,16},{4,20},{8,24},{12,28},{16,0},{20,4},{24,8},{28,12},{1,17},{... | collective-permute-start | bytes 786440 | tf_op jit(solution)/shard_map/ppermute | solution.py:113
  87.8 36.8 %all-to-all-start = ((bf16[8,16,1600]{2,1,0:T(8,128)(2,1)}), bf16[8,16,1600]{2,1,0:T(8,128)(2,1)S(1)}, u32[]{:S(2)}, u32[]{:S(2)}) async-start(bf16[8,16,1600]{2,1,0:T(8,128)(2,1)} %shard_map.123), calls=%async_computation | async-start | bytes 851968 | tf_op jit(solution)/shard_map/all_to_all | solution.py:575
  96.3 16.2 %collective-permute-start.15 = (bf16[2,256,256]{2,1,0:T(8,128)(2,1)S(1)}, bf16[2,256,256]{2,1,0:T(8,128)(2,1)S(1)}, u32[]{:S(2)}, u32[]{:S(2)}) collective-permute-start(bf16[2,256,256]{2,1,0:T(8,128)(2,1)S(1)} %get-tuple-element.62.hidden_ref), channel_id=1, source_target_pairs={{0,8},{4,12},{8,0},{12,4},{16,24},{20,28},{24,16},{28,20},{1,9},{5... | collective-permute-start | bytes 786440 | tf_op jit(solution)/shard_map/ppermute | solution.py:113
  98.4 15.0 %collective-permute-start.17 = (bf16[2,256,256]{2,1,0:T(8,128)(2,1)S(1)}, bf16[2,256,256]{2,1,0:T(8,128)(2,1)S(1)}, u32[]{:S(2)}, u32[]{:S(2)}) collective-permute-start(bf16[2,256,256]{2,1,0:T(8,128)(2,1)S(1)} %get-tuple-element.63.pre_ref), channel_id=1, source_target_pairs={{0,4},{4,0},{8,12},{12,8},{16,20},{20,16},{24,28},{28,24},{1,5},{5... | collective-permute-start | bytes 786440 | tf_op jit(solution)/shard_map/ppermute | solution.py:113
  99.9 19.9 %collective-permute-start.19 = (bf16[2,256,256]{2,1,0:T(8,128)(2,1)S(1)}, bf16[2,256,256]{2,1,0:T(8,128)(2,1)S(1)}, u32[]{:S(2)}, u32[]{:S(2)}) collective-permute-start(bf16[2,256,256]{2,1,0:T(8,128)(2,1)S(1)} %get-tuple-element.62.hidden_ref), channel_id=1, source_target_pairs={{0,4},{4,0},{8,12},{12,8},{16,20},{20,16},{24,28},{28,24},{1,5},{5... | collective-permute-start | bytes 786440 | tf_op jit(solution)/shard_map/ppermute | solution.py:113
  100.4 19.3 %collective-permute-start.20 = (bf16[2,256,256]{2,1,0:T(8,128)(2,1)S(1)}, bf16[2,256,256]{2,1,0:T(8,128)(2,1)S(1)}, u32[]{:S(2)}, u32[]{:S(2)}) collective-permute-start(bf16[2,256,256]{2,1,0:T(8,128)(2,1)S(1)} %get-tuple-element.63.pre_ref), channel_id=1, source_target_pairs={{0,8},{4,12},{8,0},{12,4},{16,24},{20,28},{24,16},{28,20},{1,9},{5... | collective-permute-start | bytes 786440 | tf_op jit(solution)/shard_map/ppermute | solution.py:113
  112.5 9.6 %collective-permute-start.16 = (bf16[2,256,256]{2,1,0:T(8,128)(2,1)S(1)}, bf16[2,256,256]{2,1,0:T(8,128)(2,1)S(1)}, u32[]{:S(2)}, u32[]{:S(2)}) collective-permute-start(bf16[2,256,256]{2,1,0:T(8,128)(2,1)S(1)} %collective-permute-done.15.hidden_ref), channel_id=1, source_target_pairs={{0,4},{4,0},{8,12},{12,8},{16,20},{20,16},{24,28},{28,24},{1,5},{5... | collective-permute-start | bytes 786440 | tf_op jit(solution)/shard_map/ppermute | solution.py:113
  113.4 8.8 %collective-permute-start.18 = (bf16[2,256,256]{2,1,0:T(8,128)(2,1)S(1)}, bf16[2,256,256]{2,1,0:T(8,128)(2,1)S(1)}, u32[]{:S(2)}, u32[]{:S(2)}) collective-permute-start(bf16[2,256,256]{2,1,0:T(8,128)(2,1)S(1)} %collective-permute-done.17.pre_ref), channel_id=1, source_target_pairs={{0,8},{4,12},{8,0},{12,4},{16,24},{20,28},{24,16},{28,20},{1,9},{5... | collective-permute-start | bytes 786440 | tf_op jit(solution)/shard_map/ppermute | solution.py:113
  122.2 2.4 %copy-start = (bf16[8,1600]{1,0:T(8,128)(2,1)S(1)}, bf16[8,1600]{1,0:T(8,128)(2,1)}, u32[]{:S(2)}) copy-start(bf16[8,1600]{1,0:T(8,128)(2,1)} %patch_ref.1) | copy-start | bytes 76804
  122.2 2.4 %copy-start.1 = (bf16[16,1600]{1,0:T(8,128)(2,1)S(1)}, bf16[16,1600]{1,0:T(8,128)(2,1)}, u32[]{:S(2)}) copy-start(bf16[16,1600]{1,0:T(8,128)(2,1)} %text_ref.1) | copy-start | bytes 153604
  122.2 2.4 %copy-start.2 = (s32[1,4]{1,0:T(1,128)S(1)}, s32[1,4]{1,0:T(1,128)}, u32[]{:S(2)}) copy-start(s32[1,4]{1,0:T(1,128)} %count_ref.1) | copy-start | bytes 52
  122.2 2.4 %copy-start.3 = (s32[1,8]{1,0:T(1,128)S(1)}, s32[1,8]{1,0:T(1,128)}, u32[]{:S(2)}) copy-start(s32[1,8]{1,0:T(1,128)} %place_ref.1) | copy-start | bytes 100

commit v7 on v6

--- a/solution.py
+++ b/solution.py
@@ -342,26 +342,20 @@
         out_ref[d] = jnp.concatenate([total[0, d], total[1, d]], axis=0).astype(jnp.bfloat16)
 
 
-def weight_grad_kernel(
-    hidden_distances, pre_distances, hidden_ref, pre_ref, grad_ref, normed_ref, *refs
-):
+def weight_grad_kernel(distances, grad_ref, normed_ref, *refs):
     project_at, expand_at, result_ref, sems = refs[-4:]
-    _, count, features, units = result_ref.shape
+    blocks = refs[: len(distances)]
+    features, units = result_ref.shape[2:]
     pieces = sems.shape[2]
     piece = features // pieces
     copies = []
-    for i in range(count):
-        for k, (block_ref, rows_ref, out_at, distances) in enumerate(
-            (
-                (pre_ref, normed_ref, expand_at, pre_distances),
-                (hidden_ref, grad_ref, project_at, hidden_distances),
-            )
-        ):
+    for i, (distance, block_ref) in enumerate(zip(distances, blocks)):
+        source = lax.axis_index("dp") ^ distance
+        columns = pl.ds(pl.multiple_of(source * units, 128), units)
+        for k, (rows_ref, out_at) in enumerate(((grad_ref, project_at), (normed_ref, expand_at))):
             result_ref[k, i] = jnp.dot(
-                rows_ref[...], block_ref[i], preferred_element_type=jnp.float32
+                rows_ref[...], block_ref[k], preferred_element_type=jnp.float32
             ).astype(jnp.bfloat16)
-            source = lax.axis_index("dp") ^ distances[i]
-            columns = pl.ds(pl.multiple_of(source * units, 128), units)
             for j in range(pieces):
                 at = pl.ds(j * piece, piece)
                 copies.append(
@@ -407,30 +401,30 @@
     ).astype(jnp.bfloat16)
 
 
-def weight_grads(
-    hidden, hidden_distances, pre, pre_distances, grad_turned, normed_turned, width, before
-):
-    count, rows, units = hidden.shape
+def weight_grads(blocks, distances, grad_turned, normed_turned, width, before):
+    count = len(blocks)
+    _, rows, units = blocks[0].shape
     features = grad_turned.shape[0]
     pieces = 2 if features % 32 == 0 else 1
     anywhere = pl.BlockSpec(memory_space=pl.ANY)
+    aliases = {2 + count: 0, 3 + count: 1} if before else {}
     return pl.pallas_call(
-        functools.partial(weight_grad_kernel, hidden_distances, pre_distances),
-        in_specs=[VMEM_SPEC] * 4 + [anywhere] * len(before),
+        functools.partial(weight_grad_kernel, distances),
+        in_specs=[VMEM_SPEC] * (2 + count) + [anywhere] * len(before),
         out_specs=[anywhere] * 2,
         out_shape=[jax.ShapeDtypeStruct((features, width), jnp.bfloat16)] * 2,
         scratch_shapes=[
             pltpu.VMEM((2, count, features, units), jnp.bfloat16),
             pltpu.SemaphoreType.DMA((2, count, pieces)),
         ],
-        input_output_aliases={4: 0, 5: 1} if before else {},
+        input_output_aliases=aliases,
         compiler_params=pltpu.CompilerParams(vmem_limit_bytes=12 << 20),
         cost_estimate=pl.CostEstimate(
             flops=4 * count * rows * features * units,
             bytes_accessed=4 * count * units * features + 4 * rows * features,
             transcendentals=0,
         ),
-    )(hidden, pre, grad_turned, normed_turned, *before)
+    )(grad_turned, normed_turned, *blocks, *before)
 
 
 def call(kernel, out_shape, smem, vmem, scratch=()):
@@ -458,15 +452,20 @@
     return call(join_kernel, jax.ShapeDtypeStruct(both, first.dtype), (), (first, second))
 
 
-def join_pairs_kernel(first_ref, second_ref, hidden_ref, pre_ref):
-    for k, out_ref in enumerate((hidden_ref, pre_ref)):
-        out_ref[0] = first_ref[k]
-        out_ref[1] = second_ref[k]
-
-
-def join_pairs(first, second):
-    out = jax.ShapeDtypeStruct(first.shape, first.dtype)
-    return call(join_pairs_kernel, [out, out], (), (first, second))
+def unit_order(dp):
+    far = 1 << (dp - 1)
+
+    def key(distance):
+        hops = distance.bit_count()
+        return (hops, hops > 1 and distance >= far, -distance)
+
+    return sorted(range(1, 2 * far), key=key)
+
+
+def gradient_groups(dp):
+    order = unit_order(dp)
+    order = order[1:dp] + order[dp : dp + 1] + order[:1] + order[dp + 1 :]
+    return [(0,)] + [tuple(order[i : i + 2]) for i in range(0, len(order), 2)]
 
 
 def move_rows_plan(
@@ -574,20 +573,14 @@
     tail = call(address_kernel, shape((replicas, 2 * slots, features), kept), (), (keep, got))
     tail = lax.all_to_all(tail, "dp", split_axis=0, concat_axis=0, tiled=True)
 
-    far_both = swap(both, "dp", dp_steps[0])
-    pairs = join_pairs(both, far_both)
-    gathered = []
-    for pair, steps in ((pairs[0], dp_steps[1:]), (pairs[1], dp_steps[:0:-1])):
-        held_pairs = {0: pair}
-        for step in steps:
-            for mask, array in list(held_pairs.items()):
-                held_pairs[mask ^ step] = swap(array, "dp", step)
-        gathered.append(held_pairs.items())
+    units_from = {0: both}
+    for step in dp_steps:
+        for distance, block in list(units_from.items()):
+            units_from[distance ^ step] = swap(block, "dp", step)
     grads = ()
-    for (hidden_mask, hidden), (pre_mask, pre) in zip(*gathered):
-        far = dp_steps[0]
+    for distances in gradient_groups(log2(replicas)):
         grads = weight_grads(
-            hidden, (hidden_mask, hidden_mask ^ far), pre, (pre_mask, pre_mask ^ far),
+            [units_from[distance] for distance in distances], distances,
             grad_turned, normed_turned, width, grads,
         )
     project_grad, expand_grad = grads

time: 126 us -> 130 us (1.032)
    pallas_call x4 -> x5, Pallas kernels: 9.43 us -> 10.6 us  [weight_grads(): pl.pallas_call(functools.partial(weight_grad_kernel, distances), in_specs...]
    pallas_call x11 -> x10, Pallas kernels: 6.54 us -> 6.5 us  [call(): pl.pallas_call(kernel, out_shape=out_shape, in_specs=[SMEM_SPEC] * len(sm...]
  transfers between devices with their start and end apart: 22 -> 22, of which waited for: 10 -> 12; matrix products, arithmetic and copies ran while one was open for 1% -> 1% of each run, Pallas kernels for 13% -> 14%
where the time goes in v7:
time: 130 us; the launch traced here: 129 us
  waiting for transfers between devices  58.9 us (45%)
  starting transfers between devices  44.6 us (34%)
  Pallas kernels  24 us (18%)
    ppermute x21, waiting for transfers between devices, swap(): return lax.ppermute(array, axis, [(i, i ^ step) for i in range(size)])  58.9 us
    ppermute x21, starting transfers between devices, swap(): return lax.ppermute(array, axis, [(i, i ^ step) for i in range(size)])  36.1 us
    pallas_call x5, Pallas kernels, weight_grads(): pl.pallas_call(functools.partial(weight_grad_kernel, distances), in_specs...  10.6 us
    all_to_all x1, starting transfers between devices, move_rows_plan(): tail = lax.all_to_all(tail, 'dp', split_axis=0, concat_axis=0, tiled=True)  8.46 us
    pallas_call x10, Pallas kernels, call(): pl.pallas_call(kernel, out_shape=out_shape, in_specs=[SMEM_SPEC] * len(sm...  6.5 us
    pallas_call x3, Pallas kernels, unpacking(): pl.pallas_call(functools.partial(kernel, group), out_shape=[*slices, *ext...  3.51 us
  transfers between devices with their start and end apart: 22, of which 12 were waited for; matrix products, arithmetic and copies ran while one was open for 1% of the time, Pallas kernels for 14%

profile of v7, /device:TPU:0, one launch (start us, length us, event | category | flops | bytes accessed | tf_op | source)
XLA Modules:
  0.0 129.1 jit_solution(3376249633759221026)
XLA Ops:
  0.6 1.0 shard_map.114.first_ref
  1.6 4.1 %collective-permute-start.6 = (bf16[1,16,1600]{2,1,0:T(8,128)(2,1)S(1)}, bf16[1,16,1600]{2,1,0:T(8,128)(2,1)S(1)}, u32[]{:S(2)}, u32[]{:S(2)}) collective-permute-start(bf16[1,16,1600]{2,1,0:T(8,128)(2,1)S(1)} %shard_map.114.first_ref), channel_id=1, source_target_pairs={{0,16},{4,20},{8,24},{12,28},{16,0},{20,4},{24,8},{28,12},{1,17},{... | collective-permute-start | bytes 153608 | tf_op jit(solution)/shard_map/ppermute | solution.py:113
  5.8 2.7 %collective-permute-done.6.second_ref = bf16[1,16,1600]{2,1,0:T(8,128)(2,1)S(1)} collective-permute-done((bf16[1,16,1600]{2,1,0:T(8,128)(2,1)S(1)}, bf16[1,16,1600]{2,1,0:T(8,128)(2,1)S(1)}, u32[]{:S(2)}, u32[]{:S(2)}) %collective-permute-start.6) | collective-permute-done | bytes 51232 | tf_op jit(solution)/shard_map/ppermute | solution.py:113
  8.5 1.4 %collective-permute-start.7 = (bf16[2,16,1600]{2,1,0:T(8,128)(2,1)S(1)}, bf16[2,16,1600]{2,1,0:T(8,128)(2,1)S(1)}, u32[]{:S(2)}, u32[]{:S(2)}) collective-permute-start(bf16[2,16,1600]{2,1,0:T(8,128)(2,1)S(1)} %shard_map.115.first_ref), channel_id=1, source_target_pairs={{0,8},{4,12},{8,0},{12,4},{16,24},{20,28},{24,16},{28,20},{1,9},{5... | collective-permute-start | bytes 307208 | tf_op jit(solution)/shard_map/ppermute | solution.py:113
  9.9 3.4 %collective-permute-done.7.second_ref = bf16[2,16,1600]{2,1,0:T(8,128)(2,1)S(1)} collective-permute-done((bf16[2,16,1600]{2,1,0:T(8,128)(2,1)S(1)}, bf16[2,16,1600]{2,1,0:T(8,128)(2,1)S(1)}, u32[]{:S(2)}, u32[]{:S(2)}) %collective-permute-start.7) | collective-permute-done | bytes 102432 | tf_op jit(solution)/shard_map/ppermute | solution.py:113
  13.3 1.8 %collective-permute-start.8 = (bf16[4,16,1600]{2,1,0:T(8,128)(2,1)S(1)}, bf16[4,16,1600]{2,1,0:T(8,128)(2,1)S(1)}, u32[]{:S(2)}, u32[]{:S(2)}) collective-permute-start(bf16[4,16,1600]{2,1,0:T(8,128)(2,1)S(1)} %shard_map.116.first_ref), channel_id=1, source_target_pairs={{0,4},{4,0},{8,12},{12,8},{16,20},{20,16},{24,28},{28,24},{1,5},{5... | collective-permute-start | bytes 614408 | tf_op jit(solution)/shard_map/ppermute | solution.py:113
  15.0 4.1 %collective-permute-done.8.second_ref = bf16[4,16,1600]{2,1,0:T(8,128)(2,1)S(1)} collective-permute-done((bf16[4,16,1600]{2,1,0:T(8,128)(2,1)S(1)}, bf16[4,16,1600]{2,1,0:T(8,128)(2,1)S(1)}, u32[]{:S(2)}, u32[]{:S(2)}) %collective-permute-start.8) | collective-permute-done | bytes 204832 | tf_op jit(solution)/shard_map/ppermute | solution.py:113
  19.2 1.8 %collective-permute-start.9 = (bf16[8,16,1600]{2,1,0:T(8,128)(2,1)S(1)}, bf16[8,16,1600]{2,1,0:T(8,128)(2,1)S(1)}, u32[]{:S(2)}, u32[]{:S(2)}) collective-permute-start(bf16[8,16,1600]{2,1,0:T(8,128)(2,1)S(1)} %shard_map.117.first_ref), channel_id=1, source_target_pairs={{0,2},{1,3},{2,0},{3,1},{4,6},{5,7},{6,4},{7,5},{8,10},{9,11},{10,... | collective-permute-start | bytes 1228808 | tf_op jit(solution)/shard_map/ppermute | solution.py:113
  21.0 6.4 %collective-permute-done.9.second_ref = bf16[8,16,1600]{2,1,0:T(8,128)(2,1)S(1)} collective-permute-done((bf16[8,16,1600]{2,1,0:T(8,128)(2,1)S(1)}, bf16[8,16,1600]{2,1,0:T(8,128)(2,1)S(1)}, u32[]{:S(2)}, u32[]{:S(2)}) %collective-permute-start.9) | collective-permute-done | bytes 409632 | tf_op jit(solution)/shard_map/ppermute | solution.py:113
  27.5 2.3 %shard_map.111 = (bf16[2,200,256]{2,1,0:T(8,128)(2,1)S(1)}, bf16[2,200,256]{2,1,0:T(8,128)(2,1)S(1)}, bf16[2,200,256]{2,1,0:T(8,128)(2,1)}, bf16[2,200,256]{2,1,...) custom-call(bf16[200,2048]{1,0:T(8,128)(2,1)} %own_expand_at.1, ...), custom_call_target="tpu_custom_call" | custom-call | tf_op jit(solution)/shard_map/pallas_call | solution.py:508
  29.9 1.8 %collective-permute-start = (bf16[2,200,256]{2,1,0:T(8,128)(2,1)S(1)}, bf16[2,200,256]{2,1,0:T(8,128)(2,1)S(1)}, u32[]{:S(2)}, u32[]{:S(2)}) collective-permute-start(bf16[2,200,256]{2,1,0:T(8,128)(2,1)S(1)} %get-tuple-element.39), channel_id=1, source_target_pairs={{0,4},{4,0},{8,12},{12,8},{16,20},{20,16},{24,28},{28,24},{1,5},{5... | collective-permute-start | bytes 614408 | tf_op jit(solution)/shard_map/ppermute | solution.py:113
  31.7 2.4 %collective-permute-start.1 = (bf16[2,200,256]{2,1,0:T(8,128)(2,1)S(1)}, bf16[2,200,256]{2,1,0:T(8,128)(2,1)S(1)}, u32[]{:S(2)}, u32[]{:S(2)}) collective-permute-start(bf16[2,200,256]{2,1,0:T(8,128)(2,1)S(1)} %get-tuple-element.40), channel_id=1, source_target_pairs={{0,16},{4,20},{8,24},{12,28},{16,0},{20,4},{24,8},{28,12},{1,17},{... | collective-permute-start | bytes 614408 | tf_op jit(solution)/shard_map/ppermute | solution.py:113
  34.1 0.3 collective-permute-start.2
  34.3 3.8 %collective-permute-start.3 = (bf16[2,200,256]{2,1,0:T(8,128)(2,1)}, bf16[2,200,256]{2,1,0:T(8,128)(2,1)S(1)}, u32[]{:S(2)}, u32[]{:S(2)}) collective-permute-start(bf16[2,200,256]{2,1,0:T(8,128)(2,1)} %get-tuple-element.42), channel_id=1, source_target_pairs={{0,24},{4,28},{8,16},{12,20},{16,8},{20,12},{24,0},{28,4},{1,25},{... | collective-permute-start | bytes 614408 | tf_op jit(solution)/shard_map/ppermute | solution.py:113
  38.2 0.7 collective-permute-start.4
  38.8 14.9 %collective-permute-done.1.refs_1_ = bf16[2,200,256]{2,1,0:T(8,128)(2,1)S(1)} collective-permute-done((bf16[2,200,256]{2,1,0:T(8,128)(2,1)S(1)}, bf16[2,200,256]{2,1,0:T(8,128)(2,1)S(1)}, u32[]{:S(2)}, u32[]{:S(2)}) %collective-permute-start.1) | collective-permute-done | bytes 204832 | tf_op jit(solution)/shard_map/ppermute | solution.py:113
  53.7 2.7 %collective-permute-start.5 = (bf16[2,200,256]{2,1,0:T(8,128)(2,1)S(1)}, bf16[2,200,256]{2,1,0:T(8,128)(2,1)S(1)}, u32[]{:S(2)}, u32[]{:S(2)}) collective-permute-start(bf16[2,200,256]{2,1,0:T(8,128)(2,1)S(1)} %get-tuple-element.46), channel_id=1, source_target_pairs={{0,28},{4,24},{8,20},{12,16},{16,12},{20,8},{24,4},{28,0},{1,29},{... | collective-permute-start | bytes 614408 | tf_op jit(solution)/shard_map/ppermute | solution.py:113
  56.4 5.9 %collective-permute-done.2.refs_2_ = bf16[2,200,256]{2,1,0:T(8,128)(2,1)S(1)} collective-permute-done((bf16[2,200,256]{2,1,0:T(8,128)(2,1)S(1)}, bf16[2,200,256]{2,1,0:T(8,128)(2,1)S(1)}, u32[]{:S(2)}, u32[]{:S(2)}) %collective-permute-start.2) | collective-permute-done | bytes 204832 | tf_op jit(solution)/shard_map/ppermute | solution.py:113
  62.2 0.7 reshape.11.gain_ref
  62.9 0.1 pad_add_fusion.me_ref
  63.0 1.1 shard_map.112
  64.2 0.6 shard_map.113
  64.8 2.0 %shard_map.119 = (bf16[256,1600]{1,0:T(8,128)(2,1)S(1)}, bf16[256,1600]{1,0:T(8,128)(2,1)S(1)}, f32[16,1600]{1,0:T(8,128)S(1)}) custom-call(s32[2]{0:T(128)S(1)} %pad_add_fusion.me_ref, bf16[16,16,1600]{2,1,0:T(8,128)(2,1)S(1)} %shard_map.118.near_ref, bf16[16,16,1600]{2,1,0:T(8,128)(2,1)S(1)} %collective-permute-done.10.far_ref, f32[1,1600]{1,0:T(1,128)S(1)} %reshape.11.gain_ref), custom_call_target="tpu_custom_call" | custom-call | tf_op jit(solution)/shard_map/pallas_call | solution.py:432
  66.8 2.4 %collective-permute-done.11.refs_0_ = bf16[2,200,256]{2,1,0:T(8,128)(2,1)} collective-permute-done((bf16[2,200,256]{2,1,0:T(8,128)(2,1)}, bf16[2,200,256]{2,1,0:T(8,128)(2,1)}, u32[]{:S(2)}, u32[]{:S(2)}) %collective-permute-start.11) | collective-permute-done | bytes 204832 | tf_op jit(solution)/shard_map/ppermute | solution.py:113
  69.2 1.8 %shard_map.120 = (bf16[1600,256]{1,0:T(8,128)(2,1)S(1)}, bf16[1600,256]{1,0:T(8,128)(2,1)S(1)}, bf16[2,256,256]{2,1,0:T(8,128)(2,1)S(1)}) custom-call(bf16[1600,256]{1,0:T(8,128)(2,1)S(1)} %get-tuple-element.47.expand_part_ref, bf16[1600,256]{1,0:T(8,128)(2,1)S(1)} %get-tuple-element.48.project_part_ref, ...), custom_call_target="tpu_custom_call", output_to_operand_aliasing={{0}: (0, {}), {1}: (1, {})} | custom-call | tf_op jit(solution)/shard_map/pallas_call | solution.py:538
  71.0 1.4 %shard_map.121 = (f32[2,16,8,1600]{3,2,1,0:T(8,128)S(1)}, bf16[2,16,8,1600]{3,2,1,0:T(8,128)(2,1)S(1)}) custom-call(s32[2]{0:T(128)S(1)} %pad_add_fusion.me_ref, bf16[2,256,256]{2,1,0:T(8,128)(2,1)S(1)} %get-tuple-element.52.both_ref.refs_0_, bf16[1600,256]{1,0:T(8,128)(2,1)S(1)} %get-tuple-element.53.expand_ref, ...), custom_call_target="tpu_custom_call" | custom-call | tf_op jit(solution)/shard_map/pallas_call | solution.py:432
  72.5 2.4 %collective-permute-done.12.got_ref = bf16[2,16,8,1600]{3,2,1,0:T(8,128)(2,1)S(1)} collective-permute-done((bf16[2,16,8,1600]{3,2,1,0:T(8,128)(2,1)S(1)}, bf16[2,16,8,1600]{3,2,1,0:T(8,128)(2,1)S(1)}, u32[]{:S(2)}, u32[]{:S(2)}) %collective-permute-start.12) | collective-permute-done | bytes 819232 | tf_op jit(solution)/shard_map/ppermute | solution.py:113
  74.9 0.2 shard_map.122
  75.1 1.8 %collective-permute-start.13 = (bf16[2,8,8,1600]{3,2,1,0:T(8,128)(2,1)S(1)}, bf16[2,8,8,1600]{3,2,1,0:T(8,128)(2,1)S(1)}, u32[]{:S(2)}, u32[]{:S(2)}) collective-permute-start(bf16[2,8,8,1600]{3,2,1,0:T(8,128)(2,1)S(1)} %get-tuple-element.58), channel_id=1, source_target_pairs={{0,2},{1,3},{2,0},{3,1},{4,6},{5,7},{6,4},{7,5},{8,10},{9,11},{10,... | collective-permute-start | bytes 1228808 | tf_op jit(solution)/shard_map/ppermute | solution.py:113
  76.9 6.4 %collective-permute-start.14 = (bf16[2,256,256]{2,1,0:T(8,128)(2,1)S(1)}, bf16[2,256,256]{2,1,0:T(8,128)(2,1)S(1)}, u32[]{:S(2)}, u32[]{:S(2)}) collective-permute-start(bf16[2,256,256]{2,1,0:T(8,128)(2,1)S(1)} %get-tuple-element.52.both_ref.refs_0_), channel_id=1, source_target_pairs={{0,16},{4,20},{8,24},{12,28},{16,0},{20,4},{24,8},{28,12},{1,17},{... | collective-permute-start | bytes 786440 | tf_op jit(solution)/shard_map/ppermute | solution.py:113
  83.3 3.7 %collective-permute-done.13.got_ref = bf16[2,8,8,1600]{3,2,1,0:T(8,128)(2,1)S(1)} collective-permute-done((bf16[2,8,8,1600]{3,2,1,0:T(8,128)(2,1)S(1)}, bf16[2,8,8,1600]{3,2,1,0:T(8,128)(2,1)S(1)}, u32[]{:S(2)}, u32[]{:S(2)}) %collective-permute-start.13) | collective-permute-done | bytes 409632 | tf_op jit(solution)/shard_map/ppermute | solution.py:113
  87.0 0.8 shard_map.123
  87.8 8.5 %all-to-all-start = ((bf16[8,16,1600]{2,1,0:T(8,128)(2,1)}), bf16[8,16,1600]{2,1,0:T(8,128)(2,1)S(1)}, u32[]{:S(2)}, u32[]{:S(2)}) async-start(bf16[8,16,1600]{2,1,0:T(8,128)(2,1)} %shard_map.123), calls=%async_computation | async-start | bytes 851968 | tf_op jit(solution)/shard_map/all_to_all | solution.py:574
  96.3 2.0 %collective-permute-start.15 = (bf16[2,256,256]{2,1,0:T(8,128)(2,1)S(1)}, bf16[2,256,256]{2,1,0:T(8,128)(2,1)S(1)}, u32[]{:S(2)}, u32[]{:S(2)}) collective-permute-start(bf16[2,256,256]{2,1,0:T(8,128)(2,1)S(1)} %collective-permute-done.14.refs_1_), channel_id=1, source_target_pairs={{0,8},{4,12},{8,0},{12,4},{16,24},{20,28},{24,16},{28,20},{1,9},{5... | collective-permute-start | bytes 786440 | tf_op jit(solution)/shard_map/ppermute | solution.py:113
  98.3 1.5 %collective-permute-start.20 = (bf16[2,256,256]{2,1,0:T(8,128)(2,1)S(1)}, bf16[2,256,256]{2,1,0:T(8,128)(2,1)S(1)}, u32[]{:S(2)}, u32[]{:S(2)}) collective-permute-start(bf16[2,256,256]{2,1,0:T(8,128)(2,1)S(1)} %get-tuple-element.52.both_ref.refs_0_), channel_id=1, source_target_pairs={{0,4},{4,0},{8,12},{12,8},{16,20},{20,16},{24,28},{28,24},{1,5},{5... | collective-permute-start | bytes 786440 | tf_op jit(solution)/shard_map/ppermute | solution.py:113
  99.8 0.6 collective-permute-start.19
  100.3 1.5 %collective-permute-start.17 = (bf16[2,256,256]{2,1,0:T(8,128)(2,1)S(1)}, bf16[2,256,256]{2,1,0:T(8,128)(2,1)S(1)}, u32[]{:S(2)}, u32[]{:S(2)}) collective-permute-start(bf16[2,256,256]{2,1,0:T(8,128)(2,1)S(1)} %collective-permute-done.14.refs_1_), channel_id=1, source_target_pairs={{0,4},{4,0},{8,12},{12,8},{16,20},{20,16},{24,28},{28,24},{1,5},{5... | collective-permute-start | bytes 786440 | tf_op jit(solution)/shard_map/ppermute | solution.py:113
  101.8 0.5 shard_map.125
  102.3 8.2 %collective-permute-done.15.refs_0_ = bf16[2,256,256]{2,1,0:T(8,128)(2,1)S(1)} collective-permute-done((bf16[2,256,256]{2,1,0:T(8,128)(2,1)S(1)}, bf16[2,256,256]{2,1,0:T(8,128)(2,1)S(1)}, u32[]{:S(2)}, u32[]{:S(2)}) %collective-permute-start.15) | collective-permute-done | bytes 262176 | tf_op jit(solution)/shard_map/ppermute | solution.py:113
  110.5 1.5 %collective-permute-start.16 = (bf16[2,256,256]{2,1,0:T(8,128)(2,1)S(1)}, bf16[2,256,256]{2,1,0:T(8,128)(2,1)S(1)}, u32[]{:S(2)}, u32[]{:S(2)}) collective-permute-start(bf16[2,256,256]{2,1,0:T(8,128)(2,1)S(1)} %collective-permute-done.15.refs_0_), channel_id=1, source_target_pairs={{0,4},{4,0},{8,12},{12,8},{16,20},{20,16},{24,28},{28,24},{1,5},{5... | collective-permute-start | bytes 786440 | tf_op jit(solution)/shard_map/ppermute | solution.py:113
  112.1 1.8 %shard_map.126 = (bf16[1600,2048]{1,0:T(8,128)(2,1)}, bf16[1600,2048]{1,0:T(8,128)(2,1)}) custom-call(bf16[1600,256]{1,0:T(8,128)(2,1)S(1)} %get-tuple-element.62.grad_ref, bf16[1600,256]{1,0:T(8,128)(2,1)S(1)} %get-tuple-element.63.normed_ref, bf16[2,256,256]{2,1,0:T(8,128)(2,1)S(1)} %get-tuple-element.52.both_ref.refs_0_), custom_call_target="tpu_custom_call" | custom-call | flops 419430400 | bytes 3276800 | tf_op jit(solution)/shard_map/pallas_call | solution.py:411
  113.9 2.4 %shard_map.127 = (bf16[1600,2048]{1,0:T(8,128)(2,1)}, bf16[1600,2048]{1,0:T(8,128)(2,1)}) custom-call(bf16[1600,256]{1,0:T(8,128)(2,1)S(1)} %get-tuple-element.62.grad_ref, bf16[1600,256]{1,0:T(8,128)(2,1)S(1)} %get-tuple-element.63.normed_ref, ...), custom_call_target="tpu_custom_call", output_to_operand_aliasing={{0}: (4, {}), {1}: (5, {})} | custom-call | flops 838860800 | bytes 4915200 | tf_op jit(solution)/shard_map/pallas_call | solution.py:411
  116.2 2.4 %shard_map.128 = (bf16[1600,2048]{1,0:T(8,128)(2,1)}, bf16[1600,2048]{1,0:T(8,128)(2,1)}) custom-call(bf16[1600,256]{1,0:T(8,128)(2,1)S(1)} %get-tuple-element.62.grad_ref, bf16[1600,256]{1,0:T(8,128)(2,1)S(1)} %get-tuple-element.63.normed_ref, ...), custom_call_target="tpu_custom_call", output_to_operand_aliasing={{0}: (4, {}), {1}: (5, {})} | custom-call | flops 838860800 | bytes 4915200 | tf_op jit(solution)/shard_map/pallas_call | solution.py:411
  118.6 2.5 %collective-permute-done.17.refs_1_ = bf16[2,256,256]{2,1,0:T(8,128)(2,1)S(1)} collective-permute-done((bf16[2,256,256]{2,1,0:T(8,128)(2,1)S(1)}, bf16[2,256,256]{2,1,0:T(8,128)(2,1)S(1)}, u32[]{:S(2)}, u32[]{:S(2)}) %collective-permute-start.17) | collective-permute-done | bytes 262176 | tf_op jit(solution)/shard_map/ppermute | solution.py:113
  121.1 2.4 %shard_map.129 = (bf16[1600,2048]{1,0:T(8,128)(2,1)}, bf16[1600,2048]{1,0:T(8,128)(2,1)}) custom-call(bf16[1600,256]{1,0:T(8,128)(2,1)S(1)} %get-tuple-element.62.grad_ref, bf16[1600,256]{1,0:T(8,128)(2,1)S(1)} %get-tuple-element.63.normed_ref, ...), custom_call_target="tpu_custom_call", output_to_operand_aliasing={{0}: (4, {}), {1}: (5, {})} | custom-call | flops 838860800 | bytes 4915200 | tf_op jit(solution)/shard_map/pallas_call | solution.py:411
  123.4 2.4 %collective-permute-done.16.refs_0_ = bf16[2,256,256]{2,1,0:T(8,128)(2,1)S(1)} collective-permute-done((bf16[2,256,256]{2,1,0:T(8,128)(2,1)S(1)}, bf16[2,256,256]{2,1,0:T(8,128)(2,1)S(1)}, u32[]{:S(2)}, u32[]{:S(2)}) %collective-permute-start.16) | collective-permute-done | bytes 262176 | tf_op jit(solution)/shard_map/ppermute | solution.py:113
  125.8 1.8 %shard_map.130 = (bf16[1600,2048]{1,0:T(8,128)(2,1)}, bf16[1600,2048]{1,0:T(8,128)(2,1)}) custom-call(bf16[1600,256]{1,0:T(8,128)(2,1)S(1)} %get-tuple-element.62.grad_ref, bf16[1600,256]{1,0:T(8,128)(2,1)S(1)} %get-tuple-element.63.normed_ref, ...), custom_call_target="tpu_custom_call", output_to_operand_aliasing={{0}: (3, {}), {1}: (4, {})} | custom-call | flops 419430400 | bytes 3276800 | tf_op jit(solution)/shard_map/pallas_call | solution.py:411
  127.7 1.5 %shard_map.124 = (bf16[16,1600]{1,0:T(8,128)(2,1)}, bf16[8,1600]{1,0:T(8,128)(2,1)}) custom-call(s32[2]{0:T(128)S(1)} %pad_add_fusion.me_ref, s32[1,4]{1,0:T(1,128)S(1)} %copy-done.2, s32[1,8]{1,0:T(1,128)S(1)} %copy-done.3, bf16[8,16,1600]{2,1,0:T(8,128)(2,1)S(1)} %all-to-all-done.tail_ref, f32[16,1600]{1,0:T(8,128)S(1)} %get-tuple-element.59.extra_ref, ...), custom_call_target="tpu_custom_call" | custom-call | tf_op jit(solution)/shard_map/pallas_call | solution.py:432
  (26 shorter events, 0.3 us)
Async XLA Ops:
  1.6 6.8 %collective-permute-start.6 = (bf16[1,16,1600]{2,1,0:T(8,128)(2,1)S(1)}, bf16[1,16,1600]{2,1,0:T(8,128)(2,1)S(1)}, u32[]{:S(2)}, u32[]{:S(2)}) collective-permute-start(bf16[1,16,1600]{2,1,0:T(8,128)(2,1)S(1)} %shard_map.114.first_ref), channel_id=1, source_target_pairs={{0,16},{4,20},{8,24},{12,28},{16,0},{20,4},{24,8},{28,12},{1,17},{... | collective-permute-start | bytes 153608 | tf_op jit(solution)/shard_map/ppermute | solution.py:113
  8.5 4.8 %collective-permute-start.7 = (bf16[2,16,1600]{2,1,0:T(8,128)(2,1)S(1)}, bf16[2,16,1600]{2,1,0:T(8,128)(2,1)S(1)}, u32[]{:S(2)}, u32[]{:S(2)}) collective-permute-start(bf16[2,16,1600]{2,1,0:T(8,128)(2,1)S(1)} %shard_map.115.first_ref), channel_id=1, source_target_pairs={{0,8},{4,12},{8,0},{12,4},{16,24},{20,28},{24,16},{28,20},{1,9},{5... | collective-permute-start | bytes 307208 | tf_op jit(solution)/shard_map/ppermute | solution.py:113
  13.3 5.9 %collective-permute-start.8 = (bf16[4,16,1600]{2,1,0:T(8,128)(2,1)S(1)}, bf16[4,16,1600]{2,1,0:T(8,128)(2,1)S(1)}, u32[]{:S(2)}, u32[]{:S(2)}) collective-permute-start(bf16[4,16,1600]{2,1,0:T(8,128)(2,1)S(1)} %shard_map.116.first_ref), channel_id=1, source_target_pairs={{0,4},{4,0},{8,12},{12,8},{16,20},{20,16},{24,28},{28,24},{1,5},{5... | collective-permute-start | bytes 614408 | tf_op jit(solution)/shard_map/ppermute | solution.py:113
  19.2 8.2 %collective-permute-start.9 = (bf16[8,16,1600]{2,1,0:T(8,128)(2,1)S(1)}, bf16[8,16,1600]{2,1,0:T(8,128)(2,1)S(1)}, u32[]{:S(2)}, u32[]{:S(2)}) collective-permute-start(bf16[8,16,1600]{2,1,0:T(8,128)(2,1)S(1)} %shard_map.117.first_ref), channel_id=1, source_target_pairs={{0,2},{1,3},{2,0},{3,1},{4,6},{5,7},{6,4},{7,5},{8,10},{9,11},{10,... | collective-permute-start | bytes 1228808 | tf_op jit(solution)/shard_map/ppermute | solution.py:113
  27.5 37.3 %collective-permute-start.10 = (bf16[16,16,1600]{2,1,0:T(8,128)(2,1)S(1)}, bf16[16,16,1600]{2,1,0:T(8,128)(2,1)S(1)}, u32[]{:S(2)}, u32[]{:S(2)}) collective-permute-start(bf16[16,16,1600]{2,1,0:T(8,128)(2,1)S(1)} %shard_map.118.near_ref), channel_id=1, source_target_pairs={{0,1},{1,0},{2,3},{3,2},{4,5},{5,4},{6,7},{7,6},{8,9},{9,8},{10,11... | collective-permute-start | bytes 2457608 | tf_op jit(solution)/shard_map/ppermute | solution.py:113
  29.9 8.3 %collective-permute-start = (bf16[2,200,256]{2,1,0:T(8,128)(2,1)S(1)}, bf16[2,200,256]{2,1,0:T(8,128)(2,1)S(1)}, u32[]{:S(2)}, u32[]{:S(2)}) collective-permute-start(bf16[2,200,256]{2,1,0:T(8,128)(2,1)S(1)} %get-tuple-element.39), channel_id=1, source_target_pairs={{0,4},{4,0},{8,12},{12,8},{16,20},{20,16},{24,28},{28,24},{1,5},{5... | collective-permute-start | bytes 614408 | tf_op jit(solution)/shard_map/ppermute | solution.py:113
  31.7 22.0 %collective-permute-start.1 = (bf16[2,200,256]{2,1,0:T(8,128)(2,1)S(1)}, bf16[2,200,256]{2,1,0:T(8,128)(2,1)S(1)}, u32[]{:S(2)}, u32[]{:S(2)}) collective-permute-start(bf16[2,200,256]{2,1,0:T(8,128)(2,1)S(1)} %get-tuple-element.40), channel_id=1, source_target_pairs={{0,16},{4,20},{8,24},{12,28},{16,0},{20,4},{24,8},{28,12},{1,17},{... | collective-permute-start | bytes 614408 | tf_op jit(solution)/shard_map/ppermute | solution.py:113
  34.1 28.2 %collective-permute-start.2 = (bf16[2,200,256]{2,1,0:T(8,128)(2,1)S(1)}, bf16[2,200,256]{2,1,0:T(8,128)(2,1)S(1)}, u32[]{:S(2)}, u32[]{:S(2)}) collective-permute-start(bf16[2,200,256]{2,1,0:T(8,128)(2,1)S(1)} %get-tuple-element.41), channel_id=1, source_target_pairs={{0,20},{4,16},{8,28},{12,24},{16,4},{20,0},{24,12},{28,8},{1,21},{... | collective-permute-start | bytes 614408 | tf_op jit(solution)/shard_map/ppermute | solution.py:113
  34.3 28.7 %collective-permute-start.3 = (bf16[2,200,256]{2,1,0:T(8,128)(2,1)}, bf16[2,200,256]{2,1,0:T(8,128)(2,1)S(1)}, u32[]{:S(2)}, u32[]{:S(2)}) collective-permute-start(bf16[2,200,256]{2,1,0:T(8,128)(2,1)} %get-tuple-element.42), channel_id=1, source_target_pairs={{0,24},{4,28},{8,16},{12,20},{16,8},{20,12},{24,0},{28,4},{1,25},{... | collective-permute-start | bytes 614408 | tf_op jit(solution)/shard_map/ppermute | solution.py:113
  38.2 26.0 %collective-permute-start.4 = (bf16[2,200,256]{2,1,0:T(8,128)(2,1)S(1)}, bf16[2,200,256]{2,1,0:T(8,128)(2,1)S(1)}, u32[]{:S(2)}, u32[]{:S(2)}) collective-permute-start(bf16[2,200,256]{2,1,0:T(8,128)(2,1)S(1)} %get-tuple-element.45), channel_id=1, source_target_pairs={{0,8},{4,12},{8,0},{12,4},{16,24},{20,28},{24,16},{28,20},{1,9},{5... | collective-permute-start | bytes 614408 | tf_op jit(solution)/shard_map/ppermute | solution.py:113
  53.7 10.5 %collective-permute-start.5 = (bf16[2,200,256]{2,1,0:T(8,128)(2,1)S(1)}, bf16[2,200,256]{2,1,0:T(8,128)(2,1)S(1)}, u32[]{:S(2)}, u32[]{:S(2)}) collective-permute-start(bf16[2,200,256]{2,1,0:T(8,128)(2,1)S(1)} %get-tuple-element.46), channel_id=1, source_target_pairs={{0,28},{4,24},{8,20},{12,16},{16,12},{20,8},{24,4},{28,0},{1,29},{... | collective-permute-start | bytes 614408 | tf_op jit(solution)/shard_map/ppermute | solution.py:113
  62.2 7.0 %collective-permute-start.11 = (bf16[2,200,256]{2,1,0:T(8,128)(2,1)}, bf16[2,200,256]{2,1,0:T(8,128)(2,1)}, u32[]{:S(2)}, u32[]{:S(2)}) collective-permute-start(bf16[2,200,256]{2,1,0:T(8,128)(2,1)} %get-tuple-element.51), channel_id=1, source_target_pairs={{0,12},{4,8},{8,4},{12,0},{16,28},{20,24},{24,20},{28,16},{1,13},{... | collective-permute-start | bytes 614408 | tf_op jit(solution)/shard_map/ppermute | solution.py:113
  72.4 2.4 %collective-permute-start.12 = (bf16[2,16,8,1600]{3,2,1,0:T(8,128)(2,1)S(1)}, bf16[2,16,8,1600]{3,2,1,0:T(8,128)(2,1)S(1)}, u32[]{:S(2)}, u32[]{:S(2)}) collective-permute-start(bf16[2,16,8,1600]{3,2,1,0:T(8,128)(2,1)S(1)} %get-tuple-element.56), channel_id=1, source_target_pairs={{0,1},{1,0},{2,3},{3,2},{4,5},{5,4},{6,7},{7,6},{8,9},{9,8},{10,11... | collective-permute-start | bytes 2457608 | tf_op jit(solution)/shard_map/ppermute | solution.py:113
  75.1 11.9 %collective-permute-start.13 = (bf16[2,8,8,1600]{3,2,1,0:T(8,128)(2,1)S(1)}, bf16[2,8,8,1600]{3,2,1,0:T(8,128)(2,1)S(1)}, u32[]{:S(2)}, u32[]{:S(2)}) collective-permute-start(bf16[2,8,8,1600]{3,2,1,0:T(8,128)(2,1)S(1)} %get-tuple-element.58), channel_id=1, source_target_pairs={{0,2},{1,3},{2,0},{3,1},{4,6},{5,7},{6,4},{7,5},{8,10},{9,11},{10,... | collective-permute-start | bytes 1228808 | tf_op jit(solution)/shard_map/ppermute | solution.py:113
  76.9 19.4 %collective-permute-start.14 = (bf16[2,256,256]{2,1,0:T(8,128)(2,1)S(1)}, bf16[2,256,256]{2,1,0:T(8,128)(2,1)S(1)}, u32[]{:S(2)}, u32[]{:S(2)}) collective-permute-start(bf16[2,256,256]{2,1,0:T(8,128)(2,1)S(1)} %get-tuple-element.52.both_ref.refs_0_), channel_id=1, source_target_pairs={{0,16},{4,20},{8,24},{12,28},{16,0},{20,4},{24,8},{28,12},{1,17},{... | collective-permute-start | bytes 786440 | tf_op jit(solution)/shard_map/ppermute | solution.py:113
  83.3 16.5 %collective-permute-start.18 = (bf16[2,256,256]{2,1,0:T(8,128)(2,1)S(1)}, bf16[2,256,256]{2,1,0:T(8,128)(2,1)S(1)}, u32[]{:S(2)}, u32[]{:S(2)}) collective-permute-start(bf16[2,256,256]{2,1,0:T(8,128)(2,1)S(1)} %get-tuple-element.52.both_ref.refs_0_), channel_id=1, source_target_pairs={{0,8},{4,12},{8,0},{12,4},{16,24},{20,28},{24,16},{28,20},{1,9},{5... | collective-permute-start | bytes 786440 | tf_op jit(solution)/shard_map/ppermute | solution.py:113
  87.8 39.8 %all-to-all-start = ((bf16[8,16,1600]{2,1,0:T(8,128)(2,1)}), bf16[8,16,1600]{2,1,0:T(8,128)(2,1)S(1)}, u32[]{:S(2)}, u32[]{:S(2)}) async-start(bf16[8,16,1600]{2,1,0:T(8,128)(2,1)} %shard_map.123), calls=%async_computation | async-start | bytes 851968 | tf_op jit(solution)/shard_map/all_to_all | solution.py:574
  96.3 14.3 %collective-permute-start.15 = (bf16[2,256,256]{2,1,0:T(8,128)(2,1)S(1)}, bf16[2,256,256]{2,1,0:T(8,128)(2,1)S(1)}, u32[]{:S(2)}, u32[]{:S(2)}) collective-permute-start(bf16[2,256,256]{2,1,0:T(8,128)(2,1)S(1)} %collective-permute-done.14.refs_1_), channel_id=1, source_target_pairs={{0,8},{4,12},{8,0},{12,4},{16,24},{20,28},{24,16},{28,20},{1,9},{5... | collective-permute-start | bytes 786440 | tf_op jit(solution)/shard_map/ppermute | solution.py:113
  98.3 15.5 %collective-permute-start.20 = (bf16[2,256,256]{2,1,0:T(8,128)(2,1)S(1)}, bf16[2,256,256]{2,1,0:T(8,128)(2,1)S(1)}, u32[]{:S(2)}, u32[]{:S(2)}) collective-permute-start(bf16[2,256,256]{2,1,0:T(8,128)(2,1)S(1)} %get-tuple-element.52.both_ref.refs_0_), channel_id=1, source_target_pairs={{0,4},{4,0},{8,12},{12,8},{16,20},{20,16},{24,28},{28,24},{1,5},{5... | collective-permute-start | bytes 786440 | tf_op jit(solution)/shard_map/ppermute | solution.py:113
  99.8 16.4 %collective-permute-start.19 = (bf16[2,256,256]{2,1,0:T(8,128)(2,1)S(1)}, bf16[2,256,256]{2,1,0:T(8,128)(2,1)S(1)}, u32[]{:S(2)}, u32[]{:S(2)}) collective-permute-start(bf16[2,256,256]{2,1,0:T(8,128)(2,1)S(1)} %collective-permute-done.18.refs_0_), channel_id=1, source_target_pairs={{0,4},{4,0},{8,12},{12,8},{16,20},{20,16},{24,28},{28,24},{1,5},{5... | collective-permute-start | bytes 786440 | tf_op jit(solution)/shard_map/ppermute | solution.py:113
  100.3 20.7 %collective-permute-start.17 = (bf16[2,256,256]{2,1,0:T(8,128)(2,1)S(1)}, bf16[2,256,256]{2,1,0:T(8,128)(2,1)S(1)}, u32[]{:S(2)}, u32[]{:S(2)}) collective-permute-start(bf16[2,256,256]{2,1,0:T(8,128)(2,1)S(1)} %collective-permute-done.14.refs_1_), channel_id=1, source_target_pairs={{0,4},{4,0},{8,12},{12,8},{16,20},{20,16},{24,28},{28,24},{1,5},{5... | collective-permute-start | bytes 786440 | tf_op jit(solution)/shard_map/ppermute | solution.py:113
  110.5 15.3 %collective-permute-start.16 = (bf16[2,256,256]{2,1,0:T(8,128)(2,1)S(1)}, bf16[2,256,256]{2,1,0:T(8,128)(2,1)S(1)}, u32[]{:S(2)}, u32[]{:S(2)}) collective-permute-start(bf16[2,256,256]{2,1,0:T(8,128)(2,1)S(1)} %collective-permute-done.15.refs_0_), channel_id=1, source_target_pairs={{0,4},{4,0},{8,12},{12,8},{16,20},{20,16},{24,28},{28,24},{1,5},{5... | collective-permute-start | bytes 786440 | tf_op jit(solution)/shard_map/ppermute | solution.py:113
  125.8 1.8 %copy-start = (bf16[8,1600]{1,0:T(8,128)(2,1)S(1)}, bf16[8,1600]{1,0:T(8,128)(2,1)}, u32[]{:S(2)}) copy-start(bf16[8,1600]{1,0:T(8,128)(2,1)} %patch_ref.1) | copy-start | bytes 76804
  125.8 1.8 %copy-start.1 = (bf16[16,1600]{1,0:T(8,128)(2,1)S(1)}, bf16[16,1600]{1,0:T(8,128)(2,1)}, u32[]{:S(2)}) copy-start(bf16[16,1600]{1,0:T(8,128)(2,1)} %text_ref.1) | copy-start | bytes 153604
  125.8 1.8 %copy-start.2 = (s32[1,4]{1,0:T(1,128)S(1)}, s32[1,4]{1,0:T(1,128)}, u32[]{:S(2)}) copy-start(s32[1,4]{1,0:T(1,128)} %count_ref.1) | copy-start | bytes 52
  125.8 1.8 %copy-start.3 = (s32[1,8]{1,0:T(1,128)S(1)}, s32[1,8]{1,0:T(1,128)}, u32[]{:S(2)}) copy-start(s32[1,8]{1,0:T(1,128)} %place_ref.1) | copy-start | bytes 100

commit v8 on v7

--- a/solution.py
+++ b/solution.py
@@ -457,7 +457,7 @@
 
     def key(distance):
         hops = distance.bit_count()
-        return (hops, hops > 1 and distance >= far, -distance)
+        return (hops, hops > 1 and distance < far, distance if hops > 1 else -distance)
 
     return sorted(range(1, 2 * far), key=key)
 
@@ -574,9 +574,11 @@
     tail = lax.all_to_all(tail, "dp", split_axis=0, concat_axis=0, tiled=True)
 
     units_from = {0: both}
-    for step in dp_steps:
-        for distance, block in list(units_from.items()):
-            units_from[distance ^ step] = swap(block, "dp", step)
+    for distance in unit_order(log2(replicas)):
+        step = distance & -distance
+        if distance == replicas - 1 and replicas > 4:
+            step *= 2
+        units_from[distance] = swap(units_from[distance ^ step], "dp", step)
     grads = ()
     for distances in gradient_groups(log2(replicas)):
         grads = weight_grads(

time: 130 us -> 128 us (0.985)
  waiting for transfers between devices: 58.9 us -> 56.9 us
    ppermute x21, waiting for transfers between devices: 58.9 us -> 56.9 us  [swap(): return lax.ppermute(array, axis, [(i, i ^ step) for i in range(size)])]
  transfers between devices with their start and end apart: 22 -> 22, of which waited for: 12 -> 11; matrix products, arithmetic and copies ran while one was open for 1% -> 1% of each run, Pallas kernels for 14% -> 14%
where the time goes in v8:
time: 128 us
  waiting for transfers between devices  56.9 us (44%)
  starting transfers between devices  45.2 us (35%)
  Pallas kernels  24 us (19%)
    ppermute x21, waiting for transfers between devices, swap(): return lax.ppermute(array, axis, [(i, i ^ step) for i in range(size)])  56.9 us
    ppermute x21, starting transfers between devices, swap(): return lax.ppermute(array, axis, [(i, i ^ step) for i in range(size)])  36.7 us
    pallas_call x5, Pallas kernels, weight_grads(): pl.pallas_call(functools.partial(weight_grad_kernel, distances), in_specs...  10.6 us
    all_to_all x1, starting transfers between devices, move_rows_plan(): tail = lax.all_to_all(tail, 'dp', split_axis=0, concat_axis=0, tiled=True)  8.46 us
    pallas_call x10, Pallas kernels, call(): pl.pallas_call(kernel, out_shape=out_shape, in_specs=[SMEM_SPEC] * len(sm...  6.5 us
    pallas_call x3, Pallas kernels, unpacking(): pl.pallas_call(functools.partial(kernel, group), out_shape=[*slices, *ext...  3.51 us
  transfers between devices with their start and end apart: 22, of which 11 were waited for; matrix products, arithmetic and copies ran while one was open for 1% of the time, Pallas kernels for 14%

profile of v8, /device:TPU:0, one launch (start us, length us, event | category | flops | bytes accessed | tf_op | source)
XLA Modules:
  0.0 127.7 jit_solution(7671755769577676157)
XLA Ops:
  0.6 1.0 shard_map.114.first_ref
  1.6 4.1 %collective-permute-start.6 = (bf16[1,16,1600]{2,1,0:T(8,128)(2,1)S(1)}, bf16[1,16,1600]{2,1,0:T(8,128)(2,1)S(1)}, u32[]{:S(2)}, u32[]{:S(2)}) collective-permute-start(bf16[1,16,1600]{2,1,0:T(8,128)(2,1)S(1)} %shard_map.114.first_ref), channel_id=1, source_target_pairs={{0,16},{4,20},{8,24},{12,28},{16,0},{20,4},{24,8},{28,12},{1,17},{... | collective-permute-start | bytes 153608 | tf_op jit(solution)/shard_map/ppermute | solution.py:113
  5.8 2.7 %collective-permute-done.6.second_ref = bf16[1,16,1600]{2,1,0:T(8,128)(2,1)S(1)} collective-permute-done((bf16[1,16,1600]{2,1,0:T(8,128)(2,1)S(1)}, bf16[1,16,1600]{2,1,0:T(8,128)(2,1)S(1)}, u32[]{:S(2)}, u32[]{:S(2)}) %collective-permute-start.6) | collective-permute-done | bytes 51232 | tf_op jit(solution)/shard_map/ppermute | solution.py:113
  8.5 1.4 %collective-permute-start.7 = (bf16[2,16,1600]{2,1,0:T(8,128)(2,1)S(1)}, bf16[2,16,1600]{2,1,0:T(8,128)(2,1)S(1)}, u32[]{:S(2)}, u32[]{:S(2)}) collective-permute-start(bf16[2,16,1600]{2,1,0:T(8,128)(2,1)S(1)} %shard_map.115.first_ref), channel_id=1, source_target_pairs={{0,8},{4,12},{8,0},{12,4},{16,24},{20,28},{24,16},{28,20},{1,9},{5... | collective-permute-start | bytes 307208 | tf_op jit(solution)/shard_map/ppermute | solution.py:113
  9.9 3.4 %collective-permute-done.7.second_ref = bf16[2,16,1600]{2,1,0:T(8,128)(2,1)S(1)} collective-permute-done((bf16[2,16,1600]{2,1,0:T(8,128)(2,1)S(1)}, bf16[2,16,1600]{2,1,0:T(8,128)(2,1)S(1)}, u32[]{:S(2)}, u32[]{:S(2)}) %collective-permute-start.7) | collective-permute-done | bytes 102432 | tf_op jit(solution)/shard_map/ppermute | solution.py:113
  13.3 1.8 %collective-permute-start.8 = (bf16[4,16,1600]{2,1,0:T(8,128)(2,1)S(1)}, bf16[4,16,1600]{2,1,0:T(8,128)(2,1)S(1)}, u32[]{:S(2)}, u32[]{:S(2)}) collective-permute-start(bf16[4,16,1600]{2,1,0:T(8,128)(2,1)S(1)} %shard_map.116.first_ref), channel_id=1, source_target_pairs={{0,4},{4,0},{8,12},{12,8},{16,20},{20,16},{24,28},{28,24},{1,5},{5... | collective-permute-start | bytes 614408 | tf_op jit(solution)/shard_map/ppermute | solution.py:113
  15.0 4.1 %collective-permute-done.8.second_ref = bf16[4,16,1600]{2,1,0:T(8,128)(2,1)S(1)} collective-permute-done((bf16[4,16,1600]{2,1,0:T(8,128)(2,1)S(1)}, bf16[4,16,1600]{2,1,0:T(8,128)(2,1)S(1)}, u32[]{:S(2)}, u32[]{:S(2)}) %collective-permute-start.8) | collective-permute-done | bytes 204832 | tf_op jit(solution)/shard_map/ppermute | solution.py:113
  19.2 1.8 %collective-permute-start.9 = (bf16[8,16,1600]{2,1,0:T(8,128)(2,1)S(1)}, bf16[8,16,1600]{2,1,0:T(8,128)(2,1)S(1)}, u32[]{:S(2)}, u32[]{:S(2)}) collective-permute-start(bf16[8,16,1600]{2,1,0:T(8,128)(2,1)S(1)} %shard_map.117.first_ref), channel_id=1, source_target_pairs={{0,2},{1,3},{2,0},{3,1},{4,6},{5,7},{6,4},{7,5},{8,10},{9,11},{10,... | collective-permute-start | bytes 1228808 | tf_op jit(solution)/shard_map/ppermute | solution.py:113
  21.0 6.4 %collective-permute-done.9.second_ref = bf16[8,16,1600]{2,1,0:T(8,128)(2,1)S(1)} collective-permute-done((bf16[8,16,1600]{2,1,0:T(8,128)(2,1)S(1)}, bf16[8,16,1600]{2,1,0:T(8,128)(2,1)S(1)}, u32[]{:S(2)}, u32[]{:S(2)}) %collective-permute-start.9) | collective-permute-done | bytes 409632 | tf_op jit(solution)/shard_map/ppermute | solution.py:113
  27.5 2.3 %shard_map.111 = (bf16[2,200,256]{2,1,0:T(8,128)(2,1)S(1)}, bf16[2,200,256]{2,1,0:T(8,128)(2,1)S(1)}, bf16[2,200,256]{2,1,0:T(8,128)(2,1)}, bf16[2,200,256]{2,1,...) custom-call(bf16[200,2048]{1,0:T(8,128)(2,1)} %own_expand_at.1, ...), custom_call_target="tpu_custom_call" | custom-call | tf_op jit(solution)/shard_map/pallas_call | solution.py:508
  29.9 1.8 %collective-permute-start = (bf16[2,200,256]{2,1,0:T(8,128)(2,1)S(1)}, bf16[2,200,256]{2,1,0:T(8,128)(2,1)S(1)}, u32[]{:S(2)}, u32[]{:S(2)}) collective-permute-start(bf16[2,200,256]{2,1,0:T(8,128)(2,1)S(1)} %get-tuple-element.39), channel_id=1, source_target_pairs={{0,4},{4,0},{8,12},{12,8},{16,20},{20,16},{24,28},{28,24},{1,5},{5... | collective-permute-start | bytes 614408 | tf_op jit(solution)/shard_map/ppermute | solution.py:113
  31.7 2.4 %collective-permute-start.1 = (bf16[2,200,256]{2,1,0:T(8,128)(2,1)S(1)}, bf16[2,200,256]{2,1,0:T(8,128)(2,1)S(1)}, u32[]{:S(2)}, u32[]{:S(2)}) collective-permute-start(bf16[2,200,256]{2,1,0:T(8,128)(2,1)S(1)} %get-tuple-element.40), channel_id=1, source_target_pairs={{0,16},{4,20},{8,24},{12,28},{16,0},{20,4},{24,8},{28,12},{1,17},{... | collective-permute-start | bytes 614408 | tf_op jit(solution)/shard_map/ppermute | solution.py:113
  34.1 0.3 collective-permute-start.2
  34.3 3.8 %collective-permute-start.3 = (bf16[2,200,256]{2,1,0:T(8,128)(2,1)}, bf16[2,200,256]{2,1,0:T(8,128)(2,1)S(1)}, u32[]{:S(2)}, u32[]{:S(2)}) collective-permute-start(bf16[2,200,256]{2,1,0:T(8,128)(2,1)} %get-tuple-element.42), channel_id=1, source_target_pairs={{0,24},{4,28},{8,16},{12,20},{16,8},{20,12},{24,0},{28,4},{1,25},{... | collective-permute-start | bytes 614408 | tf_op jit(solution)/shard_map/ppermute | solution.py:113
  38.2 0.7 collective-permute-start.4
  38.8 14.9 %collective-permute-done.1.refs_1_ = bf16[2,200,256]{2,1,0:T(8,128)(2,1)S(1)} collective-permute-done((bf16[2,200,256]{2,1,0:T(8,128)(2,1)S(1)}, bf16[2,200,256]{2,1,0:T(8,128)(2,1)S(1)}, u32[]{:S(2)}, u32[]{:S(2)}) %collective-permute-start.1) | collective-permute-done | bytes 204832 | tf_op jit(solution)/shard_map/ppermute | solution.py:113
  53.7 2.7 %collective-permute-start.5 = (bf16[2,200,256]{2,1,0:T(8,128)(2,1)S(1)}, bf16[2,200,256]{2,1,0:T(8,128)(2,1)S(1)}, u32[]{:S(2)}, u32[]{:S(2)}) collective-permute-start(bf16[2,200,256]{2,1,0:T(8,128)(2,1)S(1)} %get-tuple-element.46), channel_id=1, source_target_pairs={{0,28},{4,24},{8,20},{12,16},{16,12},{20,8},{24,4},{28,0},{1,29},{... | collective-permute-start | bytes 614408 | tf_op jit(solution)/shard_map/ppermute | solution.py:113
  56.4 5.9 %collective-permute-done.2.refs_2_ = bf16[2,200,256]{2,1,0:T(8,128)(2,1)S(1)} collective-permute-done((bf16[2,200,256]{2,1,0:T(8,128)(2,1)S(1)}, bf16[2,200,256]{2,1,0:T(8,128)(2,1)S(1)}, u32[]{:S(2)}, u32[]{:S(2)}) %collective-permute-start.2) | collective-permute-done | bytes 204832 | tf_op jit(solution)/shard_map/ppermute | solution.py:113
  62.2 0.7 reshape.11.gain_ref
  62.9 0.1 pad_add_fusion.me_ref
  63.0 1.1 shard_map.112
  64.2 0.6 shard_map.113
  64.8 2.0 %shard_map.119 = (bf16[256,1600]{1,0:T(8,128)(2,1)S(1)}, bf16[256,1600]{1,0:T(8,128)(2,1)S(1)}, f32[16,1600]{1,0:T(8,128)S(1)}) custom-call(s32[2]{0:T(128)S(1)} %pad_add_fusion.me_ref, bf16[16,16,1600]{2,1,0:T(8,128)(2,1)S(1)} %shard_map.118.near_ref, bf16[16,16,1600]{2,1,0:T(8,128)(2,1)S(1)} %collective-permute-done.10.far_ref, f32[1,1600]{1,0:T(1,128)S(1)} %reshape.11.gain_ref), custom_call_target="tpu_custom_call" | custom-call | tf_op jit(solution)/shard_map/pallas_call | solution.py:432
  66.8 2.4 %collective-permute-done.11.refs_0_ = bf16[2,200,256]{2,1,0:T(8,128)(2,1)} collective-permute-done((bf16[2,200,256]{2,1,0:T(8,128)(2,1)}, bf16[2,200,256]{2,1,0:T(8,128)(2,1)}, u32[]{:S(2)}, u32[]{:S(2)}) %collective-permute-start.11) | collective-permute-done | bytes 204832 | tf_op jit(solution)/shard_map/ppermute | solution.py:113
  69.2 1.8 %shard_map.120 = (bf16[1600,256]{1,0:T(8,128)(2,1)S(1)}, bf16[1600,256]{1,0:T(8,128)(2,1)S(1)}, bf16[2,256,256]{2,1,0:T(8,128)(2,1)S(1)}) custom-call(bf16[1600,256]{1,0:T(8,128)(2,1)S(1)} %get-tuple-element.47.expand_part_ref, bf16[1600,256]{1,0:T(8,128)(2,1)S(1)} %get-tuple-element.48.project_part_ref, ...), custom_call_target="tpu_custom_call", output_to_operand_aliasing={{0}: (0, {}), {1}: (1, {})} | custom-call | tf_op jit(solution)/shard_map/pallas_call | solution.py:538
  71.0 1.4 %shard_map.121 = (f32[2,16,8,1600]{3,2,1,0:T(8,128)S(1)}, bf16[2,16,8,1600]{3,2,1,0:T(8,128)(2,1)S(1)}) custom-call(s32[2]{0:T(128)S(1)} %pad_add_fusion.me_ref, bf16[2,256,256]{2,1,0:T(8,128)(2,1)S(1)} %get-tuple-element.52.both_ref.refs_0_, bf16[1600,256]{1,0:T(8,128)(2,1)S(1)} %get-tuple-element.53.expand_ref, ...), custom_call_target="tpu_custom_call" | custom-call | tf_op jit(solution)/shard_map/pallas_call | solution.py:432
  72.5 2.4 %collective-permute-done.12.got_ref = bf16[2,16,8,1600]{3,2,1,0:T(8,128)(2,1)S(1)} collective-permute-done((bf16[2,16,8,1600]{3,2,1,0:T(8,128)(2,1)S(1)}, bf16[2,16,8,1600]{3,2,1,0:T(8,128)(2,1)S(1)}, u32[]{:S(2)}, u32[]{:S(2)}) %collective-permute-start.12) | collective-permute-done | bytes 819232 | tf_op jit(solution)/shard_map/ppermute | solution.py:113
  74.9 0.2 shard_map.122
  75.1 1.8 %collective-permute-start.13 = (bf16[2,8,8,1600]{3,2,1,0:T(8,128)(2,1)S(1)}, bf16[2,8,8,1600]{3,2,1,0:T(8,128)(2,1)S(1)}, u32[]{:S(2)}, u32[]{:S(2)}) collective-permute-start(bf16[2,8,8,1600]{3,2,1,0:T(8,128)(2,1)S(1)} %get-tuple-element.58), channel_id=1, source_target_pairs={{0,2},{1,3},{2,0},{3,1},{4,6},{5,7},{6,4},{7,5},{8,10},{9,11},{10,... | collective-permute-start | bytes 1228808 | tf_op jit(solution)/shard_map/ppermute | solution.py:113
  76.9 6.4 %collective-permute-start.14 = (bf16[2,256,256]{2,1,0:T(8,128)(2,1)S(1)}, bf16[2,256,256]{2,1,0:T(8,128)(2,1)S(1)}, u32[]{:S(2)}, u32[]{:S(2)}) collective-permute-start(bf16[2,256,256]{2,1,0:T(8,128)(2,1)S(1)} %get-tuple-element.52.both_ref.refs_0_), channel_id=1, source_target_pairs={{0,16},{4,20},{8,24},{12,28},{16,0},{20,4},{24,8},{28,12},{1,17},{... | collective-permute-start | bytes 786440 | tf_op jit(solution)/shard_map/ppermute | solution.py:113
  83.3 3.7 %collective-permute-done.13.got_ref = bf16[2,8,8,1600]{3,2,1,0:T(8,128)(2,1)S(1)} collective-permute-done((bf16[2,8,8,1600]{3,2,1,0:T(8,128)(2,1)S(1)}, bf16[2,8,8,1600]{3,2,1,0:T(8,128)(2,1)S(1)}, u32[]{:S(2)}, u32[]{:S(2)}) %collective-permute-start.13) | collective-permute-done | bytes 409632 | tf_op jit(solution)/shard_map/ppermute | solution.py:113
  87.0 0.8 shard_map.123
  87.8 8.5 %all-to-all-start = ((bf16[8,16,1600]{2,1,0:T(8,128)(2,1)}), bf16[8,16,1600]{2,1,0:T(8,128)(2,1)S(1)}, u32[]{:S(2)}, u32[]{:S(2)}) async-start(bf16[8,16,1600]{2,1,0:T(8,128)(2,1)} %shard_map.123), calls=%async_computation | async-start | bytes 851968 | tf_op jit(solution)/shard_map/all_to_all | solution.py:574
  96.3 2.0 %collective-permute-start.18 = (bf16[2,256,256]{2,1,0:T(8,128)(2,1)S(1)}, bf16[2,256,256]{2,1,0:T(8,128)(2,1)S(1)}, u32[]{:S(2)}, u32[]{:S(2)}) collective-permute-start(bf16[2,256,256]{2,1,0:T(8,128)(2,1)S(1)} %get-tuple-element.52.both_ref.refs_0_), channel_id=1, source_target_pairs={{0,8},{4,12},{8,0},{12,4},{16,24},{20,28},{24,16},{28,20},{1,9},{5... | collective-permute-start | bytes 786440 | tf_op jit(solution)/shard_map/ppermute | solution.py:113
  98.3 1.5 %collective-permute-start.15 = (bf16[2,256,256]{2,1,0:T(8,128)(2,1)S(1)}, bf16[2,256,256]{2,1,0:T(8,128)(2,1)S(1)}, u32[]{:S(2)}, u32[]{:S(2)}) collective-permute-start(bf16[2,256,256]{2,1,0:T(8,128)(2,1)S(1)} %collective-permute-done.14.refs_1_), channel_id=1, source_target_pairs={{0,4},{4,0},{8,12},{12,8},{16,20},{20,16},{24,28},{28,24},{1,5},{5... | collective-permute-start | bytes 786440 | tf_op jit(solution)/shard_map/ppermute | solution.py:113
  99.8 0.6 collective-permute-start.20
  100.3 10.2 %collective-permute-done.18.refs_0_ = bf16[2,256,256]{2,1,0:T(8,128)(2,1)S(1)} collective-permute-done((bf16[2,256,256]{2,1,0:T(8,128)(2,1)S(1)}, bf16[2,256,256]{2,1,0:T(8,128)(2,1)S(1)}, u32[]{:S(2)}, u32[]{:S(2)}) %collective-permute-start.18) | collective-permute-done | bytes 262176 | tf_op jit(solution)/shard_map/ppermute | solution.py:113
  110.5 1.5 %collective-permute-start.19 = (bf16[2,256,256]{2,1,0:T(8,128)(2,1)S(1)}, bf16[2,256,256]{2,1,0:T(8,128)(2,1)S(1)}, u32[]{:S(2)}, u32[]{:S(2)}) collective-permute-start(bf16[2,256,256]{2,1,0:T(8,128)(2,1)S(1)} %collective-permute-done.18.refs_0_), channel_id=1, source_target_pairs={{0,4},{4,0},{8,12},{12,8},{16,20},{20,16},{24,28},{28,24},{1,5},{5... | collective-permute-start | bytes 786440 | tf_op jit(solution)/shard_map/ppermute | solution.py:113
  112.1 0.5 collective-permute-start.17
  112.6 0.5 shard_map.125
  113.1 1.6 %collective-permute-start.16 = (bf16[2,256,256]{2,1,0:T(8,128)(2,1)S(1)}, bf16[2,256,256]{2,1,0:T(8,128)(2,1)S(1)}, u32[]{:S(2)}, u32[]{:S(2)}) collective-permute-start(bf16[2,256,256]{2,1,0:T(8,128)(2,1)S(1)} %collective-permute-done.15.refs_0_), channel_id=1, source_target_pairs={{0,8},{4,12},{8,0},{12,4},{16,24},{20,28},{24,16},{28,20},{1,9},{5... | collective-permute-start | bytes 786440 | tf_op jit(solution)/shard_map/ppermute | solution.py:113
  114.7 1.8 %shard_map.126 = (bf16[1600,2048]{1,0:T(8,128)(2,1)}, bf16[1600,2048]{1,0:T(8,128)(2,1)}) custom-call(bf16[1600,256]{1,0:T(8,128)(2,1)S(1)} %get-tuple-element.62.grad_ref, bf16[1600,256]{1,0:T(8,128)(2,1)S(1)} %get-tuple-element.63.normed_ref, bf16[2,256,256]{2,1,0:T(8,128)(2,1)S(1)} %get-tuple-element.52.both_ref.refs_0_), custom_call_target="tpu_custom_call" | custom-call | flops 419430400 | bytes 3276800 | tf_op jit(solution)/shard_map/pallas_call | solution.py:411
  116.4 2.4 %shard_map.127 = (bf16[1600,2048]{1,0:T(8,128)(2,1)}, bf16[1600,2048]{1,0:T(8,128)(2,1)}) custom-call(bf16[1600,256]{1,0:T(8,128)(2,1)S(1)} %get-tuple-element.62.grad_ref, bf16[1600,256]{1,0:T(8,128)(2,1)S(1)} %get-tuple-element.63.normed_ref, ...), custom_call_target="tpu_custom_call", output_to_operand_aliasing={{0}: (4, {}), {1}: (5, {})} | custom-call | flops 838860800 | bytes 4915200 | tf_op jit(solution)/shard_map/pallas_call | solution.py:411
  118.8 2.4 %shard_map.128 = (bf16[1600,2048]{1,0:T(8,128)(2,1)}, bf16[1600,2048]{1,0:T(8,128)(2,1)}) custom-call(bf16[1600,256]{1,0:T(8,128)(2,1)S(1)} %get-tuple-element.62.grad_ref, bf16[1600,256]{1,0:T(8,128)(2,1)S(1)} %get-tuple-element.63.normed_ref, ...), custom_call_target="tpu_custom_call", output_to_operand_aliasing={{0}: (4, {}), {1}: (5, {})} | custom-call | flops 838860800 | bytes 4915200 | tf_op jit(solution)/shard_map/pallas_call | solution.py:411
  121.2 2.4 %shard_map.129 = (bf16[1600,2048]{1,0:T(8,128)(2,1)}, bf16[1600,2048]{1,0:T(8,128)(2,1)}) custom-call(bf16[1600,256]{1,0:T(8,128)(2,1)S(1)} %get-tuple-element.62.grad_ref, bf16[1600,256]{1,0:T(8,128)(2,1)S(1)} %get-tuple-element.63.normed_ref, ...), custom_call_target="tpu_custom_call", output_to_operand_aliasing={{0}: (4, {}), {1}: (5, {})} | custom-call | flops 838860800 | bytes 4915200 | tf_op jit(solution)/shard_map/pallas_call | solution.py:411
  123.6 0.8 collective-permute-done.16.refs_0_
  124.4 1.8 %shard_map.130 = (bf16[1600,2048]{1,0:T(8,128)(2,1)}, bf16[1600,2048]{1,0:T(8,128)(2,1)}) custom-call(bf16[1600,256]{1,0:T(8,128)(2,1)S(1)} %get-tuple-element.62.grad_ref, bf16[1600,256]{1,0:T(8,128)(2,1)S(1)} %get-tuple-element.63.normed_ref, ...), custom_call_target="tpu_custom_call", output_to_operand_aliasing={{0}: (3, {}), {1}: (4, {})} | custom-call | flops 419430400 | bytes 3276800 | tf_op jit(solution)/shard_map/pallas_call | solution.py:411
  126.2 1.5 %shard_map.124 = (bf16[16,1600]{1,0:T(8,128)(2,1)}, bf16[8,1600]{1,0:T(8,128)(2,1)}) custom-call(s32[2]{0:T(128)S(1)} %pad_add_fusion.me_ref, s32[1,4]{1,0:T(1,128)S(1)} %copy-done.2, s32[1,8]{1,0:T(1,128)S(1)} %copy-done.3, bf16[8,16,1600]{2,1,0:T(8,128)(2,1)S(1)} %all-to-all-done.tail_ref, f32[16,1600]{1,0:T(8,128)S(1)} %get-tuple-element.59.extra_ref, ...), custom_call_target="tpu_custom_call" | custom-call | tf_op jit(solution)/shard_map/pallas_call | solution.py:432
  (26 shorter events, 0.3 us)
Async XLA Ops:
  1.6 6.8 %collective-permute-start.6 = (bf16[1,16,1600]{2,1,0:T(8,128)(2,1)S(1)}, bf16[1,16,1600]{2,1,0:T(8,128)(2,1)S(1)}, u32[]{:S(2)}, u32[]{:S(2)}) collective-permute-start(bf16[1,16,1600]{2,1,0:T(8,128)(2,1)S(1)} %shard_map.114.first_ref), channel_id=1, source_target_pairs={{0,16},{4,20},{8,24},{12,28},{16,0},{20,4},{24,8},{28,12},{1,17},{... | collective-permute-start | bytes 153608 | tf_op jit(solution)/shard_map/ppermute | solution.py:113
  8.5 4.8 %collective-permute-start.7 = (bf16[2,16,1600]{2,1,0:T(8,128)(2,1)S(1)}, bf16[2,16,1600]{2,1,0:T(8,128)(2,1)S(1)}, u32[]{:S(2)}, u32[]{:S(2)}) collective-permute-start(bf16[2,16,1600]{2,1,0:T(8,128)(2,1)S(1)} %shard_map.115.first_ref), channel_id=1, source_target_pairs={{0,8},{4,12},{8,0},{12,4},{16,24},{20,28},{24,16},{28,20},{1,9},{5... | collective-permute-start | bytes 307208 | tf_op jit(solution)/shard_map/ppermute | solution.py:113
  13.3 5.9 %collective-permute-start.8 = (bf16[4,16,1600]{2,1,0:T(8,128)(2,1)S(1)}, bf16[4,16,1600]{2,1,0:T(8,128)(2,1)S(1)}, u32[]{:S(2)}, u32[]{:S(2)}) collective-permute-start(bf16[4,16,1600]{2,1,0:T(8,128)(2,1)S(1)} %shard_map.116.first_ref), channel_id=1, source_target_pairs={{0,4},{4,0},{8,12},{12,8},{16,20},{20,16},{24,28},{28,24},{1,5},{5... | collective-permute-start | bytes 614408 | tf_op jit(solution)/shard_map/ppermute | solution.py:113
  19.2 8.2 %collective-permute-start.9 = (bf16[8,16,1600]{2,1,0:T(8,128)(2,1)S(1)}, bf16[8,16,1600]{2,1,0:T(8,128)(2,1)S(1)}, u32[]{:S(2)}, u32[]{:S(2)}) collective-permute-start(bf16[8,16,1600]{2,1,0:T(8,128)(2,1)S(1)} %shard_map.117.first_ref), channel_id=1, source_target_pairs={{0,2},{1,3},{2,0},{3,1},{4,6},{5,7},{6,4},{7,5},{8,10},{9,11},{10,... | collective-permute-start | bytes 1228808 | tf_op jit(solution)/shard_map/ppermute | solution.py:113
  27.5 37.3 %collective-permute-start.10 = (bf16[16,16,1600]{2,1,0:T(8,128)(2,1)S(1)}, bf16[16,16,1600]{2,1,0:T(8,128)(2,1)S(1)}, u32[]{:S(2)}, u32[]{:S(2)}) collective-permute-start(bf16[16,16,1600]{2,1,0:T(8,128)(2,1)S(1)} %shard_map.118.near_ref), channel_id=1, source_target_pairs={{0,1},{1,0},{2,3},{3,2},{4,5},{5,4},{6,7},{7,6},{8,9},{9,8},{10,11... | collective-permute-start | bytes 2457608 | tf_op jit(solution)/shard_map/ppermute | solution.py:113
  29.9 8.3 %collective-permute-start = (bf16[2,200,256]{2,1,0:T(8,128)(2,1)S(1)}, bf16[2,200,256]{2,1,0:T(8,128)(2,1)S(1)}, u32[]{:S(2)}, u32[]{:S(2)}) collective-permute-start(bf16[2,200,256]{2,1,0:T(8,128)(2,1)S(1)} %get-tuple-element.39), channel_id=1, source_target_pairs={{0,4},{4,0},{8,12},{12,8},{16,20},{20,16},{24,28},{28,24},{1,5},{5... | collective-permute-start | bytes 614408 | tf_op jit(solution)/shard_map/ppermute | solution.py:113
  31.7 22.0 %collective-permute-start.1 = (bf16[2,200,256]{2,1,0:T(8,128)(2,1)S(1)}, bf16[2,200,256]{2,1,0:T(8,128)(2,1)S(1)}, u32[]{:S(2)}, u32[]{:S(2)}) collective-permute-start(bf16[2,200,256]{2,1,0:T(8,128)(2,1)S(1)} %get-tuple-element.40), channel_id=1, source_target_pairs={{0,16},{4,20},{8,24},{12,28},{16,0},{20,4},{24,8},{28,12},{1,17},{... | collective-permute-start | bytes 614408 | tf_op jit(solution)/shard_map/ppermute | solution.py:113
  34.1 28.2 %collective-permute-start.2 = (bf16[2,200,256]{2,1,0:T(8,128)(2,1)S(1)}, bf16[2,200,256]{2,1,0:T(8,128)(2,1)S(1)}, u32[]{:S(2)}, u32[]{:S(2)}) collective-permute-start(bf16[2,200,256]{2,1,0:T(8,128)(2,1)S(1)} %get-tuple-element.41), channel_id=1, source_target_pairs={{0,20},{4,16},{8,28},{12,24},{16,4},{20,0},{24,12},{28,8},{1,21},{... | collective-permute-start | bytes 614408 | tf_op jit(solution)/shard_map/ppermute | solution.py:113
  34.3 28.7 %collective-permute-start.3 = (bf16[2,200,256]{2,1,0:T(8,128)(2,1)}, bf16[2,200,256]{2,1,0:T(8,128)(2,1)S(1)}, u32[]{:S(2)}, u32[]{:S(2)}) collective-permute-start(bf16[2,200,256]{2,1,0:T(8,128)(2,1)} %get-tuple-element.42), channel_id=1, source_target_pairs={{0,24},{4,28},{8,16},{12,20},{16,8},{20,12},{24,0},{28,4},{1,25},{... | collective-permute-start | bytes 614408 | tf_op jit(solution)/shard_map/ppermute | solution.py:113
  38.2 26.0 %collective-permute-start.4 = (bf16[2,200,256]{2,1,0:T(8,128)(2,1)S(1)}, bf16[2,200,256]{2,1,0:T(8,128)(2,1)S(1)}, u32[]{:S(2)}, u32[]{:S(2)}) collective-permute-start(bf16[2,200,256]{2,1,0:T(8,128)(2,1)S(1)} %get-tuple-element.45), channel_id=1, source_target_pairs={{0,8},{4,12},{8,0},{12,4},{16,24},{20,28},{24,16},{28,20},{1,9},{5... | collective-permute-start | bytes 614408 | tf_op jit(solution)/shard_map/ppermute | solution.py:113
  53.7 10.5 %collective-permute-start.5 = (bf16[2,200,256]{2,1,0:T(8,128)(2,1)S(1)}, bf16[2,200,256]{2,1,0:T(8,128)(2,1)S(1)}, u32[]{:S(2)}, u32[]{:S(2)}) collective-permute-start(bf16[2,200,256]{2,1,0:T(8,128)(2,1)S(1)} %get-tuple-element.46), channel_id=1, source_target_pairs={{0,28},{4,24},{8,20},{12,16},{16,12},{20,8},{24,4},{28,0},{1,29},{... | collective-permute-start | bytes 614408 | tf_op jit(solution)/shard_map/ppermute | solution.py:113
  62.2 7.0 %collective-permute-start.11 = (bf16[2,200,256]{2,1,0:T(8,128)(2,1)}, bf16[2,200,256]{2,1,0:T(8,128)(2,1)}, u32[]{:S(2)}, u32[]{:S(2)}) collective-permute-start(bf16[2,200,256]{2,1,0:T(8,128)(2,1)} %get-tuple-element.51), channel_id=1, source_target_pairs={{0,12},{4,8},{8,4},{12,0},{16,28},{20,24},{24,20},{28,16},{1,13},{... | collective-permute-start | bytes 614408 | tf_op jit(solution)/shard_map/ppermute | solution.py:113
  72.4 2.4 %collective-permute-start.12 = (bf16[2,16,8,1600]{3,2,1,0:T(8,128)(2,1)S(1)}, bf16[2,16,8,1600]{3,2,1,0:T(8,128)(2,1)S(1)}, u32[]{:S(2)}, u32[]{:S(2)}) collective-permute-start(bf16[2,16,8,1600]{3,2,1,0:T(8,128)(2,1)S(1)} %get-tuple-element.56), channel_id=1, source_target_pairs={{0,1},{1,0},{2,3},{3,2},{4,5},{5,4},{6,7},{7,6},{8,9},{9,8},{10,11... | collective-permute-start | bytes 2457608 | tf_op jit(solution)/shard_map/ppermute | solution.py:113
  75.1 11.9 %collective-permute-start.13 = (bf16[2,8,8,1600]{3,2,1,0:T(8,128)(2,1)S(1)}, bf16[2,8,8,1600]{3,2,1,0:T(8,128)(2,1)S(1)}, u32[]{:S(2)}, u32[]{:S(2)}) collective-permute-start(bf16[2,8,8,1600]{3,2,1,0:T(8,128)(2,1)S(1)} %get-tuple-element.58), channel_id=1, source_target_pairs={{0,2},{1,3},{2,0},{3,1},{4,6},{5,7},{6,4},{7,5},{8,10},{9,11},{10,... | collective-permute-start | bytes 1228808 | tf_op jit(solution)/shard_map/ppermute | solution.py:113
  76.9 21.4 %collective-permute-start.14 = (bf16[2,256,256]{2,1,0:T(8,128)(2,1)S(1)}, bf16[2,256,256]{2,1,0:T(8,128)(2,1)S(1)}, u32[]{:S(2)}, u32[]{:S(2)}) collective-permute-start(bf16[2,256,256]{2,1,0:T(8,128)(2,1)S(1)} %get-tuple-element.52.both_ref.refs_0_), channel_id=1, source_target_pairs={{0,16},{4,20},{8,24},{12,28},{16,0},{20,4},{24,8},{28,12},{1,17},{... | collective-permute-start | bytes 786440 | tf_op jit(solution)/shard_map/ppermute | solution.py:113
  87.8 38.3 %all-to-all-start = ((bf16[8,16,1600]{2,1,0:T(8,128)(2,1)}), bf16[8,16,1600]{2,1,0:T(8,128)(2,1)S(1)}, u32[]{:S(2)}, u32[]{:S(2)}) async-start(bf16[8,16,1600]{2,1,0:T(8,128)(2,1)} %shard_map.123), calls=%async_computation | async-start | bytes 851968 | tf_op jit(solution)/shard_map/all_to_all | solution.py:574
  96.3 14.3 %collective-permute-start.18 = (bf16[2,256,256]{2,1,0:T(8,128)(2,1)S(1)}, bf16[2,256,256]{2,1,0:T(8,128)(2,1)S(1)}, u32[]{:S(2)}, u32[]{:S(2)}) collective-permute-start(bf16[2,256,256]{2,1,0:T(8,128)(2,1)S(1)} %get-tuple-element.52.both_ref.refs_0_), channel_id=1, source_target_pairs={{0,8},{4,12},{8,0},{12,4},{16,24},{20,28},{24,16},{28,20},{1,9},{5... | collective-permute-start | bytes 786440 | tf_op jit(solution)/shard_map/ppermute | solution.py:113
  98.3 14.8 %collective-permute-start.15 = (bf16[2,256,256]{2,1,0:T(8,128)(2,1)S(1)}, bf16[2,256,256]{2,1,0:T(8,128)(2,1)S(1)}, u32[]{:S(2)}, u32[]{:S(2)}) collective-permute-start(bf16[2,256,256]{2,1,0:T(8,128)(2,1)S(1)} %collective-permute-done.14.refs_1_), channel_id=1, source_target_pairs={{0,4},{4,0},{8,12},{12,8},{16,20},{20,16},{24,28},{28,24},{1,5},{5... | collective-permute-start | bytes 786440 | tf_op jit(solution)/shard_map/ppermute | solution.py:113
  99.8 16.7 %collective-permute-start.20 = (bf16[2,256,256]{2,1,0:T(8,128)(2,1)S(1)}, bf16[2,256,256]{2,1,0:T(8,128)(2,1)S(1)}, u32[]{:S(2)}, u32[]{:S(2)}) collective-permute-start(bf16[2,256,256]{2,1,0:T(8,128)(2,1)S(1)} %get-tuple-element.52.both_ref.refs_0_), channel_id=1, source_target_pairs={{0,4},{4,0},{8,12},{12,8},{16,20},{20,16},{24,28},{28,24},{1,5},{5... | collective-permute-start | bytes 786440 | tf_op jit(solution)/shard_map/ppermute | solution.py:113
  110.5 10.6 %collective-permute-start.19 = (bf16[2,256,256]{2,1,0:T(8,128)(2,1)S(1)}, bf16[2,256,256]{2,1,0:T(8,128)(2,1)S(1)}, u32[]{:S(2)}, u32[]{:S(2)}) collective-permute-start(bf16[2,256,256]{2,1,0:T(8,128)(2,1)S(1)} %collective-permute-done.18.refs_0_), channel_id=1, source_target_pairs={{0,4},{4,0},{8,12},{12,8},{16,20},{20,16},{24,28},{28,24},{1,5},{5... | collective-permute-start | bytes 786440 | tf_op jit(solution)/shard_map/ppermute | solution.py:113
  112.1 9.2 %collective-permute-start.17 = (bf16[2,256,256]{2,1,0:T(8,128)(2,1)S(1)}, bf16[2,256,256]{2,1,0:T(8,128)(2,1)S(1)}, u32[]{:S(2)}, u32[]{:S(2)}) collective-permute-start(bf16[2,256,256]{2,1,0:T(8,128)(2,1)S(1)} %collective-permute-done.14.refs_1_), channel_id=1, source_target_pairs={{0,8},{4,12},{8,0},{12,4},{16,24},{20,28},{24,16},{28,20},{1,9},{5... | collective-permute-start | bytes 786440 | tf_op jit(solution)/shard_map/ppermute | solution.py:113
  113.1 11.3 %collective-permute-start.16 = (bf16[2,256,256]{2,1,0:T(8,128)(2,1)S(1)}, bf16[2,256,256]{2,1,0:T(8,128)(2,1)S(1)}, u32[]{:S(2)}, u32[]{:S(2)}) collective-permute-start(bf16[2,256,256]{2,1,0:T(8,128)(2,1)S(1)} %collective-permute-done.15.refs_0_), channel_id=1, source_target_pairs={{0,8},{4,12},{8,0},{12,4},{16,24},{20,28},{24,16},{28,20},{1,9},{5... | collective-permute-start | bytes 786440 | tf_op jit(solution)/shard_map/ppermute | solution.py:113
  124.4 1.8 %copy-start = (bf16[8,1600]{1,0:T(8,128)(2,1)S(1)}, bf16[8,1600]{1,0:T(8,128)(2,1)}, u32[]{:S(2)}) copy-start(bf16[8,1600]{1,0:T(8,128)(2,1)} %patch_ref.1) | copy-start | bytes 76804
  124.4 1.8 %copy-start.1 = (bf16[16,1600]{1,0:T(8,128)(2,1)S(1)}, bf16[16,1600]{1,0:T(8,128)(2,1)}, u32[]{:S(2)}) copy-start(bf16[16,1600]{1,0:T(8,128)(2,1)} %text_ref.1) | copy-start | bytes 153604
  124.4 1.8 %copy-start.2 = (s32[1,4]{1,0:T(1,128)S(1)}, s32[1,4]{1,0:T(1,128)}, u32[]{:S(2)}) copy-start(s32[1,4]{1,0:T(1,128)} %count_ref.1) | copy-start | bytes 52
  124.4 1.8 %copy-start.3 = (s32[1,8]{1,0:T(1,128)S(1)}, s32[1,8]{1,0:T(1,128)}, u32[]{:S(2)}) copy-start(s32[1,8]{1,0:T(1,128)} %place_ref.1) | copy-start | bytes 100

commit v9 on v8

--- a/solution.py
+++ b/solution.py
@@ -165,12 +165,12 @@
     ).astype(jnp.bfloat16)
 
 
-def repack_kernel(expand_at, project_at, *refs):
+def repack_kernel(distances, expand_at, project_at, *refs):
     blocks, sems = refs[:-1], refs[-1]
     units = blocks[0].shape[2]
     copies = []
-    for i, block in enumerate(blocks):
-        start = pl.multiple_of((lax.axis_index("dp") ^ (i + 1)) * units, 128)
+    for i, (distance, block) in enumerate(zip(distances, blocks)):
+        start = pl.multiple_of((lax.axis_index("dp") ^ distance) * units, 128)
         for k, source in enumerate((expand_at, project_at)):
             copies.append(
                 pltpu.make_async_copy(
@@ -465,7 +465,8 @@
 def gradient_groups(dp):
     order = unit_order(dp)
     order = order[1:dp] + order[dp : dp + 1] + order[:1] + order[dp + 1 :]
-    return [(0,)] + [tuple(order[i : i + 2]) for i in range(0, len(order), 2)]
+    pairs = [tuple(order[i : i + 2]) for i in range(0, len(order) - 3, 2)]
+    return [(0,), *pairs, tuple(order[-3:-2]), tuple(order[-2:])]
 
 
 def move_rows_plan(
@@ -505,17 +506,23 @@
         ],
         compiler_params=pltpu.CompilerParams(vmem_limit_bytes=12 << 20),
     )(*in_hbm(counts, positions, patches, cotangent))
-    blocks = pl.pallas_call(
-        repack_kernel,
-        out_shape=[shape((2, part, units), kept)] * (replicas - 1),
-        in_specs=[hbm] * 2,
-        out_specs=[VMEM_SPEC] * (replicas - 1),
-        scratch_shapes=[pltpu.SemaphoreType.DMA((2 * replicas - 2,))],
-        compiler_params=pltpu.CompilerParams(vmem_limit_bytes=12 << 20),
-    )(*in_hbm(expand_weight, project_turned))
+    far = dp_steps[0]
+    soon = tuple(range(far, 2 * far - 1))
+    later = tuple(i for i in range(1, replicas) if i not in soon)
+    blocks = {}
+    for distances in (soon, later):
+        packed = pl.pallas_call(
+            functools.partial(repack_kernel, distances),
+            out_shape=[shape((2, part, units), kept)] * len(distances),
+            in_specs=[hbm] * 2,
+            out_specs=[VMEM_SPEC] * len(distances),
+            scratch_shapes=[pltpu.SemaphoreType.DMA((2 * len(distances),))],
+            compiler_params=pltpu.CompilerParams(vmem_limit_bytes=12 << 20),
+        )(*in_hbm(expand_weight, project_turned))
+        blocks.update(zip(distances, packed))
     arrived = []
     for distance in range(1, replicas):
-        arrived.append(swap(blocks[distance - 1], "dp", distance))
+        arrived.append(swap(blocks[distance], "dp", distance))
 
     exchanges = [("dp", step) for step in dp_steps] + [("section", step) for step in section_steps]
     for axis, step in exchanges:

time: 128 us -> 128 us (level)
  starting transfers between devices: 45.2 us -> 43.7 us
    pallas_call x1 -> x2, Pallas kernels: 2.32 us -> 3.27 us  [move_rows_plan(): pl.pallas_call(functools.partial(repack_kernel, distances), out_shape=[sh...]
  transfers between devices with their start and end apart: 22 -> 22, of which waited for: 11 -> 11; matrix products, arithmetic and copies ran while one was open for 1% -> 0% of each run, Pallas kernels for 14% -> 15%
where the time goes in v9:
time: 128 us
  waiting for transfers between devices  58 us (45%)
  starting transfers between devices  43.7 us (34%)
  Pallas kernels  24.9 us (19%)
    ppermute x21, waiting for transfers between devices, swap(): return lax.ppermute(array, axis, [(i, i ^ step) for i in range(size)])  58 us
    ppermute x21, starting transfers between devices, swap(): return lax.ppermute(array, axis, [(i, i ^ step) for i in range(size)])  36.2 us
    pallas_call x5, Pallas kernels, weight_grads(): pl.pallas_call(functools.partial(weight_grad_kernel, distances), in_specs...  10.6 us
    all_to_all x1, starting transfers between devices, move_rows_plan(): tail = lax.all_to_all(tail, 'dp', split_axis=0, concat_axis=0, tiled=True)  7.54 us
    pallas_call x10, Pallas kernels, call(): pl.pallas_call(kernel, out_shape=out_shape, in_specs=[SMEM_SPEC] * len(sm...  6.5 us
    pallas_call x3, Pallas kernels, unpacking(): pl.pallas_call(functools.partial(kernel, group), out_shape=[*slices, *ext...  3.46 us
    pallas_call x2, Pallas kernels, move_rows_plan(): pl.pallas_call(functools.partial(repack_kernel, distances), out_shape=[sh...  3.27 us
  transfers between devices with their start and end apart: 22, of which 11 were waited for; matrix products, arithmetic and copies ran while one was open for 0% of the time, Pallas kernels for 15%

profile of v9, /device:TPU:0, one launch (start us, length us, event | category | flops | bytes accessed | tf_op | source)
XLA Modules:
  0.0 127.7 jit_solution(14208565522710990063)
XLA Ops:
  0.6 1.0 shard_map.115.first_ref
  1.7 4.1 %collective-permute-start.6 = (bf16[1,16,1600]{2,1,0:T(8,128)(2,1)S(1)}, bf16[1,16,1600]{2,1,0:T(8,128)(2,1)S(1)}, u32[]{:S(2)}, u32[]{:S(2)}) collective-permute-start(bf16[1,16,1600]{2,1,0:T(8,128)(2,1)S(1)} %shard_map.115.first_ref), channel_id=1, source_target_pairs={{0,16},{4,20},{8,24},{12,28},{16,0},{20,4},{24,8},{28,12},{1,17},{... | collective-permute-start | bytes 153608 | tf_op jit(solution)/shard_map/ppermute | solution.py:113
  5.8 2.7 %collective-permute-done.6.second_ref = bf16[1,16,1600]{2,1,0:T(8,128)(2,1)S(1)} collective-permute-done((bf16[1,16,1600]{2,1,0:T(8,128)(2,1)S(1)}, bf16[1,16,1600]{2,1,0:T(8,128)(2,1)S(1)}, u32[]{:S(2)}, u32[]{:S(2)}) %collective-permute-start.6) | collective-permute-done | bytes 51232 | tf_op jit(solution)/shard_map/ppermute | solution.py:113
  8.5 1.4 %collective-permute-start.7 = (bf16[2,16,1600]{2,1,0:T(8,128)(2,1)S(1)}, bf16[2,16,1600]{2,1,0:T(8,128)(2,1)S(1)}, u32[]{:S(2)}, u32[]{:S(2)}) collective-permute-start(bf16[2,16,1600]{2,1,0:T(8,128)(2,1)S(1)} %shard_map.116.first_ref), channel_id=1, source_target_pairs={{0,8},{4,12},{8,0},{12,4},{16,24},{20,28},{24,16},{28,20},{1,9},{5... | collective-permute-start | bytes 307208 | tf_op jit(solution)/shard_map/ppermute | solution.py:113
  9.9 3.4 %collective-permute-done.7.second_ref = bf16[2,16,1600]{2,1,0:T(8,128)(2,1)S(1)} collective-permute-done((bf16[2,16,1600]{2,1,0:T(8,128)(2,1)S(1)}, bf16[2,16,1600]{2,1,0:T(8,128)(2,1)S(1)}, u32[]{:S(2)}, u32[]{:S(2)}) %collective-permute-start.7) | collective-permute-done | bytes 102432 | tf_op jit(solution)/shard_map/ppermute | solution.py:113
  13.3 1.8 %collective-permute-start.8 = (bf16[4,16,1600]{2,1,0:T(8,128)(2,1)S(1)}, bf16[4,16,1600]{2,1,0:T(8,128)(2,1)S(1)}, u32[]{:S(2)}, u32[]{:S(2)}) collective-permute-start(bf16[4,16,1600]{2,1,0:T(8,128)(2,1)S(1)} %shard_map.117.first_ref), channel_id=1, source_target_pairs={{0,4},{4,0},{8,12},{12,8},{16,20},{20,16},{24,28},{28,24},{1,5},{5... | collective-permute-start | bytes 614408 | tf_op jit(solution)/shard_map/ppermute | solution.py:113
  15.1 4.1 %collective-permute-done.8.second_ref = bf16[4,16,1600]{2,1,0:T(8,128)(2,1)S(1)} collective-permute-done((bf16[4,16,1600]{2,1,0:T(8,128)(2,1)S(1)}, bf16[4,16,1600]{2,1,0:T(8,128)(2,1)S(1)}, u32[]{:S(2)}, u32[]{:S(2)}) %collective-permute-start.8) | collective-permute-done | bytes 204832 | tf_op jit(solution)/shard_map/ppermute | solution.py:113
  19.2 1.8 %collective-permute-start.9 = (bf16[8,16,1600]{2,1,0:T(8,128)(2,1)S(1)}, bf16[8,16,1600]{2,1,0:T(8,128)(2,1)S(1)}, u32[]{:S(2)}, u32[]{:S(2)}) collective-permute-start(bf16[8,16,1600]{2,1,0:T(8,128)(2,1)S(1)} %shard_map.118.first_ref), channel_id=1, source_target_pairs={{0,2},{1,3},{2,0},{3,1},{4,6},{5,7},{6,4},{7,5},{8,10},{9,11},{10,... | collective-permute-start | bytes 1228808 | tf_op jit(solution)/shard_map/ppermute | solution.py:113
  21.0 6.4 %collective-permute-done.9.second_ref = bf16[8,16,1600]{2,1,0:T(8,128)(2,1)S(1)} collective-permute-done((bf16[8,16,1600]{2,1,0:T(8,128)(2,1)S(1)}, bf16[8,16,1600]{2,1,0:T(8,128)(2,1)S(1)}, u32[]{:S(2)}, u32[]{:S(2)}) %collective-permute-start.9) | collective-permute-done | bytes 409632 | tf_op jit(solution)/shard_map/ppermute | solution.py:113
  27.6 1.2 shard_map.112
  28.8 2.7 %collective-permute-start.1 = (bf16[2,200,256]{2,1,0:T(8,128)(2,1)S(1)}, bf16[2,200,256]{2,1,0:T(8,128)(2,1)S(1)}, u32[]{:S(2)}, u32[]{:S(2)}) collective-permute-start(bf16[2,200,256]{2,1,0:T(8,128)(2,1)S(1)} %get-tuple-element.40), channel_id=1, source_target_pairs={{0,16},{4,20},{8,24},{12,28},{16,0},{20,4},{24,8},{28,12},{1,17},{... | collective-permute-start | bytes 614408 | tf_op jit(solution)/shard_map/ppermute | solution.py:113
  31.5 1.4 %collective-permute-start.2 = (bf16[2,200,256]{2,1,0:T(8,128)(2,1)S(1)}, bf16[2,200,256]{2,1,0:T(8,128)(2,1)S(1)}, u32[]{:S(2)}, u32[]{:S(2)}) collective-permute-start(bf16[2,200,256]{2,1,0:T(8,128)(2,1)S(1)} %get-tuple-element.41), channel_id=1, source_target_pairs={{0,20},{4,16},{8,28},{12,24},{16,4},{20,0},{24,12},{28,8},{1,21},{... | collective-permute-start | bytes 614408 | tf_op jit(solution)/shard_map/ppermute | solution.py:113
  32.9 3.6 %collective-permute-start.3 = (bf16[2,200,256]{2,1,0:T(8,128)(2,1)S(1)}, bf16[2,200,256]{2,1,0:T(8,128)(2,1)S(1)}, u32[]{:S(2)}, u32[]{:S(2)}) collective-permute-start(bf16[2,200,256]{2,1,0:T(8,128)(2,1)S(1)} %get-tuple-element.42), channel_id=1, source_target_pairs={{0,24},{4,28},{8,16},{12,20},{16,8},{20,12},{24,0},{28,4},{1,25},{... | collective-permute-start | bytes 614408 | tf_op jit(solution)/shard_map/ppermute | solution.py:113
  36.5 2.1 %shard_map.111 = (bf16[2,200,256]{2,1,0:T(8,128)(2,1)}, bf16[2,200,256]{2,1,0:T(8,128)(2,1)S(1)}, bf16[2,200,256]{2,1,0:T(8,128)(2,1)}, bf16[2,200,256]{2,1,0:T(8,128)(2,1)S(1)}) custom-call(bf16[200,2048]{1,0:T(8,128)(2,1)} %own_expand_at.1, bf16[200,2048]{1,0:T(8,128)(2,1)} %bitcast.6), custom_call_target="tpu_custom_call" | custom-call | tf_op jit(solution)/shard_map/pallas_call | solution.py:514
  38.6 0.6 collective-permute-start
  39.2 11.7 %collective-permute-done.1.refs_1_ = bf16[2,200,256]{2,1,0:T(8,128)(2,1)S(1)} collective-permute-done((bf16[2,200,256]{2,1,0:T(8,128)(2,1)S(1)}, bf16[2,200,256]{2,1,0:T(8,128)(2,1)S(1)}, u32[]{:S(2)}, u32[]{:S(2)}) %collective-permute-start.1) | collective-permute-done | bytes 204832 | tf_op jit(solution)/shard_map/ppermute | solution.py:113
  50.9 0.3 collective-permute-start.4
  51.1 5.3 %collective-permute-done.2.refs_2_ = bf16[2,200,256]{2,1,0:T(8,128)(2,1)S(1)} collective-permute-done((bf16[2,200,256]{2,1,0:T(8,128)(2,1)S(1)}, bf16[2,200,256]{2,1,0:T(8,128)(2,1)S(1)}, u32[]{:S(2)}, u32[]{:S(2)}) %collective-permute-start.2) | collective-permute-done | bytes 204832 | tf_op jit(solution)/shard_map/ppermute | solution.py:113
  56.4 2.9 %collective-permute-start.5 = (bf16[2,200,256]{2,1,0:T(8,128)(2,1)S(1)}, bf16[2,200,256]{2,1,0:T(8,128)(2,1)S(1)}, u32[]{:S(2)}, u32[]{:S(2)}) collective-permute-start(bf16[2,200,256]{2,1,0:T(8,128)(2,1)S(1)} %get-tuple-element.46), channel_id=1, source_target_pairs={{0,28},{4,24},{8,20},{12,16},{16,12},{20,8},{24,4},{28,0},{1,29},{... | collective-permute-start | bytes 614408 | tf_op jit(solution)/shard_map/ppermute | solution.py:113
  59.3 2.1 %collective-permute-start.11 = (bf16[2,200,256]{2,1,0:T(8,128)(2,1)}, bf16[2,200,256]{2,1,0:T(8,128)(2,1)}, u32[]{:S(2)}, u32[]{:S(2)}) collective-permute-start(bf16[2,200,256]{2,1,0:T(8,128)(2,1)} %get-tuple-element.51), channel_id=1, source_target_pairs={{0,12},{4,8},{8,4},{12,0},{16,28},{20,24},{24,20},{28,16},{1,13},{... | collective-permute-start | bytes 614408 | tf_op jit(solution)/shard_map/ppermute | solution.py:113
  61.4 0.1 pad_add_fusion.me_ref
  61.5 1.1 shard_map.113
  62.6 2.9 %collective-permute-done.5.refs_1_ = bf16[2,200,256]{2,1,0:T(8,128)(2,1)S(1)} collective-permute-done((bf16[2,200,256]{2,1,0:T(8,128)(2,1)S(1)}, bf16[2,200,256]{2,1,0:T(8,128)(2,1)S(1)}, u32[]{:S(2)}, u32[]{:S(2)}) %collective-permute-start.5) | collective-permute-done | bytes 204832 | tf_op jit(solution)/shard_map/ppermute | solution.py:113
  65.5 0.6 shard_map.114
  66.1 2.0 %shard_map.120 = (bf16[256,1600]{1,0:T(8,128)(2,1)S(1)}, bf16[256,1600]{1,0:T(8,128)(2,1)S(1)}, f32[16,1600]{1,0:T(8,128)S(1)}) custom-call(s32[2]{0:T(128)S(1)} %pad_add_fusion.me_ref, bf16[16,16,1600]{2,1,0:T(8,128)(2,1)S(1)} %shard_map.119.near_ref, bf16[16,16,1600]{2,1,0:T(8,128)(2,1)S(1)} %collective-permute-done.10.far_ref, f32[1,1600]{1,0:T(1,128)S(1)} %reshape.11.gain_ref), custom_call_target="tpu_custom_call" | custom-call | tf_op jit(solution)/shard_map/pallas_call | solution.py:432
  68.1 2.4 %collective-permute-done.11.refs_0_ = bf16[2,200,256]{2,1,0:T(8,128)(2,1)} collective-permute-done((bf16[2,200,256]{2,1,0:T(8,128)(2,1)}, bf16[2,200,256]{2,1,0:T(8,128)(2,1)}, u32[]{:S(2)}, u32[]{:S(2)}) %collective-permute-start.11) | collective-permute-done | bytes 204832 | tf_op jit(solution)/shard_map/ppermute | solution.py:113
  70.5 1.8 %shard_map.121 = (bf16[1600,256]{1,0:T(8,128)(2,1)S(1)}, bf16[1600,256]{1,0:T(8,128)(2,1)S(1)}, bf16[2,256,256]{2,1,0:T(8,128)(2,1)S(1)}) custom-call(bf16[1600,256]{1,0:T(8,128)(2,1)S(1)} %get-tuple-element.47.expand_part_ref, bf16[1600,256]{1,0:T(8,128)(2,1)S(1)} %get-tuple-element.48.project_part_ref, ...), custom_call_target="tpu_custom_call", output_to_operand_aliasing={{0}: (0, {}), {1}: (1, {})} | custom-call | tf_op jit(solution)/shard_map/pallas_call | solution.py:545
  72.3 1.4 %shard_map.122 = (f32[2,16,8,1600]{3,2,1,0:T(8,128)S(1)}, bf16[2,16,8,1600]{3,2,1,0:T(8,128)(2,1)S(1)}) custom-call(s32[2]{0:T(128)S(1)} %pad_add_fusion.me_ref, bf16[2,256,256]{2,1,0:T(8,128)(2,1)S(1)} %get-tuple-element.52.both_ref.refs_0_, bf16[1600,256]{1,0:T(8,128)(2,1)S(1)} %get-tuple-element.53.expand_ref, ...), custom_call_target="tpu_custom_call" | custom-call | tf_op jit(solution)/shard_map/pallas_call | solution.py:432
  73.8 2.4 %collective-permute-done.12.got_ref = bf16[2,16,8,1600]{3,2,1,0:T(8,128)(2,1)S(1)} collective-permute-done((bf16[2,16,8,1600]{3,2,1,0:T(8,128)(2,1)S(1)}, bf16[2,16,8,1600]{3,2,1,0:T(8,128)(2,1)S(1)}, u32[]{:S(2)}, u32[]{:S(2)}) %collective-permute-start.12) | collective-permute-done | bytes 819232 | tf_op jit(solution)/shard_map/ppermute | solution.py:113
  76.1 0.2 shard_map.123
  76.3 1.8 %collective-permute-start.13 = (bf16[2,8,8,1600]{3,2,1,0:T(8,128)(2,1)S(1)}, bf16[2,8,8,1600]{3,2,1,0:T(8,128)(2,1)S(1)}, u32[]{:S(2)}, u32[]{:S(2)}) collective-permute-start(bf16[2,8,8,1600]{3,2,1,0:T(8,128)(2,1)S(1)} %get-tuple-element.58), channel_id=1, source_target_pairs={{0,2},{1,3},{2,0},{3,1},{4,6},{5,7},{6,4},{7,5},{8,10},{9,11},{10,... | collective-permute-start | bytes 1228808 | tf_op jit(solution)/shard_map/ppermute | solution.py:113
  78.1 5.4 %collective-permute-start.16 = (bf16[2,256,256]{2,1,0:T(8,128)(2,1)S(1)}, bf16[2,256,256]{2,1,0:T(8,128)(2,1)S(1)}, u32[]{:S(2)}, u32[]{:S(2)}) collective-permute-start(bf16[2,256,256]{2,1,0:T(8,128)(2,1)S(1)} %get-tuple-element.52.both_ref.refs_0_), channel_id=1, source_target_pairs={{0,16},{4,20},{8,24},{12,28},{16,0},{20,4},{24,8},{28,12},{1,17},{... | collective-permute-start | bytes 786440 | tf_op jit(solution)/shard_map/ppermute | solution.py:113
  83.6 4.7 %collective-permute-done.13.got_ref = bf16[2,8,8,1600]{3,2,1,0:T(8,128)(2,1)S(1)} collective-permute-done((bf16[2,8,8,1600]{3,2,1,0:T(8,128)(2,1)S(1)}, bf16[2,8,8,1600]{3,2,1,0:T(8,128)(2,1)S(1)}, u32[]{:S(2)}, u32[]{:S(2)}) %collective-permute-start.13) | collective-permute-done | bytes 409632 | tf_op jit(solution)/shard_map/ppermute | solution.py:113
  88.3 0.8 shard_map.124
  89.1 7.5 %all-to-all-start = ((bf16[8,16,1600]{2,1,0:T(8,128)(2,1)}), bf16[8,16,1600]{2,1,0:T(8,128)(2,1)S(1)}, u32[]{:S(2)}, u32[]{:S(2)}) async-start(bf16[8,16,1600]{2,1,0:T(8,128)(2,1)} %shard_map.124), calls=%async_computation | async-start | bytes 851968 | tf_op jit(solution)/shard_map/all_to_all | solution.py:581
  96.6 2.0 %collective-permute-start.14 = (bf16[2,256,256]{2,1,0:T(8,128)(2,1)S(1)}, bf16[2,256,256]{2,1,0:T(8,128)(2,1)S(1)}, u32[]{:S(2)}, u32[]{:S(2)}) collective-permute-start(bf16[2,256,256]{2,1,0:T(8,128)(2,1)S(1)} %get-tuple-element.52.both_ref.refs_0_), channel_id=1, source_target_pairs={{0,8},{4,12},{8,0},{12,4},{16,24},{20,28},{24,16},{28,20},{1,9},{5... | collective-permute-start | bytes 786440 | tf_op jit(solution)/shard_map/ppermute | solution.py:113
  98.7 1.5 %collective-permute-start.17 = (bf16[2,256,256]{2,1,0:T(8,128)(2,1)S(1)}, bf16[2,256,256]{2,1,0:T(8,128)(2,1)S(1)}, u32[]{:S(2)}, u32[]{:S(2)}) collective-permute-start(bf16[2,256,256]{2,1,0:T(8,128)(2,1)S(1)} %collective-permute-done.16.refs_1_), channel_id=1, source_target_pairs={{0,4},{4,0},{8,12},{12,8},{16,20},{20,16},{24,28},{28,24},{1,5},{5... | collective-permute-start | bytes 786440 | tf_op jit(solution)/shard_map/ppermute | solution.py:113
  100.1 0.6 collective-permute-start.20
  100.8 12.1 %collective-permute-done.14.refs_0_ = bf16[2,256,256]{2,1,0:T(8,128)(2,1)S(1)} collective-permute-done((bf16[2,256,256]{2,1,0:T(8,128)(2,1)S(1)}, bf16[2,256,256]{2,1,0:T(8,128)(2,1)S(1)}, u32[]{:S(2)}, u32[]{:S(2)}) %collective-permute-start.14) | collective-permute-done | bytes 262176 | tf_op jit(solution)/shard_map/ppermute | solution.py:113
  112.9 0.9 collective-permute-start.15
  113.8 1.1 collective-permute-start.18
  114.9 0.5 shard_map.126
  115.4 1.8 %shard_map.127 = (bf16[1600,2048]{1,0:T(8,128)(2,1)}, bf16[1600,2048]{1,0:T(8,128)(2,1)}) custom-call(bf16[1600,256]{1,0:T(8,128)(2,1)S(1)} %get-tuple-element.62.grad_ref, bf16[1600,256]{1,0:T(8,128)(2,1)S(1)} %get-tuple-element.63.normed_ref, bf16[2,256,256]{2,1,0:T(8,128)(2,1)S(1)} %get-tuple-element.52.both_ref.refs_0_), custom_call_target="tpu_custom_call" | custom-call | flops 419430400 | bytes 3276800 | tf_op jit(solution)/shard_map/pallas_call | solution.py:411
  117.2 2.4 %shard_map.128 = (bf16[1600,2048]{1,0:T(8,128)(2,1)}, bf16[1600,2048]{1,0:T(8,128)(2,1)}) custom-call(bf16[1600,256]{1,0:T(8,128)(2,1)S(1)} %get-tuple-element.62.grad_ref, bf16[1600,256]{1,0:T(8,128)(2,1)S(1)} %get-tuple-element.63.normed_ref, ...), custom_call_target="tpu_custom_call", output_to_operand_aliasing={{0}: (4, {}), {1}: (5, {})} | custom-call | flops 838860800 | bytes 4915200 | tf_op jit(solution)/shard_map/pallas_call | solution.py:411
  119.5 2.4 %shard_map.129 = (bf16[1600,2048]{1,0:T(8,128)(2,1)}, bf16[1600,2048]{1,0:T(8,128)(2,1)}) custom-call(bf16[1600,256]{1,0:T(8,128)(2,1)S(1)} %get-tuple-element.62.grad_ref, bf16[1600,256]{1,0:T(8,128)(2,1)S(1)} %get-tuple-element.63.normed_ref, ...), custom_call_target="tpu_custom_call", output_to_operand_aliasing={{0}: (4, {}), {1}: (5, {})} | custom-call | flops 838860800 | bytes 4915200 | tf_op jit(solution)/shard_map/pallas_call | solution.py:411
  121.9 1.8 %shard_map.130 = (bf16[1600,2048]{1,0:T(8,128)(2,1)}, bf16[1600,2048]{1,0:T(8,128)(2,1)}) custom-call(bf16[1600,256]{1,0:T(8,128)(2,1)S(1)} %get-tuple-element.62.grad_ref, bf16[1600,256]{1,0:T(8,128)(2,1)S(1)} %get-tuple-element.63.normed_ref, ...), custom_call_target="tpu_custom_call", output_to_operand_aliasing={{0}: (3, {}), {1}: (4, {})} | custom-call | flops 419430400 | bytes 3276800 | tf_op jit(solution)/shard_map/pallas_call | solution.py:411
  123.8 2.4 %shard_map.131 = (bf16[1600,2048]{1,0:T(8,128)(2,1)}, bf16[1600,2048]{1,0:T(8,128)(2,1)}) custom-call(bf16[1600,256]{1,0:T(8,128)(2,1)S(1)} %get-tuple-element.62.grad_ref, bf16[1600,256]{1,0:T(8,128)(2,1)S(1)} %get-tuple-element.63.normed_ref, ...), custom_call_target="tpu_custom_call", output_to_operand_aliasing={{0}: (4, {}), {1}: (5, {})} | custom-call | flops 838860800 | bytes 4915200 | tf_op jit(solution)/shard_map/pallas_call | solution.py:411
  126.2 1.5 %shard_map.125 = (bf16[16,1600]{1,0:T(8,128)(2,1)}, bf16[8,1600]{1,0:T(8,128)(2,1)}) custom-call(s32[2]{0:T(128)S(1)} %pad_add_fusion.me_ref, s32[1,4]{1,0:T(1,128)S(1)} %copy-done.2, s32[1,8]{1,0:T(1,128)S(1)} %copy-done.3, bf16[8,16,1600]{2,1,0:T(8,128)(2,1)S(1)} %all-to-all-done.tail_ref, f32[16,1600]{1,0:T(8,128)S(1)} %get-tuple-element.59.extra_ref, ...), custom_call_target="tpu_custom_call" | custom-call | tf_op jit(solution)/shard_map/pallas_call | solution.py:432
  (29 shorter events, 0.4 us)
Async XLA Ops:
  0.6 60.8 %copy-start.4 = (f32[1600]{0:T(1024)S(1)}, f32[1600]{0:T(1024)}, u32[]{:S(2)}) copy-start(f32[1600]{0:T(1024)} %param.9) | copy-start | bytes 19204
  1.7 6.8 %collective-permute-start.6 = (bf16[1,16,1600]{2,1,0:T(8,128)(2,1)S(1)}, bf16[1,16,1600]{2,1,0:T(8,128)(2,1)S(1)}, u32[]{:S(2)}, u32[]{:S(2)}) collective-permute-start(bf16[1,16,1600]{2,1,0:T(8,128)(2,1)S(1)} %shard_map.115.first_ref), channel_id=1, source_target_pairs={{0,16},{4,20},{8,24},{12,28},{16,0},{20,4},{24,8},{28,12},{1,17},{... | collective-permute-start | bytes 153608 | tf_op jit(solution)/shard_map/ppermute | solution.py:113
  8.5 4.8 %collective-permute-start.7 = (bf16[2,16,1600]{2,1,0:T(8,128)(2,1)S(1)}, bf16[2,16,1600]{2,1,0:T(8,128)(2,1)S(1)}, u32[]{:S(2)}, u32[]{:S(2)}) collective-permute-start(bf16[2,16,1600]{2,1,0:T(8,128)(2,1)S(1)} %shard_map.116.first_ref), channel_id=1, source_target_pairs={{0,8},{4,12},{8,0},{12,4},{16,24},{20,28},{24,16},{28,20},{1,9},{5... | collective-permute-start | bytes 307208 | tf_op jit(solution)/shard_map/ppermute | solution.py:113
  13.3 5.9 %collective-permute-start.8 = (bf16[4,16,1600]{2,1,0:T(8,128)(2,1)S(1)}, bf16[4,16,1600]{2,1,0:T(8,128)(2,1)S(1)}, u32[]{:S(2)}, u32[]{:S(2)}) collective-permute-start(bf16[4,16,1600]{2,1,0:T(8,128)(2,1)S(1)} %shard_map.117.first_ref), channel_id=1, source_target_pairs={{0,4},{4,0},{8,12},{12,8},{16,20},{20,16},{24,28},{28,24},{1,5},{5... | collective-permute-start | bytes 614408 | tf_op jit(solution)/shard_map/ppermute | solution.py:113
  19.2 8.2 %collective-permute-start.9 = (bf16[8,16,1600]{2,1,0:T(8,128)(2,1)S(1)}, bf16[8,16,1600]{2,1,0:T(8,128)(2,1)S(1)}, u32[]{:S(2)}, u32[]{:S(2)}) collective-permute-start(bf16[8,16,1600]{2,1,0:T(8,128)(2,1)S(1)} %shard_map.118.first_ref), channel_id=1, source_target_pairs={{0,2},{1,3},{2,0},{3,1},{4,6},{5,7},{6,4},{7,5},{8,10},{9,11},{10,... | collective-permute-start | bytes 1228808 | tf_op jit(solution)/shard_map/ppermute | solution.py:113
  27.5 38.6 %collective-permute-start.10 = (bf16[16,16,1600]{2,1,0:T(8,128)(2,1)S(1)}, bf16[16,16,1600]{2,1,0:T(8,128)(2,1)S(1)}, u32[]{:S(2)}, u32[]{:S(2)}) collective-permute-start(bf16[16,16,1600]{2,1,0:T(8,128)(2,1)S(1)} %shard_map.119.near_ref), channel_id=1, source_target_pairs={{0,1},{1,0},{2,3},{3,2},{4,5},{5,4},{6,7},{7,6},{8,9},{9,8},{10,11... | collective-permute-start | bytes 2457608 | tf_op jit(solution)/shard_map/ppermute | solution.py:113
  28.8 22.1 %collective-permute-start.1 = (bf16[2,200,256]{2,1,0:T(8,128)(2,1)S(1)}, bf16[2,200,256]{2,1,0:T(8,128)(2,1)S(1)}, u32[]{:S(2)}, u32[]{:S(2)}) collective-permute-start(bf16[2,200,256]{2,1,0:T(8,128)(2,1)S(1)} %get-tuple-element.40), channel_id=1, source_target_pairs={{0,16},{4,20},{8,24},{12,28},{16,0},{20,4},{24,8},{28,12},{1,17},{... | collective-permute-start | bytes 614408 | tf_op jit(solution)/shard_map/ppermute | solution.py:113
  31.5 24.9 %collective-permute-start.2 = (bf16[2,200,256]{2,1,0:T(8,128)(2,1)S(1)}, bf16[2,200,256]{2,1,0:T(8,128)(2,1)S(1)}, u32[]{:S(2)}, u32[]{:S(2)}) collective-permute-start(bf16[2,200,256]{2,1,0:T(8,128)(2,1)S(1)} %get-tuple-element.41), channel_id=1, source_target_pairs={{0,20},{4,16},{8,28},{12,24},{16,4},{20,0},{24,12},{28,8},{1,21},{... | collective-permute-start | bytes 614408 | tf_op jit(solution)/shard_map/ppermute | solution.py:113
  32.9 26.4 %collective-permute-start.3 = (bf16[2,200,256]{2,1,0:T(8,128)(2,1)S(1)}, bf16[2,200,256]{2,1,0:T(8,128)(2,1)S(1)}, u32[]{:S(2)}, u32[]{:S(2)}) collective-permute-start(bf16[2,200,256]{2,1,0:T(8,128)(2,1)S(1)} %get-tuple-element.42), channel_id=1, source_target_pairs={{0,24},{4,28},{8,16},{12,20},{16,8},{20,12},{24,0},{28,4},{1,25},{... | collective-permute-start | bytes 614408 | tf_op jit(solution)/shard_map/ppermute | solution.py:113
  38.6 22.9 %collective-permute-start = (bf16[2,200,256]{2,1,0:T(8,128)(2,1)}, bf16[2,200,256]{2,1,0:T(8,128)(2,1)S(1)}, u32[]{:S(2)}, u32[]{:S(2)}) collective-permute-start(bf16[2,200,256]{2,1,0:T(8,128)(2,1)} %get-tuple-element.39), channel_id=1, source_target_pairs={{0,4},{4,0},{8,12},{12,8},{16,20},{20,16},{24,28},{28,24},{1,5},{5... | collective-permute-start | bytes 614408 | tf_op jit(solution)/shard_map/ppermute | solution.py:113
  50.9 11.8 %collective-permute-start.4 = (bf16[2,200,256]{2,1,0:T(8,128)(2,1)S(1)}, bf16[2,200,256]{2,1,0:T(8,128)(2,1)S(1)}, u32[]{:S(2)}, u32[]{:S(2)}) collective-permute-start(bf16[2,200,256]{2,1,0:T(8,128)(2,1)S(1)} %get-tuple-element.45), channel_id=1, source_target_pairs={{0,8},{4,12},{8,0},{12,4},{16,24},{20,28},{24,16},{28,20},{1,9},{5... | collective-permute-start | bytes 614408 | tf_op jit(solution)/shard_map/ppermute | solution.py:113
  56.4 9.1 %collective-permute-start.5 = (bf16[2,200,256]{2,1,0:T(8,128)(2,1)S(1)}, bf16[2,200,256]{2,1,0:T(8,128)(2,1)S(1)}, u32[]{:S(2)}, u32[]{:S(2)}) collective-permute-start(bf16[2,200,256]{2,1,0:T(8,128)(2,1)S(1)} %get-tuple-element.46), channel_id=1, source_target_pairs={{0,28},{4,24},{8,20},{12,16},{16,12},{20,8},{24,4},{28,0},{1,29},{... | collective-permute-start | bytes 614408 | tf_op jit(solution)/shard_map/ppermute | solution.py:113
  59.3 11.2 %collective-permute-start.11 = (bf16[2,200,256]{2,1,0:T(8,128)(2,1)}, bf16[2,200,256]{2,1,0:T(8,128)(2,1)}, u32[]{:S(2)}, u32[]{:S(2)}) collective-permute-start(bf16[2,200,256]{2,1,0:T(8,128)(2,1)} %get-tuple-element.51), channel_id=1, source_target_pairs={{0,12},{4,8},{8,4},{12,0},{16,28},{20,24},{24,20},{28,16},{1,13},{... | collective-permute-start | bytes 614408 | tf_op jit(solution)/shard_map/ppermute | solution.py:113
  73.7 2.4 %collective-permute-start.12 = (bf16[2,16,8,1600]{3,2,1,0:T(8,128)(2,1)S(1)}, bf16[2,16,8,1600]{3,2,1,0:T(8,128)(2,1)S(1)}, u32[]{:S(2)}, u32[]{:S(2)}) collective-permute-start(bf16[2,16,8,1600]{3,2,1,0:T(8,128)(2,1)S(1)} %get-tuple-element.56), channel_id=1, source_target_pairs={{0,1},{1,0},{2,3},{3,2},{4,5},{5,4},{6,7},{7,6},{8,9},{9,8},{10,11... | collective-permute-start | bytes 2457608 | tf_op jit(solution)/shard_map/ppermute | solution.py:113
  76.3 11.9 %collective-permute-start.13 = (bf16[2,8,8,1600]{3,2,1,0:T(8,128)(2,1)S(1)}, bf16[2,8,8,1600]{3,2,1,0:T(8,128)(2,1)S(1)}, u32[]{:S(2)}, u32[]{:S(2)}) collective-permute-start(bf16[2,8,8,1600]{3,2,1,0:T(8,128)(2,1)S(1)} %get-tuple-element.58), channel_id=1, source_target_pairs={{0,2},{1,3},{2,0},{3,1},{4,6},{5,7},{6,4},{7,5},{8,10},{9,11},{10,... | collective-permute-start | bytes 1228808 | tf_op jit(solution)/shard_map/ppermute | solution.py:113
  78.1 20.5 %collective-permute-start.16 = (bf16[2,256,256]{2,1,0:T(8,128)(2,1)S(1)}, bf16[2,256,256]{2,1,0:T(8,128)(2,1)S(1)}, u32[]{:S(2)}, u32[]{:S(2)}) collective-permute-start(bf16[2,256,256]{2,1,0:T(8,128)(2,1)S(1)} %get-tuple-element.52.both_ref.refs_0_), channel_id=1, source_target_pairs={{0,16},{4,20},{8,24},{12,28},{16,0},{20,4},{24,8},{28,12},{1,17},{... | collective-permute-start | bytes 786440 | tf_op jit(solution)/shard_map/ppermute | solution.py:113
  89.1 37.1 %all-to-all-start = ((bf16[8,16,1600]{2,1,0:T(8,128)(2,1)}), bf16[8,16,1600]{2,1,0:T(8,128)(2,1)S(1)}, u32[]{:S(2)}, u32[]{:S(2)}) async-start(bf16[8,16,1600]{2,1,0:T(8,128)(2,1)} %shard_map.124), calls=%async_computation | async-start | bytes 851968 | tf_op jit(solution)/shard_map/all_to_all | solution.py:581
  96.6 16.2 %collective-permute-start.14 = (bf16[2,256,256]{2,1,0:T(8,128)(2,1)S(1)}, bf16[2,256,256]{2,1,0:T(8,128)(2,1)S(1)}, u32[]{:S(2)}, u32[]{:S(2)}) collective-permute-start(bf16[2,256,256]{2,1,0:T(8,128)(2,1)S(1)} %get-tuple-element.52.both_ref.refs_0_), channel_id=1, source_target_pairs={{0,8},{4,12},{8,0},{12,4},{16,24},{20,28},{24,16},{28,20},{1,9},{5... | collective-permute-start | bytes 786440 | tf_op jit(solution)/shard_map/ppermute | solution.py:113
  98.7 15.1 %collective-permute-start.17 = (bf16[2,256,256]{2,1,0:T(8,128)(2,1)S(1)}, bf16[2,256,256]{2,1,0:T(8,128)(2,1)S(1)}, u32[]{:S(2)}, u32[]{:S(2)}) collective-permute-start(bf16[2,256,256]{2,1,0:T(8,128)(2,1)S(1)} %collective-permute-done.16.refs_1_), channel_id=1, source_target_pairs={{0,4},{4,0},{8,12},{12,8},{16,20},{20,16},{24,28},{28,24},{1,5},{5... | collective-permute-start | bytes 786440 | tf_op jit(solution)/shard_map/ppermute | solution.py:113
  100.1 17.1 %collective-permute-start.20 = (bf16[2,256,256]{2,1,0:T(8,128)(2,1)S(1)}, bf16[2,256,256]{2,1,0:T(8,128)(2,1)S(1)}, u32[]{:S(2)}, u32[]{:S(2)}) collective-permute-start(bf16[2,256,256]{2,1,0:T(8,128)(2,1)S(1)} %get-tuple-element.52.both_ref.refs_0_), channel_id=1, source_target_pairs={{0,4},{4,0},{8,12},{12,8},{16,20},{20,16},{24,28},{28,24},{1,5},{5... | collective-permute-start | bytes 786440 | tf_op jit(solution)/shard_map/ppermute | solution.py:113
  100.7 21.2 %collective-permute-start.19 = (bf16[2,256,256]{2,1,0:T(8,128)(2,1)S(1)}, bf16[2,256,256]{2,1,0:T(8,128)(2,1)S(1)}, u32[]{:S(2)}, u32[]{:S(2)}) collective-permute-start(bf16[2,256,256]{2,1,0:T(8,128)(2,1)S(1)} %collective-permute-done.16.refs_1_), channel_id=1, source_target_pairs={{0,8},{4,12},{8,0},{12,4},{16,24},{20,28},{24,16},{28,20},{1,9},{5... | collective-permute-start | bytes 786440 | tf_op jit(solution)/shard_map/ppermute | solution.py:113
  112.9 10.9 %collective-permute-start.15 = (bf16[2,256,256]{2,1,0:T(8,128)(2,1)S(1)}, bf16[2,256,256]{2,1,0:T(8,128)(2,1)S(1)}, u32[]{:S(2)}, u32[]{:S(2)}) collective-permute-start(bf16[2,256,256]{2,1,0:T(8,128)(2,1)S(1)} %collective-permute-done.14.refs_0_), channel_id=1, source_target_pairs={{0,4},{4,0},{8,12},{12,8},{16,20},{20,16},{24,28},{28,24},{1,5},{5... | collective-permute-start | bytes 786440 | tf_op jit(solution)/shard_map/ppermute | solution.py:113
  113.8 10.0 %collective-permute-start.18 = (bf16[2,256,256]{2,1,0:T(8,128)(2,1)S(1)}, bf16[2,256,256]{2,1,0:T(8,128)(2,1)S(1)}, u32[]{:S(2)}, u32[]{:S(2)}) collective-permute-start(bf16[2,256,256]{2,1,0:T(8,128)(2,1)S(1)} %collective-permute-done.17.refs_0_), channel_id=1, source_target_pairs={{0,8},{4,12},{8,0},{12,4},{16,24},{20,28},{24,16},{28,20},{1,9},{5... | collective-permute-start | bytes 786440 | tf_op jit(solution)/shard_map/ppermute | solution.py:113
  123.7 2.4 %copy-start = (bf16[8,1600]{1,0:T(8,128)(2,1)S(1)}, bf16[8,1600]{1,0:T(8,128)(2,1)}, u32[]{:S(2)}) copy-start(bf16[8,1600]{1,0:T(8,128)(2,1)} %patch_ref.1) | copy-start | bytes 76804
  123.7 2.4 %copy-start.1 = (bf16[16,1600]{1,0:T(8,128)(2,1)S(1)}, bf16[16,1600]{1,0:T(8,128)(2,1)}, u32[]{:S(2)}) copy-start(bf16[16,1600]{1,0:T(8,128)(2,1)} %text_ref.1) | copy-start | bytes 153604
  123.8 2.4 %copy-start.2 = (s32[1,4]{1,0:T(1,128)S(1)}, s32[1,4]{1,0:T(1,128)}, u32[]{:S(2)}) copy-start(s32[1,4]{1,0:T(1,128)} %count_ref.1) | copy-start | bytes 52
  123.8 2.4 %copy-start.3 = (s32[1,8]{1,0:T(1,128)S(1)}, s32[1,8]{1,0:T(1,128)}, u32[]{:S(2)}) copy-start(s32[1,8]{1,0:T(1,128)} %place_ref.1) | copy-start | bytes 100
